TPU v7x, 32 devices: a whole 2x2x4 slice. The times are simulated.
32 devices in a mesh: clip: 8 (over z, x), tm: 4 (over y, core).
Axes of the slice: x: 2, y: 2, z: 4, core: 2. Of those that a mesh axis runs over, the one named last changes fastest.
Arguments:
- features: bfloat16 [16, 1024, 512], P('clip', 'tm'), may hold values from -6 to 6
- cotangent: bfloat16 [16, 1024, 512], P('clip', 'tm'), may hold values from -6 to 6
- clip_lengths: int32 [16], P('clip'), may hold values from 128 to 1024, as said below
- code_ids: int32 [4, 16, 1024], P(None, 'clip', 'tm'), may hold values from 0 to 1023
- step_count: int32 [1], replicated, may hold values from 2 to 20
- dilated_kernel_weight: float32 [3, 512, 256], P(None, None, 'clip'), may hold values from -0.15625 to 0.15625
- pointwise_conv: float32 [256, 512], P(None, 'clip'), may hold values from -0.75 to 0.75
- codebooks: float32 [4, 1024, 256], P(None, 'clip'), may hold values from -6 to 6
- dilated_first_moment: float32 [3, 512, 256], P(None, None, 'clip'), may hold values from -1 to 1
- dilated_second_moment: float32 [3, 512, 256], P(None, None, 'clip'), may hold values from 0.028995216 to 0.11598086
- pointwise_first: float32 [256, 512], P(None, 'clip'), may hold values from -1 to 1
- pointwise_second: float32 [256, 512], P(None, 'clip'), may hold values from 0.028995216 to 0.11598086
- codebook_first: float32 [4, 1024, 256], P(None, 'clip'), may hold values from -0.01953125 to 0.01953125
- codebook_second: float32 [4, 1024, 256], P(None, 'clip'), may hold values from 9.745614e-06 to 3.8982456e-05
Outputs:
- quantized: bfloat16 [16, 1024, 512], P('clip', 'tm')
- features_gradient: float32 [16, 1024, 512], P('clip', 'tm')
- grad_norm: float32 [1], replicated
- dilated_new: float32 [3, 512, 256], P(None, None, 'clip')
- dilated_grad: float32 [3, 512, 256], P(None, None, 'clip')
- dilated_square: float32 [3, 512, 256], P(None, None, 'clip')
- pointwise_new: float32 [256, 512], P(None, 'clip')
- pointwise_grad: float32 [256, 512], P(None, 'clip')
- pointwise_square: float32 [256, 512], P(None, 'clip')
- codebook_new: float32 [4, 1024, 256], P(None, 'clip')
- codebook_grad: float32 [4, 1024, 256], P(None, 'clip')
- codebook_square: float32 [4, 1024, 256], P(None, 'clip')
Inputs may be any that keep to these rules, and one draw needn't show every extreme that they name: `clip_lengths`: the number of valid frames of each clip; frames from it on are padding; clip 0 is always full.
All inputs are finite; a program needn't handle non-finite values.
Results may differ from a plain program's by a relative error of at most 0.001.
The roundings to bfloat16 on the way count: a program that leaves them out, or rounds other values in their place, can miss the bound.
Values may be sent and summed in bfloat16 or wider, within the bound.
No kernel may reach another device: no remote copies, remote signals or barrier semaphores. Data moves between devices by JAX's collectives and lax.ppermute only.
A program may use at most 64 MiB of HBM per device.

v0:
```python
import jax
import jax.numpy as jnp
from jax import lax
from jax.sharding import PartitionSpec as P

HID = 256
CODES = 1024
GROUPS = 2
LEVELS = 2
KERNEL = 3
DILATION = 3
DG = 256


COMMIT = 0.25
FIRST_DECAY = 0.9
SECOND_DECAY = 0.99
EPSILON = 1e-08
WEIGHT_DECAY = 0.01
BITRATE_FACTOR = 0.02
RATE_CODE = 0.5


def extended(cells, sides, width):
    for axis, dim in sides:
        count = lax.axis_size(axis)
        ends = count - 1
        head = lax.slice_in_dim(cells, 0, width, axis=dim)
        tail = lax.slice_in_dim(cells, cells.shape[dim] - width, cells.shape[dim], axis=dim)
        cells = jnp.concatenate(
            [
                lax.ppermute(tail, axis, [(i, (i + 1) % count) for i in range(ends)]),
                cells,
                lax.ppermute(head, axis, [((i + 1) % count, i) for i in range(ends)]),
            ],
            axis=dim,
        )
    return cells


def elu_slope(values):
    return jnp.where(values > 0, 1.0, jnp.exp(jnp.minimum(values, 0.0)))


def adamw_update(weight, first, second, grad, rate, completed_steps):
    first_new = FIRST_DECAY * first + (1.0 - FIRST_DECAY) * grad
    second_new = SECOND_DECAY * second + (1.0 - SECOND_DECAY) * grad * grad
    first_hat = first_new / (1.0 - FIRST_DECAY**completed_steps)
    second_hat = second_new / (1.0 - SECOND_DECAY**completed_steps)
    weight_new = weight - rate * (
        first_hat / (jnp.sqrt(second_hat) + EPSILON) + WEIGHT_DECAY * weight
    )
    return (weight_new, grad, second_new)


def shards(
    features,
    cotangent,
    clip_lengths,
    code_ids,
    step_count,
    dilated_kernel_weight,
    pointwise_conv,
    codebooks,
    dilated_first_moment,
    dilated_second_moment,
    pointwise_first,
    pointwise_second,
    codebook_first,
    codebook_second,
):
    clip_rank = lax.axis_index("clip")
    time_rank = lax.axis_index("tm")
    dilated_full, pointwise_full, table_full = (
        lax.all_gather(dilated_kernel_weight.astype(jnp.bfloat16), "clip", axis=2, tiled=True),
        lax.all_gather(pointwise_conv.astype(jnp.bfloat16), "clip", axis=1, tiled=True),
        lax.all_gather(codebooks.astype(jnp.bfloat16), "clip", axis=1, tiled=True),
    )
    clips, frames, width = features.shape
    positions = time_rank * frames + lax.broadcasted_iota(jnp.int32, (clips, frames, 1), 1)
    frame_mask = (positions < clip_lengths[:, None, None]).astype(jnp.float32)
    start = features.astype(jnp.float32) * frame_mask
    activated = jax.nn.elu(start).astype(jnp.bfloat16)
    padded = extended(activated, (("tm", 1),), DILATION)
    hidden = jnp.zeros((clips, frames, HID), jnp.float32)
    for tap_index in range(KERNEL):
        window = padded[:, tap_index * DILATION : tap_index * DILATION + frames]
        hidden = hidden + jnp.einsum(
            "btc,cd->btd", window, dilated_full[tap_index], preferred_element_type=jnp.float32
        )
    gated = jax.nn.elu(hidden).astype(jnp.bfloat16)
    latent = start + jnp.einsum(
        "btk,kd->btd", gated, pointwise_full, preferred_element_type=jnp.float32
    )
    backs = cotangent.astype(jnp.float32) * frame_mask
    latent_parts = []
    quant_parts = []
    table_grads = []
    for group in range(GROUPS):
        residual_part = latent[..., group * DG : (group + 1) * DG]
        moving_grad = backs[..., group * DG : (group + 1) * DG]
        summed = jnp.zeros_like(residual_part)
        for level in range(LEVELS):
            slot = group * LEVELS + level
            chosen = jnp.take(table_full[slot], code_ids[slot], axis=0).astype(jnp.float32)
            moving_grad = moving_grad + 2.0 * COMMIT * frame_mask * (residual_part - chosen)
            code_grad = 2.0 * frame_mask * (chosen - residual_part)
            table_grads.append(
                jax.ops.segment_sum(
                    code_grad.reshape(-1, DG), code_ids[slot].reshape(-1), num_segments=CODES
                )
            )
            residual_part = residual_part - chosen
            summed = summed + chosen
        latent_parts.append(moving_grad)
        quant_parts.append(summed)
    quantized = (jnp.concatenate(quant_parts, axis=-1) * frame_mask).astype(jnp.bfloat16)
    latent_grad = jnp.concatenate(latent_parts, axis=-1)
    table_grad = jnp.stack(table_grads, axis=0)
    branch_grad = latent_grad.astype(jnp.bfloat16)
    pointwise_grad = jnp.einsum(
        "btk,btd->kd", gated, branch_grad, preferred_element_type=jnp.float32
    )
    gated_grad = jnp.einsum(
        "btd,kd->btk", branch_grad, pointwise_full, preferred_element_type=jnp.float32
    )
    hidden_grad = (gated_grad * elu_slope(hidden)).astype(jnp.bfloat16)
    padded_grad = extended(hidden_grad, (("tm", 1),), DILATION)
    dilated_parts = []
    act_grad = jnp.zeros((clips, frames, width), jnp.float32)
    for tap_index in range(KERNEL):
        window = padded[:, tap_index * DILATION : tap_index * DILATION + frames]
        dilated_parts.append(
            jnp.einsum("btc,btd->cd", window, hidden_grad, preferred_element_type=jnp.float32)
        )
        offset = (KERNEL - 1 - tap_index) * DILATION
        act_grad = act_grad + jnp.einsum(
            "btd,cd->btc",
            padded_grad[:, offset : offset + frames],
            dilated_full[tap_index],
            preferred_element_type=jnp.float32,
        )
    dilated_grad = jnp.stack(dilated_parts, axis=0)
    features_gradient = frame_mask * (latent_grad + elu_slope(start) * act_grad)
    local_grads = (dilated_grad, pointwise_grad, table_grad)
    whole = lax.psum((local_grads[0], local_grads[1], local_grads[2]), ("clip", "tm"))
    squared = sum((jnp.sum(piece * piece) for piece in whole))
    shares = (
        lax.dynamic_slice_in_dim(
            whole[0], clip_rank * dilated_kernel_weight.shape[2], dilated_kernel_weight.shape[2], 2
        ),
        lax.dynamic_slice_in_dim(
            whole[1], clip_rank * pointwise_conv.shape[1], pointwise_conv.shape[1], 1
        ),
        lax.dynamic_slice_in_dim(whole[2], clip_rank * codebooks.shape[1], codebooks.shape[1], 1),
    )
    count = dilated_full.size + pointwise_full.size + table_full.size
    limit = jnp.sqrt(jnp.float32(count))
    gradient_norm_total = jnp.sqrt(squared)
    clip_scale_factor = limit / jnp.maximum(gradient_norm_total, limit)
    completed_steps = step_count[0].astype(jnp.float32)
    dilation_factor = adamw_update(
        dilated_kernel_weight,
        dilated_first_moment,
        dilated_second_moment,
        shares[0] * clip_scale_factor,
        BITRATE_FACTOR,
        completed_steps,
    )
    pointwise_kernel = adamw_update(
        pointwise_conv,
        pointwise_first,
        pointwise_second,
        shares[1] * clip_scale_factor,
        BITRATE_FACTOR,
        completed_steps,
    )
    codebook_tensor = adamw_update(
        codebooks,
        codebook_first,
        codebook_second,
        shares[2] * clip_scale_factor,
        RATE_CODE,
        completed_steps,
    )
    return (
        quantized,
        features_gradient,
        gradient_norm_total.reshape(1),
        dilation_factor[0],
        dilation_factor[1],
        dilation_factor[2],
        pointwise_kernel[0],
        pointwise_kernel[1],
        pointwise_kernel[2],
        codebook_tensor[0],
        codebook_tensor[1],
        codebook_tensor[2],
    )


def solution(mesh):
    in_specs = (
        P("clip", "tm", None),
        P("clip", "tm", None),
        P("clip"),
        P(None, "clip", "tm"),
        P(),
        P(None, None, "clip"),
        P(None, "clip"),
        P(None, "clip", None),
        P(None, None, "clip"),
        P(None, None, "clip"),
        P(None, "clip"),
        P(None, "clip"),
        P(None, "clip", None),
        P(None, "clip", None),
    )
    out_specs = (
        P("clip", "tm", None),
        P("clip", "tm", None),
        P(),
        P(None, None, "clip"),
        P(None, None, "clip"),
        P(None, None, "clip"),
        P(None, "clip"),
        P(None, "clip"),
        P(None, "clip"),
        P(None, "clip", None),
        P(None, "clip", None),
        P(None, "clip", None),
    )
    return jax.shard_map(shards, mesh=mesh, in_specs=in_specs, out_specs=out_specs, check_vma=False)
```

profile of v0, /device:TPU:0, one launch (start us, length us, event | category | flops | bytes accessed | tf_op | source)
XLA Modules:
  0.0 310.3 jit_solution(5738353770341371367)
XLA Ops:
  7.2 1.8 convert_element_type.54
  9.8 2.8 convert_multiply_fusion.1
  12.7 1.3 collective-permute-start.1
  14.0 3.0 collective-permute-start
  17.8 0.9 convert_element_type.64
  19.6 33.2 %all_gather.11 = bf16[256,512]{0,1:T(8,128)(2,1)S(1)} all-gather(bf16[256,64]{0,1:T(8,128)(2,1)S(1)} %convert_element_type.66), channel_id=1, replica_groups=mesh['clip'=8,'tm'=4] {'clip'}, dimensions={1}, use_global_device_ids=true | all-gather | bytes 294912 | tf_op jit(solution)/shard_map/all_gather | solution.py:76
  52.9 33.2 %all_gather.10 = bf16[3,512,256]{1,2,0:T(8,128)(2,1)S(1)} all-gather(bf16[3,512,32]{1,2,0:T(8,128)(2,1)S(1)} %convert_element_type.64), channel_id=1, replica_groups=mesh['clip'=8,'tm'=4] {'clip'}, dimensions={2}, use_global_device_ids=true | all-gather | bytes 884736 | tf_op jit(solution)/shard_map/all_gather | solution.py:75
  88.0 1.4 convolution_add_fusion.1
  89.4 1.7 slice_bitcast_fusion.3
  91.1 2.6 gather_fusion.1
  93.7 2.6 gather_fusion
  96.2 2.6 gather_fusion.3
  98.8 1.9 gather_fusion.2
  100.8 3.3 %fusion.12 = (f32[2,256,256]{2,1,0:T(8,128)S(1)}, f32[2,256,256]{2,1,0:T(8,128)S(1)}, f32[2,256,256]{2,1,0:T(8,128)}, f32[2,256,256]{2,1,0:T(8,128)}, f32[2,256,...) fusion(f32[2,256,512]{2,1,0:T(8,128)S(1)} %copy-done, ...), kind=kLoop, calls=%fused_computation.50 | loop fusion | flops 3932160 | bytes 7346176 | tf_op jit(solution)/shard_map/add | solution.py:106
  104.4 1.3 convolution_bitcast_fusion
  106.1 4.2 %scatter_custom_fusion.3 = f32[1024,256]{1,0:T(8,128)S(1)} fusion(s32[512]{0:T(512)S(1)} %bitcast.135, f32[512,256]{1,0:T(8,128)} %bitcast.127, f32[]{:T(128)} %constant.35.clone.1), kind=kCustom, calls=%fused_computation.74 | custom fusion | flops 131072 | bytes 1049088 | tf_op jit(solution)/shard_map/scatter-add | solution.py:109
  110.4 4.8 %scatter_custom_fusion.2 = f32[1024,256]{1,0:T(8,128)} fusion(s32[512]{0:T(512)S(1)} %bitcast.134, f32[512,256]{1,0:T(8,128)} %bitcast.126, f32[]{:T(128)} %constant.35.clone.1), kind=kCustom, calls=%fused_computation.76 | custom fusion | flops 131072 | bytes 1049088 | tf_op jit(solution)/shard_map/scatter-add | solution.py:109
  115.1 4.8 %scatter_custom_fusion.1 = f32[1024,256]{1,0:T(8,128)} fusion(s32[512]{0:T(512)S(1)} %bitcast.133, f32[512,256]{1,0:T(8,128)} %bitcast.125, f32[]{:T(128)} %constant.35.clone.1), kind=kCustom, calls=%fused_computation.78 | custom fusion | flops 131072 | bytes 1049088 | tf_op jit(solution)/shard_map/scatter-add | solution.py:109
  119.9 4.8 %scatter_custom_fusion = f32[1024,256]{1,0:T(8,128)} fusion(s32[512]{0:T(512)S(1)} %bitcast.132, f32[512,256]{1,0:T(8,128)} %bitcast.124, f32[]{:T(128)} %constant.35.clone.1), kind=kCustom, calls=%fused_computation.80 | custom fusion | flops 131072 | bytes 1049088 | tf_op jit(solution)/shard_map/scatter-add | solution.py:109
  125.4 1.3 pad_maximum_fusion.1
  126.8 2.3 pad_maximum_fusion
  130.0 1.4 collective-permute-start.3
  131.4 1.5 collective-permute-start.2
  134.5 1.4 collective-permute-done.2
  136.0 1.6 fusion.3
  137.6 149.0 %all-reduce.3.cloned.1.call-done = (f32[3,512,256]{1,2,0:T(8,128)}, f32[256,512]{0,1:T(8,128)}, f32[4,1024,256]{2,1,0:T(8,128)}) async-done(((f32[3,512,256]{1,2,0:T(8,128)}, f32[256,512]{0,1:T(8,128)}, f32[4,1024,256]{2,1,0:T(8,128)}), (f32[3,512,256]{1,2,0:T(8,128)}, f32[256,512]{0,1:T(8,128)}, f32[4,1024,256]{2,1,0:T(8,128)})) %all-reduce.3.cloned.1.call-update) | async-done | bytes 6291472 | tf_op jit(solution)/shard_map/psum | solution.py:146
  286.6 2.4 multiply_reduce_fusion.1
  289.0 1.8 multiply_reduce_fusion.2
  290.8 3.9 %multiply_reduce_fusion = f32[]{:T(128)} fusion(f32[4,1024,256]{2,1,0:T(8,128)} %get-tuple-element.39), kind=kLoop, calls=%fused_computation.9 | loop fusion | flops 2097151 | bytes 4194308 | tf_op jit(solution)/shard_map/reduce_sum | solution.py:147
  296.7 1.8 multiply_subtract_fusion.1
  298.5 1.5 multiply_subtract_fusion.2
  300.1 2.3 multiply_subtract_fusion
  (93 shorter events, 7.4 us)
Async XLA Ops:
  7.2 45.6 %copy-start.26 = (s32[2]{0:T(128)S(1)}, s32[2]{0:T(128)}, u32[]{:S(2)}) copy-start(s32[2]{0:T(128)} %param.18) | copy-start | bytes 28
  7.2 45.7 %copy-start.23 = (s32[4,2,256]{2,1,0:T(2,128)S(1)}, s32[4,2,256]{2,1,0:T(2,128)}, u32[]{:S(2)}) copy-start(s32[4,2,256]{2,1,0:T(2,128)} %param.19) | copy-start | bytes 24580
  7.2 82.2 %all-gather.2.cloned.1.call-start = ((), (), s32[]{:S(2)}) async-start(), calls=%async_computation | async-start | bytes 2359296 | tf_op jit(solution)/shard_map/all_gather | solution.py:77
  9.0 277.5 %all-reduce.3.cloned.1.call-start = ((), (), s32[]{:S(2)}) async-start(), calls=%async_computation.1 | async-start | bytes 12582912 | tf_op jit(solution)/shard_map/psum | solution.py:146
  9.8 78.2 %copy-start.11 = (bf16[2,256,512]{2,1,0:T(8,128)(2,1)S(1)}, bf16[2,256,512]{2,1,0:T(8,128)(2,1)}, u32[]{:S(2)}) copy-start(bf16[2,256,512]{2,1,0:T(8,128)(2,1)} %param.16) | copy-start | bytes 1572868
  12.7 73.8 %collective-permute-start.1 = (bf16[2,3,512]{2,1,0:T(4,128)(2,1)S(1)}, bf16[2,3,512]{2,1,0:T(4,128)(2,1)S(1)}, u32[]{:S(2)}, u32[]{:S(2)}) collective-permute-start(bf16[2,3,512]{2,1,0:T(4,128)(2,1)S(1)} %get-tuple-element.62), channel_id=1, source_target_pairs={{1,0},{2,1},{3,2},{5,4},{6,5},{7,6},{9,8},{10,9},{11,10},{13,12},{... | collective-permute-start | bytes 18440 | tf_op jit(solution)/shard_map/ppermute | solution.py:34
  14.0 72.9 %collective-permute-start = (bf16[2,3,512]{2,1,0:T(4,128)(2,1)S(1)}, bf16[2,3,512]{2,1,0:T(4,128)(2,1)S(1)}, u32[]{:S(2)}, u32[]{:S(2)}) collective-permute-start(bf16[2,3,512]{2,1,0:T(4,128)(2,1)S(1)} %get-tuple-element.61), channel_id=1, source_target_pairs={{0,1},{1,2},{2,3},{4,5},{5,6},{6,7},{8,9},{9,10},{10,11},{12,13},{... | collective-permute-start | bytes 18440 | tf_op jit(solution)/shard_map/ppermute | solution.py:32
  52.8 34.4 %copy-start.19 = (bf16[256,512]{0,1:T(8,128)(2,1)}, bf16[256,512]{0,1:T(8,128)(2,1)S(1)}, u32[]{:S(2)}) copy-start(bf16[256,512]{0,1:T(8,128)(2,1)S(1)} %all_gather.11) | copy-start | bytes 786436
  96.2 4.5 %copy-start = (f32[2,256,512]{2,1,0:T(8,128)S(1)}, f32[2,256,512]{2,1,0:T(8,128)}, u32[]{:S(2)}) copy-start(f32[2,256,512]{2,1,0:T(8,128)} %get-tuple-element.77) | copy-start | bytes 3145732
  100.8 3.3 %copy-start.17 = (f32[2,256,256]{2,1,0:T(8,128)S(1)}, f32[2,256,256]{2,1,0:T(8,128)}, u32[]{:S(2)}) copy-start(f32[2,256,256]{2,1,0:T(8,128)} %copy-done.16) | copy-start | bytes 1572868
  100.8 3.3 %copy-start.20 = (bf16[256,512]{0,1:T(8,128)(2,1)S(1)}, bf16[256,512]{0,1:T(8,128)(2,1)}, u32[]{:S(2)}) copy-start(bf16[256,512]{0,1:T(8,128)(2,1)} %copy-done.19) | copy-start | bytes 786436
  104.1 2.0 copy-start.7
  104.1 2.0 copy-start.9
  124.7 2.0 copy-start.1
  124.7 2.0 copy-start.2
  124.7 2.0 copy-start.3
  129.0 4.2 %copy-start.5 = (f32[2,256,256]{2,1,0:T(8,128)S(1)}, f32[2,256,256]{2,1,0:T(8,128)}, u32[]{:S(2)}) copy-start(f32[2,256,256]{2,1,0:T(8,128)} %get-tuple-element.59) | copy-start | bytes 1572868
  129.1 4.2 %copy-start.6 = (f32[2,256,256]{2,1,0:T(8,128)S(1)}, f32[2,256,256]{2,1,0:T(8,128)}, u32[]{:S(2)}) copy-start(f32[2,256,256]{2,1,0:T(8,128)} %get-tuple-element.60) | copy-start | bytes 1572868
  129.1 6.9 %copy-start.8 = (f32[2,256,256]{2,1,0:T(8,128)S(1)}, f32[2,256,256]{2,1,0:T(8,128)}, u32[]{:S(2)}) copy-start(f32[2,256,256]{2,1,0:T(8,128)} %copy-done.7) | copy-start | bytes 1572868
  129.1 6.9 %copy-start.10 = (f32[2,256,256]{2,1,0:T(8,128)S(1)}, f32[2,256,256]{2,1,0:T(8,128)}, u32[]{:S(2)}) copy-start(f32[2,256,256]{2,1,0:T(8,128)} %copy-done.9) | copy-start | bytes 1572868
  130.0 6.0 %copy-start.12 = (bf16[2,256,512]{2,1,0:T(8,128)(2,1)S(1)}, bf16[2,256,512]{2,1,0:T(8,128)(2,1)}, u32[]{:S(2)}) copy-start(bf16[2,256,512]{2,1,0:T(8,128)(2,1)} %param.16) | copy-start | bytes 1572868
  130.0 4.2 %collective-permute-start.3 = (bf16[2,3,256]{2,1,0:T(4,128)(2,1)S(1)}, bf16[2,3,256]{2,1,0:T(4,128)(2,1)S(1)}, u32[]{:S(2)}, u32[]{:S(2)}) collective-permute-start(bf16[2,3,256]{2,1,0:T(4,128)(2,1)S(1)} %get-tuple-element.64), channel_id=1, source_target_pairs={{0,1},{1,2},{2,3},{4,5},{5,6},{6,7},{8,9},{9,10},{10,11},{12,13},{... | collective-permute-start | bytes 9224 | tf_op jit(solution)/shard_map/ppermute | solution.py:32
  131.4 4.5 %collective-permute-start.2 = (bf16[2,3,256]{2,1,0:T(4,128)(2,1)S(1)}, bf16[2,3,256]{2,1,0:T(4,128)(2,1)S(1)}, u32[]{:S(2)}, u32[]{:S(2)}) collective-permute-start(bf16[2,3,256]{2,1,0:T(4,128)(2,1)S(1)} %get-tuple-element.63), channel_id=1, source_target_pairs={{1,0},{2,1},{3,2},{5,4},{6,5},{7,6},{9,8},{10,9},{11,10},{13,12},{... | collective-permute-start | bytes 9224 | tf_op jit(solution)/shard_map/ppermute | solution.py:34
  137.5 159.1 %copy-start.13 = (f32[3,512,32]{1,2,0:T(8,128)S(1)}, f32[3,512,32]{1,2,0:T(8,128)}, u32[]{:S(2)}) copy-start(f32[3,512,32]{1,2,0:T(8,128)} %param.21) | copy-start | bytes 589828
  137.5 159.2 %copy-start.21 = (f32[3,512,32]{1,2,0:T(8,128)S(1)}, f32[3,512,32]{1,2,0:T(8,128)}, u32[]{:S(2)}) copy-start(f32[3,512,32]{1,2,0:T(8,128)} %param.24) | copy-start | bytes 589828
  137.5 159.2 %copy-start.22 = (f32[3,512,32]{1,2,0:T(8,128)S(1)}, f32[3,512,32]{1,2,0:T(8,128)}, u32[]{:S(2)}) copy-start(f32[3,512,32]{1,2,0:T(8,128)} %param.25) | copy-start | bytes 589828
  137.5 161.0 %copy-start.18 = (f32[256,64]{0,1:T(8,128)S(1)}, f32[256,64]{0,1:T(8,128)}, u32[]{:S(2)}) copy-start(f32[256,64]{0,1:T(8,128)} %param.22) | copy-start | bytes 196612
  137.5 161.0 %copy-start.24 = (f32[256,64]{0,1:T(8,128)S(1)}, f32[256,64]{0,1:T(8,128)}, u32[]{:S(2)}) copy-start(f32[256,64]{0,1:T(8,128)} %param.26) | copy-start | bytes 196612
  137.5 161.0 %copy-start.25 = (f32[256,64]{0,1:T(8,128)S(1)}, f32[256,64]{0,1:T(8,128)}, u32[]{:S(2)}) copy-start(f32[256,64]{0,1:T(8,128)} %param.27) | copy-start | bytes 196612
  137.6 162.5 %copy-start.4 = (f32[4,128,256]{2,1,0:T(8,128)S(1)}, f32[4,128,256]{2,1,0:T(8,128)}, u32[]{:S(2)}) copy-start(f32[4,128,256]{2,1,0:T(8,128)} %param.23) | copy-start | bytes 1572868
  137.6 162.5 %copy-start.14 = (f32[4,128,256]{2,1,0:T(8,128)S(1)}, f32[4,128,256]{2,1,0:T(8,128)}, u32[]{:S(2)}) copy-start(f32[4,128,256]{2,1,0:T(8,128)} %param.28) | copy-start | bytes 1572868
  137.6 162.5 %copy-start.15 = (f32[4,128,256]{2,1,0:T(8,128)S(1)}, f32[4,128,256]{2,1,0:T(8,128)}, u32[]{:S(2)}) copy-start(f32[4,128,256]{2,1,0:T(8,128)} %param.29) | copy-start | bytes 1572868
  (1 other events, 0.8 us)
Sparse Core Ops, SparseCore 0:
  10.8 58.7 all-gather.1
  129.2 157.3 all-reduce.2
where the time goes:
time: 311 us; the launch traced here: 310 us
  waiting for transfers between devices  150 us (48%)
  blocking collectives  66.4 us (21%)
  other arithmetic  48.1 us (15%)
  between operations  18.6 us (6%)
  local copies, waits for them, and re-layouts  12.2 us (4%)
  starting transfers between devices  7.34 us (2%)
  matrix products  7.32 us (2%)
    psum x1, waiting for transfers between devices, shards(): lax.psum((local_grads[0], local_grads[1], local_grads[2]), ('clip', 'tm'))  149 us
    all_gather x1, blocking collectives, shards(): lax.all_gather(pointwise_conv.astype(jnp.bfloat16), 'clip', axis=1, tiled...  33.2 us
    all_gather x1, blocking collectives, shards(): lax.all_gather(dilated_kernel_weight.astype(jnp.bfloat16), 'clip', axis=2...  33.2 us
    scatter-add x4, other arithmetic, shards(): jax.ops.segment_sum(code_grad.reshape(-1, DG), code_ids[slot].reshape(-1)...  18.6 us
    gather x4, local copies, waits for them, and re-layouts, shards(): jnp.take(table_full[slot], code_ids[slot], axis=0).astype(jnp.float32)  9.65 us
    reduce_sum x3, other arithmetic, shards(): squared = sum((jnp.sum(piece * piece) for piece in whole))  8.06 us
  transfers between devices with their start and end apart: 6, of which 2 were waited for; matrix products, arithmetic and copies ran while one was open for 4% of the time, Pallas kernels for 0%

commit v1 on v0

v1 whole, which is shorter than its diff:
```python
import functools

import jax
import jax.numpy as jnp
from jax import lax
from jax.experimental import pallas as pl
from jax.experimental.pallas import tpu as pltpu
from jax.sharding import PartitionSpec as P

D = 512
HID = 256
CODES = 1024
GROUPS = 2
LEVELS = 2
SLOTS = 4
KERNEL = 3
DILATION = 3
DG = 256
PAD = 8
HALO = 6

COMMIT = 0.25
FIRST_DECAY = 0.9
SECOND_DECAY = 0.99
EPSILON = 1e-08
WEIGHT_DECAY = 0.01
BITRATE_FACTOR = 0.02
RATE_CODE = 0.5

F32 = jnp.float32
BF16 = jnp.bfloat16
NT = (((1,), (1,)), ((), ()))
TN = (((0,), (0,)), ((), ()))
LEVEL_STEPS = 256.0
TOP = 32000.0
SCALE_GROUPS = 4
VMEM_LIMIT = 56 * 1024 * 1024


def params():
    return pltpu.CompilerParams(vmem_limit_bytes=VMEM_LIMIT)


def whole(count):
    return [pl.BlockSpec(memory_space=pltpu.VMEM)] * count


def mm(a, b):
    return jnp.dot(a, b, preferred_element_type=F32)


def mmg(a, b, dims):
    return lax.dot_general(a, b, dims, preferred_element_type=F32)


def slope(v):
    return jnp.where(v > 0, 1.0, jnp.exp(jnp.minimum(v, 0.0)))


def elu(v):
    return jnp.where(v > 0, v, jnp.exp(jnp.minimum(v, 0.0)) - 1.0)


def swap(value, clip_mask, time_mask):
    clips, times = lax.axis_size("clip"), lax.axis_size("tm")
    pairs = [
        (c * times + t, (c ^ clip_mask) * times + (t ^ time_mask))
        for c in range(clips)
        for t in range(times)
    ]
    return lax.ppermute(value, ("clip", "tm"), pairs)


def forward_kernel(
    clips,
    frames,
    half,
    block,
    meta_ref,
    f_ref,
    c_ref,
    idc_ref,
    idr_ref,
    d_ref,
    pwt_ref,
    *refs,
):
    pieces = refs[:8]
    (
        quant_ref,
        keep_ref,
        send_ref,
        act_ref,
        gated_ref,
        bg_ref,
        lg_ref,
        hs_ref,
        tab_ref,
        cho_ref,
        cgs_ref,
    ) = refs[8:]
    span = frames + 2 * PAD
    rows = clips * span
    me = meta_ref[0]
    base = meta_ref[1]
    row = lax.broadcasted_iota(jnp.int32, (span, DG), 0)
    where = row - PAD + base
    marks = []
    inner = (row >= PAD) & (row < PAD + frames)
    inside = []
    for clip in range(clips):
        good = (where >= 0) & (where < meta_ref[2 + clip])
        marks.append(jnp.where(good, 1.0, 0.0))
        inside.append(jnp.where(good & inner, 2.0, 0.0))
    mask = jnp.concatenate(marks, axis=0)
    twice = jnp.concatenate(inside, axis=0)
    mask2 = jnp.concatenate([mask, mask], axis=1)
    start = f_ref[...].astype(F32) * mask2
    act = elu(start).astype(BF16)
    act_ref[...] = act
    taps = mmg(act, d_ref[...], NT)
    hidden = (
        pltpu.roll(taps[:, :HID], DILATION, 0)
        + taps[:, HID : 2 * HID]
        + pltpu.roll(taps[:, 2 * HID :], rows - DILATION, 0)
    )
    hs_ref[...] = slope(hidden)
    gated = elu(hidden).astype(BF16)
    gated_ref[...] = gated
    latent = start + mmg(gated, pwt_ref[...], NT)
    codes = lax.broadcasted_iota(jnp.int32, (rows, CODES), 1)
    for other in range(SLOTS):
        slot = me ^ other
        for x in range(2):
            piece = pieces[other * 2 + x]
            for z in range(half):
                spot = (x * half + z) * block
                tab_ref[spot : spot + block, :] = piece[z, 64 * 8 // (2 * half) :, :]
        hot = jnp.where(codes == idc_ref[slot], 1.0, 0.0).astype(BF16)
        cho_ref[slot] = mm(hot, tab_ref[...])
    for group in range(GROUPS):
        at = slice(group * DG, (group + 1) * DG)
        first = cho_ref[2 * group]
        second = cho_ref[2 * group + 1]
        residual = latent[:, at]
        gap = residual - first
        gap2 = gap - second
        grad = mask * (c_ref[:, at].astype(F32) + 2.0 * COMMIT * (gap + gap2))
        quant = (mask * (first + second)).astype(BF16)
        bg_ref[:, at] = grad.astype(BF16)
        for clip in range(clips):
            local = slice(clip * span + PAD, clip * span + PAD + frames)
            to = slice(clip * frames, (clip + 1) * frames)
            lg_ref[to, at] = grad[local]
            quant_ref[to, at] = quant[local]
            for level, diff in ((0, gap), (1, gap2)):
                code_grad = -(twice * diff)[local]
                high = code_grad.astype(BF16)
                cgs_ref[2 * group + level, to, :DG] = high
                cgs_ref[2 * group + level, to, DG:] = (code_grad - high.astype(F32)).astype(BF16)
    codes = lax.broadcasted_iota(jnp.int32, (CODES, clips * frames), 0)
    for other in range(SLOTS):
        slot = me ^ other
        hot = jnp.where(codes == idr_ref[slot], 1.0, 0.0).astype(BF16)
        both = mm(hot, cgs_ref[slot])
        total = both[:, :DG] + both[:, DG:]
        if other % 2 == 0:
            keep_ref[other // 2] = total
        else:
            send_ref[other // 2] = total


def backward_kernel(
    clips,
    frames,
    meta_ref,
    f_ref,
    act_ref,
    gated_ref,
    bg_ref,
    lg_ref,
    hs_ref,
    d_ref,
    pwt_ref,
    fg_ref,
    dil_ref,
    pw_ref,
):
    span = frames + 2 * PAD
    rows = clips * span
    base = meta_ref[1]

    def local(value):
        return jnp.concatenate(
            [value[c * span + PAD : c * span + PAD + frames] for c in range(clips)], axis=0
        )

    bg = bg_ref[...]
    hidden_grad = (mm(bg, pwt_ref[...]) * hs_ref[...]).astype(BF16)
    wide = hidden_grad.astype(F32)
    mine = local(hidden_grad)
    pw_ref[...] = mmg(local(bg), local(gated_ref[...]), TN)
    act = act_ref[...].astype(F32)
    windows = [
        local(pltpu.roll(act, DILATION, 0).astype(BF16)),
        local(act_ref[...]),
        local(pltpu.roll(act, rows - DILATION, 0).astype(BF16)),
    ]
    for tap in range(KERNEL):
        dil_ref[tap] = mmg(mine, windows[tap], TN)
    shifted = jnp.concatenate(
        [
            local(pltpu.roll(wide, rows - DILATION, 0).astype(BF16)),
            mine,
            local(pltpu.roll(wide, DILATION, 0).astype(BF16)),
        ],
        axis=1,
    )
    act_grad = mm(shifted, d_ref[...])
    row = lax.broadcasted_iota(jnp.int32, (frames, D), 0) + base
    mask = jnp.concatenate(
        [jnp.where(row < meta_ref[2 + c], 1.0, 0.0) for c in range(clips)], axis=0
    )
    start = local(f_ref[...].astype(F32)) * mask
    fg_ref[...] = mask * (lg_ref[...] + slope(start) * act_grad)


def pack_part(value):
    count = SCALE_GROUPS
    rows = value.shape[0]
    size = rows // count
    steps, levels = [], []
    for group in range(count):
        part = value[group * size : (group + 1) * size]
        top = jnp.maximum(jnp.max(jnp.abs(part), axis=0, keepdims=True), 1e-30)
        level = jnp.ceil(jnp.log2(top) * LEVEL_STEPS)
        scale = jnp.exp2(level / -LEVEL_STEPS) * TOP
        steps.append(jnp.round(part * scale).astype(jnp.int32))
        levels.append(level)
    return steps, levels


def unpack_part(steps, level):
    return steps.astype(jnp.int32).astype(F32) * (
        jnp.exp2(level.astype(jnp.int32).astype(F32) / LEVEL_STEPS) / TOP
    )


def plane_kernel(half, rows, keep_ref, got_ref, own_ref, *outs):
    for part in range(4):
        jy, x = part // 2, part % 2
        levels = []
        for z in range(half):
            at = slice((x * half + z) * rows, (x * half + z + 1) * rows)
            value = keep_ref[jy, at, :] + got_ref[jy, at, :]
            if part == 0:
                own_ref[z] = value
                continue
            out = outs[part - 1]
            steps, more = pack_part(value)
            size = rows // SCALE_GROUPS
            for group, step in enumerate(steps):
                out[z * rows + group * size : z * rows + (group + 1) * size, :] = step.astype(
                    jnp.int16
                )
            levels += more
        if part:
            tail = jnp.concatenate(levels, axis=0).astype(jnp.int32)
            outs[part - 1][half * rows :, :] = tail.astype(jnp.int16)


def line_kernel(half, sizes, *refs):
    kinds = len(sizes)
    owns = refs[:kinds]
    gots = refs[kinds : kinds + 3 * kinds]
    own_ref = refs[4 * kinds]
    outs = refs[4 * kinds + 1 :]
    for z in range(half):
        place = 0
        levels = []
        for kind, rows in enumerate(sizes):
            size = rows // SCALE_GROUPS
            value = owns[kind][z]
            pieces = [value[g * size : (g + 1) * size] for g in range(SCALE_GROUPS)]
            for got in gots[3 * kind : 3 * kind + 3]:
                tail = got[half * rows :, :]
                for g in range(SCALE_GROUPS):
                    index = z * SCALE_GROUPS + g
                    pieces[g] = pieces[g] + unpack_part(
                        got[z * rows + g * size : z * rows + (g + 1) * size, :],
                        tail[index : index + 1],
                    )
            if z == 0:
                for g in range(SCALE_GROUPS):
                    own_ref[place + g * size : place + (g + 1) * size, :] = pieces[g]
            else:
                steps, more = pack_part(jnp.concatenate(pieces, axis=0))
                for g, step in enumerate(steps):
                    outs[z - 1][place + g * size : place + (g + 1) * size, :] = step.astype(
                        jnp.int16
                    )
                levels += more
            place += rows
        if z:
            pad = jnp.zeros((outs[z - 1].shape[0] - place - len(levels), DG), F32)
            tail = jnp.concatenate(levels + [pad], axis=0).astype(jnp.int32)
            outs[z - 1][place:, :] = tail.astype(jnp.int16)


def final_kernel(half, sizes, own_ref, *refs):
    gots, out_ref = refs[:-1], refs[-1]
    place, index = 0, 0
    total = sum(sizes)
    for rows in sizes:
        size = rows // SCALE_GROUPS
        for _ in range(SCALE_GROUPS):
            at = slice(place, place + size)
            value = own_ref[at, :]
            for got in gots:
                tail = got[total:, :]
                value = value + unpack_part(got[at, :], tail[index : index + 1])
            out_ref[at, :] = value
            place += size
            index += 1


def adamw_update(weight, first, second, grad, rate, completed_steps):
    first_new = FIRST_DECAY * first + (1.0 - FIRST_DECAY) * grad
    second_new = SECOND_DECAY * second + (1.0 - SECOND_DECAY) * grad * grad
    first_hat = first_new / (1.0 - FIRST_DECAY**completed_steps)
    second_hat = second_new / (1.0 - SECOND_DECAY**completed_steps)
    weight_new = weight - rate * (
        first_hat / (jnp.sqrt(second_hat) + EPSILON) + WEIGHT_DECAY * weight
    )
    return (weight_new, grad, second_new)


def halo(features, cotangent, code_ids):
    times = lax.axis_size("tm")
    clips, frames, _ = features.shape
    ids = jnp.moveaxis(code_ids, 0, 2)
    high, low = ids // 32, ids % 32
    packed = jnp.concatenate(
        [features, cotangent, high.astype(BF16), low.astype(BF16)], axis=2
    )
    from_left = lax.ppermute(
        packed[:, frames - HALO :], "tm", [(i, i + 1) for i in range(times - 1)]
    )
    from_right = lax.ppermute(packed[:, :HALO], "tm", [(i + 1, i) for i in range(times - 1)])
    gap = ((0, 0), (PAD - HALO, 0), (0, 0)), ((0, 0), (0, PAD - HALO), (0, 0))
    left, right = jnp.pad(from_left, gap[0]), jnp.pad(from_right, gap[1])

    def around(value, low_at, high_at):
        return jnp.concatenate([left[..., low_at:high_at], value, right[..., low_at:high_at]], axis=1)

    f = around(features, 0, D)
    c = around(cotangent, D, 2 * D)

    def decoded(part):
        part = part.astype(jnp.int32)
        return part[..., 2 * D : 2 * D + SLOTS] * 32 + part[..., 2 * D + SLOTS :]

    i = jnp.concatenate([decoded(left), ids, decoded(right)], axis=1)
    rows = clips * (frames + 2 * PAD)
    return f.reshape(rows, D), c.reshape(rows, D), i.reshape(rows, SLOTS)


def shards(
    features,
    cotangent,
    clip_lengths,
    code_ids,
    step_count,
    dilated_kernel_weight,
    pointwise_conv,
    codebooks,
    dilated_first_moment,
    dilated_second_moment,
    pointwise_first,
    pointwise_second,
    codebook_first,
    codebook_second,
):
    ranks, times = lax.axis_size("clip"), lax.axis_size("tm")
    rank, time = lax.axis_index("clip"), lax.axis_index("tm")
    clips, frames, _ = features.shape
    half = ranks // 2
    out_rows = HID // ranks
    block = CODES // ranks
    small = 2 * out_rows
    rows = clips * (frames + 2 * PAD)

    taps = dilated_kernel_weight.astype(BF16).transpose(0, 2, 1)
    taps = taps.reshape(KERNEL, out_rows, 2, DG).transpose(0, 2, 1, 3).reshape(KERNEL, small, DG)
    points = pointwise_conv.astype(BF16).transpose(1, 0)[None]
    quarters = jnp.concatenate(
        [jnp.concatenate([taps, points], axis=0), codebooks.astype(BF16)], axis=1
    )
    mine = lax.dynamic_index_in_dim(quarters, time, 0, keepdims=False)

    f, c, ids = halo(features, cotangent, code_ids)

    line = [mine] + [swap(mine, 2 * z, 0) for z in range(1, half)]
    line = jnp.stack(line, axis=0)
    plane = {
        (0, 0): line,
        (0, 1): swap(line, 1, 0),
        (2, 0): swap(line, 0, 2),
        (2, 1): swap(line, 1, 2),
    }
    pieces = []
    for other in range(4):
        for x in range(2):
            value = plane[(other & 2, x)]
            pieces.append(swap(value, 0, 1) if other & 1 else value)

    order = rank ^ jnp.arange(ranks)
    stacked = jnp.stack(
        [
            jnp.stack([pieces[o * 2][:, :small], pieces[o * 2 + 1][:, :small]], axis=1).reshape(
                ranks, small, DG
            )
            for o in range(4)
        ],
        axis=0,
    )
    stacked = jnp.take(jnp.take(stacked, time ^ jnp.arange(4), axis=0), order, axis=1)
    dil = stacked[:KERNEL].reshape(KERNEL, ranks, 2, out_rows, DG)
    dil = dil.transpose(0, 1, 3, 2, 4).reshape(KERNEL * HID, D)
    pwt = stacked[3].reshape(D, HID)

    def renamed(values):
        step = (values // block) ^ rank
        place = (step & 1) * half + (step >> 1)
        return place * block + values % block

    idc = renamed(ids).T[:, :, None]
    idr = renamed(code_ids).reshape(SLOTS, 1, clips * frames)
    meta = jnp.concatenate([jnp.stack([time, time * frames]), clip_lengths]).astype(jnp.int32)

    smem = pl.BlockSpec(memory_space=pltpu.SMEM)
    shape = jax.ShapeDtypeStruct
    quant, keep, send, act, gated, bg, lg, hs = pl.pallas_call(
        functools.partial(forward_kernel, clips, frames, half, block),
        out_shape=(
            shape((clips * frames, D), BF16),
            shape((2, CODES, DG), F32),
            shape((2, CODES, DG), F32),
            shape((rows, D), BF16),
            shape((rows, HID), BF16),
            shape((rows, D), BF16),
            shape((clips * frames, D), F32),
            shape((rows, HID), F32),
        ),
        in_specs=[smem] + whole(14),
        out_specs=tuple(whole(8)),
        scratch_shapes=[
            pltpu.VMEM((CODES, DG), BF16),
            pltpu.VMEM((SLOTS, rows, DG), F32),
            pltpu.VMEM((SLOTS, clips * frames, 2 * DG), BF16),
        ],
        compiler_params=params(),
        name="forward",
    )(meta, f, c, idc, idr, dil, pwt, *pieces)

    fg, dil_grad, pw_grad = pl.pallas_call(
        functools.partial(backward_kernel, clips, frames),
        out_shape=(
            shape((clips * frames, D), F32),
            shape((KERNEL, HID, D), F32),
            shape((D, HID), F32),
        ),
        in_specs=[smem] + whole(8),
        out_specs=tuple(whole(3)),
        compiler_params=params(),
        name="backward",
    )(meta, f, act, gated, bg, lg, hs, dil, pwt)

    parts = jnp.concatenate(
        [
            dil_grad.reshape(KERNEL, ranks, out_rows, 2, DG)
            .transpose(0, 1, 3, 2, 4)
            .reshape(KERNEL, ranks, small, DG),
            pw_grad.reshape(1, ranks, small, DG),
        ],
        axis=0,
    )
    seq = jnp.concatenate([jnp.arange(0, ranks, 2), jnp.arange(1, ranks, 2)])
    parts = jnp.take(jnp.take(parts, time ^ jnp.arange(4), axis=0), rank ^ seq, axis=1)
    parts = parts.reshape(2, 2, ranks * small, DG)

    def plane_reduce(keep, send, size):
        got = swap(send, 0, 1)
        packed = half * size + half * SCALE_GROUPS
        own, to_x, to_y, to_xy = pl.pallas_call(
            functools.partial(plane_kernel, half, size),
            out_shape=(shape((half, size, DG), F32),) + (shape((packed, DG), jnp.int16),) * 3,
            in_specs=whole(2),
            out_specs=tuple(whole(4)),
            compiler_params=params(),
            name="plane",
        )(keep, got)
        return own, (swap(to_x, 1, 0), swap(to_y, 0, 2), swap(to_xy, 1, 2))

    own_c, gots_c = plane_reduce(keep, send, block)
    own_d, gots_d = plane_reduce(parts[:, 0], parts[:, 1], small)
    sizes = (small, block)
    total = small + block
    out = pl.pallas_call(
        functools.partial(line_kernel, half, sizes),
        out_shape=(shape((total, DG), F32),)
        + (shape((total + 16, DG), jnp.int16),) * (half - 1),
        in_specs=whole(8),
        out_specs=tuple(whole(half)),
        compiler_params=params(),
        name="line",
    )(own_d, own_c, *gots_d, *gots_c)
    arrived = [swap(out[z], 2 * z, 0) for z in range(1, half)]
    piece = pl.pallas_call(
        functools.partial(final_kernel, half, sizes),
        out_shape=shape((total, DG), F32),
        in_specs=whole(half),
        out_specs=whole(1)[0],
        compiler_params=params(),
        name="final",
    )(out[0], *arrived)

    pair = jnp.stack([piece, swap(piece, 0, 2)], axis=0)
    four = jnp.stack([pair, swap(pair, 0, 1)], axis=1).reshape(4, total, DG)
    four = jnp.take(four, time ^ jnp.arange(4), axis=0)
    squared = jnp.sum(four * four).reshape(1, 1)
    step = 1
    while step < ranks:
        squared = squared + swap(squared, step, 0)
        step *= 2
    squared = squared.reshape(())

    dil_raw = four[:KERNEL, :small].reshape(KERNEL, 2, out_rows, DG)
    dil_raw = dil_raw.transpose(0, 1, 3, 2).reshape(KERNEL, D, out_rows)
    pw_raw = four[3, :small].T
    table_raw = four[:, small:]
    count = KERNEL * D * HID + D * HID + SLOTS * CODES * DG
    limit = jnp.sqrt(jnp.float32(count))
    norm = jnp.sqrt(squared)
    clip_scale = limit / jnp.maximum(norm, limit)
    steps = step_count[0].astype(F32)
    dil_out = adamw_update(
        dilated_kernel_weight,
        dilated_first_moment,
        dilated_second_moment,
        dil_raw * clip_scale,
        BITRATE_FACTOR,
        steps,
    )
    pw_out = adamw_update(
        pointwise_conv,
        pointwise_first,
        pointwise_second,
        pw_raw * clip_scale,
        BITRATE_FACTOR,
        steps,
    )
    table_out = adamw_update(
        codebooks,
        codebook_first,
        codebook_second,
        table_raw * clip_scale,
        RATE_CODE,
        steps,
    )
    return (
        quant.reshape(clips, frames, D),
        fg.reshape(clips, frames, D),
        norm.reshape(1),
        *dil_out,
        *pw_out,
        *table_out,
    )


def solution(mesh):
    in_specs = (
        P("clip", "tm", None),
        P("clip", "tm", None),
        P("clip"),
        P(None, "clip", "tm"),
        P(),
        P(None, None, "clip"),
        P(None, "clip"),
        P(None, "clip", None),
        P(None, None, "clip"),
        P(None, None, "clip"),
        P(None, "clip"),
        P(None, "clip"),
        P(None, "clip", None),
        P(None, "clip", None),
    )
    out_specs = (
        P("clip", "tm", None),
        P("clip", "tm", None),
        P(),
        P(None, None, "clip"),
        P(None, None, "clip"),
        P(None, None, "clip"),
        P(None, "clip"),
        P(None, "clip"),
        P(None, "clip"),
        P(None, "clip", None),
        P(None, "clip", None),
        P(None, "clip", None),
    )
    return jax.shard_map(shards, mesh=mesh, in_specs=in_specs, out_specs=out_specs, check_vma=False)
```

time: 311 us -> 167 us (0.54)
  waiting for transfers between devices: 150 us -> 50.6 us
  blocking collectives: 66.4 us -> 0 us
  other arithmetic: 48.1 us -> 17 us
  starting transfers between devices: 7.34 us -> 35.8 us
  Pallas kernels: 0 us -> 26.8 us
  local copies, waits for them, and re-layouts: 12.2 us -> 29.4 us
  between operations: 18.6 us -> 5.95 us
  matrix products: 7.32 us -> 0 us
    psum x1 -> x0, waiting for transfers between devices: 149 us -> none  [shards(): lax.psum((local_grads[0], local_grads[1], local_grads[2]), ('clip', 'tm'))]
    all_gather x2 -> x0, blocking collectives: 66.4 us -> none  [the longest x1 33.2 us: shards(): lax.all_gather(pointwise_conv.astype(jnp.bfloat16), 'clip', axis=1, tiled...]
    ppermute x4 -> x28, waiting for transfers between devices: 1.44 us -> 50.6 us  [the longest x26 50.6 us: swap(): return lax.ppermute(value, ('clip', 'tm'), pairs)]
    ppermute x4 -> x28, starting transfers between devices: 7.26 us -> 35.8 us  [the longest x26 31.3 us: swap(): return lax.ppermute(value, ('clip', 'tm'), pairs)]
    pallas_call x0 -> x6, Pallas kernels: none -> 26.8 us  [the longest x1 11.1 us: shards(): pl.pallas_call(functools.partial(forward_kernel, clips, frames, half, blo...]
    scatter-add x4 -> x0, other arithmetic: 18.6 us -> none  [shards(): jax.ops.segment_sum(code_grad.reshape(-1, DG), code_ids[slot].reshape(-1)...]
    dot_general x12 -> x0, matrix products: 7.32 us -> none  [the longest x3 2.16 us: shards(): jnp.einsum('btd,cd->btc', padded_grad[:, offset:offset + frames], dilated...]
    reduce_sum x3 -> x1, other arithmetic: 8.06 us -> 0.89 us  [shards(): squared = jnp.sum(four * four).reshape(1, 1)]
  transfers between devices with their start and end apart: 6 -> 28, of which waited for: 2 -> 13; matrix products, arithmetic and copies ran while one was open for 4% -> 17% of each run, Pallas kernels for 0% -> 7%
where the time goes in v1:
time: 167 us; the launch traced here: 166 us
  waiting for transfers between devices  50.6 us (30%)
  starting transfers between devices  35.8 us (21%)
  local copies, waits for them, and re-layouts  29.4 us (18%)
  Pallas kernels  26.8 us (16%)
  other arithmetic  17 us (10%)
  between operations  5.95 us (4%)
    ppermute x26, waiting for transfers between devices, swap(): return lax.ppermute(value, ('clip', 'tm'), pairs)  50.6 us
    ppermute x26, starting transfers between devices, swap(): return lax.ppermute(value, ('clip', 'tm'), pairs)  31.3 us
    pallas_call x1, Pallas kernels, shards(): pl.pallas_call(functools.partial(forward_kernel, clips, frames, half, blo...  11.1 us
    unnamed x74, local copies, waits for them, and re-layouts  7.32 us
    concatenate x1, local copies, waits for them, and re-layouts, halo(): jnp.concatenate([features, cotangent, high.astype(BF16), low.astype(BF16)...  6.32 us
    pallas_call x2, Pallas kernels, plane_reduce(): pl.pallas_call(functools.partial(plane_kernel, half, size), out_shape=(sh...  6.18 us
    pallas_call x1, Pallas kernels, shards(): pl.pallas_call(functools.partial(backward_kernel, clips, frames), out_sha...  4.97 us
    gather x2, local copies, waits for them, and re-layouts, shards(): jnp.take(jnp.take(parts, time ^ jnp.arange(4), axis=0), rank ^ seq, axis=1)  3.81 us
  transfers between devices with their start and end apart: 28, of which 13 were waited for; matrix products, arithmetic and copies ran while one was open for 17% of the time, Pallas kernels for 7%

profile of v1, /device:TPU:0, one launch (start us, length us, event | category | flops | bytes accessed | tf_op | source)
XLA Modules:
  0.0 165.5 jit_solution(14498648362016220045)
XLA Ops:
  4.3 3.0 %collective-permute-start.2 = (bf16[192,256]{1,0:T(8,128)(2,1)}, bf16[192,256]{1,0:T(8,128)(2,1)}, u32[]{:S(2)}, u32[]{:S(2)}) collective-permute-start(bf16[192,256]{1,0:T(8,128)(2,1)} %bitcast.12), channel_id=1, source_target_pairs={{0,8},{1,9},{2,10},{3,11},{4,12},{5,13},{6,14},{7,15},{8,0},{9,1},... | collective-permute-start | bytes 294920 | tf_op jit(solution)/shard_map/ppermute | solution.py:71
  7.4 2.6 %collective-permute-start.3 = (bf16[192,256]{1,0:T(8,128)(2,1)}, bf16[192,256]{1,0:T(8,128)(2,1)}, u32[]{:S(2)}, u32[]{:S(2)}) collective-permute-start(bf16[192,256]{1,0:T(8,128)(2,1)} %bitcast.12), channel_id=1, source_target_pairs={{0,16},{1,17},{2,18},{3,19},{4,20},{5,21},{6,22},{7,23},{8,24},{9,... | collective-permute-start | bytes 294920 | tf_op jit(solution)/shard_map/ppermute | solution.py:71
  10.8 1.7 %fusion.1 = (bf16[2,256,4]{2,0,1:T(2,128)(2,1)}, bf16[2,256,4]{2,0,1:T(2,128)(2,1)}) fusion(s32[4,2,256]{0,1,2:T(2,128)S(1)} %copy.115), kind=kLoop, calls=%fused_computation.38 | loop fusion | flops 43008 | bytes 16384 | tf_op jit(solution)/shard_map/convert_element_type | solution.py:344
  13.7 6.3 %concatenate.43 = bf16[2,256,1032]{2,0,1:T(2,128)(2,1)S(1)} concatenate(bf16[2,256,512]{2,0,1:T(2,128)(2,1)S(1)} %copy.116, bf16[2,256,512]{2,0,1:T(2,128)(2,1)S(1)} %copy.117, bf16[2,256,4]{2,0,1:T(2,128)(2,1)} %get-tuple-element.75, bf16[2,256,4]{2,0,1:T(2,128)(2,1)} %get-tuple-element.74), dimensions={2} | concatenate | bytes 2113536 | tf_op jit(solution)/shard_map/concatenate | solution.py:343
  21.4 3.2 %collective-permute-start = (bf16[2,6,1032]{2,0,1:T(2,128)(2,1)S(1)}, bf16[2,6,1032]{2,0,1:T(2,128)(2,1)S(1)}, u32[]{:S(2)}, u32[]{:S(2)}) collective-permute-start(bf16[2,6,1032]{2,0,1:T(2,128)(2,1)S(1)} %get-tuple-element.70), channel_id=1, source_target_pairs={{0,1},{1,2},{2,3},{4,5},{5,6},{6,7},{8,9},{9,10},{10,11},{12,13},{... | collective-permute-start | bytes 74312 | tf_op jit(solution)/shard_map/ppermute | solution.py:346
  28.2 3.5 %collective-permute-start.9 = (bf16[4,192,256]{2,1,0:T(8,128)(2,1)S(1)}, bf16[4,192,256]{2,1,0:T(8,128)(2,1)S(1)}, u32[]{:S(2)}, u32[]{:S(2)}) collective-permute-start(bf16[4,192,256]{2,1,0:T(8,128)(2,1)S(1)} %pad_maximum_fusion.5.refs_0_), channel_id=1, source_target_pairs={{0,6},{1,7},{2,4},{3,5},{4,2},{5,3},{6,0},{7,1},{8,14},{9,15},{10,... | collective-permute-start | bytes 1179656 | tf_op jit(solution)/shard_map/ppermute | solution.py:71
  32.5 1.4 copy.129.idc_ref
  35.4 6.3 %collective-permute-done.9.refs_5_ = bf16[4,192,256]{2,1,0:T(8,128)(2,1)S(1)} collective-permute-done((bf16[4,192,256]{2,1,0:T(8,128)(2,1)S(1)}, bf16[4,192,256]{2,1,0:T(8,128)(2,1)S(1)}, u32[]{:S(2)}, u32[]{:S(2)}) %collective-permute-start.9) | collective-permute-done | bytes 393248 | tf_op jit(solution)/shard_map/ppermute | solution.py:71
  41.7 8.2 %collective-permute-done.8.refs_4_ = bf16[4,192,256]{2,1,0:T(8,128)(2,1)S(1)} collective-permute-done((bf16[4,192,256]{2,1,0:T(8,128)(2,1)S(1)}, bf16[4,192,256]{2,1,0:T(8,128)(2,1)S(1)}, u32[]{:S(2)}, u32[]{:S(2)}) %collective-permute-start.8) | collective-permute-done | bytes 393248 | tf_op jit(solution)/shard_map/ppermute | solution.py:71
  57.7 11.1 %forward.1 = (bf16[512,512]{1,0:T(8,128)(2,1)}, f32[2,1024,256]{2,1,0:T(8,128)}, f32[2,1024,256]{2,1,0:T(8,128)}, bf16[544,512]{1,0:T(8,128)(2,1)}, bf16[544,256...) custom-call(s32[4]{0:T(128)} %pad_add_fusion.1.meta_ref, ...), custom_call_target="tpu_custom_call" | custom-call | tf_op jit(solution)/shard_map/forward/pallas_call | solution.py:443
  69.0 5.0 %backward.1 = (f32[512,512]{1,0:T(8,128)}, f32[3,256,512]{2,1,0:T(8,128)}, f32[512,256]{1,0:T(8,128)}) custom-call(s32[4]{0:T(128)} %pad_add_fusion.1.meta_ref, bf16[544,512]{1,0:T(8,128)(2,1)} %bitcast.110, bf16[544,512]{1,0:T(8,128)(2,1)} %get-tuple-element.36.act_ref, bf16[544,256]{1,0:T(8,128)(2,1)} %get-tuple-element.37.gated_ref, ...), custom_call_target="tpu_custom_call" | custom-call | tf_op jit(solution)/shard_map/backward/pallas_call | solution.py:466
  74.0 2.3 %reshape.193 = f32[3,8,32,2,256]{4,3,2,1,0:T(2,128)S(1)} reshape(f32[3,256,512]{2,1,0:T(8,128)} %get-tuple-element.42) | data formatting | bytes 3145728 | tf_op jit(solution)/shard_map/reshape | solution.py:481
  77.4 2.1 %gather_fusion.2 = f32[4,8,64,256]{3,2,1,0:T(8,128)} fusion(f32[4,8,64,256]{3,2,1,0:T(8,128)S(1)} %pad_maximum_fusion, s32[1024]{0:T(1024)S(1)} %pad_clamp_fusion.2), kind=kCustom, calls=%fused_computation.2 | custom fusion | bytes 4194320 | tf_op jit(solution)/shard_map/jit(_take)/gather | solution.py:489
  79.5 1.9 %broadcast_select_fusion = f32[4,8,64,256]{3,2,1,0:T(8,128)S(1)} fusion(f32[4,8,64,256]{3,2,1,0:T(8,128)} %gather_fusion.2, pred[4]{0:T(512)(128)(4,1)S(1)} %compare_and_fusion.1), kind=kLoop, calls=%fused_computation.11 | loop fusion | flops 524288 | bytes 4194308 | tf_op jit(solution)/shard_map/jit(_take)/select_n | solution.py:489
  81.4 2.1 %gather_fusion.3 = f32[8,4,64,256]{3,2,1,0:T(8,128)} fusion(f32[4,8,64,256]{3,2,1,0:T(8,128)S(1)} %broadcast_select_fusion, s32[1024]{0:T(1024)S(1)} %pad_clamp_fusion), kind=kCustom, calls=%fused_computation.3 | custom fusion | bytes 4194336 | tf_op jit(solution)/shard_map/jit(_take)/gather | solution.py:489
  83.5 1.7 %copy.131 = f32[4,8,64,256]{3,2,1,0:T(8,128)S(1)} copy(f32[4,8,64,256]{3,2,0,1:T(8,128)} %bitcast.104) | data formatting | bytes 4194304 | tf_op jit(solution)/shard_map/jit(_take)/gather | solution.py:489
  87.0 2.3 %collective-permute-done.12.got_ref = f32[2,512,256]{2,1,0:T(8,128)S(1)} collective-permute-done((f32[2,512,256]{2,1,0:T(8,128)S(1)}, f32[2,512,256]{2,1,0:T(8,128)S(1)}, u32[]{:S(2)}, u32[]{:S(2)}) %collective-permute-start.12) | collective-permute-done | bytes 1048608 | tf_op jit(solution)/shard_map/ppermute | solution.py:71
  90.3 2.6 %plane.2 = (f32[4,64,256]{2,1,0:T(8,128)}, s16[272,256]{1,0:T(8,128)(2,1)}, s16[272,256]{1,0:T(8,128)(2,1)}, s16[272,256]{1,0:T(8,128)(2,1)}) custom-call(f32[2,512,256]{2,1,0:T(8,128)} %get-tuple-element.69.keep_ref, f32[2,512,256]{2,1,0:T(8,128)} %copy-done.4), custom_call_target="tpu_custom_call" | custom-call | tf_op jit(solution)/shard_map/plane/pallas_call | solution.py:495
  92.9 1.3 collective-permute-start.14
  94.3 3.6 %plane.3 = (f32[4,128,256]{2,1,0:T(8,128)}, s16[528,256]{1,0:T(8,128)(2,1)}, s16[528,256]{1,0:T(8,128)(2,1)}, s16[528,256]{1,0:T(8,128)(2,1)}) custom-call(f32[2,1024,256]{2,1,0:T(8,128)} %get-tuple-element.45.keep_ref, f32[2,1024,256]{2,1,0:T(8,128)} %collective-permute-done.13.got_ref), custom_call_target="tpu_custom_call" | custom-call | tf_op jit(solution)/shard_map/plane/pallas_call | solution.py:495
  99.1 2.2 %collective-permute-start.19 = (s16[528,256]{1,0:T(8,128)(2,1)}, s16[528,256]{1,0:T(8,128)(2,1)S(1)}, u32[]{:S(2)}, u32[]{:S(2)}) collective-permute-start(s16[528,256]{1,0:T(8,128)(2,1)} %get-tuple-element.53), channel_id=1, source_target_pairs={{0,6},{1,7},{2,4},{3,5},{4,2},{5,3},{6,0},{7,1},{8,14},{9,15},{10,... | collective-permute-start | bytes 811016 | tf_op jit(solution)/shard_map/ppermute | solution.py:71
  101.7 1.8 %collective-permute-start.16 = (s16[272,256]{1,0:T(8,128)(2,1)S(1)}, s16[272,256]{1,0:T(8,128)(2,1)S(1)}, u32[]{:S(2)}, u32[]{:S(2)}) collective-permute-start(s16[272,256]{1,0:T(8,128)(2,1)S(1)} %copy-done.33), channel_id=1, source_target_pairs={{0,6},{1,7},{2,4},{3,5},{4,2},{5,3},{6,0},{7,1},{8,14},{9,15},{10,... | collective-permute-start | bytes 417800 | tf_op jit(solution)/shard_map/ppermute | solution.py:71
  103.6 15.1 %collective-permute-done.15.refs_3_ = s16[272,256]{1,0:T(8,128)(2,1)S(1)} collective-permute-done((s16[272,256]{1,0:T(8,128)(2,1)S(1)}, s16[272,256]{1,0:T(8,128)(2,1)S(1)}, u32[]{:S(2)}, u32[]{:S(2)}) %collective-permute-start.15) | collective-permute-done | bytes 139296 | tf_op jit(solution)/shard_map/ppermute | solution.py:71
  119.7 2.7 %line.1 = (f32[192,256]{1,0:T(8,128)}, s16[208,256]{1,0:T(8,128)(2,1)}, s16[208,256]{1,0:T(8,128)(2,1)}, s16[208,256]{1,0:T(8,128)(2,1)}) custom-call(f32[4,64,256]{2,1,0:T(8,128)} %get-tuple-element.44.refs_0_, f32[4,128,256]{2,1,0:T(8,128)} %get-tuple-element.47.refs_1_, s16[272,256]{1,0:T(8,128)(2,1)} %copy-done.23, s16[272,256]{1,0:T(8,128)(2,1)} %copy-done.24, ...), custom_call_target="tpu_custom_call" | custom-call | tf_op jit(solution)/shard_map/line/pallas_call | solution.py:509
  123.1 3.5 %collective-permute-start.21 = (s16[208,256]{1,0:T(8,128)(2,1)}, s16[208,256]{1,0:T(8,128)(2,1)S(1)}, u32[]{:S(2)}, u32[]{:S(2)}) collective-permute-start(s16[208,256]{1,0:T(8,128)(2,1)} %get-tuple-element.56), channel_id=1, source_target_pairs={{0,16},{1,17},{2,18},{3,19},{4,20},{5,21},{6,22},{7,23},{8,24},{9,... | collective-permute-start | bytes 319496 | tf_op jit(solution)/shard_map/ppermute | solution.py:71
  126.8 1.7 %collective-permute-done.20.refs_0_ = s16[208,256]{1,0:T(8,128)(2,1)S(1)} collective-permute-done((s16[208,256]{1,0:T(8,128)(2,1)}, s16[208,256]{1,0:T(8,128)(2,1)S(1)}, u32[]{:S(2)}, u32[]{:S(2)}) %collective-permute-start.20) | collective-permute-done | bytes 106528 | tf_op jit(solution)/shard_map/ppermute | solution.py:71
  128.5 5.8 %collective-permute-done.21.refs_1_ = s16[208,256]{1,0:T(8,128)(2,1)S(1)} collective-permute-done((s16[208,256]{1,0:T(8,128)(2,1)}, s16[208,256]{1,0:T(8,128)(2,1)S(1)}, u32[]{:S(2)}, u32[]{:S(2)}) %collective-permute-start.21) | collective-permute-done | bytes 106528 | tf_op jit(solution)/shard_map/ppermute | solution.py:71
  134.9 1.9 %final.1 = f32[192,256]{1,0:T(8,128)} custom-call(f32[192,256]{1,0:T(8,128)} %get-tuple-element.54.own_ref, s16[208,256]{1,0:T(8,128)(2,1)} %copy-done.26, s16[208,256]{1,0:T(8,128)(2,1)} %copy-done.27, s16[208,256]{1,0:T(8,128)(2,1)} %copy-done.28), custom_call_target="tpu_custom_call" | custom-call | tf_op jit(solution)/shard_map/final/pallas_call | solution.py:519
  137.3 5.3 %collective-permute-done.23 = f32[192,256]{1,0:T(8,128)S(1)} collective-permute-done((f32[192,256]{1,0:T(8,128)}, f32[192,256]{1,0:T(8,128)S(1)}, u32[]{:S(2)}, u32[]{:S(2)}) %collective-permute-start.23) | collective-permute-done | bytes 196640 | tf_op jit(solution)/shard_map/ppermute | solution.py:71
  148.4 2.3 %collective-permute-done.25 = f32[1,1]{1,0:T(1,128)} collective-permute-done((f32[1,1]{1,0:T(1,128)}, f32[1,1]{1,0:T(1,128)}, u32[]{:S(2)}, u32[]{:S(2)}) %collective-permute-start.25) | collective-permute-done | bytes 36 | tf_op jit(solution)/shard_map/ppermute | solution.py:71
  152.0 3.0 %collective-permute-start.26 = (f32[1,1]{1,0:T(1,128)}, f32[1,1]{1,0:T(1,128)}, u32[]{:S(2)}, u32[]{:S(2)}) collective-permute-start(f32[1,1]{1,0:T(1,128)} %add.178), channel_id=1, source_target_pairs={{0,8},{1,9},{2,10},{3,11},{4,12},{5,13},{6,14},{7,15},{8,0},{9,1},... | collective-permute-start | bytes 20 | tf_op jit(solution)/shard_map/ppermute | solution.py:71
  156.2 4.0 %collective-permute-start.27 = (f32[1,1]{1,0:T(1,128)}, f32[1,1]{1,0:T(1,128)}, u32[]{:S(2)}, u32[]{:S(2)}) collective-permute-start(f32[1,1]{1,0:T(1,128)} %add.179), channel_id=1, source_target_pairs={{0,16},{1,17},{2,18},{3,19},{4,20},{5,21},{6,22},{7,23},{8,24},{9,... | collective-permute-start | bytes 20 | tf_op jit(solution)/shard_map/ppermute | solution.py:71
  (189 shorter events, 37.9 us)
Async XLA Ops:
  4.3 22.7 %collective-permute-start.2 = (bf16[192,256]{1,0:T(8,128)(2,1)}, bf16[192,256]{1,0:T(8,128)(2,1)}, u32[]{:S(2)}, u32[]{:S(2)}) collective-permute-start(bf16[192,256]{1,0:T(8,128)(2,1)} %bitcast.12), channel_id=1, source_target_pairs={{0,8},{1,9},{2,10},{3,11},{4,12},{5,13},{6,14},{7,15},{8,0},{9,1},... | collective-permute-start | bytes 294920 | tf_op jit(solution)/shard_map/ppermute | solution.py:71
  7.4 19.7 %collective-permute-start.3 = (bf16[192,256]{1,0:T(8,128)(2,1)}, bf16[192,256]{1,0:T(8,128)(2,1)}, u32[]{:S(2)}, u32[]{:S(2)}) collective-permute-start(bf16[192,256]{1,0:T(8,128)(2,1)} %bitcast.12), channel_id=1, source_target_pairs={{0,16},{1,17},{2,18},{3,19},{4,20},{5,21},{6,22},{7,23},{8,24},{9,... | collective-permute-start | bytes 294920 | tf_op jit(solution)/shard_map/ppermute | solution.py:71
  10.0 17.1 %collective-permute-start.4 = (bf16[192,256]{1,0:T(8,128)(2,1)}, bf16[192,256]{1,0:T(8,128)(2,1)}, u32[]{:S(2)}, u32[]{:S(2)}) collective-permute-start(bf16[192,256]{1,0:T(8,128)(2,1)} %bitcast.12), channel_id=1, source_target_pairs={{0,24},{1,25},{2,26},{3,27},{4,28},{5,29},{6,30},{7,31},{8,16},{9,... | collective-permute-start | bytes 294920 | tf_op jit(solution)/shard_map/ppermute | solution.py:71
  20.1 6.2 %collective-permute-start.1 = (bf16[2,6,1032]{2,0,1:T(2,128)(2,1)S(1)}, bf16[2,6,1032]{2,0,1:T(2,128)(2,1)S(1)}, u32[]{:S(2)}, u32[]{:S(2)}) collective-permute-start(bf16[2,6,1032]{2,0,1:T(2,128)(2,1)S(1)} %get-tuple-element.71), channel_id=1, source_target_pairs={{1,0},{2,1},{3,2},{5,4},{6,5},{7,6},{9,8},{10,9},{11,10},{13,12},{... | collective-permute-start | bytes 74312 | tf_op jit(solution)/shard_map/ppermute | solution.py:349
  21.4 5.0 %collective-permute-start = (bf16[2,6,1032]{2,0,1:T(2,128)(2,1)S(1)}, bf16[2,6,1032]{2,0,1:T(2,128)(2,1)S(1)}, u32[]{:S(2)}, u32[]{:S(2)}) collective-permute-start(bf16[2,6,1032]{2,0,1:T(2,128)(2,1)S(1)} %get-tuple-element.70), channel_id=1, source_target_pairs={{0,1},{1,2},{2,3},{4,5},{5,6},{6,7},{8,9},{9,10},{10,11},{12,13},{... | collective-permute-start | bytes 74312 | tf_op jit(solution)/shard_map/ppermute | solution.py:346
  28.2 21.8 %copy-start = (bf16[4,192,256]{2,1,0:T(8,128)(2,1)}, bf16[4,192,256]{2,1,0:T(8,128)(2,1)S(1)}, u32[]{:S(2)}) copy-start(bf16[4,192,256]{2,1,0:T(8,128)(2,1)S(1)} %pad_maximum_fusion.5.refs_0_) | copy-start | bytes 1179652
  28.2 13.5 %collective-permute-start.9 = (bf16[4,192,256]{2,1,0:T(8,128)(2,1)S(1)}, bf16[4,192,256]{2,1,0:T(8,128)(2,1)S(1)}, u32[]{:S(2)}, u32[]{:S(2)}) collective-permute-start(bf16[4,192,256]{2,1,0:T(8,128)(2,1)S(1)} %pad_maximum_fusion.5.refs_0_), channel_id=1, source_target_pairs={{0,6},{1,7},{2,4},{3,5},{4,2},{5,3},{6,0},{7,1},{8,14},{9,15},{10,... | collective-permute-start | bytes 1179656 | tf_op jit(solution)/shard_map/ppermute | solution.py:71
  34.8 15.1 %collective-permute-start.8 = (bf16[4,192,256]{2,1,0:T(8,128)(2,1)S(1)}, bf16[4,192,256]{2,1,0:T(8,128)(2,1)S(1)}, u32[]{:S(2)}, u32[]{:S(2)}) collective-permute-start(bf16[4,192,256]{2,1,0:T(8,128)(2,1)S(1)} %pad_maximum_fusion.5.refs_0_), channel_id=1, source_target_pairs={{0,2},{1,3},{2,0},{3,1},{4,6},{5,7},{6,4},{7,5},{8,10},{9,11},{10,... | collective-permute-start | bytes 1179656 | tf_op jit(solution)/shard_map/ppermute | solution.py:71
  34.8 15.2 %collective-permute-start.5 = (bf16[4,192,256]{2,1,0:T(8,128)(2,1)S(1)}, bf16[4,192,256]{2,1,0:T(8,128)(2,1)S(1)}, u32[]{:S(2)}, u32[]{:S(2)}) collective-permute-start(bf16[4,192,256]{2,1,0:T(8,128)(2,1)S(1)} %pad_maximum_fusion.5.refs_0_), channel_id=1, source_target_pairs={{0,4},{1,5},{2,6},{3,7},{4,0},{5,1},{6,2},{7,3},{8,12},{9,13},{10,... | collective-permute-start | bytes 1179656 | tf_op jit(solution)/shard_map/ppermute | solution.py:71
  35.4 15.3 %collective-permute-start.6 = (bf16[4,192,256]{2,1,0:T(8,128)(2,1)S(1)}, bf16[4,192,256]{2,1,0:T(8,128)(2,1)S(1)}, u32[]{:S(2)}, u32[]{:S(2)}) collective-permute-start(bf16[4,192,256]{2,1,0:T(8,128)(2,1)S(1)} %pad_maximum_fusion.5.refs_0_), channel_id=1, source_target_pairs={{0,1},{1,0},{2,3},{3,2},{4,5},{5,4},{6,7},{7,6},{8,9},{9,8},{10,11... | collective-permute-start | bytes 1179656 | tf_op jit(solution)/shard_map/ppermute | solution.py:71
  41.7 9.1 %collective-permute-start.11 = (bf16[4,192,256]{2,1,0:T(8,128)(2,1)S(1)}, bf16[4,192,256]{2,1,0:T(8,128)(2,1)S(1)}, u32[]{:S(2)}, u32[]{:S(2)}) collective-permute-start(bf16[4,192,256]{2,1,0:T(8,128)(2,1)S(1)} %collective-permute-done.9.refs_5_), channel_id=1, source_target_pairs={{0,1},{1,0},{2,3},{3,2},{4,5},{5,4},{6,7},{7,6},{8,9},{9,8},{10,11... | collective-permute-start | bytes 1179656 | tf_op jit(solution)/shard_map/ppermute | solution.py:71
  50.1 1.8 %collective-permute-start.10 = (bf16[4,192,256]{2,1,0:T(8,128)(2,1)S(1)}, bf16[4,192,256]{2,1,0:T(8,128)(2,1)S(1)}, u32[]{:S(2)}, u32[]{:S(2)}) collective-permute-start(bf16[4,192,256]{2,1,0:T(8,128)(2,1)S(1)} %collective-permute-done.8.refs_4_), channel_id=1, source_target_pairs={{0,1},{1,0},{2,3},{3,2},{4,5},{5,4},{6,7},{7,6},{8,9},{9,8},{10,11... | collective-permute-start | bytes 1179656 | tf_op jit(solution)/shard_map/ppermute | solution.py:71
  50.2 2.3 %collective-permute-start.7 = (bf16[4,192,256]{2,1,0:T(8,128)(2,1)S(1)}, bf16[4,192,256]{2,1,0:T(8,128)(2,1)S(1)}, u32[]{:S(2)}, u32[]{:S(2)}) collective-permute-start(bf16[4,192,256]{2,1,0:T(8,128)(2,1)S(1)} %collective-permute-done.5.refs_1_), channel_id=1, source_target_pairs={{0,1},{1,0},{2,3},{3,2},{4,5},{5,4},{6,7},{7,6},{8,9},{9,8},{10,11... | collective-permute-start | bytes 1179656 | tf_op jit(solution)/shard_map/ppermute | solution.py:71
  68.8 25.5 %collective-permute-start.13 = (f32[2,1024,256]{2,1,0:T(8,128)}, f32[2,1024,256]{2,1,0:T(8,128)}, u32[]{:S(2)}, u32[]{:S(2)}) collective-permute-start(f32[2,1024,256]{2,1,0:T(8,128)} %get-tuple-element.46), channel_id=1, source_target_pairs={{0,1},{1,0},{2,3},{3,2},{4,5},{5,4},{6,7},{7,6},{8,9},{9,8},{10,11... | collective-permute-start | bytes 6291464 | tf_op jit(solution)/shard_map/ppermute | solution.py:71
  86.6 2.7 %collective-permute-start.12 = (f32[2,512,256]{2,1,0:T(8,128)S(1)}, f32[2,512,256]{2,1,0:T(8,128)S(1)}, u32[]{:S(2)}, u32[]{:S(2)}) collective-permute-start(f32[2,512,256]{2,1,0:T(8,128)S(1)} %get-tuple-element.68), channel_id=1, source_target_pairs={{0,1},{1,0},{2,3},{3,2},{4,5},{5,4},{6,7},{7,6},{8,9},{9,8},{10,11... | collective-permute-start | bytes 3145736 | tf_op jit(solution)/shard_map/ppermute | solution.py:71
  92.9 8.8 %collective-permute-start.14 = (s16[272,256]{1,0:T(8,128)(2,1)}, s16[272,256]{1,0:T(8,128)(2,1)S(1)}, u32[]{:S(2)}, u32[]{:S(2)}) collective-permute-start(s16[272,256]{1,0:T(8,128)(2,1)} %get-tuple-element.48), channel_id=1, source_target_pairs={{0,4},{1,5},{2,6},{3,7},{4,0},{5,1},{6,2},{7,3},{8,12},{9,13},{10,... | collective-permute-start | bytes 417800 | tf_op jit(solution)/shard_map/ppermute | solution.py:71
  97.9 20.9 %collective-permute-start.17 = (s16[528,256]{1,0:T(8,128)(2,1)}, s16[528,256]{1,0:T(8,128)(2,1)S(1)}, u32[]{:S(2)}, u32[]{:S(2)}) collective-permute-start(s16[528,256]{1,0:T(8,128)(2,1)} %get-tuple-element.51), channel_id=1, source_target_pairs={{0,4},{1,5},{2,6},{3,7},{4,0},{5,1},{6,2},{7,3},{8,12},{9,13},{10,... | collective-permute-start | bytes 811016 | tf_op jit(solution)/shard_map/ppermute | solution.py:71
  98.6 20.2 %collective-permute-start.18 = (s16[528,256]{1,0:T(8,128)(2,1)}, s16[528,256]{1,0:T(8,128)(2,1)S(1)}, u32[]{:S(2)}, u32[]{:S(2)}) collective-permute-start(s16[528,256]{1,0:T(8,128)(2,1)} %get-tuple-element.52), channel_id=1, source_target_pairs={{0,2},{1,3},{2,0},{3,1},{4,6},{5,7},{6,4},{7,5},{8,10},{9,11},{10,... | collective-permute-start | bytes 811016 | tf_op jit(solution)/shard_map/ppermute | solution.py:71
  99.1 19.7 %collective-permute-start.19 = (s16[528,256]{1,0:T(8,128)(2,1)}, s16[528,256]{1,0:T(8,128)(2,1)S(1)}, u32[]{:S(2)}, u32[]{:S(2)}) collective-permute-start(s16[528,256]{1,0:T(8,128)(2,1)} %get-tuple-element.53), channel_id=1, source_target_pairs={{0,6},{1,7},{2,4},{3,5},{4,2},{5,3},{6,0},{7,1},{8,14},{9,15},{10,... | collective-permute-start | bytes 811016 | tf_op jit(solution)/shard_map/ppermute | solution.py:71
  101.4 17.4 %collective-permute-start.15 = (s16[272,256]{1,0:T(8,128)(2,1)S(1)}, s16[272,256]{1,0:T(8,128)(2,1)S(1)}, u32[]{:S(2)}, u32[]{:S(2)}) collective-permute-start(s16[272,256]{1,0:T(8,128)(2,1)S(1)} %copy-done.34), channel_id=1, source_target_pairs={{0,2},{1,3},{2,0},{3,1},{4,6},{5,7},{6,4},{7,5},{8,10},{9,11},{10,... | collective-permute-start | bytes 417800 | tf_op jit(solution)/shard_map/ppermute | solution.py:71
  101.7 17.1 %copy-start.23 = (s16[272,256]{1,0:T(8,128)(2,1)}, s16[272,256]{1,0:T(8,128)(2,1)S(1)}, u32[]{:S(2)}) copy-start(s16[272,256]{1,0:T(8,128)(2,1)S(1)} %collective-permute-done.14.refs_2_) | copy-start | bytes 417796
  101.7 17.0 %collective-permute-start.16 = (s16[272,256]{1,0:T(8,128)(2,1)S(1)}, s16[272,256]{1,0:T(8,128)(2,1)S(1)}, u32[]{:S(2)}, u32[]{:S(2)}) collective-permute-start(s16[272,256]{1,0:T(8,128)(2,1)S(1)} %copy-done.33), channel_id=1, source_target_pairs={{0,6},{1,7},{2,4},{3,5},{4,2},{5,3},{6,0},{7,1},{8,14},{9,15},{10,... | collective-permute-start | bytes 417800 | tf_op jit(solution)/shard_map/ppermute | solution.py:71
  122.4 6.1 %collective-permute-start.20 = (s16[208,256]{1,0:T(8,128)(2,1)}, s16[208,256]{1,0:T(8,128)(2,1)S(1)}, u32[]{:S(2)}, u32[]{:S(2)}) collective-permute-start(s16[208,256]{1,0:T(8,128)(2,1)} %get-tuple-element.55), channel_id=1, source_target_pairs={{0,8},{1,9},{2,10},{3,11},{4,12},{5,13},{6,14},{7,15},{8,0},{9,1},... | collective-permute-start | bytes 319496 | tf_op jit(solution)/shard_map/ppermute | solution.py:71
  123.1 11.2 %collective-permute-start.21 = (s16[208,256]{1,0:T(8,128)(2,1)}, s16[208,256]{1,0:T(8,128)(2,1)S(1)}, u32[]{:S(2)}, u32[]{:S(2)}) collective-permute-start(s16[208,256]{1,0:T(8,128)(2,1)} %get-tuple-element.56), channel_id=1, source_target_pairs={{0,16},{1,17},{2,18},{3,19},{4,20},{5,21},{6,22},{7,23},{8,24},{9,... | collective-permute-start | bytes 319496 | tf_op jit(solution)/shard_map/ppermute | solution.py:71
  126.6 7.7 %collective-permute-start.22 = (s16[208,256]{1,0:T(8,128)(2,1)}, s16[208,256]{1,0:T(8,128)(2,1)S(1)}, u32[]{:S(2)}, u32[]{:S(2)}) collective-permute-start(s16[208,256]{1,0:T(8,128)(2,1)} %get-tuple-element.57), channel_id=1, source_target_pairs={{0,24},{1,25},{2,26},{3,27},{4,28},{5,29},{6,30},{7,31},{8,16},{9,... | collective-permute-start | bytes 319496 | tf_op jit(solution)/shard_map/ppermute | solution.py:71
  136.8 5.9 %collective-permute-start.23 = (f32[192,256]{1,0:T(8,128)}, f32[192,256]{1,0:T(8,128)S(1)}, u32[]{:S(2)}, u32[]{:S(2)}) collective-permute-start(f32[192,256]{1,0:T(8,128)} %final.1), channel_id=1, source_target_pairs={{0,2},{1,3},{2,0},{3,1},{4,6},{5,7},{6,4},{7,5},{8,10},{9,11},{10,... | collective-permute-start | bytes 589832 | tf_op jit(solution)/shard_map/ppermute | solution.py:71
  143.7 1.8 %collective-permute-start.24 = (f32[2,192,256]{2,1,0:T(8,128)S(1)}, f32[2,192,256]{2,1,0:T(8,128)S(1)}, u32[]{:S(2)}, u32[]{:S(2)}) collective-permute-start(f32[2,192,256]{2,1,0:T(8,128)S(1)} %get-tuple-element.73), channel_id=1, source_target_pairs={{0,1},{1,0},{2,3},{3,2},{4,5},{5,4},{6,7},{7,6},{8,9},{9,8},{10,11... | collective-permute-start | bytes 1179656 | tf_op jit(solution)/shard_map/ppermute | solution.py:71
  145.6 15.9 %copy-start.3 = (f32[4,128,256]{2,1,0:T(8,128)S(1)}, f32[4,128,256]{2,1,0:T(8,128)}, u32[]{:S(2)}) copy-start(f32[4,128,256]{2,1,0:T(8,128)} %param.21) | copy-start | bytes 1572868
  145.6 15.9 %copy-start.14 = (f32[4,128,256]{2,1,0:T(8,128)S(1)}, f32[4,128,256]{2,1,0:T(8,128)}, u32[]{:S(2)}) copy-start(f32[4,128,256]{2,1,0:T(8,128)} %param.26) | copy-start | bytes 1572868
  147.1 3.6 %collective-permute-start.25 = (f32[1,1]{1,0:T(1,128)}, f32[1,1]{1,0:T(1,128)}, u32[]{:S(2)}, u32[]{:S(2)}) collective-permute-start(f32[1,1]{1,0:T(1,128)} %bitcast.51), channel_id=1, source_target_pairs={{0,4},{1,5},{2,6},{3,7},{4,0},{5,1},{6,2},{7,3},{8,12},{9,13},{10,... | collective-permute-start | bytes 20 | tf_op jit(solution)/shard_map/ppermute | solution.py:71
  152.0 3.6 %collective-permute-start.26 = (f32[1,1]{1,0:T(1,128)}, f32[1,1]{1,0:T(1,128)}, u32[]{:S(2)}, u32[]{:S(2)}) collective-permute-start(f32[1,1]{1,0:T(1,128)} %add.178), channel_id=1, source_target_pairs={{0,8},{1,9},{2,10},{3,11},{4,12},{5,13},{6,14},{7,15},{8,0},{9,1},... | collective-permute-start | bytes 20 | tf_op jit(solution)/shard_map/ppermute | solution.py:71
  156.2 4.5 %collective-permute-start.27 = (f32[1,1]{1,0:T(1,128)}, f32[1,1]{1,0:T(1,128)}, u32[]{:S(2)}, u32[]{:S(2)}) collective-permute-start(f32[1,1]{1,0:T(1,128)} %add.179), channel_id=1, source_target_pairs={{0,16},{1,17},{2,18},{3,19},{4,20},{5,21},{6,22},{7,23},{8,24},{9,... | collective-permute-start | bytes 20 | tf_op jit(solution)/shard_map/ppermute | solution.py:71
  (31 other events, 124.1 us)

commit v2 on v1

v2 whole, which is shorter than its diff:
```python
import functools

import jax
import jax.numpy as jnp
from jax import lax
from jax.experimental import pallas as pl
from jax.experimental.pallas import tpu as pltpu
from jax.sharding import PartitionSpec as P

D = 512
HID = 256
CODES = 1024
GROUPS = 2
LEVELS = 2
SLOTS = 4
KERNEL = 3
DILATION = 3
DG = 256
PAD = 8

COMMIT = 0.25
FIRST_DECAY = 0.9
SECOND_DECAY = 0.99
EPSILON = 1e-08
WEIGHT_DECAY = 0.01
BITRATE_FACTOR = 0.02
RATE_CODE = 0.5

F32 = jnp.float32
BF16 = jnp.bfloat16
NT = (((1,), (1,)), ((), ()))
TN = (((0,), (0,)), ((), ()))
LEVEL_STEPS = 256.0
TOP = 32000.0
SCALE_GROUPS = 4
MIB = 1024 * 1024


def params(mib=6):
    return pltpu.CompilerParams(vmem_limit_bytes=mib * MIB)


def whole(count):
    return [pl.BlockSpec(memory_space=pltpu.VMEM)] * count


def mm(a, b):
    return jnp.dot(a, b, preferred_element_type=F32)


def mmg(a, b, dims):
    return lax.dot_general(a, b, dims, preferred_element_type=F32)


def slope(v):
    return jnp.where(v > 0, 1.0, jnp.exp(jnp.minimum(v, 0.0)))


def elu(v):
    return jnp.where(v > 0, v, jnp.exp(jnp.minimum(v, 0.0)) - 1.0)


def swap(value, clip_mask, time_mask):
    clips, times = lax.axis_size("clip"), lax.axis_size("tm")
    pairs = [
        (c * times + t, (c ^ clip_mask) * times + (t ^ time_mask))
        for c in range(clips)
        for t in range(times)
    ]
    return lax.ppermute(value, ("clip", "tm"), pairs)


def prep_kernel(dil_ref, pw_ref, table_ref, out_ref):
    time = lax.axis_index("tm")
    out_rows = dil_ref.shape[1]

    @pl.when(time < KERNEL)
    def _():
        tap = jnp.minimum(time, KERNEL - 1)
        for side in range(2):
            out_ref[side * out_rows : (side + 1) * out_rows, :] = dil_ref[
                tap, :, side * DG : (side + 1) * DG
            ].astype(BF16)

    @pl.when(time == KERNEL)
    def _():
        out_ref[: 2 * out_rows, :] = pw_ref[...].astype(BF16)

    out_ref[2 * out_rows :, :] = table_ref[time].astype(BF16)


def renamed(values, ranks):
    block = CODES // ranks
    step = (values // block) ^ lax.axis_index("clip")
    place = (step % 2) * (ranks // 2) + step // 2
    return place * block + values % block


def masks(clips, frames, len_ref, columns):
    span = frames + 2 * PAD
    row = lax.broadcasted_iota(jnp.int32, (span, columns), 0)
    where = row - PAD + lax.axis_index("tm") * frames
    inner = (row >= PAD) & (row < PAD + frames)
    marks, inside = [], []
    for clip in range(clips):
        good = (where >= 0) & (where < len_ref[clip])
        marks.append(jnp.where(good, 1.0, 0.0))
        inside.append(jnp.where(good & inner, 2.0, 0.0))
    return jnp.concatenate(marks, axis=0), jnp.concatenate(inside, axis=0)


def early_kernel(ranks, len_ref, f_ref, left_ref, right_ref, ids_ref, start_ref, act_ref, hot_ref, hott_ref):
    clips, frames, _ = f_ref.shape
    mask, _ = masks(clips, frames, len_ref, D)
    start = mask * jnp.concatenate(
        [
            part[c].astype(F32)
            for c in range(clips)
            for part in (left_ref.at[:, :, :D], f_ref, right_ref.at[:, :, :D])
        ],
        axis=0,
    )
    start_ref[...] = start
    act_ref[...] = elu(start).astype(BF16)
    rows = start.shape[0]
    codes = lax.broadcasted_iota(jnp.int32, (rows, CODES), 1)
    spots = lax.broadcasted_iota(jnp.int32, (CODES, frames), 0)
    ids = ids_ref[...]
    turned = []
    for c in range(clips):
        own = jnp.concatenate([ids[:, c].astype(F32), jnp.zeros((8 - SLOTS, frames), F32)], axis=0)
        for part in (left_ref, None, right_ref):
            if part is None:
                turned.append(own.T[:, :SLOTS].astype(jnp.int32))
            else:
                high = part[c, :, 2 * D : 2 * D + SLOTS].astype(F32)
                low = part[c, :, 2 * D + SLOTS :].astype(F32)
                turned.append((high * 32.0 + low).astype(jnp.int32))
    turned = renamed(jnp.concatenate(turned, axis=0), ranks)
    for slot in range(SLOTS):
        hot_ref[slot] = jnp.where(codes == turned[:, slot : slot + 1], 1.0, 0.0).astype(BF16)
        for c in range(clips):
            line = renamed(ids[slot, c : c + 1, :], ranks)
            hott_ref[slot, :, c * frames : (c + 1) * frames] = jnp.where(
                spots == line, 1.0, 0.0
            ).astype(BF16)


def assembled(ranks, pieces, d_ref, pwt_ref, all_ref):
    half, small = ranks // 2, 2 * HID // ranks
    out_rows = small // 2
    time, rank = lax.axis_index("tm"), lax.axis_index("clip")
    for other in range(4):
        for x in range(2):
            piece = pieces[other * 2 + x]
            for z in range(half):
                at = pl.multiple_of((rank ^ (2 * z + x)) * out_rows, out_rows)
                for side in range(2):
                    all_ref[time ^ other, pl.ds(at, out_rows), side * DG : (side + 1) * DG] = piece[
                        z, side * out_rows : (side + 1) * out_rows, :
                    ]
    for tap in range(KERNEL):
        d_ref[tap * HID : (tap + 1) * HID, :] = all_ref[tap]
    for r in range(ranks):
        for side in range(2):
            to = r * small + side * out_rows
            pwt_ref[to : to + out_rows, :] = all_ref[
                KERNEL, r * out_rows : (r + 1) * out_rows, side * DG : (side + 1) * DG
            ]


def conv_kernel(ranks, assemble, start_ref, act_ref, *refs):
    if assemble:
        pieces, refs = refs[:8], refs[8:]
        d_ref, pwt_ref, gated_ref, hs_ref, latent_ref, all_ref = refs
        assembled(ranks, pieces, d_ref, pwt_ref, all_ref)
    else:
        d_ref, pwt_ref, gated_ref, hs_ref, latent_ref = refs
    rows = start_ref.shape[0]
    taps = mmg(act_ref[...], d_ref[...], NT)
    hidden = (
        pltpu.roll(taps[:, :HID], DILATION, 0)
        + taps[:, HID : 2 * HID]
        + pltpu.roll(taps[:, 2 * HID :], rows - DILATION, 0)
    )
    hs_ref[...] = slope(hidden)
    gated = elu(hidden).astype(BF16)
    gated_ref[...] = gated
    latent_ref[...] = start_ref[...] + mmg(gated, pwt_ref[...], NT)


def quant_kernel(ranks, len_ref, latent_ref, c_ref, left_ref, right_ref, hot_ref, hott_ref, *refs):
    half, block = ranks // 2, CODES // ranks
    pieces = refs[:8]
    quant_ref, keep_ref, send_ref, bg_ref, lg_ref, tab_ref, cgs_ref = refs[8:]
    clips, frames, _ = c_ref.shape
    span = frames + 2 * PAD
    time = lax.axis_index("tm")
    mask, twice = masks(clips, frames, len_ref, DG)
    for other in range(SLOTS):
        slot = time ^ other
        for x in range(2):
            piece = pieces[other * 2 + x]
            for z in range(half):
                spot = (x * half + z) * block
                tab_ref[slot, spot : spot + block, :] = piece[z, 2 * HID // ranks :, :]
    for group in range(GROUPS):
        at = slice(group * DG, (group + 1) * DG)
        beyond = slice(D + group * DG, D + (group + 1) * DG)
        first = mm(hot_ref[2 * group], tab_ref[2 * group])
        second = mm(hot_ref[2 * group + 1], tab_ref[2 * group + 1])
        cot = jnp.concatenate(
            [
                part.astype(F32)
                for c in range(clips)
                for part in (left_ref[c, :, beyond], c_ref[c, :, at], right_ref[c, :, beyond])
            ],
            axis=0,
        )
        residual = latent_ref[:, at]
        gap = residual - first
        gap2 = gap - second
        grad = mask * (cot + 2.0 * COMMIT * (gap + gap2))
        quant = (mask * (first + second)).astype(BF16)
        bg_ref[:, at] = grad.astype(BF16)
        for clip in range(clips):
            local = slice(clip * span + PAD, clip * span + PAD + frames)
            to = slice(clip * frames, (clip + 1) * frames)
            lg_ref[to, at] = grad[local]
            quant_ref[clip, :, at] = quant[local]
            for level, diff in ((0, gap), (1, gap2)):
                code_grad = -(twice * diff)[local]
                high = code_grad.astype(BF16)
                cgs_ref[2 * group + level, to, :DG] = high
                cgs_ref[2 * group + level, to, DG:] = (code_grad - high.astype(F32)).astype(BF16)
    for other in range(SLOTS):
        slot = time ^ other
        both = mm(hott_ref[slot], cgs_ref[slot])
        total = both[:, :DG] + both[:, DG:]
        if other % 2 == 0:
            keep_ref[other // 2] = total
        else:
            send_ref[other // 2] = total


def backward_kernel(
    ranks,
    assemble,
    clips,
    len_ref,
    start_ref,
    act_ref,
    gated_ref,
    bg_ref,
    lg_ref,
    hs_ref,
    d_ref,
    pwt_ref,
    fg_ref,
    *outs,
):
    rows = start_ref.shape[0]
    span = rows // clips
    frames = span - 2 * PAD

    def local(value):
        return jnp.concatenate(
            [value[c * span + PAD : c * span + PAD + frames] for c in range(clips)], axis=0
        )

    bg = bg_ref[...]
    hidden_grad = (mm(bg, pwt_ref[...]) * hs_ref[...]).astype(BF16)
    wide = hidden_grad.astype(F32)
    mine = local(hidden_grad)
    pw_grad = mmg(local(bg), local(gated_ref[...]), TN)
    act = act_ref[...].astype(F32)
    windows = [
        local(pltpu.roll(act, DILATION, 0).astype(BF16)),
        local(act_ref[...]),
        local(pltpu.roll(act, rows - DILATION, 0).astype(BF16)),
    ]
    dil_grads = [mmg(mine, windows[tap], TN) for tap in range(KERNEL)]
    if assemble:
        keep_ref, send_ref, all_ref = outs
        half, small = ranks // 2, 2 * HID // ranks
        out_rows = small // 2
        time, rank = lax.axis_index("tm"), lax.axis_index("clip")
        for tap in range(KERNEL):
            all_ref[tap] = dil_grads[tap]
        for r in range(ranks):
            for side in range(2):
                at = r * small + side * out_rows
                all_ref[KERNEL, r * out_rows : (r + 1) * out_rows, side * DG : (side + 1) * DG] = (
                    pw_grad[at : at + out_rows]
                )
        for other in range(4):
            out = (keep_ref, send_ref)[other % 2]
            for x in range(2):
                for z in range(half):
                    at = pl.multiple_of((rank ^ (2 * z + x)) * out_rows, out_rows)
                    to = (x * half + z) * small
                    for side in range(2):
                        out[other // 2, to + side * out_rows : to + (side + 1) * out_rows, :] = (
                            all_ref[
                                time ^ other, pl.ds(at, out_rows), side * DG : (side + 1) * DG
                            ]
                        )
    else:
        dil_ref, pw_ref = outs
        for tap in range(KERNEL):
            dil_ref[tap] = dil_grads[tap]
        pw_ref[...] = pw_grad
    shifted = jnp.concatenate(
        [
            local(pltpu.roll(wide, rows - DILATION, 0).astype(BF16)),
            mine,
            local(pltpu.roll(wide, DILATION, 0).astype(BF16)),
        ],
        axis=1,
    )
    act_grad = mm(shifted, d_ref[...])
    row = lax.broadcasted_iota(jnp.int32, (frames, D), 0) + lax.axis_index("tm") * frames
    for c in range(clips):
        to = slice(c * frames, (c + 1) * frames)
        mask = jnp.where(row < len_ref[c], 1.0, 0.0)
        start = start_ref[c * span + PAD : c * span + PAD + frames, :]
        fg_ref[c] = mask * (lg_ref[to, :] + slope(start) * act_grad[to])


def pack_part(value):
    count = SCALE_GROUPS
    rows = value.shape[0]
    size = rows // count
    steps, levels = [], []
    for group in range(count):
        part = value[group * size : (group + 1) * size]
        top = jnp.maximum(jnp.max(jnp.abs(part), axis=0, keepdims=True), 1e-30)
        level = jnp.ceil(jnp.log2(top) * LEVEL_STEPS)
        scale = jnp.exp2(level / -LEVEL_STEPS) * TOP
        steps.append(jnp.round(part * scale).astype(jnp.int32))
        levels.append(level)
    return steps, levels


def unpack_part(steps, level):
    return steps.astype(jnp.int32).astype(F32) * (
        jnp.exp2(level.astype(jnp.int32).astype(F32) / LEVEL_STEPS) / TOP
    )


def plane_kernel(half, rows, keep_ref, got_ref, own_ref, *outs):
    for part in range(4):
        jy, x = part // 2, part % 2
        levels = []
        for z in range(half):
            at = slice((x * half + z) * rows, (x * half + z + 1) * rows)
            value = keep_ref[jy, at, :] + got_ref[jy, at, :]
            if part == 0:
                own_ref[z] = value
                continue
            out = outs[part - 1]
            steps, more = pack_part(value)
            size = rows // SCALE_GROUPS
            for group, step in enumerate(steps):
                out[z * rows + group * size : z * rows + (group + 1) * size, :] = step.astype(
                    jnp.int16
                )
            levels += more
        if part:
            tail = jnp.concatenate(levels, axis=0).astype(jnp.int32)
            outs[part - 1][half * rows :, :] = tail.astype(jnp.int16)


def line_kernel(half, rows, own_in, *refs):
    gots, own_ref, outs = refs[:3], refs[3], refs[4:]
    size = rows // SCALE_GROUPS
    for z in range(half):
        value = own_in[z]
        pieces = [value[g * size : (g + 1) * size] for g in range(SCALE_GROUPS)]
        for got in gots:
            tail = got[half * rows :, :]
            for g in range(SCALE_GROUPS):
                index = z * SCALE_GROUPS + g
                pieces[g] = pieces[g] + unpack_part(
                    got[z * rows + g * size : z * rows + (g + 1) * size, :],
                    tail[index : index + 1],
                )
        if z == 0:
            for g in range(SCALE_GROUPS):
                own_ref[g * size : (g + 1) * size, :] = pieces[g]
            continue
        steps, levels = pack_part(jnp.concatenate(pieces, axis=0))
        out = outs[z - 1]
        for g, step in enumerate(steps):
            out[g * size : (g + 1) * size, :] = step.astype(jnp.int16)
        pad = jnp.zeros((out.shape[0] - rows - len(levels), DG), F32)
        tail = jnp.concatenate(levels + [pad], axis=0).astype(jnp.int32)
        out[rows:, :] = tail.astype(jnp.int16)


def final_kernel(half, sizes, *refs):
    out_ref, square_ref = refs[-2:]
    squares = jnp.zeros((1, DG), F32)
    place = 0
    for kind, rows in enumerate(sizes):
        own_ref, *gots = refs[kind * half : (kind + 1) * half]
        size = rows // SCALE_GROUPS
        for g in range(SCALE_GROUPS):
            at = slice(g * size, (g + 1) * size)
            value = own_ref[at, :]
            for got in gots:
                value = value + unpack_part(got[at, :], got[rows:, :][g : g + 1])
            out_ref[place : place + size, :] = value
            squares = squares + jnp.sum(value * value, axis=0, keepdims=True)
            place += size
    square_ref[...] = jnp.broadcast_to(jnp.sum(squares, axis=1, keepdims=True), (8, 128))


def stepped(weight, first, second, grad, rate, fix1, fix2):
    first_new = FIRST_DECAY * first + (1.0 - FIRST_DECAY) * grad
    second_new = SECOND_DECAY * second + (1.0 - SECOND_DECAY) * grad * grad
    change = (first_new * fix1) / (jnp.sqrt(second_new * fix2) + EPSILON) + WEIGHT_DECAY * weight
    return weight - rate * change, second_new


def update_kernel(fix_ref, square_ref, *refs):
    pieces = refs[:4]
    dil, pw, table = refs[4:7], refs[7:10], refs[10:13]
    norm_ref = refs[13]
    dil_out, pw_out, table_out = refs[14:17], refs[17:20], refs[20:23]
    out_rows = dil[0].shape[1]
    small = 2 * out_rows
    time = lax.axis_index("tm")
    count = KERNEL * D * HID + D * HID + SLOTS * CODES * DG
    norm = jnp.sqrt(square_ref[...][:1, :1])
    limit = jnp.sqrt(jnp.full((1, 1), float(count), F32))
    scale = limit / jnp.maximum(norm, limit)
    norm_ref[...] = jnp.broadcast_to(norm, norm_ref.shape)
    fixes = (fix_ref[0], fix_ref[1])
    for other in range(4):
        quarter = time ^ other
        piece = pieces[other]
        grad = piece[small:, :] * scale
        state = [v[quarter] for v in table]
        weight, second = stepped(*state, grad, RATE_CODE, *fixes)
        table_out[0][quarter] = weight
        table_out[1][quarter] = grad
        table_out[2][quarter] = second

        @pl.when(quarter < KERNEL)
        def _():
            tap = jnp.minimum(quarter, KERNEL - 1)
            for side in range(2):
                to = slice(side * DG, (side + 1) * DG)
                grad = piece[side * out_rows : (side + 1) * out_rows, :] * scale
                state = [v[tap, :, to] for v in dil]
                weight, second = stepped(*state, grad, BITRATE_FACTOR, *fixes)
                dil_out[0][tap, :, to] = weight
                dil_out[1][tap, :, to] = grad
                dil_out[2][tap, :, to] = second

        @pl.when(quarter == KERNEL)
        def _():
            grad = piece[:small, :] * scale
            weight, second = stepped(*[v[...] for v in pw], grad, BITRATE_FACTOR, *fixes)
            pw_out[0][...] = weight
            pw_out[1][...] = grad
            pw_out[2][...] = second


def halo(features, cotangent, code_ids):
    times = lax.axis_size("tm")
    frames = features.shape[1]
    ids = jnp.moveaxis(code_ids, 0, 2)

    def packed(low, high):
        part = ids[:, low:high]
        return jnp.concatenate(
            [
                features[:, low:high],
                cotangent[:, low:high],
                (part // 32).astype(BF16),
                (part % 32).astype(BF16),
            ],
            axis=2,
        )

    from_left = lax.ppermute(
        packed(frames - PAD, frames), "tm", [(i, i + 1) for i in range(times - 1)]
    )
    from_right = lax.ppermute(packed(0, PAD), "tm", [(i + 1, i) for i in range(times - 1)])
    return from_left, from_right


def shards(
    features,
    cotangent,
    clip_lengths,
    code_ids,
    step_count,
    dilated_kernel_weight,
    pointwise_conv,
    codebooks,
    dilated_first_moment,
    dilated_second_moment,
    pointwise_first,
    pointwise_second,
    codebook_first,
    codebook_second,
):
    ranks = lax.axis_size("clip")
    rank, time = lax.axis_index("clip"), lax.axis_index("tm")
    clips, frames, _ = features.shape
    half = ranks // 2
    out_rows = HID // ranks
    block = CODES // ranks
    small = 2 * out_rows
    rows = clips * (frames + 2 * PAD)
    smem = pl.BlockSpec(memory_space=pltpu.SMEM)
    shape = jax.ShapeDtypeStruct
    assemble = out_rows % 16 == 0
    dil_state = [
        v.transpose(0, 2, 1)
        for v in (dilated_kernel_weight, dilated_first_moment, dilated_second_moment)
    ]
    pw_state = [v.T for v in (pointwise_conv, pointwise_first, pointwise_second)]
    table_state = [codebooks, codebook_first, codebook_second]

    if assemble:
        mine = pl.pallas_call(
            prep_kernel,
            out_shape=shape((small + block, DG), BF16),
            in_specs=whole(3),
            out_specs=whole(1)[0],
            compiler_params=params(),
            name="prep",
        )(dil_state[0], pw_state[0], codebooks)
    else:
        taps = dil_state[0].astype(BF16).reshape(KERNEL, out_rows, 2, DG).transpose(0, 2, 1, 3)
        quarters = jnp.concatenate(
            [taps.reshape(KERNEL, small, DG), pw_state[0].astype(BF16)[None]], axis=0
        )
        quarters = jnp.concatenate([quarters, codebooks.astype(BF16)], axis=1)
        mine = lax.dynamic_index_in_dim(quarters, time, 0, keepdims=False)

    line = jnp.stack([mine] + [swap(mine, 2 * z, 0) for z in range(1, half)], axis=0)
    features, cotangent, code_ids, line = lax.optimization_barrier(
        (features, cotangent, code_ids, line)
    )
    plane = [line, swap(line, 1, 0), swap(line, 0, 2), swap(line, 1, 2)]
    left, right = halo(features, cotangent, code_ids)

    start, act, hot, hott = pl.pallas_call(
        functools.partial(early_kernel, ranks),
        out_shape=(
            shape((rows, D), F32),
            shape((rows, D), BF16),
            shape((SLOTS, rows, CODES), BF16),
            shape((SLOTS, CODES, clips * frames), BF16),
        ),
        in_specs=[smem] + whole(4),
        out_specs=tuple(whole(4)),
        compiler_params=params(8),
        name="early",
    )(clip_lengths, features, left, right, code_ids)

    plane[3], hot = lax.optimization_barrier((plane[3], hot))
    pieces = []
    for other in range(4):
        for value in plane[other & 2 : (other & 2) + 2]:
            pieces.append(swap(value, 0, 1) if other & 1 else value)

    weights = (shape((KERNEL * HID, D), BF16), shape((D, HID), BF16))
    given = pieces
    if not assemble:
        order = rank ^ jnp.arange(ranks)
        stacked = jnp.stack(
            [
                jnp.stack([v[:, :small] for v in pieces[2 * o : 2 * o + 2]], axis=1).reshape(
                    ranks, small, DG
                )
                for o in range(4)
            ],
            axis=0,
        )
        stacked = jnp.take(jnp.take(stacked, time ^ jnp.arange(4), axis=0), order, axis=1)
        dil = stacked[:KERNEL].reshape(KERNEL, ranks, 2, out_rows, DG)
        dil = dil.transpose(0, 1, 3, 2, 4).reshape(KERNEL * HID, D)
        given = [dil, stacked[3].reshape(D, HID)]
    outs = pl.pallas_call(
        functools.partial(conv_kernel, ranks, assemble),
        out_shape=(weights if assemble else ())
        + (shape((rows, HID), BF16), shape((rows, HID), F32), shape((rows, D), F32)),
        in_specs=whole(2 + len(given)),
        out_specs=tuple(whole(5 if assemble else 3)),
        scratch_shapes=[pltpu.VMEM((4, HID, D), BF16)] if assemble else [],
        compiler_params=params(10),
        name="conv",
    )(start, act, *given)
    dil, pwt, gated, hs, latent = tuple(outs) if assemble else tuple(given) + tuple(outs)

    quant, keep, send, bg, lg = pl.pallas_call(
        functools.partial(quant_kernel, ranks),
        out_shape=(
            shape((clips, frames, D), BF16),
            shape((2, CODES, DG), F32),
            shape((2, CODES, DG), F32),
            shape((rows, D), BF16),
            shape((clips * frames, D), F32),
        ),
        in_specs=[smem] + whole(14),
        out_specs=tuple(whole(5)),
        scratch_shapes=[
            pltpu.VMEM((SLOTS, CODES, DG), BF16),
            pltpu.VMEM((SLOTS, clips * frames, 2 * DG), BF16),
        ],
        compiler_params=params(16),
        name="quant",
    )(clip_lengths, latent, cotangent, left, right, hot, hott, *pieces)

    if assemble:
        grads = (shape((2, ranks * small, DG), F32),) * 2
    else:
        grads = (shape((KERNEL, HID, D), F32), shape((D, HID), F32))
    fg, first_grad, second_grad = pl.pallas_call(
        functools.partial(backward_kernel, ranks, assemble, clips),
        out_shape=(shape((clips, frames, D), F32),) + grads,
        in_specs=[smem] + whole(8),
        out_specs=tuple(whole(3)),
        scratch_shapes=[pltpu.VMEM((4, HID, D), F32)] if assemble else [],
        compiler_params=params(16),
        name="backward",
    )(clip_lengths, start, act, gated, bg, lg, hs, dil, pwt)

    if assemble:
        keep_d, send_d = first_grad, second_grad
    else:
        parts = jnp.concatenate(
            [
                first_grad.reshape(KERNEL, ranks, out_rows, 2, DG)
                .transpose(0, 1, 3, 2, 4)
                .reshape(KERNEL, ranks, small, DG),
                second_grad.reshape(1, ranks, small, DG),
            ],
            axis=0,
        )
        seq = jnp.concatenate([jnp.arange(0, ranks, 2), jnp.arange(1, ranks, 2)])
        parts = jnp.take(jnp.take(parts, time ^ jnp.arange(4), axis=0), rank ^ seq, axis=1)
        parts = parts.reshape(2, 2, ranks * small, DG)
        keep_d, send_d = parts[:, 0], parts[:, 1]

    def plane_sent(keep, got, size, tag):
        packed = half * size + half * SCALE_GROUPS
        own, to_x, to_y, to_xy = pl.pallas_call(
            functools.partial(plane_kernel, half, size),
            out_shape=(shape((half, size, DG), F32),) + (shape((packed, DG), jnp.int16),) * 3,
            in_specs=whole(2),
            out_specs=tuple(whole(4)),
            compiler_params=params(),
            name="plane_" + tag,
        )(keep, got)
        return own, swap(to_x, 1, 0), swap(to_y, 0, 2), swap(to_xy, 1, 2)

    def line_sent(parts, size, tag):
        out = pl.pallas_call(
            functools.partial(line_kernel, half, size),
            out_shape=(shape((size, DG), F32),)
            + (shape((size + 16, DG), jnp.int16),) * (half - 1),
            in_specs=whole(4),
            out_specs=tuple(whole(half)),
            compiler_params=params(),
            name="line_" + tag,
        )(*parts)
        return [out[0]] + [swap(out[z], 2 * z, 0) for z in range(1, half)]

    got_c, got_d = swap(send, 0, 1), swap(send_d, 0, 1)
    parts_c = plane_sent(keep, got_c, block, "codes")
    own_c, keep_d = lax.optimization_barrier((parts_c[0], keep_d))
    parts_d = plane_sent(keep_d, got_d, small, "conv")
    parts_c = line_sent((own_c,) + parts_c[1:], block, "codes")
    own_d, first_c = lax.optimization_barrier((parts_d[0], parts_c[0]))
    parts_c = [first_c] + parts_c[1:]
    parts_d = line_sent((own_d,) + parts_d[1:], small, "conv")
    total = small + block
    piece, squared = pl.pallas_call(
        functools.partial(final_kernel, half, (small, block)),
        out_shape=(shape((total, DG), F32), shape((8, 128), F32)),
        in_specs=whole(2 * half),
        out_specs=tuple(whole(2)),
        compiler_params=params(),
        name="final",
    )(*parts_d, *parts_c)

    fours = [piece, None, swap(piece, 0, 2), None]
    step = 1
    while step < ranks:
        squared = squared + swap(squared, step, 0)
        step *= 2
    across, squared = lax.optimization_barrier((fours[2], squared))
    fours[1], fours[2], fours[3] = swap(piece, 0, 1), across, swap(across, 0, 1)
    squared = squared + swap(squared, 0, 2)
    squared = squared + swap(squared, 0, 1)
    steps = step_count[0].astype(F32)
    decays = jnp.stack([1.0 / (1.0 - FIRST_DECAY**steps), 1.0 / (1.0 - SECOND_DECAY**steps)])
    if assemble:
        state = dil_state + pw_state + table_state
        norm, *new = pl.pallas_call(
            update_kernel,
            out_shape=(shape((8, 128), F32),) + tuple(shape(v.shape, F32) for v in state),
            in_specs=[smem] + whole(14),
            out_specs=tuple(whole(10)),
            compiler_params=params(),
            name="update",
        )(decays, squared, *fours, *state)
        norm = norm[0, :1]
        dil_new, pw_new, table_new = new[:3], new[3:6], new[6:]
    else:
        four = jnp.take(jnp.stack(fours, axis=0), time ^ jnp.arange(4), axis=0)
        raw = four[:KERNEL, :small].reshape(KERNEL, 2, out_rows, DG)
        raw = raw.transpose(0, 2, 1, 3).reshape(KERNEL, out_rows, D)
        count = KERNEL * D * HID + D * HID + SLOTS * CODES * DG
        limit = jnp.sqrt(jnp.float32(count))
        norm = jnp.sqrt(squared[0, :1])
        scale = limit / jnp.maximum(norm[0], limit)
        new = []
        for state, grad, rate in (
            (dil_state, raw, BITRATE_FACTOR),
            (pw_state, four[3, :small], BITRATE_FACTOR),
            (table_state, four[:, small:], RATE_CODE),
        ):
            grad = grad * scale
            weight, second = stepped(*state, grad, rate, decays[0], decays[1])
            new.append((weight, grad, second))
        dil_new, pw_new, table_new = new
    return (
        quant,
        fg,
        norm,
        *[v.transpose(0, 2, 1) for v in dil_new],
        *[v.T for v in pw_new],
        *table_new,
    )


def solution(mesh):
    in_specs = (
        P("clip", "tm", None),
        P("clip", "tm", None),
        P("clip"),
        P(None, "clip", "tm"),
        P(),
        P(None, None, "clip"),
        P(None, "clip"),
        P(None, "clip", None),
        P(None, None, "clip"),
        P(None, None, "clip"),
        P(None, "clip"),
        P(None, "clip"),
        P(None, "clip", None),
        P(None, "clip", None),
    )
    out_specs = (
        P("clip", "tm", None),
        P("clip", "tm", None),
        P(),
        P(None, None, "clip"),
        P(None, None, "clip"),
        P(None, None, "clip"),
        P(None, "clip"),
        P(None, "clip"),
        P(None, "clip"),
        P(None, "clip", None),
        P(None, "clip", None),
        P(None, "clip", None),
    )
    return jax.shard_map(shards, mesh=mesh, in_specs=in_specs, out_specs=out_specs, check_vma=False)
```

time: 167 us -> 112 us (0.67)
  local copies, waits for them, and re-layouts: 29.4 us -> 5.18 us
  other arithmetic: 17 us -> 0.18 us
  waiting for transfers between devices: 50.6 us -> 38.9 us
  starting transfers between devices: 35.8 us -> 46.9 us
  Pallas kernels: 26.8 us -> 18.2 us
  between operations: 5.95 us -> 1.79 us
    ppermute x26 -> x32, starting transfers between devices: 31.3 us -> 44.3 us  [swap(): return lax.ppermute(value, ('clip', 'tm'), pairs)]
    ppermute x26 -> x32, waiting for transfers between devices: 50.6 us -> 38.9 us  [swap(): return lax.ppermute(value, ('clip', 'tm'), pairs)]
    pallas_call x6 -> x11, Pallas kernels: 26.8 us -> 18.2 us  [the longest x1 4.89 us: shards(): pl.pallas_call(functools.partial(quant_kernel, ranks), out_shape=(shape((...]
    gather x6 -> x0, local copies, waits for them, and re-layouts: 7.73 us -> none  [the longest x2 3.81 us: shards(): jnp.take(jnp.take(parts, time ^ jnp.arange(4), axis=0), rank ^ seq, axis=1)]
    concatenate x2, local copies, waits for them, and re-layouts: 6.47 us -> 0.19 us  [packed(): jnp.concatenate([features[:, low:high], cotangent[:, low:high], (part //...]
    unnamed x74 -> x32, local copies, waits for them, and re-layouts: 7.32 us -> 2.87 us
    reshape x6 -> x0, local copies, waits for them, and re-layouts: 4 us -> none  [the longest x2 2.47 us: shards(): dil_grad.reshape(KERNEL, ranks, out_rows, 2, DG).transpose(0, 1, 3, 2, 4)]
    convert_element_type x5 -> x3, other arithmetic: 3.9 us -> 0.04 us  [the longest x2 0.03 us: packed(): (part % 32).astype(BF16)]
  transfers between devices with their start and end apart: 28 -> 34, of which waited for: 13 -> 18; matrix products, arithmetic and copies ran while one was open for 17% -> 2% of each run, Pallas kernels for 7% -> 8%
where the time goes in v2:
time: 112 us; the launch traced here: 111 us
  starting transfers between devices  46.9 us (42%)
  waiting for transfers between devices  38.9 us (35%)
  Pallas kernels  18.2 us (16%)
  local copies, waits for them, and re-layouts  5.18 us (5%)
  between operations  1.79 us (2%)
    ppermute x32, starting transfers between devices, swap(): return lax.ppermute(value, ('clip', 'tm'), pairs)  44.3 us
    ppermute x32, waiting for transfers between devices, swap(): return lax.ppermute(value, ('clip', 'tm'), pairs)  38.9 us
    pallas_call x1, Pallas kernels, shards(): pl.pallas_call(functools.partial(quant_kernel, ranks), out_shape=(shape((...  4.89 us
    pallas_call x1, Pallas kernels, shards(): pl.pallas_call(functools.partial(early_kernel, ranks), out_shape=(shape((...  4.32 us
    pallas_call x1, Pallas kernels, shards(): pl.pallas_call(functools.partial(backward_kernel, ranks, assemble, clips)...  3.25 us
    unnamed x32, local copies, waits for them, and re-layouts  2.87 us
    pallas_call x1, Pallas kernels, shards(): pl.pallas_call(update_kernel, out_shape=(shape((8, 128), F32),) + tuple((...  2.74 us
  transfers between devices with their start and end apart: 34, of which 18 were waited for; matrix products, arithmetic and copies ran while one was open for 2% of the time, Pallas kernels for 8%

profile of v2, /device:TPU:0, one launch (start us, length us, event | category | flops | bytes accessed | tf_op | source)
XLA Modules:
  0.0 111.2 jit_solution(18393680287693979513)
XLA Ops:
  3.5 3.1 %collective-permute-start = (bf16[192,256]{1,0:T(8,128)(2,1)S(1)}, bf16[192,256]{1,0:T(8,128)(2,1)S(1)}, u32[]{:S(2)}, u32[]{:S(2)}) collective-permute-start(bf16[192,256]{1,0:T(8,128)(2,1)S(1)} %prep.1), channel_id=1, source_target_pairs={{0,8},{1,9},{2,10},{3,11},{4,12},{5,13},{6,14},{7,15},{8,0},{9,1},... | collective-permute-start | bytes 294920 | tf_op jit(solution)/shard_map/ppermute | solution.py:70
  6.6 2.6 %collective-permute-start.1 = (bf16[192,256]{1,0:T(8,128)(2,1)S(1)}, bf16[192,256]{1,0:T(8,128)(2,1)S(1)}, u32[]{:S(2)}, u32[]{:S(2)}) collective-permute-start(bf16[192,256]{1,0:T(8,128)(2,1)S(1)} %prep.1), channel_id=1, source_target_pairs={{0,16},{1,17},{2,18},{3,19},{4,20},{5,21},{6,22},{7,23},{8,24},{9,... | collective-permute-start | bytes 294920 | tf_op jit(solution)/shard_map/ppermute | solution.py:70
  9.4 7.6 %collective-permute-done.1 = bf16[192,256]{1,0:T(8,128)(2,1)S(1)} collective-permute-done((bf16[192,256]{1,0:T(8,128)(2,1)S(1)}, bf16[192,256]{1,0:T(8,128)(2,1)S(1)}, u32[]{:S(2)}, u32[]{:S(2)}) %collective-permute-start.1) | collective-permute-done | bytes 98336 | tf_op jit(solution)/shard_map/ppermute | solution.py:70
  17.1 2.5 %collective-permute-start.9 = (bf16[4,192,256]{2,1,0:T(8,128)(2,1)S(1)}, bf16[4,192,256]{2,1,0:T(8,128)(2,1)S(1)}, u32[]{:S(2)}, u32[]{:S(2)}) collective-permute-start(bf16[4,192,256]{2,1,0:T(8,128)(2,1)S(1)} %pad_maximum_fusion.refs_0_), channel_id=1, source_target_pairs={{0,6},{1,7},{2,4},{3,5},{4,2},{5,3},{6,0},{7,1},{8,14},{9,15},{10,... | collective-permute-start | bytes 1179656 | tf_op jit(solution)/shard_map/ppermute | solution.py:70
  22.4 1.3 %collective-permute-start.3 = (bf16[2,8,1032]{2,1,0:T(8,128)(2,1)S(1)}, bf16[2,8,1032]{2,1,0:T(8,128)(2,1)S(1)}, u32[]{:S(2)}, u32[]{:S(2)}) collective-permute-start(bf16[2,8,1032]{2,1,0:T(8,128)(2,1)S(1)} %concatenate.6), channel_id=1, source_target_pairs={{0,1},{1,2},{2,3},{4,5},{5,6},{6,7},{8,9},{9,10},{10,11},{12,13},{... | collective-permute-start | bytes 99080 | tf_op jit(solution)/shard_map/ppermute | solution.py:488
  23.8 1.3 %collective-permute-start.4 = (bf16[2,8,1032]{2,1,0:T(8,128)(2,1)S(1)}, bf16[2,8,1032]{2,1,0:T(8,128)(2,1)S(1)}, u32[]{:S(2)}, u32[]{:S(2)}) collective-permute-start(bf16[2,8,1032]{2,1,0:T(8,128)(2,1)S(1)} %concatenate.7), channel_id=1, source_target_pairs={{1,0},{2,1},{3,2},{5,4},{6,5},{7,6},{9,8},{10,9},{11,10},{13,12},{... | collective-permute-start | bytes 99080 | tf_op jit(solution)/shard_map/ppermute | solution.py:491
  25.1 9.9 %collective-permute-start.6 = (bf16[4,192,256]{2,1,0:T(8,128)(2,1)S(1)}, bf16[4,192,256]{2,1,0:T(8,128)(2,1)S(1)}, u32[]{:S(2)}, u32[]{:S(2)}) collective-permute-start(bf16[4,192,256]{2,1,0:T(8,128)(2,1)S(1)} %pad_maximum_fusion.refs_0_), channel_id=1, source_target_pairs={{0,1},{1,0},{2,3},{3,2},{4,5},{5,4},{6,7},{7,6},{8,9},{9,8},{10,11... | collective-permute-start | bytes 1179656 | tf_op jit(solution)/shard_map/ppermute | solution.py:70
  35.0 4.3 %early.1 = (f32[544,512]{1,0:T(8,128)S(1)}, bf16[544,512]{1,0:T(8,128)(2,1)S(1)}, bf16[4,544,1024]{2,1,0:T(8,128)(2,1)S(1)}, bf16[4,1024,512]{2,1,0:T(8,128)(2,1)S(1)}) custom-call(s32[2]{0:T(128)S(1)} %copy-done.15, bf16[2,256,512]{2,1,0:T(8,128)(2,1)S(1)} %copy-done.5, bf16[2,8,1032]{2,1,0:T(8,128)(2,1)S(1)} %collective-permute-done.3.left_ref, ...), custom_call_target="tpu_custom_call" | custom-call | tf_op jit(solution)/shard_map/early/pallas_call | solution.py:553
  42.5 1.2 %conv.1 = (bf16[768,512]{1,0:T(8,128)(2,1)S(1)}, bf16[512,256]{1,0:T(8,128)(2,1)S(1)}, bf16[544,256]{1,0:T(8,128)(2,1)S(1)}, f32[544,256]{1,0:T(8,128)S(1)}, f32[544,512]{1,0:T(8,128)S(1)}) custom-call(f32[544,512]{1,0:T(8,128)S(1)} %get-tuple-element.72.start_ref, bf16[544,512]{1,0:T(8,128)(2,1)S(1)} %get-tuple-element.73.act_ref, ...), custom_call_target="tpu_custom_call" | custom-call | tf_op jit(solution)/shard_map/conv/pallas_call | solution.py:590
  43.8 4.9 %quant.1 = (bf16[2,256,512]{2,1,0:T(8,128)(2,1)}, f32[2,1024,256]{2,1,0:T(8,128)S(1)}, f32[2,1024,256]{2,1,0:T(8,128)S(1)}, bf16[544,512]{1,0:T(8,128)(2,1)S(1)}, f32[512,512]{1,0:T(8,128)S(1)}) custom-call(s32[2]{0:T(128)S(1)} %copy-done.15, f32[544,512]{1,0:T(8,128)S(1)} %get-tuple-element.77.latent_ref, bf16[2,256,512]{2,1,0:T(8,128)(2,1)S(1)} %copy-done.4, ...), custom_call_target="tpu_custom_call" | custom-call | tf_op jit(solution)/shard_map/quant/pallas_call | solution.py:602
  49.1 3.2 %backward.1 = (f32[2,256,512]{2,1,0:T(8,128)}, f32[2,512,256]{2,1,0:T(8,128)S(1)}, f32[2,512,256]{2,1,0:T(8,128)S(1)}) custom-call(s32[2]{0:T(128)S(1)} %copy-done.15, f32[544,512]{1,0:T(8,128)S(1)} %get-tuple-element.72.start_ref, bf16[544,512]{1,0:T(8,128)(2,1)S(1)} %get-tuple-element.73.act_ref, bf16[544,256]{1,0:T(8,128)(2,1)S(1)} %get-tuple-element.81.gated_ref, ...), custom_call_target="tpu_custom_call" | custom-call | tf_op jit(solution)/shard_map/backward/pallas_call | solution.py:625
  53.4 1.6 %collective-permute-start.14 = (s16[528,256]{1,0:T(8,128)(2,1)S(1)}, s16[528,256]{1,0:T(8,128)(2,1)S(1)}, u32[]{:S(2)}, u32[]{:S(2)}) collective-permute-start(s16[528,256]{1,0:T(8,128)(2,1)S(1)} %get-tuple-element.96), channel_id=1, source_target_pairs={{0,4},{1,5},{2,6},{3,7},{4,0},{5,1},{6,2},{7,3},{8,12},{9,13},{10,... | collective-permute-start | bytes 811016 | tf_op jit(solution)/shard_map/ppermute | solution.py:70
  56.0 1.1 %collective-permute-start.16 = (s16[528,256]{1,0:T(8,128)(2,1)S(1)}, s16[528,256]{1,0:T(8,128)(2,1)S(1)}, u32[]{:S(2)}, u32[]{:S(2)}) collective-permute-start(s16[528,256]{1,0:T(8,128)(2,1)S(1)} %get-tuple-element.98), channel_id=1, source_target_pairs={{0,6},{1,7},{2,4},{3,5},{4,2},{5,3},{6,0},{7,1},{8,14},{9,15},{10,... | collective-permute-start | bytes 811016 | tf_op jit(solution)/shard_map/ppermute | solution.py:70
  57.6 1.4 %collective-permute-start.17 = (s16[272,256]{1,0:T(8,128)(2,1)S(1)}, s16[272,256]{1,0:T(8,128)(2,1)S(1)}, u32[]{:S(2)}, u32[]{:S(2)}) collective-permute-start(s16[272,256]{1,0:T(8,128)(2,1)S(1)} %get-tuple-element.101), channel_id=1, source_target_pairs={{0,4},{1,5},{2,6},{3,7},{4,0},{5,1},{6,2},{7,3},{8,12},{9,13},{10,... | collective-permute-start | bytes 417800 | tf_op jit(solution)/shard_map/ppermute | solution.py:70
  60.0 2.7 %collective-permute-done.14.refs_0_ = s16[528,256]{1,0:T(8,128)(2,1)S(1)} collective-permute-done((s16[528,256]{1,0:T(8,128)(2,1)S(1)}, s16[528,256]{1,0:T(8,128)(2,1)S(1)}, u32[]{:S(2)}, u32[]{:S(2)}) %collective-permute-start.14) | collective-permute-done | bytes 270368 | tf_op jit(solution)/shard_map/ppermute | solution.py:70
  62.8 2.0 %collective-permute-start.19 = (s16[272,256]{1,0:T(8,128)(2,1)S(1)}, s16[272,256]{1,0:T(8,128)(2,1)S(1)}, u32[]{:S(2)}, u32[]{:S(2)}) collective-permute-start(s16[272,256]{1,0:T(8,128)(2,1)S(1)} %get-tuple-element.103), channel_id=1, source_target_pairs={{0,6},{1,7},{2,4},{3,5},{4,2},{5,3},{6,0},{7,1},{8,14},{9,15},{10,... | collective-permute-start | bytes 417800 | tf_op jit(solution)/shard_map/ppermute | solution.py:70
  64.8 5.2 %collective-permute-done.15.refs_1_ = s16[528,256]{1,0:T(8,128)(2,1)S(1)} collective-permute-done((s16[528,256]{1,0:T(8,128)(2,1)S(1)}, s16[528,256]{1,0:T(8,128)(2,1)S(1)}, u32[]{:S(2)}, u32[]{:S(2)}) %collective-permute-start.15) | collective-permute-done | bytes 270368 | tf_op jit(solution)/shard_map/ppermute | solution.py:70
  71.6 2.2 %collective-permute-done.18.refs_1_ = s16[272,256]{1,0:T(8,128)(2,1)S(1)} collective-permute-done((s16[272,256]{1,0:T(8,128)(2,1)S(1)}, s16[272,256]{1,0:T(8,128)(2,1)S(1)}, u32[]{:S(2)}, u32[]{:S(2)}) %collective-permute-start.18) | collective-permute-done | bytes 139296 | tf_op jit(solution)/shard_map/ppermute | solution.py:70
  73.8 1.9 %collective-permute-done.19.refs_2_ = s16[272,256]{1,0:T(8,128)(2,1)S(1)} collective-permute-done((s16[272,256]{1,0:T(8,128)(2,1)S(1)}, s16[272,256]{1,0:T(8,128)(2,1)S(1)}, u32[]{:S(2)}, u32[]{:S(2)}) %collective-permute-start.19) | collective-permute-done | bytes 139296 | tf_op jit(solution)/shard_map/ppermute | solution.py:70
  75.9 2.4 %collective-permute-start.20 = (s16[80,256]{1,0:T(8,128)(2,1)S(1)}, s16[80,256]{1,0:T(8,128)(2,1)S(1)}, u32[]{:S(2)}, u32[]{:S(2)}) collective-permute-start(s16[80,256]{1,0:T(8,128)(2,1)S(1)} %get-tuple-element.105), channel_id=1, source_target_pairs={{0,8},{1,9},{2,10},{3,11},{4,12},{5,13},{6,14},{7,15},{8,0},{9,1},... | collective-permute-start | bytes 122888 | tf_op jit(solution)/shard_map/ppermute | solution.py:70
  78.4 2.9 %collective-permute-start.24 = (s16[144,256]{1,0:T(8,128)(2,1)S(1)}, s16[144,256]{1,0:T(8,128)(2,1)S(1)}, u32[]{:S(2)}, u32[]{:S(2)}) collective-permute-start(s16[144,256]{1,0:T(8,128)(2,1)S(1)} %get-tuple-element.110), channel_id=1, source_target_pairs={{0,16},{1,17},{2,18},{3,19},{4,20},{5,21},{6,22},{7,23},{8,24},{9,... | collective-permute-start | bytes 221192 | tf_op jit(solution)/shard_map/ppermute | solution.py:70
  81.3 1.4 %collective-permute-start.25 = (s16[144,256]{1,0:T(8,128)(2,1)S(1)}, s16[144,256]{1,0:T(8,128)(2,1)S(1)}, u32[]{:S(2)}, u32[]{:S(2)}) collective-permute-start(s16[144,256]{1,0:T(8,128)(2,1)S(1)} %get-tuple-element.111), channel_id=1, source_target_pairs={{0,24},{1,25},{2,26},{3,27},{4,28},{5,29},{6,30},{7,31},{8,16},{9,... | collective-permute-start | bytes 221192 | tf_op jit(solution)/shard_map/ppermute | solution.py:70
  82.9 2.3 %collective-permute-start.22 = (s16[80,256]{1,0:T(8,128)(2,1)S(1)}, s16[80,256]{1,0:T(8,128)(2,1)S(1)}, u32[]{:S(2)}, u32[]{:S(2)}) collective-permute-start(s16[80,256]{1,0:T(8,128)(2,1)S(1)} %get-tuple-element.107), channel_id=1, source_target_pairs={{0,24},{1,25},{2,26},{3,27},{4,28},{5,29},{6,30},{7,31},{8,16},{9,... | collective-permute-start | bytes 122888 | tf_op jit(solution)/shard_map/ppermute | solution.py:70
  85.2 5.8 %collective-permute-done.21.refs_2_ = s16[80,256]{1,0:T(8,128)(2,1)S(1)} collective-permute-done((s16[80,256]{1,0:T(8,128)(2,1)S(1)}, s16[80,256]{1,0:T(8,128)(2,1)S(1)}, u32[]{:S(2)}, u32[]{:S(2)}) %collective-permute-start.21) | collective-permute-done | bytes 40992 | tf_op jit(solution)/shard_map/ppermute | solution.py:70
  91.1 1.3 %collective-permute-start.27 = (f32[8,128]{1,0:T(8,128)S(1)}, f32[8,128]{1,0:T(8,128)S(1)}, u32[]{:S(2)}, u32[]{:S(2)}) collective-permute-start(f32[8,128]{1,0:T(8,128)S(1)} %get-tuple-element.113), channel_id=1, source_target_pairs={{0,4},{1,5},{2,6},{3,7},{4,0},{5,1},{6,2},{7,3},{8,12},{9,13},{10,... | collective-permute-start | bytes 12296 | tf_op jit(solution)/shard_map/ppermute | solution.py:70
  92.4 2.4 %collective-permute-done.27 = f32[8,128]{1,0:T(8,128)S(1)} collective-permute-done((f32[8,128]{1,0:T(8,128)S(1)}, f32[8,128]{1,0:T(8,128)S(1)}, u32[]{:S(2)}, u32[]{:S(2)}) %collective-permute-start.27) | collective-permute-done | bytes 4128 | tf_op jit(solution)/shard_map/ppermute | solution.py:70
  95.8 2.6 %collective-permute-done.28 = f32[8,128]{1,0:T(8,128)S(1)} collective-permute-done((f32[8,128]{1,0:T(8,128)S(1)}, f32[8,128]{1,0:T(8,128)S(1)}, u32[]{:S(2)}, u32[]{:S(2)}) %collective-permute-start.28) | collective-permute-done | bytes 4128 | tf_op jit(solution)/shard_map/ppermute | solution.py:70
  98.4 1.6 %collective-permute-start.29 = (f32[8,128]{1,0:T(8,128)S(1)}, f32[8,128]{1,0:T(8,128)S(1)}, u32[]{:S(2)}, u32[]{:S(2)}) collective-permute-start(f32[8,128]{1,0:T(8,128)S(1)} %add.30), channel_id=1, source_target_pairs={{0,16},{1,17},{2,18},{3,19},{4,20},{5,21},{6,22},{7,23},{8,24},{9,... | collective-permute-start | bytes 12296 | tf_op jit(solution)/shard_map/ppermute | solution.py:70
  100.1 2.9 %collective-permute-done.29 = f32[8,128]{1,0:T(8,128)S(1)} collective-permute-done((f32[8,128]{1,0:T(8,128)S(1)}, f32[8,128]{1,0:T(8,128)S(1)}, u32[]{:S(2)}, u32[]{:S(2)}) %collective-permute-start.29) | collective-permute-done | bytes 4128 | tf_op jit(solution)/shard_map/ppermute | solution.py:70
  103.0 2.0 %collective-permute-start.30 = (f32[8,128]{1,0:T(8,128)S(1)}, f32[8,128]{1,0:T(8,128)S(1)}, u32[]{:S(2)}, u32[]{:S(2)}) collective-permute-start(f32[8,128]{1,0:T(8,128)S(1)} %add.31), channel_id=1, source_target_pairs={{0,2},{1,3},{2,0},{3,1},{4,6},{5,7},{6,4},{7,5},{8,10},{9,11},{10,... | collective-permute-start | bytes 12296 | tf_op jit(solution)/shard_map/ppermute | solution.py:70
  106.7 1.1 collective-permute-done.31
  107.9 2.7 %update.1 = (f32[8,128]{1,0:T(8,128)S(1)}, f32[3,32,512]{2,1,0:T(8,128)}, f32[3,32,512]{2,1,0:T(8,128)}, f32[3,32,512]{2,1,0:T(8,128)}, f32[64,256]{1,0:T(8,128)...) custom-call(f32[2]{0:T(128)S(1)} %pad_maximum_fusion.1.fix_ref, ...), custom_call_target="tpu_custom_call" | custom-call | tf_op jit(solution)/shard_map/update/pallas_call | solution.py:707
  (94 shorter events, 18.0 us)
Async XLA Ops:
  3.5 5.9 %collective-permute-start = (bf16[192,256]{1,0:T(8,128)(2,1)S(1)}, bf16[192,256]{1,0:T(8,128)(2,1)S(1)}, u32[]{:S(2)}, u32[]{:S(2)}) collective-permute-start(bf16[192,256]{1,0:T(8,128)(2,1)S(1)} %prep.1), channel_id=1, source_target_pairs={{0,8},{1,9},{2,10},{3,11},{4,12},{5,13},{6,14},{7,15},{8,0},{9,1},... | collective-permute-start | bytes 294920 | tf_op jit(solution)/shard_map/ppermute | solution.py:70
  6.6 10.4 %collective-permute-start.1 = (bf16[192,256]{1,0:T(8,128)(2,1)S(1)}, bf16[192,256]{1,0:T(8,128)(2,1)S(1)}, u32[]{:S(2)}, u32[]{:S(2)}) collective-permute-start(bf16[192,256]{1,0:T(8,128)(2,1)S(1)} %prep.1), channel_id=1, source_target_pairs={{0,16},{1,17},{2,18},{3,19},{4,20},{5,21},{6,22},{7,23},{8,24},{9,... | collective-permute-start | bytes 294920 | tf_op jit(solution)/shard_map/ppermute | solution.py:70
  9.2 7.8 %collective-permute-start.2 = (bf16[192,256]{1,0:T(8,128)(2,1)S(1)}, bf16[192,256]{1,0:T(8,128)(2,1)S(1)}, u32[]{:S(2)}, u32[]{:S(2)}) collective-permute-start(bf16[192,256]{1,0:T(8,128)(2,1)S(1)} %prep.1), channel_id=1, source_target_pairs={{0,24},{1,25},{2,26},{3,27},{4,28},{5,29},{6,30},{7,31},{8,16},{9,... | collective-permute-start | bytes 294920 | tf_op jit(solution)/shard_map/ppermute | solution.py:70
  17.1 22.3 %collective-permute-start.9 = (bf16[4,192,256]{2,1,0:T(8,128)(2,1)S(1)}, bf16[4,192,256]{2,1,0:T(8,128)(2,1)S(1)}, u32[]{:S(2)}, u32[]{:S(2)}) collective-permute-start(bf16[4,192,256]{2,1,0:T(8,128)(2,1)S(1)} %pad_maximum_fusion.refs_0_), channel_id=1, source_target_pairs={{0,6},{1,7},{2,4},{3,5},{4,2},{5,3},{6,0},{7,1},{8,14},{9,15},{10,... | collective-permute-start | bytes 1179656 | tf_op jit(solution)/shard_map/ppermute | solution.py:70
  19.6 20.5 %collective-permute-start.8 = (bf16[4,192,256]{2,1,0:T(8,128)(2,1)S(1)}, bf16[4,192,256]{2,1,0:T(8,128)(2,1)S(1)}, u32[]{:S(2)}, u32[]{:S(2)}) collective-permute-start(bf16[4,192,256]{2,1,0:T(8,128)(2,1)S(1)} %pad_maximum_fusion.refs_0_), channel_id=1, source_target_pairs={{0,2},{1,3},{2,0},{3,1},{4,6},{5,7},{6,4},{7,5},{8,10},{9,11},{10,... | collective-permute-start | bytes 1179656 | tf_op jit(solution)/shard_map/ppermute | solution.py:70
  20.1 20.1 %collective-permute-start.5 = (bf16[4,192,256]{2,1,0:T(8,128)(2,1)S(1)}, bf16[4,192,256]{2,1,0:T(8,128)(2,1)S(1)}, u32[]{:S(2)}, u32[]{:S(2)}) collective-permute-start(bf16[4,192,256]{2,1,0:T(8,128)(2,1)S(1)} %pad_maximum_fusion.refs_0_), channel_id=1, source_target_pairs={{0,4},{1,5},{2,6},{3,7},{4,0},{5,1},{6,2},{7,3},{8,12},{9,13},{10,... | collective-permute-start | bytes 1179656 | tf_op jit(solution)/shard_map/ppermute | solution.py:70
  22.4 2.7 %collective-permute-start.3 = (bf16[2,8,1032]{2,1,0:T(8,128)(2,1)S(1)}, bf16[2,8,1032]{2,1,0:T(8,128)(2,1)S(1)}, u32[]{:S(2)}, u32[]{:S(2)}) collective-permute-start(bf16[2,8,1032]{2,1,0:T(8,128)(2,1)S(1)} %concatenate.6), channel_id=1, source_target_pairs={{0,1},{1,2},{2,3},{4,5},{5,6},{6,7},{8,9},{9,10},{10,11},{12,13},{... | collective-permute-start | bytes 99080 | tf_op jit(solution)/shard_map/ppermute | solution.py:488
  23.8 11.2 %collective-permute-start.4 = (bf16[2,8,1032]{2,1,0:T(8,128)(2,1)S(1)}, bf16[2,8,1032]{2,1,0:T(8,128)(2,1)S(1)}, u32[]{:S(2)}, u32[]{:S(2)}) collective-permute-start(bf16[2,8,1032]{2,1,0:T(8,128)(2,1)S(1)} %concatenate.7), channel_id=1, source_target_pairs={{1,0},{2,1},{3,2},{5,4},{6,5},{7,6},{9,8},{10,9},{11,10},{13,12},{... | collective-permute-start | bytes 99080 | tf_op jit(solution)/shard_map/ppermute | solution.py:491
  25.1 15.5 %collective-permute-start.6 = (bf16[4,192,256]{2,1,0:T(8,128)(2,1)S(1)}, bf16[4,192,256]{2,1,0:T(8,128)(2,1)S(1)}, u32[]{:S(2)}, u32[]{:S(2)}) collective-permute-start(bf16[4,192,256]{2,1,0:T(8,128)(2,1)S(1)} %pad_maximum_fusion.refs_0_), channel_id=1, source_target_pairs={{0,1},{1,0},{2,3},{3,2},{4,5},{5,4},{6,7},{7,6},{8,9},{9,8},{10,11... | collective-permute-start | bytes 1179656 | tf_op jit(solution)/shard_map/ppermute | solution.py:70
  39.3 2.1 %collective-permute-start.11 = (bf16[4,192,256]{2,1,0:T(8,128)(2,1)S(1)}, bf16[4,192,256]{2,1,0:T(8,128)(2,1)S(1)}, u32[]{:S(2)}, u32[]{:S(2)}) collective-permute-start(bf16[4,192,256]{2,1,0:T(8,128)(2,1)S(1)} %collective-permute-done.9.refs_5_), channel_id=1, source_target_pairs={{0,1},{1,0},{2,3},{3,2},{4,5},{5,4},{6,7},{7,6},{8,9},{9,8},{10,11... | collective-permute-start | bytes 1179656 | tf_op jit(solution)/shard_map/ppermute | solution.py:70
  40.2 2.4 %collective-permute-start.7 = (bf16[4,192,256]{2,1,0:T(8,128)(2,1)S(1)}, bf16[4,192,256]{2,1,0:T(8,128)(2,1)S(1)}, u32[]{:S(2)}, u32[]{:S(2)}) collective-permute-start(bf16[4,192,256]{2,1,0:T(8,128)(2,1)S(1)} %collective-permute-done.5.refs_1_), channel_id=1, source_target_pairs={{0,1},{1,0},{2,3},{3,2},{4,5},{5,4},{6,7},{7,6},{8,9},{9,8},{10,11... | collective-permute-start | bytes 1179656 | tf_op jit(solution)/shard_map/ppermute | solution.py:70
  48.7 4.2 %collective-permute-start.12 = (f32[2,1024,256]{2,1,0:T(8,128)S(1)}, f32[2,1024,256]{2,1,0:T(8,128)S(1)}, u32[]{:S(2)}, u32[]{:S(2)}) collective-permute-start(f32[2,1024,256]{2,1,0:T(8,128)S(1)} %get-tuple-element.89), channel_id=1, source_target_pairs={{0,1},{1,0},{2,3},{3,2},{4,5},{5,4},{6,7},{7,6},{8,9},{9,8},{10,11... | collective-permute-start | bytes 6291464 | tf_op jit(solution)/shard_map/ppermute | solution.py:70
  52.3 4.9 %collective-permute-start.13 = (f32[2,512,256]{2,1,0:T(8,128)S(1)}, f32[2,512,256]{2,1,0:T(8,128)S(1)}, u32[]{:S(2)}, u32[]{:S(2)}) collective-permute-start(f32[2,512,256]{2,1,0:T(8,128)S(1)} %get-tuple-element.93), channel_id=1, source_target_pairs={{0,1},{1,0},{2,3},{3,2},{4,5},{5,4},{6,7},{7,6},{8,9},{9,8},{10,11... | collective-permute-start | bytes 3145736 | tf_op jit(solution)/shard_map/ppermute | solution.py:70
  53.4 9.4 %collective-permute-start.14 = (s16[528,256]{1,0:T(8,128)(2,1)S(1)}, s16[528,256]{1,0:T(8,128)(2,1)S(1)}, u32[]{:S(2)}, u32[]{:S(2)}) collective-permute-start(s16[528,256]{1,0:T(8,128)(2,1)S(1)} %get-tuple-element.96), channel_id=1, source_target_pairs={{0,4},{1,5},{2,6},{3,7},{4,0},{5,1},{6,2},{7,3},{8,12},{9,13},{10,... | collective-permute-start | bytes 811016 | tf_op jit(solution)/shard_map/ppermute | solution.py:70
  55.0 15.0 %collective-permute-start.15 = (s16[528,256]{1,0:T(8,128)(2,1)S(1)}, s16[528,256]{1,0:T(8,128)(2,1)S(1)}, u32[]{:S(2)}, u32[]{:S(2)}) collective-permute-start(s16[528,256]{1,0:T(8,128)(2,1)S(1)} %get-tuple-element.97), channel_id=1, source_target_pairs={{0,2},{1,3},{2,0},{3,1},{4,6},{5,7},{6,4},{7,5},{8,10},{9,11},{10,... | collective-permute-start | bytes 811016 | tf_op jit(solution)/shard_map/ppermute | solution.py:70
  56.0 14.2 %collective-permute-start.16 = (s16[528,256]{1,0:T(8,128)(2,1)S(1)}, s16[528,256]{1,0:T(8,128)(2,1)S(1)}, u32[]{:S(2)}, u32[]{:S(2)}) collective-permute-start(s16[528,256]{1,0:T(8,128)(2,1)S(1)} %get-tuple-element.98), channel_id=1, source_target_pairs={{0,6},{1,7},{2,4},{3,5},{4,2},{5,3},{6,0},{7,1},{8,14},{9,15},{10,... | collective-permute-start | bytes 811016 | tf_op jit(solution)/shard_map/ppermute | solution.py:70
  57.6 14.0 %collective-permute-start.17 = (s16[272,256]{1,0:T(8,128)(2,1)S(1)}, s16[272,256]{1,0:T(8,128)(2,1)S(1)}, u32[]{:S(2)}, u32[]{:S(2)}) collective-permute-start(s16[272,256]{1,0:T(8,128)(2,1)S(1)} %get-tuple-element.101), channel_id=1, source_target_pairs={{0,4},{1,5},{2,6},{3,7},{4,0},{5,1},{6,2},{7,3},{8,12},{9,13},{10,... | collective-permute-start | bytes 417800 | tf_op jit(solution)/shard_map/ppermute | solution.py:70
  59.0 14.8 %collective-permute-start.18 = (s16[272,256]{1,0:T(8,128)(2,1)S(1)}, s16[272,256]{1,0:T(8,128)(2,1)S(1)}, u32[]{:S(2)}, u32[]{:S(2)}) collective-permute-start(s16[272,256]{1,0:T(8,128)(2,1)S(1)} %get-tuple-element.102), channel_id=1, source_target_pairs={{0,2},{1,3},{2,0},{3,1},{4,6},{5,7},{6,4},{7,5},{8,10},{9,11},{10,... | collective-permute-start | bytes 417800 | tf_op jit(solution)/shard_map/ppermute | solution.py:70
  62.8 12.9 %collective-permute-start.19 = (s16[272,256]{1,0:T(8,128)(2,1)S(1)}, s16[272,256]{1,0:T(8,128)(2,1)S(1)}, u32[]{:S(2)}, u32[]{:S(2)}) collective-permute-start(s16[272,256]{1,0:T(8,128)(2,1)S(1)} %get-tuple-element.103), channel_id=1, source_target_pairs={{0,6},{1,7},{2,4},{3,5},{4,2},{5,3},{6,0},{7,1},{8,14},{9,15},{10,... | collective-permute-start | bytes 417800 | tf_op jit(solution)/shard_map/ppermute | solution.py:70
  75.9 7.0 %collective-permute-start.20 = (s16[80,256]{1,0:T(8,128)(2,1)S(1)}, s16[80,256]{1,0:T(8,128)(2,1)S(1)}, u32[]{:S(2)}, u32[]{:S(2)}) collective-permute-start(s16[80,256]{1,0:T(8,128)(2,1)S(1)} %get-tuple-element.105), channel_id=1, source_target_pairs={{0,8},{1,9},{2,10},{3,11},{4,12},{5,13},{6,14},{7,15},{8,0},{9,1},... | collective-permute-start | bytes 122888 | tf_op jit(solution)/shard_map/ppermute | solution.py:70
  78.3 12.6 %collective-permute-start.23 = (s16[144,256]{1,0:T(8,128)(2,1)S(1)}, s16[144,256]{1,0:T(8,128)(2,1)S(1)}, u32[]{:S(2)}, u32[]{:S(2)}) collective-permute-start(s16[144,256]{1,0:T(8,128)(2,1)S(1)} %get-tuple-element.109), channel_id=1, source_target_pairs={{0,8},{1,9},{2,10},{3,11},{4,12},{5,13},{6,14},{7,15},{8,0},{9,1},... | collective-permute-start | bytes 221192 | tf_op jit(solution)/shard_map/ppermute | solution.py:70
  78.4 12.5 %collective-permute-start.24 = (s16[144,256]{1,0:T(8,128)(2,1)S(1)}, s16[144,256]{1,0:T(8,128)(2,1)S(1)}, u32[]{:S(2)}, u32[]{:S(2)}) collective-permute-start(s16[144,256]{1,0:T(8,128)(2,1)S(1)} %get-tuple-element.110), channel_id=1, source_target_pairs={{0,16},{1,17},{2,18},{3,19},{4,20},{5,21},{6,22},{7,23},{8,24},{9,... | collective-permute-start | bytes 221192 | tf_op jit(solution)/shard_map/ppermute | solution.py:70
  81.3 9.6 %collective-permute-start.25 = (s16[144,256]{1,0:T(8,128)(2,1)S(1)}, s16[144,256]{1,0:T(8,128)(2,1)S(1)}, u32[]{:S(2)}, u32[]{:S(2)}) collective-permute-start(s16[144,256]{1,0:T(8,128)(2,1)S(1)} %get-tuple-element.111), channel_id=1, source_target_pairs={{0,24},{1,25},{2,26},{3,27},{4,28},{5,29},{6,30},{7,31},{8,16},{9,... | collective-permute-start | bytes 221192 | tf_op jit(solution)/shard_map/ppermute | solution.py:70
  82.7 8.2 %collective-permute-start.21 = (s16[80,256]{1,0:T(8,128)(2,1)S(1)}, s16[80,256]{1,0:T(8,128)(2,1)S(1)}, u32[]{:S(2)}, u32[]{:S(2)}) collective-permute-start(s16[80,256]{1,0:T(8,128)(2,1)S(1)} %get-tuple-element.106), channel_id=1, source_target_pairs={{0,16},{1,17},{2,18},{3,19},{4,20},{5,21},{6,22},{7,23},{8,24},{9,... | collective-permute-start | bytes 122888 | tf_op jit(solution)/shard_map/ppermute | solution.py:70
  82.9 8.0 %collective-permute-start.22 = (s16[80,256]{1,0:T(8,128)(2,1)S(1)}, s16[80,256]{1,0:T(8,128)(2,1)S(1)}, u32[]{:S(2)}, u32[]{:S(2)}) collective-permute-start(s16[80,256]{1,0:T(8,128)(2,1)S(1)} %get-tuple-element.107), channel_id=1, source_target_pairs={{0,24},{1,25},{2,26},{3,27},{4,28},{5,29},{6,30},{7,31},{8,16},{9,... | collective-permute-start | bytes 122888 | tf_op jit(solution)/shard_map/ppermute | solution.py:70
  91.1 11.8 %collective-permute-start.26 = (f32[192,256]{1,0:T(8,128)S(1)}, f32[192,256]{1,0:T(8,128)S(1)}, u32[]{:S(2)}, u32[]{:S(2)}) collective-permute-start(f32[192,256]{1,0:T(8,128)S(1)} %get-tuple-element.112.refs_0_), channel_id=1, source_target_pairs={{0,2},{1,3},{2,0},{3,1},{4,6},{5,7},{6,4},{7,5},{8,10},{9,11},{10,... | collective-permute-start | bytes 589832 | tf_op jit(solution)/shard_map/ppermute | solution.py:70
  91.1 3.7 %collective-permute-start.27 = (f32[8,128]{1,0:T(8,128)S(1)}, f32[8,128]{1,0:T(8,128)S(1)}, u32[]{:S(2)}, u32[]{:S(2)}) collective-permute-start(f32[8,128]{1,0:T(8,128)S(1)} %get-tuple-element.113), channel_id=1, source_target_pairs={{0,4},{1,5},{2,6},{3,7},{4,0},{5,1},{6,2},{7,3},{8,12},{9,13},{10,... | collective-permute-start | bytes 12296 | tf_op jit(solution)/shard_map/ppermute | solution.py:70
  94.8 3.6 %collective-permute-start.28 = (f32[8,128]{1,0:T(8,128)S(1)}, f32[8,128]{1,0:T(8,128)S(1)}, u32[]{:S(2)}, u32[]{:S(2)}) collective-permute-start(f32[8,128]{1,0:T(8,128)S(1)} %add.29), channel_id=1, source_target_pairs={{0,8},{1,9},{2,10},{3,11},{4,12},{5,13},{6,14},{7,15},{8,0},{9,1},... | collective-permute-start | bytes 12296 | tf_op jit(solution)/shard_map/ppermute | solution.py:70
  98.4 4.5 %collective-permute-start.29 = (f32[8,128]{1,0:T(8,128)S(1)}, f32[8,128]{1,0:T(8,128)S(1)}, u32[]{:S(2)}, u32[]{:S(2)}) collective-permute-start(f32[8,128]{1,0:T(8,128)S(1)} %add.30), channel_id=1, source_target_pairs={{0,16},{1,17},{2,18},{3,19},{4,20},{5,21},{6,22},{7,23},{8,24},{9,... | collective-permute-start | bytes 12296 | tf_op jit(solution)/shard_map/ppermute | solution.py:70
  100.1 7.7 %collective-permute-start.32 = (f32[192,256]{1,0:T(8,128)S(1)}, f32[192,256]{1,0:T(8,128)S(1)}, u32[]{:S(2)}, u32[]{:S(2)}) collective-permute-start(f32[192,256]{1,0:T(8,128)S(1)} %get-tuple-element.112.refs_0_), channel_id=1, source_target_pairs={{0,1},{1,0},{2,3},{3,2},{4,5},{5,4},{6,7},{7,6},{8,9},{9,8},{10,11... | collective-permute-start | bytes 589832 | tf_op jit(solution)/shard_map/ppermute | solution.py:70
  103.0 4.9 %collective-permute-start.33 = (f32[192,256]{1,0:T(8,128)S(1)}, f32[192,256]{1,0:T(8,128)S(1)}, u32[]{:S(2)}, u32[]{:S(2)}) collective-permute-start(f32[192,256]{1,0:T(8,128)S(1)} %collective-permute-done.26.refs_2_), channel_id=1, source_target_pairs={{0,1},{1,0},{2,3},{3,2},{4,5},{5,4},{6,7},{7,6},{8,9},{9,8},{10,11... | collective-permute-start | bytes 589832 | tf_op jit(solution)/shard_map/ppermute | solution.py:70
  103.0 3.7 %collective-permute-start.30 = (f32[8,128]{1,0:T(8,128)S(1)}, f32[8,128]{1,0:T(8,128)S(1)}, u32[]{:S(2)}, u32[]{:S(2)}) collective-permute-start(f32[8,128]{1,0:T(8,128)S(1)} %add.31), channel_id=1, source_target_pairs={{0,2},{1,3},{2,0},{3,1},{4,6},{5,7},{6,4},{7,5},{8,10},{9,11},{10,... | collective-permute-start | bytes 12296 | tf_op jit(solution)/shard_map/ppermute | solution.py:70
  (18 other events, 560.5 us)

commit v3 on v2

v3 whole, which is shorter than its diff:
```python
import functools

import jax
import jax.numpy as jnp
from jax import lax
from jax.experimental import pallas as pl
from jax.experimental.pallas import tpu as pltpu
from jax.sharding import PartitionSpec as P

D = 512
HID = 256
CODES = 1024
GROUPS = 2
LEVELS = 2
SLOTS = 4
KERNEL = 3
DILATION = 3
DG = 256
PAD = 8

COMMIT = 0.25
FIRST_DECAY = 0.9
SECOND_DECAY = 0.99
EPSILON = 1e-08
WEIGHT_DECAY = 0.01
BITRATE_FACTOR = 0.02
RATE_CODE = 0.5

F32 = jnp.float32
BF16 = jnp.bfloat16
NT = (((1,), (1,)), ((), ()))
TN = (((0,), (0,)), ((), ()))
LEVEL_STEPS = 256.0
TOP = 32000.0
SCALE_GROUPS = 4
MIB = 1024 * 1024


def params(mib=6):
    return pltpu.CompilerParams(vmem_limit_bytes=mib * MIB)


def whole(count):
    return [pl.BlockSpec(memory_space=pltpu.VMEM)] * count


def mm(a, b):
    return jnp.dot(a, b, preferred_element_type=F32)


def mmg(a, b, dims):
    return lax.dot_general(a, b, dims, preferred_element_type=F32)


def slope(v):
    return jnp.where(v > 0, 1.0, jnp.exp(jnp.minimum(v, 0.0)))


def elu(v):
    return jnp.where(v > 0, v, jnp.exp(jnp.minimum(v, 0.0)) - 1.0)


def swap(value, clip_mask, time_mask):
    clips, times = lax.axis_size("clip"), lax.axis_size("tm")
    pairs = [
        (c * times + t, (c ^ clip_mask) * times + (t ^ time_mask))
        for c in range(clips)
        for t in range(times)
    ]
    return lax.ppermute(value, ("clip", "tm"), pairs)


def prep_kernel(dil_hbm, pw_hbm, table_hbm, conv_ref, code_ref, dil_ref, pw_ref, table_ref, sems):
    time = lax.axis_index("tm")
    bit = time % 2
    out_rows = pw_ref.shape[0] // 2
    second = jnp.minimum(2 + bit, KERNEL - 1)
    copies = [
        pltpu.make_async_copy(table_hbm.at[time], table_ref, sems.at[0]),
        pltpu.make_async_copy(dil_hbm.at[bit], dil_ref.at[0], sems.at[1]),
        pltpu.make_async_copy(dil_hbm.at[second], dil_ref.at[1], sems.at[2]),
        pltpu.make_async_copy(pw_hbm, pw_ref, sems.at[3]),
    ]
    for copy in copies:
        copy.start()
    copies[0].wait()
    code_ref[...] = table_ref[...].astype(BF16)
    for copy in copies[1:]:
        copy.wait()
    for side in range(2):
        for part in range(2):
            conv_ref[part, side * out_rows : (side + 1) * out_rows, :] = dil_ref[
                part, :, side * DG : (side + 1) * DG
            ].astype(BF16)

    @pl.when(bit == 1)
    def _():
        conv_ref[1] = pw_ref[...].astype(BF16)


def renamed(values, ranks):
    block = CODES // ranks
    step = (values // block) ^ lax.axis_index("clip")
    place = (step % 2) * (ranks // 2) + step // 2
    return place * block + values % block


def masks(clips, frames, len_ref, columns):
    base = lax.axis_index("tm") * frames

    def mark(first, count, clip):
        where = lax.broadcasted_iota(jnp.int32, (count, columns), 0) + first
        return jnp.where((where >= 0) & (where < len_ref[clip]), 1.0, 0.0)

    own = [mark(base, frames, c) for c in range(clips)]
    margins = [
        mark(first, PAD, c) for c in range(clips) for first in (base - PAD, base + frames)
    ]
    return jnp.concatenate(own + margins, axis=0)


def widened(value, clip, clips, frames):
    at = clips * frames + 2 * PAD * clip
    return jnp.concatenate(
        [
            value[at : at + PAD],
            value[clip * frames : (clip + 1) * frames],
            value[at + PAD : at + 2 * PAD],
        ],
        axis=0,
    )


def pack_kernel(f_hbm, c_hbm, ids_hbm, near_ref, far_ref, buf, ids_ref, sems):
    clips, frames, _ = f_hbm.shape
    edge = 2 * PAD
    odd = lax.axis_index("tm") % 2
    copies = [pltpu.make_async_copy(ids_hbm, ids_ref, sems.at[4])]
    for kind, source in enumerate((f_hbm, c_hbm)):
        for side, at in enumerate((frames - edge, 0)):
            copies.append(
                pltpu.make_async_copy(
                    source.at[:, pl.ds(at, edge), :], buf.at[kind, side], sems.at[2 * kind + side]
                )
            )
    for copy in copies:
        copy.start()
    for copy in copies:
        copy.wait()
    outs = []
    for side in range(2):
        at = slice(PAD, 2 * PAD) if side == 0 else slice(0, PAD)
        parts = []
        for c in range(clips):
            ids = ids_ref[:, c, :]
            if side == 0:
                ids = pltpu.roll(ids, PAD, 1)
            both = jnp.concatenate([ids // 32, ids % 32], axis=0).astype(F32)
            both = jnp.concatenate([both, jnp.zeros((8, 2 * D - frames), F32)], axis=1)
            ends = [buf[kind, side, c].astype(F32)[at] for kind in range(2)]
            parts.append(jnp.concatenate([jnp.concatenate(ends, axis=1), both], axis=0))
        outs.append(parts)
    for c in range(clips):
        last, first = outs[0][c], outs[1][c]
        near_ref[c] = jnp.where(odd == 1, first, last).astype(BF16)
        far_ref[c] = jnp.where(odd == 1, last, first).astype(BF16)


def own_kernel(ranks, ids_ref, hot_ref, hott_ref):
    _, clips, frames = ids_ref.shape
    codes = lax.broadcasted_iota(jnp.int32, (frames, CODES), 1)
    spots = lax.broadcasted_iota(jnp.int32, (CODES, frames), 0)
    for c in range(clips):
        ids = renamed(ids_ref[:, c, :], ranks)
        turned = jnp.concatenate([ids.astype(F32), jnp.zeros((8 - SLOTS, frames), F32)], axis=0)
        turned = turned.T.astype(jnp.int32)
        at = slice(c * frames, (c + 1) * frames)
        for slot in range(SLOTS):
            hot_ref[slot, at, :] = jnp.where(codes == turned[:, slot : slot + 1], 1.0, 0.0).astype(
                BF16
            )
            hott_ref[slot, :, at] = jnp.where(spots == ids[slot : slot + 1], 1.0, 0.0).astype(BF16)
    hot_ref[:, clips * frames :, :] = jnp.zeros((SLOTS, 2 * PAD * clips, CODES), BF16)


def margin_kernel(ranks, len_ref, f_ref, near_ref, far_ref, old_ref, start_ref, act_ref, cot_ref, hot_ref):
    del old_ref
    clips, frames, _ = f_ref.shape
    odd = lax.axis_index("tm") % 2
    both = []
    for c in range(clips):
        near, far = near_ref[c].astype(F32), far_ref[c].astype(F32)
        both += [jnp.where(odd == 1, near, far), jnp.where(odd == 1, far, near)]
    start = masks(clips, frames, len_ref, D) * jnp.concatenate(
        [f_ref[c].astype(F32) for c in range(clips)] + [part[:PAD, :D] for part in both], axis=0
    )
    start_ref[...] = start
    act_ref[...] = elu(start).astype(BF16)
    cot_ref[...] = jnp.concatenate([part[:PAD, D:] for part in both], axis=0)
    turned = jnp.concatenate([part[PAD:, :128].T[:PAD] for part in both], axis=0)
    ids = renamed((turned[:, :SLOTS] * 32.0 + turned[:, SLOTS : 2 * SLOTS]).astype(jnp.int32), ranks)
    codes = lax.broadcasted_iota(jnp.int32, (2 * PAD * clips, CODES), 1)
    for slot in range(SLOTS):
        hot_ref[slot, clips * frames :, :] = jnp.where(
            codes == ids[:, slot : slot + 1], 1.0, 0.0
        ).astype(BF16)


def assembled(ranks, pieces, d_ref, pwt_ref, all_ref):
    half, small = ranks // 2, 2 * HID // ranks
    out_rows = small // 2
    bit, rank = lax.axis_index("tm") % 2, lax.axis_index("clip")
    for other in range(2):
        for z in range(half):
            piece = pieces[other * half + z]
            for x in range(2):
                at = pl.multiple_of((rank ^ (2 * z + x)) * out_rows, out_rows)
                for part in range(2):
                    for side in range(2):
                        all_ref[
                            2 * part + (bit ^ other),
                            pl.ds(at, out_rows),
                            side * DG : (side + 1) * DG,
                        ] = piece[x, part, side * out_rows : (side + 1) * out_rows, :]
    for tap in range(KERNEL):
        d_ref[tap * HID : (tap + 1) * HID, :] = all_ref[tap]
    for r in range(ranks):
        for side in range(2):
            to = r * small + side * out_rows
            pwt_ref[to : to + out_rows, :] = all_ref[
                KERNEL, r * out_rows : (r + 1) * out_rows, side * DG : (side + 1) * DG
            ]


def conv_kernel(ranks, assemble, clips, start_ref, act_ref, *refs):
    if assemble:
        pieces, refs = refs[:ranks], refs[ranks:]
        d_ref, pwt_ref, gated_ref, hs_ref, latent_ref, all_ref = refs
        assembled(ranks, pieces, d_ref, pwt_ref, all_ref)
    else:
        d_ref, pwt_ref, gated_ref, hs_ref, latent_ref = refs
    rows = start_ref.shape[0]
    taps = mmg(act_ref[...], d_ref[...], NT)
    frames = rows // clips - 2 * PAD
    span = frames + 2 * PAD
    own, margins = [], []
    for c in range(clips):
        wide = widened(taps, c, clips, frames)
        part = (
            pltpu.roll(wide[:, :HID], DILATION, 0)
            + wide[:, HID : 2 * HID]
            + pltpu.roll(wide[:, 2 * HID :], span - DILATION, 0)
        )
        own.append(part[PAD : PAD + frames])
        margins += [part[:PAD], part[PAD + frames :]]
    hidden = jnp.concatenate(own + margins, axis=0)
    hs_ref[...] = slope(hidden)
    gated = elu(hidden).astype(BF16)
    gated_ref[...] = gated
    latent_ref[...] = start_ref[...] + mmg(gated, pwt_ref[...], NT)


def quant_kernel(ranks, len_ref, latent_ref, c_ref, cot_ref, hot_ref, hott_ref, *refs):
    half, block = ranks // 2, CODES // ranks
    pieces, refs = refs[:8], refs[8:]
    quant_ref, keep_ref, send_ref, bg_ref, lg_ref, tab_ref, cgs_ref = refs
    clips, frames, _ = c_ref.shape
    time = lax.axis_index("tm")
    mask = masks(clips, frames, len_ref, DG)
    local = clips * frames
    twice = 2.0 * mask[:local]
    for other in range(SLOTS):
        slot = time ^ other
        for x in range(2):
            for z in range(half):
                spot = (x * half + z) * block
                tab_ref[slot, spot : spot + block, :] = pieces[2 * other + x][z]
    for group in range(GROUPS):
        at = slice(group * DG, (group + 1) * DG)
        first = mm(hot_ref[2 * group], tab_ref[2 * group])
        second = mm(hot_ref[2 * group + 1], tab_ref[2 * group + 1])
        cot = jnp.concatenate(
            [c_ref[c, :, at].astype(F32) for c in range(clips)] + [cot_ref[:, at]], axis=0
        )
        residual = latent_ref[:, at]
        gap = residual - first
        gap2 = gap - second
        grad = mask * (cot + 2.0 * COMMIT * (gap + gap2))
        quant = (mask * (first + second))[:local].astype(BF16)
        bg_ref[:, at] = grad.astype(BF16)
        lg_ref[:, at] = grad[:local]
        for clip in range(clips):
            quant_ref[clip, :, at] = quant[clip * frames : (clip + 1) * frames]
        for level, diff in ((0, gap), (1, gap2)):
            code_grad = -(twice * diff[:local])
            high = code_grad.astype(BF16)
            cgs_ref[2 * group + level, :, :DG] = high
            cgs_ref[2 * group + level, :, DG:] = (code_grad - high.astype(F32)).astype(BF16)
    for other in range(SLOTS):
        slot = time ^ other
        pair = mm(hott_ref[slot], cgs_ref[slot])
        total = pair[:, :DG] + pair[:, DG:]
        if other % 2 == 0:
            keep_ref[other // 2] = total
        else:
            send_ref[other // 2] = total


def backward_kernel(
    ranks,
    assemble,
    clips,
    len_ref,
    start_ref,
    act_ref,
    gated_ref,
    bg_ref,
    lg_ref,
    hs_ref,
    d_ref,
    pwt_ref,
    fg_ref,
    *outs,
):
    rows = start_ref.shape[0]
    span = rows // clips
    frames = span - 2 * PAD
    local = clips * frames
    bg = bg_ref[...]
    hidden_grad = (mm(bg, pwt_ref[...]) * hs_ref[...]).astype(BF16)
    mine = hidden_grad[:local]
    pw_grad = mmg(bg[:local], gated_ref[:local, :], TN)

    def moved(value, shift):
        return jnp.concatenate(
            [
                pltpu.roll(widened(value, c, clips, frames), shift % span, 0)[PAD : PAD + frames]
                for c in range(clips)
            ],
            axis=0,
        ).astype(BF16)

    act = act_ref[...].astype(F32)
    windows = [moved(act, DILATION), act_ref[:local, :], moved(act, -DILATION)]
    dil_grads = [mmg(mine, windows[tap], TN) for tap in range(KERNEL)]
    if assemble:
        keep_ref, send_ref, all_ref = outs
        half, small = ranks // 2, 2 * HID // ranks
        out_rows = small // 2
        time, rank = lax.axis_index("tm"), lax.axis_index("clip")
        for tap in range(KERNEL):
            all_ref[tap] = dil_grads[tap]
        for r in range(ranks):
            for side in range(2):
                at = r * small + side * out_rows
                all_ref[KERNEL, r * out_rows : (r + 1) * out_rows, side * DG : (side + 1) * DG] = (
                    pw_grad[at : at + out_rows]
                )
        for other in range(4):
            out = (keep_ref, send_ref)[other % 2]
            for x in range(2):
                for z in range(half):
                    at = pl.multiple_of((rank ^ (2 * z + x)) * out_rows, out_rows)
                    to = (x * half + z) * small
                    for side in range(2):
                        out[other // 2, to + side * out_rows : to + (side + 1) * out_rows, :] = (
                            all_ref[
                                time ^ other, pl.ds(at, out_rows), side * DG : (side + 1) * DG
                            ]
                        )
    else:
        dil_ref, pw_ref = outs
        for tap in range(KERNEL):
            dil_ref[tap] = dil_grads[tap]
        pw_ref[...] = pw_grad
    wide = hidden_grad.astype(F32)
    shifted = jnp.concatenate([moved(wide, -DILATION), mine, moved(wide, DILATION)], axis=1)
    act_grad = mm(shifted, d_ref[...])
    row = lax.broadcasted_iota(jnp.int32, (frames, D), 0) + lax.axis_index("tm") * frames
    for c in range(clips):
        to = slice(c * frames, (c + 1) * frames)
        mask = jnp.where(row < len_ref[c], 1.0, 0.0)
        start = start_ref[to, :]
        fg_ref[c] = mask * (lg_ref[to, :] + slope(start) * act_grad[to])


def pack_part(value):
    count = SCALE_GROUPS
    rows = value.shape[0]
    size = rows // count
    steps, levels = [], []
    for group in range(count):
        part = value[group * size : (group + 1) * size]
        top = jnp.maximum(jnp.max(jnp.abs(part), axis=0, keepdims=True), 1e-30)
        level = jnp.ceil(jnp.log2(top) * LEVEL_STEPS)
        scale = jnp.exp2(level / -LEVEL_STEPS) * TOP
        steps.append(jnp.round(part * scale).astype(jnp.int32))
        levels.append(level)
    return steps, levels


def unpack_part(steps, level):
    return steps.astype(jnp.int32).astype(F32) * (
        jnp.exp2(level.astype(jnp.int32).astype(F32) / LEVEL_STEPS) / TOP
    )


def send_kernel(groups, rows, keep_ref, got_ref, own_ref, *outs):
    size = rows // SCALE_GROUPS
    for part, blocks in enumerate(groups):
        levels = []
        for place, (jy, start) in enumerate(blocks):
            at = slice(start * rows, (start + 1) * rows)
            value = keep_ref[jy, at, :] + got_ref[jy, at, :]
            if part == 0:
                own_ref[place] = value
                continue
            steps, more = pack_part(value)
            for group, step in enumerate(steps):
                spot = place * rows + group * size
                outs[part - 1][spot : spot + size, :] = step.astype(jnp.int16)
            levels += more
        if part:
            tail = jnp.concatenate(levels, axis=0).astype(jnp.int32)
            outs[part - 1][len(blocks) * rows :, :] = tail.astype(jnp.int16)


def pass_kernel(rows, own_in, *refs):
    blocks = own_in.shape[0]
    gots, own_ref, outs = refs[:-blocks], refs[-blocks], refs[1 - blocks :]
    size = rows // SCALE_GROUPS
    for place in range(blocks):
        value = own_in[place]
        pieces = [value[g * size : (g + 1) * size] for g in range(SCALE_GROUPS)]
        for got in gots:
            tail = got[blocks * rows :, :]
            for g in range(SCALE_GROUPS):
                index = place * SCALE_GROUPS + g
                spot = place * rows + g * size
                pieces[g] = pieces[g] + unpack_part(
                    got[spot : spot + size, :], tail[index : index + 1]
                )
        if place == 0:
            for g in range(SCALE_GROUPS):
                own_ref[g * size : (g + 1) * size, :] = pieces[g]
            continue
        steps, levels = pack_part(jnp.concatenate(pieces, axis=0))
        out = outs[place - 1]
        for g, step in enumerate(steps):
            out[g * size : (g + 1) * size, :] = step.astype(jnp.int16)
        pad = jnp.zeros((out.shape[0] - rows - len(levels), DG), F32)
        tail = jnp.concatenate(levels + [pad], axis=0).astype(jnp.int32)
        out[rows:, :] = tail.astype(jnp.int16)


def final_kernel(sizes, counts, *refs):
    out_ref, square_ref = refs[-2:]
    squares = jnp.zeros((1, DG), F32)
    place = 0
    for kind, rows in enumerate(sizes):
        own_ref, *gots = refs[sum(counts[:kind]) : sum(counts[: kind + 1])]
        size = rows // SCALE_GROUPS
        for g in range(SCALE_GROUPS):
            at = slice(g * size, (g + 1) * size)
            value = own_ref[at, :]
            for got in gots:
                value = value + unpack_part(got[at, :], got[rows:, :][g : g + 1])
            out_ref[place : place + size, :] = value
            squares = squares + jnp.sum(value * value, axis=0, keepdims=True)
            place += size
    square_ref[...] = jnp.broadcast_to(jnp.sum(squares, axis=1, keepdims=True), (8, 128))


def stepped(weight, first, second, grad, rate, fix1, fix2):
    first_new = FIRST_DECAY * first + (1.0 - FIRST_DECAY) * grad
    second_new = SECOND_DECAY * second + (1.0 - SECOND_DECAY) * grad * grad
    change = (first_new * fix1) / (jnp.sqrt(second_new * fix2) + EPSILON) + WEIGHT_DECAY * weight
    return weight - rate * change, second_new


def update_kernel(fix_ref, square_ref, *refs):
    pieces = refs[:4]
    dil, pw, table = refs[4:7], refs[7:10], refs[10:13]
    norm_ref = refs[13]
    dil_hbm, pw_hbm, table_hbm = refs[14:17], refs[17:20], refs[20:23]
    dil_out, pw_out, table_out = refs[23:26], refs[26:29], refs[29:32]
    sems = refs[32]
    out_rows = dil[0].shape[1]
    small = 2 * out_rows
    time = lax.axis_index("tm")
    count = KERNEL * D * HID + D * HID + SLOTS * CODES * DG
    norm = jnp.sqrt(square_ref[...][:1, :1])
    limit = jnp.sqrt(jnp.full((1, 1), float(count), F32))
    scale = limit / jnp.maximum(norm, limit)
    norm_ref[...] = norm
    fixes = (fix_ref[0], fix_ref[1])
    copies = []
    for other in range(4):
        quarter = time ^ other
        piece = pieces[other]
        grad = piece[small:, :] * scale
        state = [v[quarter] for v in table]
        weight, second = stepped(*state, grad, RATE_CODE, *fixes)
        for kind, value in enumerate((weight, grad, second)):
            table_out[kind][quarter] = value
            copies.append(
                pltpu.make_async_copy(
                    table_out[kind].at[quarter], table_hbm[kind].at[quarter], sems.at[len(copies)]
                )
            )
            copies[-1].start()

        @pl.when(quarter < KERNEL)
        def _():
            tap = jnp.minimum(quarter, KERNEL - 1)
            for side in range(2):
                to = slice(side * DG, (side + 1) * DG)
                grad = piece[side * out_rows : (side + 1) * out_rows, :] * scale
                state = [v[tap, :, to] for v in dil]
                weight, second = stepped(*state, grad, BITRATE_FACTOR, *fixes)
                dil_out[0][tap, :, to] = weight
                dil_out[1][tap, :, to] = grad
                dil_out[2][tap, :, to] = second

        @pl.when(quarter == KERNEL)
        def _():
            grad = piece[:small, :] * scale
            weight, second = stepped(*[v[...] for v in pw], grad, BITRATE_FACTOR, *fixes)
            pw_out[0][...] = weight
            pw_out[1][...] = grad
            pw_out[2][...] = second

    for kind in range(3):
        for outs, hbms in ((dil_out, dil_hbm), (pw_out, pw_hbm)):
            copies.append(pltpu.make_async_copy(outs[kind], hbms[kind], sems.at[len(copies)]))
            copies[-1].start()
    for copy in copies:
        copy.wait()


def shards(
    features,
    cotangent,
    clip_lengths,
    code_ids,
    step_count,
    dilated_kernel_weight,
    pointwise_conv,
    codebooks,
    dilated_first_moment,
    dilated_second_moment,
    pointwise_first,
    pointwise_second,
    codebook_first,
    codebook_second,
):
    ranks, times = lax.axis_size("clip"), lax.axis_size("tm")
    rank, time = lax.axis_index("clip"), lax.axis_index("tm")
    clips, frames, _ = features.shape
    half = ranks // 2
    out_rows = HID // ranks
    block = CODES // ranks
    small = 2 * out_rows
    rows = clips * (frames + 2 * PAD)
    smem = pl.BlockSpec(memory_space=pltpu.SMEM)
    hbm = pl.BlockSpec(memory_space=pltpu.HBM)
    shape = jax.ShapeDtypeStruct

    def held(*values):
        return [pltpu.with_memory_space_constraint(v, pltpu.HBM) for v in values]

    assemble = out_rows % 16 == 0
    dil_state = [
        v.transpose(0, 2, 1)
        for v in (dilated_kernel_weight, dilated_first_moment, dilated_second_moment)
    ]
    pw_state = [v.T for v in (pointwise_conv, pointwise_first, pointwise_second)]
    table_state = [codebooks, codebook_first, codebook_second]

    if assemble:
        mine_d, mine_c = pl.pallas_call(
            prep_kernel,
            out_shape=(shape((2, small, DG), BF16), shape((block, DG), BF16)),
            in_specs=[hbm] * 3,
            out_specs=tuple(whole(2)),
            scratch_shapes=[
                pltpu.VMEM((2, out_rows, D), F32),
                pltpu.VMEM((small, DG), F32),
                pltpu.VMEM((block, DG), F32),
                pltpu.SemaphoreType.DMA((4,)),
            ],
            compiler_params=params(),
            name="prep",
        )(*held(dil_state[0], pw_state[0], codebooks))
    else:
        taps = dil_state[0].astype(BF16).reshape(KERNEL, out_rows, 2, DG).transpose(0, 2, 1, 3)
        quarters = jnp.concatenate(
            [taps.reshape(KERNEL, small, DG), pw_state[0].astype(BF16)[None]], axis=0
        )
        mine_d = jnp.take(quarters, time % 2 + jnp.array([0, 2]), axis=0)
        mine_c = lax.dynamic_index_in_dim(codebooks, time, 0, keepdims=False).astype(BF16)

    mine_c, mine_d, late_ids = lax.optimization_barrier((mine_c, mine_d, code_ids))
    near, far = pl.pallas_call(
        pack_kernel,
        out_shape=(shape((clips, 2 * PAD, 2 * D), BF16),) * 2,
        in_specs=[hbm] * 3,
        out_specs=tuple(whole(2)),
        scratch_shapes=[
            pltpu.VMEM((2, 2, clips, 2 * PAD, D), BF16),
            pltpu.VMEM(code_ids.shape, jnp.int32),
            pltpu.SemaphoreType.DMA((5,)),
        ],
        compiler_params=params(),
        name="pack",
    )(*held(features, cotangent, late_ids))
    line_c = [swap(mine_c, 2 * z, 0) for z in range(1, half)]
    across = swap(mine_d, 1, 0)
    near = lax.ppermute(near, "tm", [(i, i ^ 1) for i in range(times)])
    pairs = [(i, i + 1) for i in range(1, times - 1, 2)]
    far = lax.ppermute(far, "tm", pairs + [(b, a) for a, b in pairs])
    near, far, across, *line_c = lax.optimization_barrier((near, far, across, *line_c))
    line_c = jnp.stack([mine_c] + line_c, axis=0)
    pair_d = jnp.stack([mine_d, across], axis=0)
    line_c, pair_d, late_ids = lax.optimization_barrier((line_c, pair_d, code_ids))
    hot, hott = pl.pallas_call(
        functools.partial(own_kernel, ranks),
        out_shape=(
            shape((SLOTS, rows, CODES), BF16),
            shape((SLOTS, CODES, clips * frames), BF16),
        ),
        in_specs=whole(1),
        out_specs=tuple(whole(2)),
        compiler_params=params(8),
        name="own",
    )(late_ids)
    plane_c = [line_c, swap(line_c, 1, 0), swap(line_c, 0, 2), swap(line_c, 1, 2)]
    line_d = [pair_d] + [swap(pair_d, 2 * z, 0) for z in range(1, half)]

    start, act, cot, hot = pl.pallas_call(
        functools.partial(margin_kernel, ranks),
        out_shape=(
            shape((rows, D), F32),
            shape((rows, D), BF16),
            shape((2 * PAD * clips, D), F32),
            shape(hot.shape, BF16),
        ),
        in_specs=[smem] + whole(4),
        out_specs=tuple(whole(4)),
        input_output_aliases={4: 3},
        compiler_params=params(8),
        name="margin",
    )(clip_lengths, features, near, far, hot)

    act, *gone = lax.optimization_barrier((act, *plane_c, *line_d))
    plane_c, line_d = gone[:4], gone[4:]
    pieces_d = line_d + [swap(v, 0, 1) for v in line_d]
    turned = [swap(v, 0, 1) for v in plane_c]
    pieces_c = plane_c[:2] + turned[:2] + plane_c[2:] + turned[2:]

    weights = (shape((KERNEL * HID, D), BF16), shape((D, HID), BF16))
    given = pieces_d
    if not assemble:
        order = rank ^ jnp.arange(ranks)
        stacked = jnp.stack(pieces_d, axis=0).reshape(2, half, 2, 2, small, DG)
        stacked = jnp.take(stacked, time % 2 ^ jnp.arange(2), axis=0)
        stacked = stacked.transpose(3, 0, 1, 2, 4, 5).reshape(4, ranks, small, DG)
        stacked = jnp.take(stacked, order, axis=1)
        dil = stacked[:KERNEL].reshape(KERNEL, ranks, 2, out_rows, DG)
        dil = dil.transpose(0, 1, 3, 2, 4).reshape(KERNEL * HID, D)
        given = [dil, stacked[3].reshape(D, HID)]
    outs = pl.pallas_call(
        functools.partial(conv_kernel, ranks, assemble, clips),
        out_shape=(weights if assemble else ())
        + (shape((rows, HID), BF16), shape((rows, HID), F32), shape((rows, D), F32)),
        in_specs=whole(2 + len(given)),
        out_specs=tuple(whole(5 if assemble else 3)),
        scratch_shapes=[pltpu.VMEM((4, HID, D), BF16)] if assemble else [],
        compiler_params=params(10),
        name="conv",
    )(start, act, *given)
    dil, pwt, gated, hs, latent = tuple(outs) if assemble else tuple(given) + tuple(outs)

    quant, keep, send, bg, lg = pl.pallas_call(
        functools.partial(quant_kernel, ranks),
        out_shape=(
            shape((clips, frames, D), BF16),
            shape((2, CODES, DG), F32),
            shape((2, CODES, DG), F32),
            shape((rows, D), BF16),
            shape((clips * frames, D), F32),
        ),
        in_specs=[smem] + whole(5 + len(pieces_c)),
        out_specs=tuple(whole(5)),
        scratch_shapes=[
            pltpu.VMEM((SLOTS, CODES, DG), BF16),
            pltpu.VMEM((SLOTS, clips * frames, 2 * DG), BF16),
        ],
        compiler_params=params(16),
        name="quant",
    )(clip_lengths, latent, cotangent, cot, hot, hott, *pieces_c)

    if assemble:
        grads = (shape((2, ranks * small, DG), F32),) * 2
    else:
        grads = (shape((KERNEL, HID, D), F32), shape((D, HID), F32))
    fg, first_grad, second_grad = pl.pallas_call(
        functools.partial(backward_kernel, ranks, assemble, clips),
        out_shape=(shape((clips, frames, D), F32),) + grads,
        in_specs=[smem] + whole(8),
        out_specs=tuple(whole(3)),
        scratch_shapes=[pltpu.VMEM((4, HID, D), F32)] if assemble else [],
        compiler_params=params(16),
        name="backward",
    )(clip_lengths, start, act, gated, bg, lg, hs, dil, pwt)

    if assemble:
        keep_d, send_d = first_grad, second_grad
    else:
        parts = jnp.concatenate(
            [
                first_grad.reshape(KERNEL, ranks, out_rows, 2, DG)
                .transpose(0, 1, 3, 2, 4)
                .reshape(KERNEL, ranks, small, DG),
                second_grad.reshape(1, ranks, small, DG),
            ],
            axis=0,
        )
        seq = jnp.concatenate([jnp.arange(0, ranks, 2), jnp.arange(1, ranks, 2)])
        parts = jnp.take(jnp.take(parts, time ^ jnp.arange(4), axis=0), rank ^ seq, axis=1)
        parts = parts.reshape(2, 2, ranks * small, DG)
        keep_d, send_d = parts[:, 0], parts[:, 1]

    def sent(keep, got, groups, size, tag):
        count = len(groups[0])
        packed = count * size + count * SCALE_GROUPS
        return pl.pallas_call(
            functools.partial(send_kernel, groups, size),
            out_shape=(shape((count, size, DG), F32),)
            + (shape((packed, DG), jnp.int16),) * (len(groups) - 1),
            in_specs=whole(2),
            out_specs=tuple(whole(len(groups))),
            compiler_params=params(),
            name="send_" + tag,
        )(keep, got)

    def passed(parts, size, tag):
        count = parts[0].shape[0]
        return pl.pallas_call(
            functools.partial(pass_kernel, size),
            out_shape=(shape((size, DG), F32),)
            + (shape((size + 16, DG), jnp.int16),) * (count - 1),
            in_specs=whole(len(parts)),
            out_specs=tuple(whole(count)),
            compiler_params=params(),
            name="pass_" + tag,
        )(*parts)

    def over_plane(parts):
        return [parts[0], swap(parts[1], 1, 0), swap(parts[2], 0, 2), swap(parts[3], 1, 2)]

    def over_line(parts):
        return [parts[0]] + [swap(parts[z], 2 * z, 0) for z in range(1, half)]

    by_plane = [[(jy, x * half + z) for z in range(half)] for jy in range(2) for x in range(2)]
    by_line = [[(jy, x * half + z) for jy in range(2) for x in range(2)] for z in range(half)]
    got_c, got_d = swap(send, 0, 1), swap(send_d, 0, 1)
    parts_c = over_plane(sent(keep, got_c, by_plane, block, "codes"))
    parts_c[0], keep_d = lax.optimization_barrier((parts_c[0], keep_d))
    parts_d = over_line(sent(keep_d, got_d, by_line, small, "conv"))
    parts_c = over_line(passed(parts_c, block, "codes"))
    parts_c[1], parts_d[0] = lax.optimization_barrier((parts_c[1], parts_d[0]))
    parts_d = over_plane(passed(parts_d, small, "conv"))
    total = small + block
    piece, squared = pl.pallas_call(
        functools.partial(final_kernel, (small, block), (4, half)),
        out_shape=(shape((total, DG), F32), shape((8, 128), F32)),
        in_specs=whole(4 + half),
        out_specs=tuple(whole(2)),
        compiler_params=params(),
        name="final",
    )(*parts_d, *parts_c)

    across = swap(piece, 0, 2)
    squared = squared + swap(squared, 0, 1)
    squared = (squared + swap(squared, 1, 0)) + (swap(squared, 0, 2) + swap(squared, 1, 2))
    step = 2
    while step < ranks:
        squared = squared + swap(squared, step, 0)
        if step == 2:
            across, squared = lax.optimization_barrier((across, squared))
        step *= 2
    fours = [piece, swap(piece, 0, 1), across, swap(across, 0, 1)]
    steps = step_count[0].astype(F32)
    decays = jnp.stack([1.0 / (1.0 - FIRST_DECAY**steps), 1.0 / (1.0 - SECOND_DECAY**steps)])
    if assemble:
        state = dil_state + pw_state + table_state
        norm, *new = pl.pallas_call(
            update_kernel,
            out_shape=(shape((1, 1), F32),) + tuple(shape(v.shape, F32) for v in state),
            in_specs=[smem] + whole(14),
            out_specs=tuple(whole(1) + [hbm] * 9),
            scratch_shapes=[pltpu.VMEM(v.shape, F32) for v in state]
            + [pltpu.SemaphoreType.DMA((18,))],
            compiler_params=params(8),
            name="update",
        )(decays, squared, *fours, *state)
        norm = norm.reshape(1)
        dil_new, pw_new, table_new = new[:3], new[3:6], new[6:]
    else:
        four = jnp.take(jnp.stack(fours, axis=0), time ^ jnp.arange(4), axis=0)
        raw = four[:KERNEL, :small].reshape(KERNEL, 2, out_rows, DG)
        raw = raw.transpose(0, 2, 1, 3).reshape(KERNEL, out_rows, D)
        count = KERNEL * D * HID + D * HID + SLOTS * CODES * DG
        limit = jnp.sqrt(jnp.float32(count))
        norm = jnp.sqrt(squared[0, :1])
        scale = limit / jnp.maximum(norm[0], limit)
        new = []
        for state, grad, rate in (
            (dil_state, raw, BITRATE_FACTOR),
            (pw_state, four[3, :small], BITRATE_FACTOR),
            (table_state, four[:, small:], RATE_CODE),
        ):
            grad = grad * scale
            weight, second = stepped(*state, grad, rate, decays[0], decays[1])
            new.append((weight, grad, second))
        dil_new, pw_new, table_new = new
    return (
        quant,
        fg,
        norm,
        *[v.transpose(0, 2, 1) for v in dil_new],
        *[v.T for v in pw_new],
        *table_new,
    )


def solution(mesh):
    in_specs = (
        P("clip", "tm", None),
        P("clip", "tm", None),
        P("clip"),
        P(None, "clip", "tm"),
        P(),
        P(None, None, "clip"),
        P(None, "clip"),
        P(None, "clip", None),
        P(None, None, "clip"),
        P(None, None, "clip"),
        P(None, "clip"),
        P(None, "clip"),
        P(None, "clip", None),
        P(None, "clip", None),
    )
    out_specs = (
        P("clip", "tm", None),
        P("clip", "tm", None),
        P(),
        P(None, None, "clip"),
        P(None, None, "clip"),
        P(None, None, "clip"),
        P(None, "clip"),
        P(None, "clip"),
        P(None, "clip"),
        P(None, "clip", None),
        P(None, "clip", None),
        P(None, "clip", None),
    )
    return jax.shard_map(shards, mesh=mesh, in_specs=in_specs, out_specs=out_specs, check_vma=False)
```

time: 112 us -> 97.5 us (0.87)
  waiting for transfers between devices: 38.9 us -> 28 us
  local copies, waits for them, and re-layouts: 5.18 us -> 0.07 us
  Pallas kernels: 18.2 us -> 20.4 us
    ppermute x32 -> x41, waiting for transfers between devices: 38.9 us -> 28 us  [swap(): return lax.ppermute(value, ('clip', 'tm'), pairs)]
    unnamed x32 -> x26, local copies, waits for them, and re-layouts: 2.87 us -> 0.07 us
    pallas_call x9 -> x11, Pallas kernels: 10.1 us -> 12.3 us  [the longest x1 2.95 us: shards(): pl.pallas_call(update_kernel, out_shape=(shape((1, 1), F32),) + tuple((sh...]
    ppermute x2, starting transfers between devices: 2.56 us -> 0.74 us  [the longest x1 0.66 us: shards(): far = lax.ppermute(far, 'tm', pairs + [(b, a) for a, b in pairs])]
    ppermute x32 -> x41, starting transfers between devices: 44.3 us -> 45.9 us  [swap(): return lax.ppermute(value, ('clip', 'tm'), pairs)]
    slice x2 -> x0, local copies, waits for them, and re-layouts: 1.29 us -> none  [the longest x1 0.78 us: packed(): cotangent[:, low:high]]
  transfers between devices with their start and end apart: 34 -> 43, of which waited for: 18 -> 18; matrix products, arithmetic and copies ran while one was open for 2% -> 0% of each run, Pallas kernels for 8% -> 12%
where the time goes in v3:
time: 97.5 us; the launch traced here: 97.2 us
  starting transfers between devices  46.6 us (48%)
  waiting for transfers between devices  28 us (29%)
  Pallas kernels  20.4 us (21%)
  between operations  1.99 us (2%)
    ppermute x41, starting transfers between devices, swap(): return lax.ppermute(value, ('clip', 'tm'), pairs)  45.9 us
    ppermute x41, waiting for transfers between devices, swap(): return lax.ppermute(value, ('clip', 'tm'), pairs)  28 us
    pallas_call x1, Pallas kernels, shards(): pl.pallas_call(functools.partial(quant_kernel, ranks), out_shape=(shape((...  4.94 us
    pallas_call x1, Pallas kernels, shards(): pl.pallas_call(functools.partial(backward_kernel, ranks, assemble, clips)...  3.19 us
    pallas_call x1, Pallas kernels, shards(): pl.pallas_call(update_kernel, out_shape=(shape((1, 1), F32),) + tuple((sh...  2.95 us
    pallas_call x1, Pallas kernels, shards(): pl.pallas_call(functools.partial(own_kernel, ranks), out_shape=(shape((SL...  2.82 us
  transfers between devices with their start and end apart: 43, of which 18 were waited for; matrix products, arithmetic and copies ran while one was open for 0% of the time, Pallas kernels for 12%

profile of v3, /device:TPU:0, one launch (start us, length us, event | category | flops | bytes accessed | tf_op | source)
XLA Modules:
  0.0 97.2 jit_solution(2166841187869257777)
XLA Ops:
  1.8 3.1 %collective-permute-start.3 = (bf16[128,256]{1,0:T(8,128)(2,1)S(1)}, bf16[128,256]{1,0:T(8,128)(2,1)S(1)}, u32[]{:S(2)}, u32[]{:S(2)}) collective-permute-start(bf16[128,256]{1,0:T(8,128)(2,1)S(1)} %get-tuple-element.96), channel_id=1, source_target_pairs={{0,8},{1,9},{2,10},{3,11},{4,12},{5,13},{6,14},{7,15},{8,0},{9,1},... | collective-permute-start | bytes 196616 | tf_op jit(solution)/shard_map/ppermute | solution.py:70
  4.8 2.6 %collective-permute-start.4 = (bf16[128,256]{1,0:T(8,128)(2,1)S(1)}, bf16[128,256]{1,0:T(8,128)(2,1)S(1)}, u32[]{:S(2)}, u32[]{:S(2)}) collective-permute-start(bf16[128,256]{1,0:T(8,128)(2,1)S(1)} %get-tuple-element.96), channel_id=1, source_target_pairs={{0,16},{1,17},{2,18},{3,19},{4,20},{5,21},{6,22},{7,23},{8,24},{9,... | collective-permute-start | bytes 196616 | tf_op jit(solution)/shard_map/ppermute | solution.py:70
  9.2 1.8 %collective-permute-start.2 = (bf16[2,64,256]{2,1,0:T(8,128)(2,1)S(1)}, bf16[2,64,256]{2,1,0:T(8,128)(2,1)S(1)}, u32[]{:S(2)}, u32[]{:S(2)}) collective-permute-start(bf16[2,64,256]{2,1,0:T(8,128)(2,1)S(1)} %get-tuple-element.95), channel_id=1, source_target_pairs={{0,4},{1,5},{2,6},{3,7},{4,0},{5,1},{6,2},{7,3},{8,12},{9,13},{10,... | collective-permute-start | bytes 196616 | tf_op jit(solution)/shard_map/ppermute | solution.py:70
  12.1 1.4 %collective-permute-done.5 = bf16[128,256]{1,0:T(8,128)(2,1)S(1)} collective-permute-done((bf16[128,256]{1,0:T(8,128)(2,1)S(1)}, bf16[128,256]{1,0:T(8,128)(2,1)S(1)}, u32[]{:S(2)}, u32[]{:S(2)}) %collective-permute-start.5) | collective-permute-done | bytes 65568 | tf_op jit(solution)/shard_map/ppermute | solution.py:70
  13.6 2.0 %collective-permute-start.10 = (bf16[2,2,64,256]{3,2,1,0:T(8,128)(2,1)S(1)}, bf16[2,2,64,256]{3,2,1,0:T(8,128)(2,1)S(1)}, u32[]{:S(2)}, u32[]{:S(2)}) collective-permute-start(bf16[2,2,64,256]{3,2,1,0:T(8,128)(2,1)S(1)} %pad_maximum_fusion.1.refs_0_), channel_id=1, source_target_pairs={{0,16},{1,17},{2,18},{3,19},{4,20},{5,21},{6,22},{7,23},{8,24},{9,... | collective-permute-start | bytes 393224 | tf_op jit(solution)/shard_map/ppermute | solution.py:70
  15.6 1.5 %collective-permute-start.6 = (bf16[4,128,256]{2,1,0:T(8,128)(2,1)S(1)}, bf16[4,128,256]{2,1,0:T(8,128)(2,1)S(1)}, u32[]{:S(2)}, u32[]{:S(2)}) collective-permute-start(bf16[4,128,256]{2,1,0:T(8,128)(2,1)S(1)} %pad_maximum_fusion.refs_0_), channel_id=1, source_target_pairs={{0,4},{1,5},{2,6},{3,7},{4,0},{5,1},{6,2},{7,3},{8,12},{9,13},{10,... | collective-permute-start | bytes 786440 | tf_op jit(solution)/shard_map/ppermute | solution.py:70
  17.0 3.4 %collective-permute-start.7 = (bf16[4,128,256]{2,1,0:T(8,128)(2,1)S(1)}, bf16[4,128,256]{2,1,0:T(8,128)(2,1)S(1)}, u32[]{:S(2)}, u32[]{:S(2)}) collective-permute-start(bf16[4,128,256]{2,1,0:T(8,128)(2,1)S(1)} %pad_maximum_fusion.refs_0_), channel_id=1, source_target_pairs={{0,2},{1,3},{2,0},{3,1},{4,6},{5,7},{6,4},{7,5},{8,10},{9,11},{10,... | collective-permute-start | bytes 786440 | tf_op jit(solution)/shard_map/ppermute | solution.py:70
  20.4 2.0 %collective-permute-start.11 = (bf16[2,2,64,256]{3,2,1,0:T(8,128)(2,1)S(1)}, bf16[2,2,64,256]{3,2,1,0:T(8,128)(2,1)S(1)}, u32[]{:S(2)}, u32[]{:S(2)}) collective-permute-start(bf16[2,2,64,256]{3,2,1,0:T(8,128)(2,1)S(1)} %pad_maximum_fusion.1.refs_0_), channel_id=1, source_target_pairs={{0,24},{1,25},{2,26},{3,27},{4,28},{5,29},{6,30},{7,31},{8,16},{9,... | collective-permute-start | bytes 393224 | tf_op jit(solution)/shard_map/ppermute | solution.py:70
  23.7 2.8 %own.1 = (bf16[4,544,1024]{2,1,0:T(8,128)(2,1)S(1)}, bf16[4,1024,512]{2,1,0:T(8,128)(2,1)S(1)}) custom-call(s32[4,2,256]{2,1,0:T(2,128)S(1)} %copy-done.11), custom_call_target="tpu_custom_call" | custom-call | tf_op jit(solution)/shard_map/own/pallas_call | solution.py:626
  26.6 1.4 %margin.1 = (f32[544,512]{1,0:T(8,128)S(1)}, bf16[544,512]{1,0:T(8,128)(2,1)S(1)}, f32[32,512]{1,0:T(8,128)S(1)}, bf16[4,544,1024]{2,1,0:T(8,128)(2,1)S(1)}) custom-call(s32[2]{0:T(128)S(1)} %copy-done.12, bf16[2,256,512]{2,1,0:T(8,128)(2,1)S(1)} %copy-done.2, ...), custom_call_target="tpu_custom_call", output_to_operand_aliasing={{3}: (4, {})} | custom-call | tf_op jit(solution)/shard_map/margin/pallas_call | solution.py:640
  28.0 2.0 %collective-permute-done.9.refs_1_ = bf16[2,2,64,256]{3,2,1,0:T(8,128)(2,1)S(1)} collective-permute-done((bf16[2,2,64,256]{3,2,1,0:T(8,128)(2,1)S(1)}, bf16[2,2,64,256]{3,2,1,0:T(8,128)(2,1)S(1)}, u32[]{:S(2)}, u32[]{:S(2)}) %collective-permute-start.9) | collective-permute-done | bytes 131104 | tf_op jit(solution)/shard_map/ppermute | solution.py:70
  30.0 2.0 %collective-permute-done.7.refs_4_ = bf16[4,128,256]{2,1,0:T(8,128)(2,1)S(1)} collective-permute-done((bf16[4,128,256]{2,1,0:T(8,128)(2,1)S(1)}, bf16[4,128,256]{2,1,0:T(8,128)(2,1)S(1)}, u32[]{:S(2)}, u32[]{:S(2)}) %collective-permute-start.7) | collective-permute-done | bytes 262176 | tf_op jit(solution)/shard_map/ppermute | solution.py:70
  34.1 1.5 %collective-permute-done.15.refs_7_ = bf16[2,2,64,256]{3,2,1,0:T(8,128)(2,1)S(1)} collective-permute-done((bf16[2,2,64,256]{3,2,1,0:T(8,128)(2,1)S(1)}, bf16[2,2,64,256]{3,2,1,0:T(8,128)(2,1)S(1)}, u32[]{:S(2)}, u32[]{:S(2)}) %collective-permute-start.15) | collective-permute-done | bytes 131104 | tf_op jit(solution)/shard_map/ppermute | solution.py:70
  36.9 4.9 %quant.1 = (bf16[2,256,512]{2,1,0:T(8,128)(2,1)}, f32[2,1024,256]{2,1,0:T(8,128)S(1)}, f32[2,1024,256]{2,1,0:T(8,128)S(1)}, bf16[544,512]{1,0:T(8,128)(2,1)S(1)}, f32[512,512]{1,0:T(8,128)S(1)}) custom-call(s32[2]{0:T(128)S(1)} %copy-done.12, f32[544,512]{1,0:T(8,128)S(1)} %get-tuple-element.114.latent_ref, bf16[2,256,512]{2,1,0:T(8,128)(2,1)S(1)} %copy-done, ...), custom_call_target="tpu_custom_call" | custom-call | tf_op jit(solution)/shard_map/quant/pallas_call | solution.py:684
  42.2 3.2 %backward.1 = (f32[2,256,512]{2,1,0:T(8,128)}, f32[2,512,256]{2,1,0:T(8,128)S(1)}, f32[2,512,256]{2,1,0:T(8,128)S(1)}) custom-call(s32[2]{0:T(128)S(1)} %copy-done.12, f32[544,512]{1,0:T(8,128)S(1)} %get-tuple-element.105.start_ref, bf16[544,512]{1,0:T(8,128)(2,1)S(1)} %get-tuple-element.109.act_ref, bf16[544,256]{1,0:T(8,128)(2,1)S(1)} %get-tuple-element.123.gated_ref, ...), custom_call_target="tpu_custom_call" | custom-call | tf_op jit(solution)/shard_map/backward/pallas_call | solution.py:707
  47.6 2.5 %collective-permute-start.23 = (s16[528,256]{1,0:T(8,128)(2,1)S(1)}, s16[528,256]{1,0:T(8,128)(2,1)S(1)}, u32[]{:S(2)}, u32[]{:S(2)}) collective-permute-start(s16[528,256]{1,0:T(8,128)(2,1)S(1)} %get-tuple-element.137), channel_id=1, source_target_pairs={{0,6},{1,7},{2,4},{3,5},{4,2},{5,3},{6,0},{7,1},{8,14},{9,15},{10,... | collective-permute-start | bytes 811016 | tf_op jit(solution)/shard_map/ppermute | solution.py:70
  50.7 2.5 %collective-permute-start.26 = (s16[272,256]{1,0:T(8,128)(2,1)S(1)}, s16[272,256]{1,0:T(8,128)(2,1)S(1)}, u32[]{:S(2)}, u32[]{:S(2)}) collective-permute-start(s16[272,256]{1,0:T(8,128)(2,1)S(1)} %get-tuple-element.143), channel_id=1, source_target_pairs={{0,8},{1,9},{2,10},{3,11},{4,12},{5,13},{6,14},{7,15},{8,0},{9,1},... | collective-permute-start | bytes 417800 | tf_op jit(solution)/shard_map/ppermute | solution.py:70
  53.6 2.3 %collective-permute-done.21.refs_0_ = s16[528,256]{1,0:T(8,128)(2,1)S(1)} collective-permute-done((s16[528,256]{1,0:T(8,128)(2,1)S(1)}, s16[528,256]{1,0:T(8,128)(2,1)S(1)}, u32[]{:S(2)}, u32[]{:S(2)}) %collective-permute-start.21) | collective-permute-done | bytes 270368 | tf_op jit(solution)/shard_map/ppermute | solution.py:70
  55.9 2.3 %collective-permute-start.28 = (s16[272,256]{1,0:T(8,128)(2,1)S(1)}, s16[272,256]{1,0:T(8,128)(2,1)S(1)}, u32[]{:S(2)}, u32[]{:S(2)}) collective-permute-start(s16[272,256]{1,0:T(8,128)(2,1)S(1)} %get-tuple-element.145), channel_id=1, source_target_pairs={{0,24},{1,25},{2,26},{3,27},{4,28},{5,29},{6,30},{7,31},{8,16},{9,... | collective-permute-start | bytes 417800 | tf_op jit(solution)/shard_map/ppermute | solution.py:70
  58.2 3.2 %collective-permute-done.22.refs_1_ = s16[528,256]{1,0:T(8,128)(2,1)S(1)} collective-permute-done((s16[528,256]{1,0:T(8,128)(2,1)S(1)}, s16[528,256]{1,0:T(8,128)(2,1)S(1)}, u32[]{:S(2)}, u32[]{:S(2)}) %collective-permute-start.22) | collective-permute-done | bytes 270368 | tf_op jit(solution)/shard_map/ppermute | solution.py:70
  61.7 2.5 %collective-permute-start.24 = (s16[144,256]{1,0:T(8,128)(2,1)S(1)}, s16[144,256]{1,0:T(8,128)(2,1)S(1)}, u32[]{:S(2)}, u32[]{:S(2)}) collective-permute-start(s16[144,256]{1,0:T(8,128)(2,1)S(1)} %get-tuple-element.138), channel_id=1, source_target_pairs={{0,8},{1,9},{2,10},{3,11},{4,12},{5,13},{6,14},{7,15},{8,0},{9,1},... | collective-permute-start | bytes 221192 | tf_op jit(solution)/shard_map/ppermute | solution.py:70
  64.3 1.6 %collective-permute-start.32 = (s16[144,256]{1,0:T(8,128)(2,1)S(1)}, s16[144,256]{1,0:T(8,128)(2,1)S(1)}, u32[]{:S(2)}, u32[]{:S(2)}) collective-permute-start(s16[144,256]{1,0:T(8,128)(2,1)S(1)} %get-tuple-element.152), channel_id=1, source_target_pairs={{0,16},{1,17},{2,18},{3,19},{4,20},{5,21},{6,22},{7,23},{8,24},{9,... | collective-permute-start | bytes 221192 | tf_op jit(solution)/shard_map/ppermute | solution.py:70
  66.8 3.0 %collective-permute-start.33 = (s16[144,256]{1,0:T(8,128)(2,1)S(1)}, s16[144,256]{1,0:T(8,128)(2,1)S(1)}, u32[]{:S(2)}, u32[]{:S(2)}) collective-permute-start(s16[144,256]{1,0:T(8,128)(2,1)S(1)} %get-tuple-element.153), channel_id=1, source_target_pairs={{0,24},{1,25},{2,26},{3,27},{4,28},{5,29},{6,30},{7,31},{8,16},{9,... | collective-permute-start | bytes 221192 | tf_op jit(solution)/shard_map/ppermute | solution.py:70
  70.7 1.6 %collective-permute-start.30 = (s16[80,256]{1,0:T(8,128)(2,1)S(1)}, s16[80,256]{1,0:T(8,128)(2,1)S(1)}, u32[]{:S(2)}, u32[]{:S(2)}) collective-permute-start(s16[80,256]{1,0:T(8,128)(2,1)S(1)} %get-tuple-element.148), channel_id=1, source_target_pairs={{0,2},{1,3},{2,0},{3,1},{4,6},{5,7},{6,4},{7,5},{8,10},{9,11},{10,... | collective-permute-start | bytes 122888 | tf_op jit(solution)/shard_map/ppermute | solution.py:70
  74.7 2.5 %collective-permute-done.31.refs_3_ = s16[80,256]{1,0:T(8,128)(2,1)S(1)} collective-permute-done((s16[80,256]{1,0:T(8,128)(2,1)S(1)}, s16[80,256]{1,0:T(8,128)(2,1)S(1)}, u32[]{:S(2)}, u32[]{:S(2)}) %collective-permute-start.31) | collective-permute-done | bytes 40992 | tf_op jit(solution)/shard_map/ppermute | solution.py:70
  78.9 1.5 %collective-permute-start.37 = (f32[8,128]{1,0:T(8,128)S(1)}, f32[8,128]{1,0:T(8,128)S(1)}, u32[]{:S(2)}, u32[]{:S(2)}) collective-permute-start(f32[8,128]{1,0:T(8,128)S(1)} %add.18), channel_id=1, source_target_pairs={{0,2},{1,3},{2,0},{3,1},{4,6},{5,7},{6,4},{7,5},{8,10},{9,11},{10,... | collective-permute-start | bytes 12296 | tf_op jit(solution)/shard_map/ppermute | solution.py:70
  80.4 1.7 %collective-permute-start.38 = (f32[8,128]{1,0:T(8,128)S(1)}, f32[8,128]{1,0:T(8,128)S(1)}, u32[]{:S(2)}, u32[]{:S(2)}) collective-permute-start(f32[8,128]{1,0:T(8,128)S(1)} %add.18), channel_id=1, source_target_pairs={{0,6},{1,7},{2,4},{3,5},{4,2},{5,3},{6,0},{7,1},{8,14},{9,15},{10,... | collective-permute-start | bytes 12296 | tf_op jit(solution)/shard_map/ppermute | solution.py:70
  82.5 2.5 %collective-permute-done.38 = f32[8,128]{1,0:T(8,128)S(1)} collective-permute-done((f32[8,128]{1,0:T(8,128)S(1)}, f32[8,128]{1,0:T(8,128)S(1)}, u32[]{:S(2)}, u32[]{:S(2)}) %collective-permute-start.38) | collective-permute-done | bytes 4128 | tf_op jit(solution)/shard_map/ppermute | solution.py:70
  85.0 2.0 %collective-permute-start.39 = (f32[8,128]{1,0:T(8,128)S(1)}, f32[8,128]{1,0:T(8,128)S(1)}, u32[]{:S(2)}, u32[]{:S(2)}) collective-permute-start(f32[8,128]{1,0:T(8,128)S(1)} %add_add_fusion), channel_id=1, source_target_pairs={{0,8},{1,9},{2,10},{3,11},{4,12},{5,13},{6,14},{7,15},{8,0},{9,1},... | collective-permute-start | bytes 12296 | tf_op jit(solution)/shard_map/ppermute | solution.py:70
  87.0 1.6 %collective-permute-done.39 = f32[8,128]{1,0:T(8,128)S(1)} collective-permute-done((f32[8,128]{1,0:T(8,128)S(1)}, f32[8,128]{1,0:T(8,128)S(1)}, u32[]{:S(2)}, u32[]{:S(2)}) %collective-permute-start.39) | collective-permute-done | bytes 4128 | tf_op jit(solution)/shard_map/ppermute | solution.py:70
  90.6 3.4 %collective-permute-done.40 = f32[8,128]{1,0:T(8,128)S(1)} collective-permute-done((f32[8,128]{1,0:T(8,128)S(1)}, f32[8,128]{1,0:T(8,128)S(1)}, u32[]{:S(2)}, u32[]{:S(2)}) %collective-permute-start.40) | collective-permute-done | bytes 4128 | tf_op jit(solution)/shard_map/ppermute | solution.py:70
  94.1 2.9 %update.1 = (f32[1,1]{1,0:T(1,128)}, f32[3,32,512]{2,1,0:T(8,128)}, f32[3,32,512]{2,1,0:T(8,128)}, f32[3,32,512]{2,1,0:T(8,128)}, f32[64,256]{1,0:T(8,128)}, /*i...) custom-call(f32[2]{0:T(128)S(1)} %pad_maximum_fusion.2.fix_ref, ...), custom_call_target="tpu_custom_call" | custom-call | tf_op jit(solution)/shard_map/update/pallas_call | solution.py:798
  (100 shorter events, 20.1 us)
Async XLA Ops:
  1.8 7.4 %collective-permute-start.3 = (bf16[128,256]{1,0:T(8,128)(2,1)S(1)}, bf16[128,256]{1,0:T(8,128)(2,1)S(1)}, u32[]{:S(2)}, u32[]{:S(2)}) collective-permute-start(bf16[128,256]{1,0:T(8,128)(2,1)S(1)} %get-tuple-element.96), channel_id=1, source_target_pairs={{0,8},{1,9},{2,10},{3,11},{4,12},{5,13},{6,14},{7,15},{8,0},{9,1},... | collective-permute-start | bytes 196616 | tf_op jit(solution)/shard_map/ppermute | solution.py:70
  4.8 7.3 %collective-permute-start.4 = (bf16[128,256]{1,0:T(8,128)(2,1)S(1)}, bf16[128,256]{1,0:T(8,128)(2,1)S(1)}, u32[]{:S(2)}, u32[]{:S(2)}) collective-permute-start(bf16[128,256]{1,0:T(8,128)(2,1)S(1)} %get-tuple-element.96), channel_id=1, source_target_pairs={{0,16},{1,17},{2,18},{3,19},{4,20},{5,21},{6,22},{7,23},{8,24},{9,... | collective-permute-start | bytes 196616 | tf_op jit(solution)/shard_map/ppermute | solution.py:70
  7.4 6.1 %collective-permute-start.5 = (bf16[128,256]{1,0:T(8,128)(2,1)S(1)}, bf16[128,256]{1,0:T(8,128)(2,1)S(1)}, u32[]{:S(2)}, u32[]{:S(2)}) collective-permute-start(bf16[128,256]{1,0:T(8,128)(2,1)S(1)} %get-tuple-element.96), channel_id=1, source_target_pairs={{0,24},{1,25},{2,26},{3,27},{4,28},{5,29},{6,30},{7,31},{8,16},{9,... | collective-permute-start | bytes 196616 | tf_op jit(solution)/shard_map/ppermute | solution.py:70
  8.4 5.1 %collective-permute-start = (bf16[2,16,1024]{2,1,0:T(8,128)(2,1)S(1)}, bf16[2,16,1024]{2,1,0:T(8,128)(2,1)S(1)}, u32[]{:S(2)}, u32[]{:S(2)}) collective-permute-start(bf16[2,16,1024]{2,1,0:T(8,128)(2,1)S(1)} %get-tuple-element.93), channel_id=1, source_target_pairs={{0,1},{1,0},{2,3},{3,2},{4,5},{5,4},{6,7},{7,6},{8,9},{9,8},{10,11... | collective-permute-start | bytes 196616 | tf_op jit(solution)/shard_map/ppermute | solution.py:619
  8.5 5.0 %collective-permute-start.1 = (bf16[2,16,1024]{2,1,0:T(8,128)(2,1)S(1)}, bf16[2,16,1024]{2,1,0:T(8,128)(2,1)S(1)}, u32[]{:S(2)}, u32[]{:S(2)}) collective-permute-start(bf16[2,16,1024]{2,1,0:T(8,128)(2,1)S(1)} %get-tuple-element.94), channel_id=1, source_target_pairs={{1,2},{2,1},{5,6},{6,5},{9,10},{10,9},{13,14},{14,13},{17,18},{18,... | collective-permute-start | bytes 196616 | tf_op jit(solution)/shard_map/ppermute | solution.py:621
  9.2 4.3 %collective-permute-start.2 = (bf16[2,64,256]{2,1,0:T(8,128)(2,1)S(1)}, bf16[2,64,256]{2,1,0:T(8,128)(2,1)S(1)}, u32[]{:S(2)}, u32[]{:S(2)}) collective-permute-start(bf16[2,64,256]{2,1,0:T(8,128)(2,1)S(1)} %get-tuple-element.95), channel_id=1, source_target_pairs={{0,4},{1,5},{2,6},{3,7},{4,0},{5,1},{6,2},{7,3},{8,12},{9,13},{10,... | collective-permute-start | bytes 196616 | tf_op jit(solution)/shard_map/ppermute | solution.py:70
  13.6 9.2 %collective-permute-start.10 = (bf16[2,2,64,256]{3,2,1,0:T(8,128)(2,1)S(1)}, bf16[2,2,64,256]{3,2,1,0:T(8,128)(2,1)S(1)}, u32[]{:S(2)}, u32[]{:S(2)}) collective-permute-start(bf16[2,2,64,256]{3,2,1,0:T(8,128)(2,1)S(1)} %pad_maximum_fusion.1.refs_0_), channel_id=1, source_target_pairs={{0,16},{1,17},{2,18},{3,19},{4,20},{5,21},{6,22},{7,23},{8,24},{9,... | collective-permute-start | bytes 393224 | tf_op jit(solution)/shard_map/ppermute | solution.py:70
  15.6 14.5 %collective-permute-start.6 = (bf16[4,128,256]{2,1,0:T(8,128)(2,1)S(1)}, bf16[4,128,256]{2,1,0:T(8,128)(2,1)S(1)}, u32[]{:S(2)}, u32[]{:S(2)}) collective-permute-start(bf16[4,128,256]{2,1,0:T(8,128)(2,1)S(1)} %pad_maximum_fusion.refs_0_), channel_id=1, source_target_pairs={{0,4},{1,5},{2,6},{3,7},{4,0},{5,1},{6,2},{7,3},{8,12},{9,13},{10,... | collective-permute-start | bytes 786440 | tf_op jit(solution)/shard_map/ppermute | solution.py:70
  17.0 15.0 %collective-permute-start.7 = (bf16[4,128,256]{2,1,0:T(8,128)(2,1)S(1)}, bf16[4,128,256]{2,1,0:T(8,128)(2,1)S(1)}, u32[]{:S(2)}, u32[]{:S(2)}) collective-permute-start(bf16[4,128,256]{2,1,0:T(8,128)(2,1)S(1)} %pad_maximum_fusion.refs_0_), channel_id=1, source_target_pairs={{0,2},{1,3},{2,0},{3,1},{4,6},{5,7},{6,4},{7,5},{8,10},{9,11},{10,... | collective-permute-start | bytes 786440 | tf_op jit(solution)/shard_map/ppermute | solution.py:70
  20.4 11.6 %collective-permute-start.8 = (bf16[4,128,256]{2,1,0:T(8,128)(2,1)S(1)}, bf16[4,128,256]{2,1,0:T(8,128)(2,1)S(1)}, u32[]{:S(2)}, u32[]{:S(2)}) collective-permute-start(bf16[4,128,256]{2,1,0:T(8,128)(2,1)S(1)} %pad_maximum_fusion.refs_0_), channel_id=1, source_target_pairs={{0,6},{1,7},{2,4},{3,5},{4,2},{5,3},{6,0},{7,1},{8,14},{9,15},{10,... | collective-permute-start | bytes 786440 | tf_op jit(solution)/shard_map/ppermute | solution.py:70
  20.4 7.6 %collective-permute-start.11 = (bf16[2,2,64,256]{3,2,1,0:T(8,128)(2,1)S(1)}, bf16[2,2,64,256]{3,2,1,0:T(8,128)(2,1)S(1)}, u32[]{:S(2)}, u32[]{:S(2)}) collective-permute-start(bf16[2,2,64,256]{3,2,1,0:T(8,128)(2,1)S(1)} %pad_maximum_fusion.1.refs_0_), channel_id=1, source_target_pairs={{0,24},{1,25},{2,26},{3,27},{4,28},{5,29},{6,30},{7,31},{8,16},{9,... | collective-permute-start | bytes 393224 | tf_op jit(solution)/shard_map/ppermute | solution.py:70
  22.8 7.2 %collective-permute-start.9 = (bf16[2,2,64,256]{3,2,1,0:T(8,128)(2,1)S(1)}, bf16[2,2,64,256]{3,2,1,0:T(8,128)(2,1)S(1)}, u32[]{:S(2)}, u32[]{:S(2)}) collective-permute-start(bf16[2,2,64,256]{3,2,1,0:T(8,128)(2,1)S(1)} %pad_maximum_fusion.1.refs_0_), channel_id=1, source_target_pairs={{0,8},{1,9},{2,10},{3,11},{4,12},{5,13},{6,14},{7,15},{8,0},{9,1},... | collective-permute-start | bytes 393224 | tf_op jit(solution)/shard_map/ppermute | solution.py:70
  32.6 4.3 %collective-permute-start.16 = (bf16[4,128,256]{2,1,0:T(8,128)(2,1)S(1)}, bf16[4,128,256]{2,1,0:T(8,128)(2,1)S(1)}, u32[]{:S(2)}, u32[]{:S(2)}) collective-permute-start(bf16[4,128,256]{2,1,0:T(8,128)(2,1)S(1)} %pad_maximum_fusion.refs_0_), channel_id=1, source_target_pairs={{0,1},{1,0},{2,3},{3,2},{4,5},{5,4},{6,7},{7,6},{8,9},{9,8},{10,11... | collective-permute-start | bytes 786440 | tf_op jit(solution)/shard_map/ppermute | solution.py:70
  41.8 4.2 %collective-permute-start.20 = (f32[2,1024,256]{2,1,0:T(8,128)S(1)}, f32[2,1024,256]{2,1,0:T(8,128)S(1)}, u32[]{:S(2)}, u32[]{:S(2)}) collective-permute-start(f32[2,1024,256]{2,1,0:T(8,128)S(1)} %get-tuple-element.131), channel_id=1, source_target_pairs={{0,1},{1,0},{2,3},{3,2},{4,5},{5,4},{6,7},{7,6},{8,9},{9,8},{10,11... | collective-permute-start | bytes 6291464 | tf_op jit(solution)/shard_map/ppermute | solution.py:70
  45.4 4.8 %collective-permute-start.25 = (f32[2,512,256]{2,1,0:T(8,128)S(1)}, f32[2,512,256]{2,1,0:T(8,128)S(1)}, u32[]{:S(2)}, u32[]{:S(2)}) collective-permute-start(f32[2,512,256]{2,1,0:T(8,128)S(1)} %get-tuple-element.140), channel_id=1, source_target_pairs={{0,1},{1,0},{2,3},{3,2},{4,5},{5,4},{6,7},{7,6},{8,9},{9,8},{10,11... | collective-permute-start | bytes 3145736 | tf_op jit(solution)/shard_map/ppermute | solution.py:70
  46.5 9.4 %collective-permute-start.21 = (s16[528,256]{1,0:T(8,128)(2,1)S(1)}, s16[528,256]{1,0:T(8,128)(2,1)S(1)}, u32[]{:S(2)}, u32[]{:S(2)}) collective-permute-start(s16[528,256]{1,0:T(8,128)(2,1)S(1)} %get-tuple-element.135), channel_id=1, source_target_pairs={{0,4},{1,5},{2,6},{3,7},{4,0},{5,1},{6,2},{7,3},{8,12},{9,13},{10,... | collective-permute-start | bytes 811016 | tf_op jit(solution)/shard_map/ppermute | solution.py:70
  47.1 14.2 %collective-permute-start.22 = (s16[528,256]{1,0:T(8,128)(2,1)S(1)}, s16[528,256]{1,0:T(8,128)(2,1)S(1)}, u32[]{:S(2)}, u32[]{:S(2)}) collective-permute-start(s16[528,256]{1,0:T(8,128)(2,1)S(1)} %get-tuple-element.136), channel_id=1, source_target_pairs={{0,2},{1,3},{2,0},{3,1},{4,6},{5,7},{6,4},{7,5},{8,10},{9,11},{10,... | collective-permute-start | bytes 811016 | tf_op jit(solution)/shard_map/ppermute | solution.py:70
  47.6 13.7 %collective-permute-start.23 = (s16[528,256]{1,0:T(8,128)(2,1)S(1)}, s16[528,256]{1,0:T(8,128)(2,1)S(1)}, u32[]{:S(2)}, u32[]{:S(2)}) collective-permute-start(s16[528,256]{1,0:T(8,128)(2,1)S(1)} %get-tuple-element.137), channel_id=1, source_target_pairs={{0,6},{1,7},{2,4},{3,5},{4,2},{5,3},{6,0},{7,1},{8,14},{9,15},{10,... | collective-permute-start | bytes 811016 | tf_op jit(solution)/shard_map/ppermute | solution.py:70
  50.7 19.1 %collective-permute-start.26 = (s16[272,256]{1,0:T(8,128)(2,1)S(1)}, s16[272,256]{1,0:T(8,128)(2,1)S(1)}, u32[]{:S(2)}, u32[]{:S(2)}) collective-permute-start(s16[272,256]{1,0:T(8,128)(2,1)S(1)} %get-tuple-element.143), channel_id=1, source_target_pairs={{0,8},{1,9},{2,10},{3,11},{4,12},{5,13},{6,14},{7,15},{8,0},{9,1},... | collective-permute-start | bytes 417800 | tf_op jit(solution)/shard_map/ppermute | solution.py:70
  53.2 16.5 %collective-permute-start.27 = (s16[272,256]{1,0:T(8,128)(2,1)S(1)}, s16[272,256]{1,0:T(8,128)(2,1)S(1)}, u32[]{:S(2)}, u32[]{:S(2)}) collective-permute-start(s16[272,256]{1,0:T(8,128)(2,1)S(1)} %get-tuple-element.144), channel_id=1, source_target_pairs={{0,16},{1,17},{2,18},{3,19},{4,20},{5,21},{6,22},{7,23},{8,24},{9,... | collective-permute-start | bytes 417800 | tf_op jit(solution)/shard_map/ppermute | solution.py:70
  55.9 13.9 %collective-permute-start.28 = (s16[272,256]{1,0:T(8,128)(2,1)S(1)}, s16[272,256]{1,0:T(8,128)(2,1)S(1)}, u32[]{:S(2)}, u32[]{:S(2)}) collective-permute-start(s16[272,256]{1,0:T(8,128)(2,1)S(1)} %get-tuple-element.145), channel_id=1, source_target_pairs={{0,24},{1,25},{2,26},{3,27},{4,28},{5,29},{6,30},{7,31},{8,16},{9,... | collective-permute-start | bytes 417800 | tf_op jit(solution)/shard_map/ppermute | solution.py:70
  61.7 5.1 %collective-permute-start.24 = (s16[144,256]{1,0:T(8,128)(2,1)S(1)}, s16[144,256]{1,0:T(8,128)(2,1)S(1)}, u32[]{:S(2)}, u32[]{:S(2)}) collective-permute-start(s16[144,256]{1,0:T(8,128)(2,1)S(1)} %get-tuple-element.138), channel_id=1, source_target_pairs={{0,8},{1,9},{2,10},{3,11},{4,12},{5,13},{6,14},{7,15},{8,0},{9,1},... | collective-permute-start | bytes 221192 | tf_op jit(solution)/shard_map/ppermute | solution.py:70
  64.3 9.3 %collective-permute-start.32 = (s16[144,256]{1,0:T(8,128)(2,1)S(1)}, s16[144,256]{1,0:T(8,128)(2,1)S(1)}, u32[]{:S(2)}, u32[]{:S(2)}) collective-permute-start(s16[144,256]{1,0:T(8,128)(2,1)S(1)} %get-tuple-element.152), channel_id=1, source_target_pairs={{0,16},{1,17},{2,18},{3,19},{4,20},{5,21},{6,22},{7,23},{8,24},{9,... | collective-permute-start | bytes 221192 | tf_op jit(solution)/shard_map/ppermute | solution.py:70
  66.8 6.8 %collective-permute-start.33 = (s16[144,256]{1,0:T(8,128)(2,1)S(1)}, s16[144,256]{1,0:T(8,128)(2,1)S(1)}, u32[]{:S(2)}, u32[]{:S(2)}) collective-permute-start(s16[144,256]{1,0:T(8,128)(2,1)S(1)} %get-tuple-element.153), channel_id=1, source_target_pairs={{0,24},{1,25},{2,26},{3,27},{4,28},{5,29},{6,30},{7,31},{8,16},{9,... | collective-permute-start | bytes 221192 | tf_op jit(solution)/shard_map/ppermute | solution.py:70
  70.0 4.1 %collective-permute-start.29 = (s16[80,256]{1,0:T(8,128)(2,1)S(1)}, s16[80,256]{1,0:T(8,128)(2,1)S(1)}, u32[]{:S(2)}, u32[]{:S(2)}) collective-permute-start(s16[80,256]{1,0:T(8,128)(2,1)S(1)} %get-tuple-element.147), channel_id=1, source_target_pairs={{0,4},{1,5},{2,6},{3,7},{4,0},{5,1},{6,2},{7,3},{8,12},{9,13},{10,... | collective-permute-start | bytes 122888 | tf_op jit(solution)/shard_map/ppermute | solution.py:70
  70.7 4.0 %collective-permute-start.30 = (s16[80,256]{1,0:T(8,128)(2,1)S(1)}, s16[80,256]{1,0:T(8,128)(2,1)S(1)}, u32[]{:S(2)}, u32[]{:S(2)}) collective-permute-start(s16[80,256]{1,0:T(8,128)(2,1)S(1)} %get-tuple-element.148), channel_id=1, source_target_pairs={{0,2},{1,3},{2,0},{3,1},{4,6},{5,7},{6,4},{7,5},{8,10},{9,11},{10,... | collective-permute-start | bytes 122888 | tf_op jit(solution)/shard_map/ppermute | solution.py:70
  72.3 4.9 %collective-permute-start.31 = (s16[80,256]{1,0:T(8,128)(2,1)S(1)}, s16[80,256]{1,0:T(8,128)(2,1)S(1)}, u32[]{:S(2)}, u32[]{:S(2)}) collective-permute-start(s16[80,256]{1,0:T(8,128)(2,1)S(1)} %get-tuple-element.149), channel_id=1, source_target_pairs={{0,6},{1,7},{2,4},{3,5},{4,2},{5,3},{6,0},{7,1},{8,14},{9,15},{10,... | collective-permute-start | bytes 122888 | tf_op jit(solution)/shard_map/ppermute | solution.py:70
  80.4 4.6 %collective-permute-start.38 = (f32[8,128]{1,0:T(8,128)S(1)}, f32[8,128]{1,0:T(8,128)S(1)}, u32[]{:S(2)}, u32[]{:S(2)}) collective-permute-start(f32[8,128]{1,0:T(8,128)S(1)} %add.18), channel_id=1, source_target_pairs={{0,6},{1,7},{2,4},{3,5},{4,2},{5,3},{6,0},{7,1},{8,14},{9,15},{10,... | collective-permute-start | bytes 12296 | tf_op jit(solution)/shard_map/ppermute | solution.py:70
  82.1 6.6 %collective-permute-start.34 = (f32[192,256]{1,0:T(8,128)S(1)}, f32[192,256]{1,0:T(8,128)S(1)}, u32[]{:S(2)}, u32[]{:S(2)}) collective-permute-start(f32[192,256]{1,0:T(8,128)S(1)} %get-tuple-element.154.refs_0_), channel_id=1, source_target_pairs={{0,2},{1,3},{2,0},{3,1},{4,6},{5,7},{6,4},{7,5},{8,10},{9,11},{10,... | collective-permute-start | bytes 589832 | tf_op jit(solution)/shard_map/ppermute | solution.py:70
  87.0 7.0 %collective-permute-start.41 = (f32[192,256]{1,0:T(8,128)S(1)}, f32[192,256]{1,0:T(8,128)S(1)}, u32[]{:S(2)}, u32[]{:S(2)}) collective-permute-start(f32[192,256]{1,0:T(8,128)S(1)} %get-tuple-element.154.refs_0_), channel_id=1, source_target_pairs={{0,1},{1,0},{2,3},{3,2},{4,5},{5,4},{6,7},{7,6},{8,9},{9,8},{10,11... | collective-permute-start | bytes 589832 | tf_op jit(solution)/shard_map/ppermute | solution.py:70
  88.6 5.4 %collective-permute-start.42 = (f32[192,256]{1,0:T(8,128)S(1)}, f32[192,256]{1,0:T(8,128)S(1)}, u32[]{:S(2)}, u32[]{:S(2)}) collective-permute-start(f32[192,256]{1,0:T(8,128)S(1)} %collective-permute-done.34.refs_2_), channel_id=1, source_target_pairs={{0,1},{1,0},{2,3},{3,2},{4,5},{5,4},{6,7},{7,6},{8,9},{9,8},{10,11... | collective-permute-start | bytes 589832 | tf_op jit(solution)/shard_map/ppermute | solution.py:70
  89.4 4.6 %collective-permute-start.40 = (f32[8,128]{1,0:T(8,128)S(1)}, f32[8,128]{1,0:T(8,128)S(1)}, u32[]{:S(2)}, u32[]{:S(2)}) collective-permute-start(f32[8,128]{1,0:T(8,128)S(1)} %add.22), channel_id=1, source_target_pairs={{0,16},{1,17},{2,18},{3,19},{4,20},{5,21},{6,22},{7,23},{8,24},{9,... | collective-permute-start | bytes 12296 | tf_op jit(solution)/shard_map/ppermute | solution.py:70
  (24 other events, 508.1 us)

commit v4 on v3

--- a/solution.py
+++ b/solution.py
@@ -263,7 +263,7 @@
 def quant_kernel(ranks, len_ref, latent_ref, c_ref, cot_ref, hot_ref, hott_ref, *refs):
     half, block = ranks // 2, CODES // ranks
     pieces, refs = refs[:8], refs[8:]
-    quant_ref, keep_ref, send_ref, bg_ref, lg_ref, tab_ref, cgs_ref = refs
+    quant_ref, send_ref, bg_ref, lg_ref, cgs_ref, tab_ref = refs
     clips, frames, _ = c_ref.shape
     time = lax.axis_index("tm")
     mask = masks(clips, frames, len_ref, DG)
@@ -296,14 +296,19 @@
             high = code_grad.astype(BF16)
             cgs_ref[2 * group + level, :, :DG] = high
             cgs_ref[2 * group + level, :, DG:] = (code_grad - high.astype(F32)).astype(BF16)
-    for other in range(SLOTS):
-        slot = time ^ other
+    scattered(1, hott_ref, cgs_ref, send_ref)
+
+
+def scattered(bit, hott_ref, cgs_ref, out_ref):
+    time = lax.axis_index("tm")
+    for far in range(2):
+        slot = time ^ (2 * far + bit)
         pair = mm(hott_ref[slot], cgs_ref[slot])
-        total = pair[:, :DG] + pair[:, DG:]
-        if other % 2 == 0:
-            keep_ref[other // 2] = total
-        else:
-            send_ref[other // 2] = total
+        out_ref[far] = pair[:, :DG] + pair[:, DG:]
+
+
+def keep_kernel(hott_ref, cgs_ref, keep_ref):
+    scattered(0, hott_ref, cgs_ref, keep_ref)
 
 
 def backward_kernel(
@@ -468,7 +473,8 @@
             out_ref[place : place + size, :] = value
             squares = squares + jnp.sum(value * value, axis=0, keepdims=True)
             place += size
-    square_ref[...] = jnp.broadcast_to(jnp.sum(squares, axis=1, keepdims=True), (8, 128))
+    square = jnp.sum(squares, axis=1, keepdims=True)
+    square_ref[...] = jnp.broadcast_to(square[None], square_ref.shape)
 
 
 def stepped(weight, first, second, grad, rate, fix1, fix2):
@@ -489,7 +495,7 @@
     small = 2 * out_rows
     time = lax.axis_index("tm")
     count = KERNEL * D * HID + D * HID + SLOTS * CODES * DG
-    norm = jnp.sqrt(square_ref[...][:1, :1])
+    norm = jnp.sqrt(jnp.sum(square_ref[...], axis=0)[:1, :1])
     limit = jnp.sqrt(jnp.full((1, 1), float(count), F32))
     scale = limit / jnp.maximum(norm, limit)
     norm_ref[...] = norm
@@ -619,10 +625,10 @@
     near = lax.ppermute(near, "tm", [(i, i ^ 1) for i in range(times)])
     pairs = [(i, i + 1) for i in range(1, times - 1, 2)]
     far = lax.ppermute(far, "tm", pairs + [(b, a) for a, b in pairs])
-    near, far, across, *line_c = lax.optimization_barrier((near, far, across, *line_c))
+    near, far, *line_c = lax.optimization_barrier((near, far, *line_c))
     line_c = jnp.stack([mine_c] + line_c, axis=0)
     pair_d = jnp.stack([mine_d, across], axis=0)
-    line_c, pair_d, late_ids = lax.optimization_barrier((line_c, pair_d, code_ids))
+    line_c, late_ids = lax.optimization_barrier((line_c, code_ids))
     hot, hott = pl.pallas_call(
         functools.partial(own_kernel, ranks),
         out_shape=(
@@ -652,8 +658,7 @@
         name="margin",
     )(clip_lengths, features, near, far, hot)
 
-    act, *gone = lax.optimization_barrier((act, *plane_c, *line_d))
-    plane_c, line_d = gone[:4], gone[4:]
+    act, *line_d = lax.optimization_barrier((act, *line_d))
     pieces_d = line_d + [swap(v, 0, 1) for v in line_d]
     turned = [swap(v, 0, 1) for v in plane_c]
     pieces_c = plane_c[:2] + turned[:2] + plane_c[2:] + turned[2:]
@@ -681,24 +686,32 @@
     )(start, act, *given)
     dil, pwt, gated, hs, latent = tuple(outs) if assemble else tuple(given) + tuple(outs)
 
-    quant, keep, send, bg, lg = pl.pallas_call(
+    quant, send, bg, lg, cgs = pl.pallas_call(
         functools.partial(quant_kernel, ranks),
         out_shape=(
             shape((clips, frames, D), BF16),
             shape((2, CODES, DG), F32),
-            shape((2, CODES, DG), F32),
             shape((rows, D), BF16),
             shape((clips * frames, D), F32),
+            shape((SLOTS, clips * frames, 2 * DG), BF16),
         ),
         in_specs=[smem] + whole(5 + len(pieces_c)),
         out_specs=tuple(whole(5)),
         scratch_shapes=[
             pltpu.VMEM((SLOTS, CODES, DG), BF16),
-            pltpu.VMEM((SLOTS, clips * frames, 2 * DG), BF16),
         ],
         compiler_params=params(16),
         name="quant",
     )(clip_lengths, latent, cotangent, cot, hot, hott, *pieces_c)
+
+    keep = pl.pallas_call(
+        keep_kernel,
+        out_shape=shape((2, CODES, DG), F32),
+        in_specs=whole(2),
+        out_specs=whole(1)[0],
+        compiler_params=params(8),
+        name="keep",
+    )(hott, cgs)
 
     if assemble:
         grads = (shape((2, ranks * small, DG), F32),) * 2
@@ -772,9 +785,9 @@
     parts_c[1], parts_d[0] = lax.optimization_barrier((parts_c[1], parts_d[0]))
     parts_d = over_plane(passed(parts_d, small, "conv"))
     total = small + block
-    piece, squared = pl.pallas_call(
+    piece, squares = pl.pallas_call(
         functools.partial(final_kernel, (small, block), (4, half)),
-        out_shape=(shape((total, DG), F32), shape((8, 128), F32)),
+        out_shape=(shape((total, DG), F32), shape((ranks * times, 8, 128), F32)),
         in_specs=whole(4 + half),
         out_specs=tuple(whole(2)),
         compiler_params=params(),
@@ -782,14 +795,7 @@
     )(*parts_d, *parts_c)
 
     across = swap(piece, 0, 2)
-    squared = squared + swap(squared, 0, 1)
-    squared = (squared + swap(squared, 1, 0)) + (swap(squared, 0, 2) + swap(squared, 1, 2))
-    step = 2
-    while step < ranks:
-        squared = squared + swap(squared, step, 0)
-        if step == 2:
-            across, squared = lax.optimization_barrier((across, squared))
-        step *= 2
+    squares = lax.all_to_all(squares, ("clip", "tm"), 0, 0, tiled=True)
     fours = [piece, swap(piece, 0, 1), across, swap(across, 0, 1)]
     steps = step_count[0].astype(F32)
     decays = jnp.stack([1.0 / (1.0 - FIRST_DECAY**steps), 1.0 / (1.0 - SECOND_DECAY**steps)])
@@ -804,7 +810,7 @@
             + [pltpu.SemaphoreType.DMA((18,))],
             compiler_params=params(8),
             name="update",
-        )(decays, squared, *fours, *state)
+        )(decays, squares, *fours, *state)
         norm = norm.reshape(1)
         dil_new, pw_new, table_new = new[:3], new[3:6], new[6:]
     else:
@@ -813,7 +819,7 @@
         raw = raw.transpose(0, 2, 1, 3).reshape(KERNEL, out_rows, D)
         count = KERNEL * D * HID + D * HID + SLOTS * CODES * DG
         limit = jnp.sqrt(jnp.float32(count))
-        norm = jnp.sqrt(squared[0, :1])
+        norm = jnp.sqrt(jnp.sum(squares, axis=0)[0, :1])
         scale = limit / jnp.maximum(norm[0], limit)
         new = []
         for state, grad, rate in (

time: 97.5 us -> 91.4 us (0.937)
  waiting for transfers between devices: 28 us -> 23.5 us
  starting transfers between devices: 46.6 us -> 44.3 us
    ppermute x41 -> x35, waiting for transfers between devices: 28 us -> 18.9 us  [swap(): return lax.ppermute(value, ('clip', 'tm'), pairs)]
    ppermute x41 -> x35, starting transfers between devices: 45.9 us -> 41 us  [swap(): return lax.ppermute(value, ('clip', 'tm'), pairs)]
    all_to_all x0 -> x1, waiting for transfers between devices: none -> 4.62 us  [shards(): squares = lax.all_to_all(squares, ('clip', 'tm'), 0, 0, tiled=True)]
    all_to_all x0 -> x1, starting transfers between devices: none -> 2.58 us  [shards(): squares = lax.all_to_all(squares, ('clip', 'tm'), 0, 0, tiled=True)]
    pallas_call x0 -> x1, Pallas kernels: none -> 1.24 us  [shards(): pl.pallas_call(keep_kernel, out_shape=shape((2, CODES, DG), F32), in_spec...]
    pallas_call x1, Pallas kernels: 4.94 us -> 3.84 us  [shards(): pl.pallas_call(functools.partial(quant_kernel, ranks), out_shape=(shape((...]
  transfers between devices with their start and end apart: 43 -> 38, of which waited for: 18 -> 13; matrix products, arithmetic and copies ran while one was open for 0% -> 0% of each run, Pallas kernels for 12% -> 14%
where the time goes in v4:
time: 91.4 us; the launch traced here: 91.1 us
  starting transfers between devices  44.3 us (48%)
  waiting for transfers between devices  23.5 us (26%)
  Pallas kernels  21.1 us (23%)
  between operations  1.98 us (2%)
    ppermute x35, starting transfers between devices, swap(): return lax.ppermute(value, ('clip', 'tm'), pairs)  41 us
    ppermute x35, waiting for transfers between devices, swap(): return lax.ppermute(value, ('clip', 'tm'), pairs)  18.9 us
    all_to_all x1, waiting for transfers between devices, shards(): squares = lax.all_to_all(squares, ('clip', 'tm'), 0, 0, tiled=True)  4.62 us
    pallas_call x1, Pallas kernels, shards(): pl.pallas_call(functools.partial(quant_kernel, ranks), out_shape=(shape((...  3.84 us
    pallas_call x1, Pallas kernels, shards(): pl.pallas_call(functools.partial(backward_kernel, ranks, assemble, clips)...  3.18 us
    pallas_call x1, Pallas kernels, shards(): pl.pallas_call(update_kernel, out_shape=(shape((1, 1), F32),) + tuple((sh...  2.98 us
    pallas_call x1, Pallas kernels, shards(): pl.pallas_call(functools.partial(own_kernel, ranks), out_shape=(shape((SL...  2.82 us
    all_to_all x1, starting transfers between devices, shards(): squares = lax.all_to_all(squares, ('clip', 'tm'), 0, 0, tiled=True)  2.58 us
  transfers between devices with their start and end apart: 38, of which 13 were waited for; matrix products, arithmetic and copies ran while one was open for 0% of the time, Pallas kernels for 14%

profile of v4, /device:TPU:0, one launch (start us, length us, event | category | flops | bytes accessed | tf_op | source)
XLA Modules:
  0.0 91.1 jit_solution(12730048518595960824)
XLA Ops:
  0.7 1.1 %prep.1 = (bf16[2,64,256]{2,1,0:T(8,128)(2,1)S(1)}, bf16[128,256]{1,0:T(8,128)(2,1)S(1)}) custom-call(f32[3,32,512]{2,1,0:T(8,128)} %bitcast.19, f32[64,256]{1,0:T(8,128)} %bitcast.21, f32[4,128,256]{2,1,0:T(8,128)} %refs_10_.1), custom_call_target="tpu_custom_call" | custom-call | tf_op jit(solution)/shard_map/prep/pallas_call | solution.py:587
  1.8 3.0 %collective-permute-start.5 = (bf16[2,64,256]{2,1,0:T(8,128)(2,1)S(1)}, bf16[2,64,256]{2,1,0:T(8,128)(2,1)S(1)}, u32[]{:S(2)}, u32[]{:S(2)}) collective-permute-start(bf16[2,64,256]{2,1,0:T(8,128)(2,1)S(1)} %get-tuple-element.97), channel_id=1, source_target_pairs={{0,4},{1,5},{2,6},{3,7},{4,0},{5,1},{6,2},{7,3},{8,12},{9,13},{10,... | collective-permute-start | bytes 196616 | tf_op jit(solution)/shard_map/ppermute | solution.py:70
  4.8 1.6 %collective-permute-start.2 = (bf16[128,256]{1,0:T(8,128)(2,1)S(1)}, bf16[128,256]{1,0:T(8,128)(2,1)S(1)}, u32[]{:S(2)}, u32[]{:S(2)}) collective-permute-start(bf16[128,256]{1,0:T(8,128)(2,1)S(1)} %get-tuple-element.87), channel_id=1, source_target_pairs={{0,8},{1,9},{2,10},{3,11},{4,12},{5,13},{6,14},{7,15},{8,0},{9,1},... | collective-permute-start | bytes 196616 | tf_op jit(solution)/shard_map/ppermute | solution.py:70
  6.3 2.6 %collective-permute-start.3 = (bf16[128,256]{1,0:T(8,128)(2,1)S(1)}, bf16[128,256]{1,0:T(8,128)(2,1)S(1)}, u32[]{:S(2)}, u32[]{:S(2)}) collective-permute-start(bf16[128,256]{1,0:T(8,128)(2,1)S(1)} %get-tuple-element.87), channel_id=1, source_target_pairs={{0,16},{1,17},{2,18},{3,19},{4,20},{5,21},{6,22},{7,23},{8,24},{9,... | collective-permute-start | bytes 196616 | tf_op jit(solution)/shard_map/ppermute | solution.py:70
  11.7 1.6 %collective-permute-done.3 = bf16[128,256]{1,0:T(8,128)(2,1)S(1)} collective-permute-done((bf16[128,256]{1,0:T(8,128)(2,1)S(1)}, bf16[128,256]{1,0:T(8,128)(2,1)S(1)}, u32[]{:S(2)}, u32[]{:S(2)}) %collective-permute-start.3) | collective-permute-done | bytes 65568 | tf_op jit(solution)/shard_map/ppermute | solution.py:70
  13.3 1.8 %collective-permute-start.7 = (bf16[2,2,64,256]{3,2,1,0:T(8,128)(2,1)S(1)}, bf16[2,2,64,256]{3,2,1,0:T(8,128)(2,1)S(1)}, u32[]{:S(2)}, u32[]{:S(2)}) collective-permute-start(bf16[2,2,64,256]{3,2,1,0:T(8,128)(2,1)S(1)} %pad_maximum_fusion.1.refs_0_), channel_id=1, source_target_pairs={{0,16},{1,17},{2,18},{3,19},{4,20},{5,21},{6,22},{7,23},{8,24},{9,... | collective-permute-start | bytes 393224 | tf_op jit(solution)/shard_map/ppermute | solution.py:70
  15.2 1.3 %collective-permute-start.8 = (bf16[2,2,64,256]{3,2,1,0:T(8,128)(2,1)S(1)}, bf16[2,2,64,256]{3,2,1,0:T(8,128)(2,1)S(1)}, u32[]{:S(2)}, u32[]{:S(2)}) collective-permute-start(bf16[2,2,64,256]{3,2,1,0:T(8,128)(2,1)S(1)} %pad_maximum_fusion.1.refs_0_), channel_id=1, source_target_pairs={{0,24},{1,25},{2,26},{3,27},{4,28},{5,29},{6,30},{7,31},{8,16},{9,... | collective-permute-start | bytes 393224 | tf_op jit(solution)/shard_map/ppermute | solution.py:70
  17.2 2.0 %collective-permute-start.16 = (bf16[4,128,256]{2,1,0:T(8,128)(2,1)S(1)}, bf16[4,128,256]{2,1,0:T(8,128)(2,1)S(1)}, u32[]{:S(2)}, u32[]{:S(2)}) collective-permute-start(bf16[4,128,256]{2,1,0:T(8,128)(2,1)S(1)} %pad_maximum_fusion.refs_0_), channel_id=1, source_target_pairs={{0,2},{1,3},{2,0},{3,1},{4,6},{5,7},{6,4},{7,5},{8,10},{9,11},{10,... | collective-permute-start | bytes 786440 | tf_op jit(solution)/shard_map/ppermute | solution.py:70
  19.2 1.4 %collective-permute-start.17 = (bf16[4,128,256]{2,1,0:T(8,128)(2,1)S(1)}, bf16[4,128,256]{2,1,0:T(8,128)(2,1)S(1)}, u32[]{:S(2)}, u32[]{:S(2)}) collective-permute-start(bf16[4,128,256]{2,1,0:T(8,128)(2,1)S(1)} %pad_maximum_fusion.refs_0_), channel_id=1, source_target_pairs={{0,6},{1,7},{2,4},{3,5},{4,2},{5,3},{6,0},{7,1},{8,14},{9,15},{10,... | collective-permute-start | bytes 786440 | tf_op jit(solution)/shard_map/ppermute | solution.py:70
  20.6 2.8 %own.1 = (bf16[4,544,1024]{2,1,0:T(8,128)(2,1)S(1)}, bf16[4,1024,512]{2,1,0:T(8,128)(2,1)S(1)}) custom-call(s32[4,2,256]{2,1,0:T(2,128)S(1)} %copy-done.11), custom_call_target="tpu_custom_call" | custom-call | tf_op jit(solution)/shard_map/own/pallas_call | solution.py:632
  23.4 1.4 %margin.1 = (f32[544,512]{1,0:T(8,128)S(1)}, bf16[544,512]{1,0:T(8,128)(2,1)S(1)}, f32[32,512]{1,0:T(8,128)S(1)}, bf16[4,544,1024]{2,1,0:T(8,128)(2,1)S(1)}) custom-call(s32[2]{0:T(128)S(1)} %copy-done.12, bf16[2,256,512]{2,1,0:T(8,128)(2,1)S(1)} %copy-done.2, ...), custom_call_target="tpu_custom_call", output_to_operand_aliasing={{3}: (4, {})} | custom-call | tf_op jit(solution)/shard_map/margin/pallas_call | solution.py:646
  28.3 3.4 %collective-permute-done.16.refs_4_ = bf16[4,128,256]{2,1,0:T(8,128)(2,1)S(1)} collective-permute-done((bf16[4,128,256]{2,1,0:T(8,128)(2,1)S(1)}, bf16[4,128,256]{2,1,0:T(8,128)(2,1)S(1)}, u32[]{:S(2)}, u32[]{:S(2)}) %collective-permute-start.16) | collective-permute-done | bytes 262176 | tf_op jit(solution)/shard_map/ppermute | solution.py:70
  32.3 1.5 %collective-permute-done.9.refs_4_ = bf16[2,2,64,256]{3,2,1,0:T(8,128)(2,1)S(1)} collective-permute-done((bf16[2,2,64,256]{3,2,1,0:T(8,128)(2,1)S(1)}, bf16[2,2,64,256]{3,2,1,0:T(8,128)(2,1)S(1)}, u32[]{:S(2)}, u32[]{:S(2)}) %collective-permute-start.9) | collective-permute-done | bytes 131104 | tf_op jit(solution)/shard_map/ppermute | solution.py:70
  33.8 1.2 %conv.1 = (bf16[768,512]{1,0:T(8,128)(2,1)S(1)}, bf16[512,256]{1,0:T(8,128)(2,1)S(1)}, bf16[544,256]{1,0:T(8,128)(2,1)S(1)}, f32[544,256]{1,0:T(8,128)S(1)}, f32[544,512]{1,0:T(8,128)S(1)}) custom-call(f32[544,512]{1,0:T(8,128)S(1)} %get-tuple-element.95.start_ref, bf16[544,512]{1,0:T(8,128)(2,1)S(1)} %get-tuple-element.98.act_ref, ...), custom_call_target="tpu_custom_call" | custom-call | tf_op jit(solution)/shard_map/conv/pallas_call | solution.py:677
  35.1 3.8 %quant.1 = (bf16[2,256,512]{2,1,0:T(8,128)(2,1)}, f32[2,1024,256]{2,1,0:T(8,128)S(1)}, bf16[544,512]{1,0:T(8,128)(2,1)S(1)}, f32[512,512]{1,0:T(8,128)S(1)}, bf16[4,512,512]{2,1,0:T(8,128)(2,1)S(1)}) custom-call(s32[2]{0:T(128)S(1)} %copy-done.12, f32[544,512]{1,0:T(8,128)S(1)} %get-tuple-element.103.latent_ref, bf16[2,256,512]{2,1,0:T(8,128)(2,1)S(1)} %copy-done, ...), custom_call_target="tpu_custom_call" | custom-call | tf_op jit(solution)/shard_map/quant/pallas_call | solution.py:689
  39.1 3.2 %backward.1 = (f32[2,256,512]{2,1,0:T(8,128)}, f32[2,512,256]{2,1,0:T(8,128)S(1)}, f32[2,512,256]{2,1,0:T(8,128)S(1)}) custom-call(s32[2]{0:T(128)S(1)} %copy-done.12, f32[544,512]{1,0:T(8,128)S(1)} %get-tuple-element.95.start_ref, bf16[544,512]{1,0:T(8,128)(2,1)S(1)} %get-tuple-element.98.act_ref, bf16[544,256]{1,0:T(8,128)(2,1)S(1)} %get-tuple-element.109.gated_ref, ...), custom_call_target="tpu_custom_call" | custom-call | tf_op jit(solution)/shard_map/backward/pallas_call | solution.py:720
  42.7 1.2 %keep.1.keep_ref = f32[2,1024,256]{2,1,0:T(8,128)S(1)} custom-call(bf16[4,1024,512]{2,1,0:T(8,128)(2,1)S(1)} %get-tuple-element.106.hott_ref, bf16[4,512,512]{2,1,0:T(8,128)(2,1)S(1)} %get-tuple-element.116.cgs_ref), custom_call_target="tpu_custom_call" | custom-call | tf_op jit(solution)/shard_map/keep/pallas_call | solution.py:707
  44.5 1.6 %collective-permute-start.21 = (s16[528,256]{1,0:T(8,128)(2,1)S(1)}, s16[528,256]{1,0:T(8,128)(2,1)S(1)}, u32[]{:S(2)}, u32[]{:S(2)}) collective-permute-start(s16[528,256]{1,0:T(8,128)(2,1)S(1)} %get-tuple-element.121), channel_id=1, source_target_pairs={{0,4},{1,5},{2,6},{3,7},{4,0},{5,1},{6,2},{7,3},{8,12},{9,13},{10,... | collective-permute-start | bytes 811016 | tf_op jit(solution)/shard_map/ppermute | solution.py:70
  46.0 2.0 %collective-permute-start.23 = (s16[528,256]{1,0:T(8,128)(2,1)S(1)}, s16[528,256]{1,0:T(8,128)(2,1)S(1)}, u32[]{:S(2)}, u32[]{:S(2)}) collective-permute-start(s16[528,256]{1,0:T(8,128)(2,1)S(1)} %get-tuple-element.123), channel_id=1, source_target_pairs={{0,6},{1,7},{2,4},{3,5},{4,2},{5,3},{6,0},{7,1},{8,14},{9,15},{10,... | collective-permute-start | bytes 811016 | tf_op jit(solution)/shard_map/ppermute | solution.py:70
  49.3 3.5 %collective-permute-start.27 = (s16[272,256]{1,0:T(8,128)(2,1)S(1)}, s16[272,256]{1,0:T(8,128)(2,1)S(1)}, u32[]{:S(2)}, u32[]{:S(2)}) collective-permute-start(s16[272,256]{1,0:T(8,128)(2,1)S(1)} %get-tuple-element.130), channel_id=1, source_target_pairs={{0,16},{1,17},{2,18},{3,19},{4,20},{5,21},{6,22},{7,23},{8,24},{9,... | collective-permute-start | bytes 417800 | tf_op jit(solution)/shard_map/ppermute | solution.py:70
  52.8 1.1 %collective-permute-done.21.refs_0_ = s16[528,256]{1,0:T(8,128)(2,1)S(1)} collective-permute-done((s16[528,256]{1,0:T(8,128)(2,1)S(1)}, s16[528,256]{1,0:T(8,128)(2,1)S(1)}, u32[]{:S(2)}, u32[]{:S(2)}) %collective-permute-start.21) | collective-permute-done | bytes 270368 | tf_op jit(solution)/shard_map/ppermute | solution.py:70
  53.9 3.5 %collective-permute-start.28 = (s16[272,256]{1,0:T(8,128)(2,1)S(1)}, s16[272,256]{1,0:T(8,128)(2,1)S(1)}, u32[]{:S(2)}, u32[]{:S(2)}) collective-permute-start(s16[272,256]{1,0:T(8,128)(2,1)S(1)} %get-tuple-element.131), channel_id=1, source_target_pairs={{0,24},{1,25},{2,26},{3,27},{4,28},{5,29},{6,30},{7,31},{8,16},{9,... | collective-permute-start | bytes 417800 | tf_op jit(solution)/shard_map/ppermute | solution.py:70
  57.4 2.7 %collective-permute-done.22.refs_1_ = s16[528,256]{1,0:T(8,128)(2,1)S(1)} collective-permute-done((s16[528,256]{1,0:T(8,128)(2,1)S(1)}, s16[528,256]{1,0:T(8,128)(2,1)S(1)}, u32[]{:S(2)}, u32[]{:S(2)}) %collective-permute-start.22) | collective-permute-done | bytes 270368 | tf_op jit(solution)/shard_map/ppermute | solution.py:70
  61.1 3.5 %collective-permute-start.32 = (s16[144,256]{1,0:T(8,128)(2,1)S(1)}, s16[144,256]{1,0:T(8,128)(2,1)S(1)}, u32[]{:S(2)}, u32[]{:S(2)}) collective-permute-start(s16[144,256]{1,0:T(8,128)(2,1)S(1)} %get-tuple-element.138), channel_id=1, source_target_pairs={{0,16},{1,17},{2,18},{3,19},{4,20},{5,21},{6,22},{7,23},{8,24},{9,... | collective-permute-start | bytes 221192 | tf_op jit(solution)/shard_map/ppermute | solution.py:70
  65.1 3.4 %collective-permute-start.33 = (s16[144,256]{1,0:T(8,128)(2,1)S(1)}, s16[144,256]{1,0:T(8,128)(2,1)S(1)}, u32[]{:S(2)}, u32[]{:S(2)}) collective-permute-start(s16[144,256]{1,0:T(8,128)(2,1)S(1)} %get-tuple-element.139), channel_id=1, source_target_pairs={{0,24},{1,25},{2,26},{3,27},{4,28},{5,29},{6,30},{7,31},{8,16},{9,... | collective-permute-start | bytes 221192 | tf_op jit(solution)/shard_map/ppermute | solution.py:70
  69.2 1.5 %collective-permute-start.30 = (s16[80,256]{1,0:T(8,128)(2,1)S(1)}, s16[80,256]{1,0:T(8,128)(2,1)S(1)}, u32[]{:S(2)}, u32[]{:S(2)}) collective-permute-start(s16[80,256]{1,0:T(8,128)(2,1)S(1)} %get-tuple-element.134), channel_id=1, source_target_pairs={{0,2},{1,3},{2,0},{3,1},{4,6},{5,7},{6,4},{7,5},{8,10},{9,11},{10,... | collective-permute-start | bytes 122888 | tf_op jit(solution)/shard_map/ppermute | solution.py:70
  70.8 1.6 %collective-permute-start.31 = (s16[80,256]{1,0:T(8,128)(2,1)S(1)}, s16[80,256]{1,0:T(8,128)(2,1)S(1)}, u32[]{:S(2)}, u32[]{:S(2)}) collective-permute-start(s16[80,256]{1,0:T(8,128)(2,1)S(1)} %get-tuple-element.135), channel_id=1, source_target_pairs={{0,6},{1,7},{2,4},{3,5},{4,2},{5,3},{6,0},{7,1},{8,14},{9,15},{10,... | collective-permute-start | bytes 122888 | tf_op jit(solution)/shard_map/ppermute | solution.py:70
  73.2 2.6 %collective-permute-done.31.refs_3_ = s16[80,256]{1,0:T(8,128)(2,1)S(1)} collective-permute-done((s16[80,256]{1,0:T(8,128)(2,1)S(1)}, s16[80,256]{1,0:T(8,128)(2,1)S(1)}, u32[]{:S(2)}, u32[]{:S(2)}) %collective-permute-start.31) | collective-permute-done | bytes 40992 | tf_op jit(solution)/shard_map/ppermute | solution.py:70
  77.0 2.6 %all-to-all-start = ((f32[32,8,128]{2,1,0:T(8,128)}), f32[32,8,128]{2,1,0:T(8,128)S(1)}, u32[]{:S(2)}, u32[]{:S(2)}) async-start(f32[32,8,128]{2,1,0:T(8,128)} %get-tuple-element.140), calls=%async_computation | async-start | bytes 262144 | tf_op jit(solution)/shard_map/all_to_all | solution.py:798
  79.8 2.5 %collective-permute-done.35.refs_2_ = f32[192,256]{1,0:T(8,128)S(1)} collective-permute-done((f32[192,256]{1,0:T(8,128)S(1)}, f32[192,256]{1,0:T(8,128)S(1)}, u32[]{:S(2)}, u32[]{:S(2)}) %collective-permute-start.35) | collective-permute-done | bytes 196640 | tf_op jit(solution)/shard_map/ppermute | solution.py:70
  83.2 4.6 %all-to-all-done.square_ref = f32[32,8,128]{2,1,0:T(8,128)S(1)} async-done(((f32[32,8,128]{2,1,0:T(8,128)}), f32[32,8,128]{2,1,0:T(8,128)S(1)}, u32[]{:S(2)}, u32[]{:S(2)}) %all-to-all-start) | async-done | bytes 131104 | tf_op jit(solution)/shard_map/all_to_all | solution.py:798
  87.9 3.0 %update.1 = (f32[1,1]{1,0:T(1,128)}, f32[3,32,512]{2,1,0:T(8,128)}, f32[3,32,512]{2,1,0:T(8,128)}, f32[3,32,512]{2,1,0:T(8,128)}, f32[64,256]{1,0:T(8,128)}, /*i...) custom-call(f32[2]{0:T(128)S(1)} %pad_maximum_fusion.2.fix_ref, ...), custom_call_target="tpu_custom_call" | custom-call | tf_op jit(solution)/shard_map/update/pallas_call | solution.py:804
  (87 shorter events, 14.4 us)
Async XLA Ops:
  1.8 8.5 %collective-permute-start.5 = (bf16[2,64,256]{2,1,0:T(8,128)(2,1)S(1)}, bf16[2,64,256]{2,1,0:T(8,128)(2,1)S(1)}, u32[]{:S(2)}, u32[]{:S(2)}) collective-permute-start(bf16[2,64,256]{2,1,0:T(8,128)(2,1)S(1)} %get-tuple-element.97), channel_id=1, source_target_pairs={{0,4},{1,5},{2,6},{3,7},{4,0},{5,1},{6,2},{7,3},{8,12},{9,13},{10,... | collective-permute-start | bytes 196616 | tf_op jit(solution)/shard_map/ppermute | solution.py:70
  4.8 6.2 %collective-permute-start.2 = (bf16[128,256]{1,0:T(8,128)(2,1)S(1)}, bf16[128,256]{1,0:T(8,128)(2,1)S(1)}, u32[]{:S(2)}, u32[]{:S(2)}) collective-permute-start(bf16[128,256]{1,0:T(8,128)(2,1)S(1)} %get-tuple-element.87), channel_id=1, source_target_pairs={{0,8},{1,9},{2,10},{3,11},{4,12},{5,13},{6,14},{7,15},{8,0},{9,1},... | collective-permute-start | bytes 196616 | tf_op jit(solution)/shard_map/ppermute | solution.py:70
  6.3 7.0 %collective-permute-start.3 = (bf16[128,256]{1,0:T(8,128)(2,1)S(1)}, bf16[128,256]{1,0:T(8,128)(2,1)S(1)}, u32[]{:S(2)}, u32[]{:S(2)}) collective-permute-start(bf16[128,256]{1,0:T(8,128)(2,1)S(1)} %get-tuple-element.87), channel_id=1, source_target_pairs={{0,16},{1,17},{2,18},{3,19},{4,20},{5,21},{6,22},{7,23},{8,24},{9,... | collective-permute-start | bytes 196616 | tf_op jit(solution)/shard_map/ppermute | solution.py:70
  8.9 6.2 %collective-permute-start.4 = (bf16[128,256]{1,0:T(8,128)(2,1)S(1)}, bf16[128,256]{1,0:T(8,128)(2,1)S(1)}, u32[]{:S(2)}, u32[]{:S(2)}) collective-permute-start(bf16[128,256]{1,0:T(8,128)(2,1)S(1)} %get-tuple-element.87), channel_id=1, source_target_pairs={{0,24},{1,25},{2,26},{3,27},{4,28},{5,29},{6,30},{7,31},{8,16},{9,... | collective-permute-start | bytes 196616 | tf_op jit(solution)/shard_map/ppermute | solution.py:70
  10.1 6.4 %collective-permute-start = (bf16[2,16,1024]{2,1,0:T(8,128)(2,1)S(1)}, bf16[2,16,1024]{2,1,0:T(8,128)(2,1)S(1)}, u32[]{:S(2)}, u32[]{:S(2)}) collective-permute-start(bf16[2,16,1024]{2,1,0:T(8,128)(2,1)S(1)} %get-tuple-element.85), channel_id=1, source_target_pairs={{0,1},{1,0},{2,3},{3,2},{4,5},{5,4},{6,7},{7,6},{8,9},{9,8},{10,11... | collective-permute-start | bytes 196616 | tf_op jit(solution)/shard_map/ppermute | solution.py:625
  10.2 6.3 %collective-permute-start.1 = (bf16[2,16,1024]{2,1,0:T(8,128)(2,1)S(1)}, bf16[2,16,1024]{2,1,0:T(8,128)(2,1)S(1)}, u32[]{:S(2)}, u32[]{:S(2)}) collective-permute-start(bf16[2,16,1024]{2,1,0:T(8,128)(2,1)S(1)} %get-tuple-element.86), channel_id=1, source_target_pairs={{1,2},{2,1},{5,6},{6,5},{9,10},{10,9},{13,14},{14,13},{17,18},{18,... | collective-permute-start | bytes 196616 | tf_op jit(solution)/shard_map/ppermute | solution.py:627
  10.9 8.3 %collective-permute-start.6 = (bf16[2,2,64,256]{3,2,1,0:T(8,128)(2,1)S(1)}, bf16[2,2,64,256]{3,2,1,0:T(8,128)(2,1)S(1)}, u32[]{:S(2)}, u32[]{:S(2)}) collective-permute-start(bf16[2,2,64,256]{3,2,1,0:T(8,128)(2,1)S(1)} %pad_maximum_fusion.1.refs_0_), channel_id=1, source_target_pairs={{0,8},{1,9},{2,10},{3,11},{4,12},{5,13},{6,14},{7,15},{8,0},{9,1},... | collective-permute-start | bytes 393224 | tf_op jit(solution)/shard_map/ppermute | solution.py:70
  13.3 12.5 %collective-permute-start.7 = (bf16[2,2,64,256]{3,2,1,0:T(8,128)(2,1)S(1)}, bf16[2,2,64,256]{3,2,1,0:T(8,128)(2,1)S(1)}, u32[]{:S(2)}, u32[]{:S(2)}) collective-permute-start(bf16[2,2,64,256]{3,2,1,0:T(8,128)(2,1)S(1)} %pad_maximum_fusion.1.refs_0_), channel_id=1, source_target_pairs={{0,16},{1,17},{2,18},{3,19},{4,20},{5,21},{6,22},{7,23},{8,24},{9,... | collective-permute-start | bytes 393224 | tf_op jit(solution)/shard_map/ppermute | solution.py:70
  15.2 10.7 %collective-permute-start.8 = (bf16[2,2,64,256]{3,2,1,0:T(8,128)(2,1)S(1)}, bf16[2,2,64,256]{3,2,1,0:T(8,128)(2,1)S(1)}, u32[]{:S(2)}, u32[]{:S(2)}) collective-permute-start(bf16[2,2,64,256]{3,2,1,0:T(8,128)(2,1)S(1)} %pad_maximum_fusion.1.refs_0_), channel_id=1, source_target_pairs={{0,24},{1,25},{2,26},{3,27},{4,28},{5,29},{6,30},{7,31},{8,16},{9,... | collective-permute-start | bytes 393224 | tf_op jit(solution)/shard_map/ppermute | solution.py:70
  16.6 11.4 %collective-permute-start.13 = (bf16[4,128,256]{2,1,0:T(8,128)(2,1)S(1)}, bf16[4,128,256]{2,1,0:T(8,128)(2,1)S(1)}, u32[]{:S(2)}, u32[]{:S(2)}) collective-permute-start(bf16[4,128,256]{2,1,0:T(8,128)(2,1)S(1)} %pad_maximum_fusion.refs_0_), channel_id=1, source_target_pairs={{0,4},{1,5},{2,6},{3,7},{4,0},{5,1},{6,2},{7,3},{8,12},{9,13},{10,... | collective-permute-start | bytes 786440 | tf_op jit(solution)/shard_map/ppermute | solution.py:70
  17.2 14.5 %collective-permute-start.16 = (bf16[4,128,256]{2,1,0:T(8,128)(2,1)S(1)}, bf16[4,128,256]{2,1,0:T(8,128)(2,1)S(1)}, u32[]{:S(2)}, u32[]{:S(2)}) collective-permute-start(bf16[4,128,256]{2,1,0:T(8,128)(2,1)S(1)} %pad_maximum_fusion.refs_0_), channel_id=1, source_target_pairs={{0,2},{1,3},{2,0},{3,1},{4,6},{5,7},{6,4},{7,5},{8,10},{9,11},{10,... | collective-permute-start | bytes 786440 | tf_op jit(solution)/shard_map/ppermute | solution.py:70
  19.2 12.5 %collective-permute-start.17 = (bf16[4,128,256]{2,1,0:T(8,128)(2,1)S(1)}, bf16[4,128,256]{2,1,0:T(8,128)(2,1)S(1)}, u32[]{:S(2)}, u32[]{:S(2)}) collective-permute-start(bf16[4,128,256]{2,1,0:T(8,128)(2,1)S(1)} %pad_maximum_fusion.refs_0_), channel_id=1, source_target_pairs={{0,6},{1,7},{2,4},{3,5},{4,2},{5,3},{6,0},{7,1},{8,14},{9,15},{10,... | collective-permute-start | bytes 786440 | tf_op jit(solution)/shard_map/ppermute | solution.py:70
  27.4 4.8 %collective-permute-start.12 = (bf16[2,2,64,256]{3,2,1,0:T(8,128)(2,1)S(1)}, bf16[2,2,64,256]{3,2,1,0:T(8,128)(2,1)S(1)}, u32[]{:S(2)}, u32[]{:S(2)}) collective-permute-start(bf16[2,2,64,256]{3,2,1,0:T(8,128)(2,1)S(1)} %collective-permute-done.8.refs_3_), channel_id=1, source_target_pairs={{0,1},{1,0},{2,3},{3,2},{4,5},{5,4},{6,7},{7,6},{8,9},{9,8},{10,11... | collective-permute-start | bytes 393224 | tf_op jit(solution)/shard_map/ppermute | solution.py:70
  27.8 7.3 %collective-permute-start.14 = (bf16[4,128,256]{2,1,0:T(8,128)(2,1)S(1)}, bf16[4,128,256]{2,1,0:T(8,128)(2,1)S(1)}, u32[]{:S(2)}, u32[]{:S(2)}) collective-permute-start(bf16[4,128,256]{2,1,0:T(8,128)(2,1)S(1)} %pad_maximum_fusion.refs_0_), channel_id=1, source_target_pairs={{0,1},{1,0},{2,3},{3,2},{4,5},{5,4},{6,7},{7,6},{8,9},{9,8},{10,11... | collective-permute-start | bytes 786440 | tf_op jit(solution)/shard_map/ppermute | solution.py:70
  27.9 7.1 %collective-permute-start.15 = (bf16[4,128,256]{2,1,0:T(8,128)(2,1)S(1)}, bf16[4,128,256]{2,1,0:T(8,128)(2,1)S(1)}, u32[]{:S(2)}, u32[]{:S(2)}) collective-permute-start(bf16[4,128,256]{2,1,0:T(8,128)(2,1)S(1)} %collective-permute-done.13.refs_1_), channel_id=1, source_target_pairs={{0,1},{1,0},{2,3},{3,2},{4,5},{5,4},{6,7},{7,6},{8,9},{9,8},{10,11... | collective-permute-start | bytes 786440 | tf_op jit(solution)/shard_map/ppermute | solution.py:70
  38.9 5.0 %collective-permute-start.20 = (f32[2,1024,256]{2,1,0:T(8,128)S(1)}, f32[2,1024,256]{2,1,0:T(8,128)S(1)}, u32[]{:S(2)}, u32[]{:S(2)}) collective-permute-start(f32[2,1024,256]{2,1,0:T(8,128)S(1)} %get-tuple-element.117), channel_id=1, source_target_pairs={{0,1},{1,0},{2,3},{3,2},{4,5},{5,4},{6,7},{7,6},{8,9},{9,8},{10,11... | collective-permute-start | bytes 6291464 | tf_op jit(solution)/shard_map/ppermute | solution.py:70
  42.3 5.8 %collective-permute-start.25 = (f32[2,512,256]{2,1,0:T(8,128)S(1)}, f32[2,512,256]{2,1,0:T(8,128)S(1)}, u32[]{:S(2)}, u32[]{:S(2)}) collective-permute-start(f32[2,512,256]{2,1,0:T(8,128)S(1)} %get-tuple-element.126), channel_id=1, source_target_pairs={{0,1},{1,0},{2,3},{3,2},{4,5},{5,4},{6,7},{7,6},{8,9},{9,8},{10,11... | collective-permute-start | bytes 3145736 | tf_op jit(solution)/shard_map/ppermute | solution.py:70
  44.5 9.4 %collective-permute-start.21 = (s16[528,256]{1,0:T(8,128)(2,1)S(1)}, s16[528,256]{1,0:T(8,128)(2,1)S(1)}, u32[]{:S(2)}, u32[]{:S(2)}) collective-permute-start(s16[528,256]{1,0:T(8,128)(2,1)S(1)} %get-tuple-element.121), channel_id=1, source_target_pairs={{0,4},{1,5},{2,6},{3,7},{4,0},{5,1},{6,2},{7,3},{8,12},{9,13},{10,... | collective-permute-start | bytes 811016 | tf_op jit(solution)/shard_map/ppermute | solution.py:70
  46.0 14.0 %collective-permute-start.22 = (s16[528,256]{1,0:T(8,128)(2,1)S(1)}, s16[528,256]{1,0:T(8,128)(2,1)S(1)}, u32[]{:S(2)}, u32[]{:S(2)}) collective-permute-start(s16[528,256]{1,0:T(8,128)(2,1)S(1)} %get-tuple-element.122), channel_id=1, source_target_pairs={{0,2},{1,3},{2,0},{3,1},{4,6},{5,7},{6,4},{7,5},{8,10},{9,11},{10,... | collective-permute-start | bytes 811016 | tf_op jit(solution)/shard_map/ppermute | solution.py:70
  46.0 14.0 %collective-permute-start.23 = (s16[528,256]{1,0:T(8,128)(2,1)S(1)}, s16[528,256]{1,0:T(8,128)(2,1)S(1)}, u32[]{:S(2)}, u32[]{:S(2)}) collective-permute-start(s16[528,256]{1,0:T(8,128)(2,1)S(1)} %get-tuple-element.123), channel_id=1, source_target_pairs={{0,6},{1,7},{2,4},{3,5},{4,2},{5,3},{6,0},{7,1},{8,14},{9,15},{10,... | collective-permute-start | bytes 811016 | tf_op jit(solution)/shard_map/ppermute | solution.py:70
  48.5 20.1 %collective-permute-start.26 = (s16[272,256]{1,0:T(8,128)(2,1)S(1)}, s16[272,256]{1,0:T(8,128)(2,1)S(1)}, u32[]{:S(2)}, u32[]{:S(2)}) collective-permute-start(s16[272,256]{1,0:T(8,128)(2,1)S(1)} %get-tuple-element.129), channel_id=1, source_target_pairs={{0,8},{1,9},{2,10},{3,11},{4,12},{5,13},{6,14},{7,15},{8,0},{9,1},... | collective-permute-start | bytes 417800 | tf_op jit(solution)/shard_map/ppermute | solution.py:70
  49.3 19.2 %collective-permute-start.27 = (s16[272,256]{1,0:T(8,128)(2,1)S(1)}, s16[272,256]{1,0:T(8,128)(2,1)S(1)}, u32[]{:S(2)}, u32[]{:S(2)}) collective-permute-start(s16[272,256]{1,0:T(8,128)(2,1)S(1)} %get-tuple-element.130), channel_id=1, source_target_pairs={{0,16},{1,17},{2,18},{3,19},{4,20},{5,21},{6,22},{7,23},{8,24},{9,... | collective-permute-start | bytes 417800 | tf_op jit(solution)/shard_map/ppermute | solution.py:70
  53.9 14.7 %collective-permute-start.28 = (s16[272,256]{1,0:T(8,128)(2,1)S(1)}, s16[272,256]{1,0:T(8,128)(2,1)S(1)}, u32[]{:S(2)}, u32[]{:S(2)}) collective-permute-start(s16[272,256]{1,0:T(8,128)(2,1)S(1)} %get-tuple-element.131), channel_id=1, source_target_pairs={{0,24},{1,25},{2,26},{3,27},{4,28},{5,29},{6,30},{7,31},{8,16},{9,... | collective-permute-start | bytes 417800 | tf_op jit(solution)/shard_map/ppermute | solution.py:70
  60.4 4.7 %collective-permute-start.24 = (s16[144,256]{1,0:T(8,128)(2,1)S(1)}, s16[144,256]{1,0:T(8,128)(2,1)S(1)}, u32[]{:S(2)}, u32[]{:S(2)}) collective-permute-start(s16[144,256]{1,0:T(8,128)(2,1)S(1)} %get-tuple-element.124), channel_id=1, source_target_pairs={{0,8},{1,9},{2,10},{3,11},{4,12},{5,13},{6,14},{7,15},{8,0},{9,1},... | collective-permute-start | bytes 221192 | tf_op jit(solution)/shard_map/ppermute | solution.py:70
  61.1 11.2 %collective-permute-start.32 = (s16[144,256]{1,0:T(8,128)(2,1)S(1)}, s16[144,256]{1,0:T(8,128)(2,1)S(1)}, u32[]{:S(2)}, u32[]{:S(2)}) collective-permute-start(s16[144,256]{1,0:T(8,128)(2,1)S(1)} %get-tuple-element.138), channel_id=1, source_target_pairs={{0,16},{1,17},{2,18},{3,19},{4,20},{5,21},{6,22},{7,23},{8,24},{9,... | collective-permute-start | bytes 221192 | tf_op jit(solution)/shard_map/ppermute | solution.py:70
  65.1 7.2 %collective-permute-start.33 = (s16[144,256]{1,0:T(8,128)(2,1)S(1)}, s16[144,256]{1,0:T(8,128)(2,1)S(1)}, u32[]{:S(2)}, u32[]{:S(2)}) collective-permute-start(s16[144,256]{1,0:T(8,128)(2,1)S(1)} %get-tuple-element.139), channel_id=1, source_target_pairs={{0,24},{1,25},{2,26},{3,27},{4,28},{5,29},{6,30},{7,31},{8,16},{9,... | collective-permute-start | bytes 221192 | tf_op jit(solution)/shard_map/ppermute | solution.py:70
  68.8 4.1 %collective-permute-start.29 = (s16[80,256]{1,0:T(8,128)(2,1)S(1)}, s16[80,256]{1,0:T(8,128)(2,1)S(1)}, u32[]{:S(2)}, u32[]{:S(2)}) collective-permute-start(s16[80,256]{1,0:T(8,128)(2,1)S(1)} %get-tuple-element.133), channel_id=1, source_target_pairs={{0,4},{1,5},{2,6},{3,7},{4,0},{5,1},{6,2},{7,3},{8,12},{9,13},{10,... | collective-permute-start | bytes 122888 | tf_op jit(solution)/shard_map/ppermute | solution.py:70
  69.2 4.0 %collective-permute-start.30 = (s16[80,256]{1,0:T(8,128)(2,1)S(1)}, s16[80,256]{1,0:T(8,128)(2,1)S(1)}, u32[]{:S(2)}, u32[]{:S(2)}) collective-permute-start(s16[80,256]{1,0:T(8,128)(2,1)S(1)} %get-tuple-element.134), channel_id=1, source_target_pairs={{0,2},{1,3},{2,0},{3,1},{4,6},{5,7},{6,4},{7,5},{8,10},{9,11},{10,... | collective-permute-start | bytes 122888 | tf_op jit(solution)/shard_map/ppermute | solution.py:70
  70.8 5.0 %collective-permute-start.31 = (s16[80,256]{1,0:T(8,128)(2,1)S(1)}, s16[80,256]{1,0:T(8,128)(2,1)S(1)}, u32[]{:S(2)}, u32[]{:S(2)}) collective-permute-start(s16[80,256]{1,0:T(8,128)(2,1)S(1)} %get-tuple-element.135), channel_id=1, source_target_pairs={{0,6},{1,7},{2,4},{3,5},{4,2},{5,3},{6,0},{7,1},{8,14},{9,15},{10,... | collective-permute-start | bytes 122888 | tf_op jit(solution)/shard_map/ppermute | solution.py:70
  76.7 5.7 %collective-permute-start.35 = (f32[192,256]{1,0:T(8,128)S(1)}, f32[192,256]{1,0:T(8,128)S(1)}, u32[]{:S(2)}, u32[]{:S(2)}) collective-permute-start(f32[192,256]{1,0:T(8,128)S(1)} %get-tuple-element.141.refs_0_), channel_id=1, source_target_pairs={{0,2},{1,3},{2,0},{3,1},{4,6},{5,7},{6,4},{7,5},{8,10},{9,11},{10,... | collective-permute-start | bytes 589832 | tf_op jit(solution)/shard_map/ppermute | solution.py:70
  77.0 10.8 %all-to-all-start = ((f32[32,8,128]{2,1,0:T(8,128)}), f32[32,8,128]{2,1,0:T(8,128)S(1)}, u32[]{:S(2)}, u32[]{:S(2)}) async-start(f32[32,8,128]{2,1,0:T(8,128)} %get-tuple-element.140), calls=%async_computation | async-start | bytes 262144 | tf_op jit(solution)/shard_map/all_to_all | solution.py:798
  82.3 5.5 %collective-permute-start.36 = (f32[192,256]{1,0:T(8,128)S(1)}, f32[192,256]{1,0:T(8,128)S(1)}, u32[]{:S(2)}, u32[]{:S(2)}) collective-permute-start(f32[192,256]{1,0:T(8,128)S(1)} %collective-permute-done.35.refs_2_), channel_id=1, source_target_pairs={{0,1},{1,0},{2,3},{3,2},{4,5},{5,4},{6,7},{7,6},{8,9},{9,8},{10,11... | collective-permute-start | bytes 589832 | tf_op jit(solution)/shard_map/ppermute | solution.py:70
  (19 other events, 449.0 us)

commit v5 on v4

--- a/solution.py
+++ b/solution.py
@@ -183,7 +183,30 @@
     hot_ref[:, clips * frames :, :] = jnp.zeros((SLOTS, 2 * PAD * clips, CODES), BF16)
 
 
-def margin_kernel(ranks, len_ref, f_ref, near_ref, far_ref, old_ref, start_ref, act_ref, cot_ref, hot_ref):
+def moved(value, shift, clips, frames):
+    span = frames + 2 * PAD
+    return jnp.concatenate(
+        [
+            pltpu.roll(widened(value, c, clips, frames), shift % span, 0)[PAD : PAD + frames]
+            for c in range(clips)
+        ],
+        axis=0,
+    ).astype(BF16)
+
+
+def margin_kernel(
+    ranks,
+    len_ref,
+    f_ref,
+    near_ref,
+    far_ref,
+    old_ref,
+    start_ref,
+    act_ref,
+    window_ref,
+    cot_ref,
+    hot_ref,
+):
     del old_ref
     clips, frames, _ = f_ref.shape
     odd = lax.axis_index("tm") % 2
@@ -195,7 +218,14 @@
         [f_ref[c].astype(F32) for c in range(clips)] + [part[:PAD, :D] for part in both], axis=0
     )
     start_ref[...] = start
-    act_ref[...] = elu(start).astype(BF16)
+    act = elu(start).astype(BF16)
+    act_ref[...] = act
+    wide = act.astype(F32)
+    for tap in range(KERNEL):
+        shift = (1 - tap) * DILATION
+        window_ref[:, tap * D : (tap + 1) * D] = (
+            moved(wide, shift, clips, frames) if shift else act[: clips * frames]
+        )
     cot_ref[...] = jnp.concatenate([part[:PAD, D:] for part in both], axis=0)
     turned = jnp.concatenate([part[PAD:, :128].T[:PAD] for part in both], axis=0)
     ids = renamed((turned[:, :SLOTS] * 32.0 + turned[:, SLOTS : 2 * SLOTS]).astype(jnp.int32), ranks)
@@ -268,7 +298,7 @@
     time = lax.axis_index("tm")
     mask = masks(clips, frames, len_ref, DG)
     local = clips * frames
-    twice = 2.0 * mask[:local]
+    twice = -2.0 * mask[:local]
     for other in range(SLOTS):
         slot = time ^ other
         for x in range(2):
@@ -285,69 +315,62 @@
         residual = latent_ref[:, at]
         gap = residual - first
         gap2 = gap - second
-        grad = mask * (cot + 2.0 * COMMIT * (gap + gap2))
+        both = gap + gap2
+        grad = mask * (cot + (both if COMMIT == 0.5 else 2.0 * COMMIT * both))
         quant = (mask * (first + second))[:local].astype(BF16)
         bg_ref[:, at] = grad.astype(BF16)
         lg_ref[:, at] = grad[:local]
         for clip in range(clips):
             quant_ref[clip, :, at] = quant[clip * frames : (clip + 1) * frames]
         for level, diff in ((0, gap), (1, gap2)):
-            code_grad = -(twice * diff[:local])
+            code_grad = twice * diff[:local]
             high = code_grad.astype(BF16)
             cgs_ref[2 * group + level, :, :DG] = high
             cgs_ref[2 * group + level, :, DG:] = (code_grad - high.astype(F32)).astype(BF16)
-    scattered(1, hott_ref, cgs_ref, send_ref)
-
-
-def scattered(bit, hott_ref, cgs_ref, out_ref):
-    time = lax.axis_index("tm")
+    size = block // SCALE_GROUPS
     for far in range(2):
-        slot = time ^ (2 * far + bit)
-        pair = mm(hott_ref[slot], cgs_ref[slot])
-        out_ref[far] = pair[:, :DG] + pair[:, DG:]
+        total = summed(2 * far + 1, hott_ref, cgs_ref)
+        levels = []
+        for place in range(ranks):
+            steps, more = pack_part(total[place * block : (place + 1) * block])
+            for group, step in enumerate(steps):
+                at = place * block + group * size
+                send_ref[far, at : at + size, :] = step.astype(jnp.int16)
+            levels += more
+        levels = jnp.concatenate(levels, axis=0).astype(jnp.int32)
+        send_ref[far, CODES:, :] = levels.astype(jnp.int16)
+
+
+def summed(other, hott_ref, cgs_ref):
+    slot = lax.axis_index("tm") ^ other
+    pair = mm(hott_ref[slot], cgs_ref[slot])
+    return pair[:, :DG] + pair[:, DG:]
 
 
 def keep_kernel(hott_ref, cgs_ref, keep_ref):
-    scattered(0, hott_ref, cgs_ref, keep_ref)
+    for far in range(2):
+        keep_ref[far] = summed(2 * far, hott_ref, cgs_ref)
 
 
 def backward_kernel(
     ranks,
     assemble,
     clips,
-    len_ref,
-    start_ref,
-    act_ref,
+    window_ref,
     gated_ref,
     bg_ref,
-    lg_ref,
     hs_ref,
-    d_ref,
     pwt_ref,
-    fg_ref,
+    hg_ref,
     *outs,
 ):
-    rows = start_ref.shape[0]
-    span = rows // clips
-    frames = span - 2 * PAD
-    local = clips * frames
+    local = window_ref.shape[0]
     bg = bg_ref[...]
     hidden_grad = (mm(bg, pwt_ref[...]) * hs_ref[...]).astype(BF16)
-    mine = hidden_grad[:local]
+    hg_ref[...] = hidden_grad
+    dil_all = mmg(hidden_grad[:local], window_ref[...], TN)
+    dil_grads = [dil_all[:, tap * D : (tap + 1) * D] for tap in range(KERNEL)]
     pw_grad = mmg(bg[:local], gated_ref[:local, :], TN)
-
-    def moved(value, shift):
-        return jnp.concatenate(
-            [
-                pltpu.roll(widened(value, c, clips, frames), shift % span, 0)[PAD : PAD + frames]
-                for c in range(clips)
-            ],
-            axis=0,
-        ).astype(BF16)
-
-    act = act_ref[...].astype(F32)
-    windows = [moved(act, DILATION), act_ref[:local, :], moved(act, -DILATION)]
-    dil_grads = [mmg(mine, windows[tap], TN) for tap in range(KERNEL)]
     if assemble:
         keep_ref, send_ref, all_ref = outs
         half, small = ranks // 2, 2 * HID // ranks
@@ -378,15 +401,26 @@
         for tap in range(KERNEL):
             dil_ref[tap] = dil_grads[tap]
         pw_ref[...] = pw_grad
-    wide = hidden_grad.astype(F32)
-    shifted = jnp.concatenate([moved(wide, -DILATION), mine, moved(wide, DILATION)], axis=1)
+
+
+def features_kernel(clips, len_ref, start_ref, lg_ref, hg_ref, d_ref, fg_ref):
+    frames = start_ref.shape[0] // clips - 2 * PAD
+    local = clips * frames
+    wide = hg_ref[...].astype(F32)
+    shifted = jnp.concatenate(
+        [
+            moved(wide, -DILATION, clips, frames),
+            hg_ref[:local, :],
+            moved(wide, DILATION, clips, frames),
+        ],
+        axis=1,
+    )
     act_grad = mm(shifted, d_ref[...])
     row = lax.broadcasted_iota(jnp.int32, (frames, D), 0) + lax.axis_index("tm") * frames
     for c in range(clips):
         to = slice(c * frames, (c + 1) * frames)
         mask = jnp.where(row < len_ref[c], 1.0, 0.0)
-        start = start_ref[to, :]
-        fg_ref[c] = mask * (lg_ref[to, :] + slope(start) * act_grad[to])
+        fg_ref[c] = mask * (lg_ref[to, :] + slope(start_ref[to, :]) * act_grad[to])
 
 
 def pack_part(value):
@@ -416,7 +450,21 @@
         levels = []
         for place, (jy, start) in enumerate(blocks):
             at = slice(start * rows, (start + 1) * rows)
-            value = keep_ref[jy, at, :] + got_ref[jy, at, :]
+            if got_ref.dtype == F32:
+                other = got_ref[jy, at, :]
+            else:
+                top = (got_ref.shape[1] // (rows + SCALE_GROUPS)) * rows + start * SCALE_GROUPS
+                other = jnp.concatenate(
+                    [
+                        unpack_part(
+                            got_ref[jy, start * rows + g * size : start * rows + (g + 1) * size, :],
+                            got_ref[jy, top : top + SCALE_GROUPS, :][g : g + 1],
+                        )
+                        for g in range(SCALE_GROUPS)
+                    ],
+                    axis=0,
+                )
+            value = keep_ref[jy, at, :] + other
             if part == 0:
                 own_ref[place] = value
                 continue
@@ -643,17 +691,18 @@
     plane_c = [line_c, swap(line_c, 1, 0), swap(line_c, 0, 2), swap(line_c, 1, 2)]
     line_d = [pair_d] + [swap(pair_d, 2 * z, 0) for z in range(1, half)]
 
-    start, act, cot, hot = pl.pallas_call(
+    start, act, windows, cot, hot = pl.pallas_call(
         functools.partial(margin_kernel, ranks),
         out_shape=(
             shape((rows, D), F32),
             shape((rows, D), BF16),
+            shape((clips * frames, KERNEL * D), BF16),
             shape((2 * PAD * clips, D), F32),
             shape(hot.shape, BF16),
         ),
         in_specs=[smem] + whole(4),
-        out_specs=tuple(whole(4)),
-        input_output_aliases={4: 3},
+        out_specs=tuple(whole(5)),
+        input_output_aliases={4: 4},
         compiler_params=params(8),
         name="margin",
     )(clip_lengths, features, near, far, hot)
@@ -690,7 +739,7 @@
         functools.partial(quant_kernel, ranks),
         out_shape=(
             shape((clips, frames, D), BF16),
-            shape((2, CODES, DG), F32),
+            shape((2, CODES + SCALE_GROUPS * ranks, DG), jnp.int16),
             shape((rows, D), BF16),
             shape((clips * frames, D), F32),
             shape((SLOTS, clips * frames, 2 * DG), BF16),
@@ -717,15 +766,23 @@
         grads = (shape((2, ranks * small, DG), F32),) * 2
     else:
         grads = (shape((KERNEL, HID, D), F32), shape((D, HID), F32))
-    fg, first_grad, second_grad = pl.pallas_call(
+    hg, first_grad, second_grad = pl.pallas_call(
         functools.partial(backward_kernel, ranks, assemble, clips),
-        out_shape=(shape((clips, frames, D), F32),) + grads,
-        in_specs=[smem] + whole(8),
+        out_shape=(shape((rows, HID), BF16),) + grads,
+        in_specs=whole(5),
         out_specs=tuple(whole(3)),
         scratch_shapes=[pltpu.VMEM((4, HID, D), F32)] if assemble else [],
         compiler_params=params(16),
         name="backward",
-    )(clip_lengths, start, act, gated, bg, lg, hs, dil, pwt)
+    )(windows, gated, bg, hs, pwt)
+    fg = pl.pallas_call(
+        functools.partial(features_kernel, clips),
+        out_shape=shape((clips, frames, D), F32),
+        in_specs=[smem] + whole(4),
+        out_specs=whole(1)[0],
+        compiler_params=params(12),
+        name="features",
+    )(clip_lengths, start, lg, hg, dil)
 
     if assemble:
         keep_d, send_d = first_grad, second_grad
@@ -781,6 +838,7 @@
     parts_c = over_plane(sent(keep, got_c, by_plane, block, "codes"))
     parts_c[0], keep_d = lax.optimization_barrier((parts_c[0], keep_d))
     parts_d = over_line(sent(keep_d, got_d, by_line, small, "conv"))
+    fg, parts_c[0] = lax.optimization_barrier((fg, parts_c[0]))
     parts_c = over_line(passed(parts_c, block, "codes"))
     parts_c[1], parts_d[0] = lax.optimization_barrier((parts_c[1], parts_d[0]))
     parts_d = over_plane(passed(parts_d, small, "conv"))

time: 91.4 us -> 90 us (0.985)
  waiting for transfers between devices: 23.5 us -> 20.8 us
  Pallas kernels: 21.1 us -> 22.3 us
    ppermute x35, waiting for transfers between devices: 18.9 us -> 16.1 us  [swap(): return lax.ppermute(value, ('clip', 'tm'), pairs)]
    pallas_call x0 -> x1, Pallas kernels: none -> 2.23 us  [shards(): pl.pallas_call(functools.partial(features_kernel, clips), out_shape=shape...]
    pallas_call x1, Pallas kernels: 3.18 us -> 1.37 us  [shards(): pl.pallas_call(functools.partial(backward_kernel, ranks, assemble, clips)...]
  transfers between devices with their start and end apart: 38 -> 38, of which waited for: 13 -> 13; matrix products, arithmetic and copies ran while one was open for 0% -> 0% of each run, Pallas kernels for 14% -> 15%
where the time goes in v5:
time: 90 us; the launch traced here: 89.7 us
  starting transfers between devices  44.4 us (49%)
  Pallas kernels  22.3 us (25%)
  waiting for transfers between devices  20.8 us (23%)
  between operations  1.98 us (2%)
    ppermute x35, starting transfers between devices, swap(): return lax.ppermute(value, ('clip', 'tm'), pairs)  41.1 us
    ppermute x35, waiting for transfers between devices, swap(): return lax.ppermute(value, ('clip', 'tm'), pairs)  16.1 us
    all_to_all x1, waiting for transfers between devices, shards(): squares = lax.all_to_all(squares, ('clip', 'tm'), 0, 0, tiled=True)  4.75 us
    pallas_call x1, Pallas kernels, shards(): pl.pallas_call(functools.partial(quant_kernel, ranks), out_shape=(shape((...  4.04 us
    pallas_call x1, Pallas kernels, shards(): pl.pallas_call(update_kernel, out_shape=(shape((1, 1), F32),) + tuple((sh...  2.98 us
    pallas_call x1, Pallas kernels, shards(): pl.pallas_call(functools.partial(own_kernel, ranks), out_shape=(shape((SL...  2.82 us
    all_to_all x1, starting transfers between devices, shards(): squares = lax.all_to_all(squares, ('clip', 'tm'), 0, 0, tiled=True)  2.58 us
    pallas_call x1, Pallas kernels, shards(): pl.pallas_call(functools.partial(features_kernel, clips), out_shape=shape...  2.23 us
  transfers between devices with their start and end apart: 38, of which 13 were waited for; matrix products, arithmetic and copies ran while one was open for 0% of the time, Pallas kernels for 15%

profile of v5, /device:TPU:0, one launch (start us, length us, event | category | flops | bytes accessed | tf_op | source)
XLA Modules:
  0.0 89.7 jit_solution(10127973799906844346)
XLA Ops:
  0.7 1.1 %prep.1 = (bf16[2,64,256]{2,1,0:T(8,128)(2,1)S(1)}, bf16[128,256]{1,0:T(8,128)(2,1)S(1)}) custom-call(f32[3,32,512]{2,1,0:T(8,128)} %bitcast.19, f32[64,256]{1,0:T(8,128)} %bitcast.21, f32[4,128,256]{2,1,0:T(8,128)} %refs_10_.1), custom_call_target="tpu_custom_call" | custom-call | tf_op jit(solution)/shard_map/prep/pallas_call | solution.py:635
  1.8 3.0 %collective-permute-start.5 = (bf16[2,64,256]{2,1,0:T(8,128)(2,1)S(1)}, bf16[2,64,256]{2,1,0:T(8,128)(2,1)S(1)}, u32[]{:S(2)}, u32[]{:S(2)}) collective-permute-start(bf16[2,64,256]{2,1,0:T(8,128)(2,1)S(1)} %get-tuple-element.100), channel_id=1, source_target_pairs={{0,4},{1,5},{2,6},{3,7},{4,0},{5,1},{6,2},{7,3},{8,12},{9,13},{10,... | collective-permute-start | bytes 196616 | tf_op jit(solution)/shard_map/ppermute | solution.py:70
  4.8 1.6 %collective-permute-start.2 = (bf16[128,256]{1,0:T(8,128)(2,1)S(1)}, bf16[128,256]{1,0:T(8,128)(2,1)S(1)}, u32[]{:S(2)}, u32[]{:S(2)}) collective-permute-start(bf16[128,256]{1,0:T(8,128)(2,1)S(1)} %get-tuple-element.90), channel_id=1, source_target_pairs={{0,8},{1,9},{2,10},{3,11},{4,12},{5,13},{6,14},{7,15},{8,0},{9,1},... | collective-permute-start | bytes 196616 | tf_op jit(solution)/shard_map/ppermute | solution.py:70
  6.3 2.6 %collective-permute-start.3 = (bf16[128,256]{1,0:T(8,128)(2,1)S(1)}, bf16[128,256]{1,0:T(8,128)(2,1)S(1)}, u32[]{:S(2)}, u32[]{:S(2)}) collective-permute-start(bf16[128,256]{1,0:T(8,128)(2,1)S(1)} %get-tuple-element.90), channel_id=1, source_target_pairs={{0,16},{1,17},{2,18},{3,19},{4,20},{5,21},{6,22},{7,23},{8,24},{9,... | collective-permute-start | bytes 196616 | tf_op jit(solution)/shard_map/ppermute | solution.py:70
  11.7 1.6 %collective-permute-done.3 = bf16[128,256]{1,0:T(8,128)(2,1)S(1)} collective-permute-done((bf16[128,256]{1,0:T(8,128)(2,1)S(1)}, bf16[128,256]{1,0:T(8,128)(2,1)S(1)}, u32[]{:S(2)}, u32[]{:S(2)}) %collective-permute-start.3) | collective-permute-done | bytes 65568 | tf_op jit(solution)/shard_map/ppermute | solution.py:70
  13.3 1.8 %collective-permute-start.7 = (bf16[2,2,64,256]{3,2,1,0:T(8,128)(2,1)S(1)}, bf16[2,2,64,256]{3,2,1,0:T(8,128)(2,1)S(1)}, u32[]{:S(2)}, u32[]{:S(2)}) collective-permute-start(bf16[2,2,64,256]{3,2,1,0:T(8,128)(2,1)S(1)} %pad_maximum_fusion.1.refs_0_), channel_id=1, source_target_pairs={{0,16},{1,17},{2,18},{3,19},{4,20},{5,21},{6,22},{7,23},{8,24},{9,... | collective-permute-start | bytes 393224 | tf_op jit(solution)/shard_map/ppermute | solution.py:70
  15.2 1.3 %collective-permute-start.8 = (bf16[2,2,64,256]{3,2,1,0:T(8,128)(2,1)S(1)}, bf16[2,2,64,256]{3,2,1,0:T(8,128)(2,1)S(1)}, u32[]{:S(2)}, u32[]{:S(2)}) collective-permute-start(bf16[2,2,64,256]{3,2,1,0:T(8,128)(2,1)S(1)} %pad_maximum_fusion.1.refs_0_), channel_id=1, source_target_pairs={{0,24},{1,25},{2,26},{3,27},{4,28},{5,29},{6,30},{7,31},{8,16},{9,... | collective-permute-start | bytes 393224 | tf_op jit(solution)/shard_map/ppermute | solution.py:70
  17.2 2.0 %collective-permute-start.16 = (bf16[4,128,256]{2,1,0:T(8,128)(2,1)S(1)}, bf16[4,128,256]{2,1,0:T(8,128)(2,1)S(1)}, u32[]{:S(2)}, u32[]{:S(2)}) collective-permute-start(bf16[4,128,256]{2,1,0:T(8,128)(2,1)S(1)} %pad_maximum_fusion.refs_0_), channel_id=1, source_target_pairs={{0,2},{1,3},{2,0},{3,1},{4,6},{5,7},{6,4},{7,5},{8,10},{9,11},{10,... | collective-permute-start | bytes 786440 | tf_op jit(solution)/shard_map/ppermute | solution.py:70
  19.2 1.4 %collective-permute-start.17 = (bf16[4,128,256]{2,1,0:T(8,128)(2,1)S(1)}, bf16[4,128,256]{2,1,0:T(8,128)(2,1)S(1)}, u32[]{:S(2)}, u32[]{:S(2)}) collective-permute-start(bf16[4,128,256]{2,1,0:T(8,128)(2,1)S(1)} %pad_maximum_fusion.refs_0_), channel_id=1, source_target_pairs={{0,6},{1,7},{2,4},{3,5},{4,2},{5,3},{6,0},{7,1},{8,14},{9,15},{10,... | collective-permute-start | bytes 786440 | tf_op jit(solution)/shard_map/ppermute | solution.py:70
  20.6 2.8 %own.1 = (bf16[4,544,1024]{2,1,0:T(8,128)(2,1)S(1)}, bf16[4,1024,512]{2,1,0:T(8,128)(2,1)S(1)}) custom-call(s32[4,2,256]{2,1,0:T(2,128)S(1)} %copy-done.11), custom_call_target="tpu_custom_call" | custom-call | tf_op jit(solution)/shard_map/own/pallas_call | solution.py:680
  23.4 1.7 %margin.1 = (f32[544,512]{1,0:T(8,128)S(1)}, bf16[544,512]{1,0:T(8,128)(2,1)S(1)}, bf16[512,1536]{1,0:T(8,128)(2,1)S(1)}, f32[32,512]{1,0:T(8,128)S(1)}, bf16[4,544,1024]{2,1,0:T(8,128)(2,1)S(1)}) custom-call(s32[2]{0:T(128)S(1)} %copy-done.12, bf16[2,256,512]{2,1,0:T(8,128)(2,1)S(1)} %copy-done.2, ...), custom_call_target="tpu_custom_call", output_to_operand_aliasing={{4}: (4, {})} | custom-call | tf_op jit(solution)/shard_map/margin/pallas_call | solution.py:694
  28.3 3.4 %collective-permute-done.16.refs_4_ = bf16[4,128,256]{2,1,0:T(8,128)(2,1)S(1)} collective-permute-done((bf16[4,128,256]{2,1,0:T(8,128)(2,1)S(1)}, bf16[4,128,256]{2,1,0:T(8,128)(2,1)S(1)}, u32[]{:S(2)}, u32[]{:S(2)}) %collective-permute-start.16) | collective-permute-done | bytes 262176 | tf_op jit(solution)/shard_map/ppermute | solution.py:70
  32.3 1.5 %collective-permute-done.9.refs_4_ = bf16[2,2,64,256]{3,2,1,0:T(8,128)(2,1)S(1)} collective-permute-done((bf16[2,2,64,256]{3,2,1,0:T(8,128)(2,1)S(1)}, bf16[2,2,64,256]{3,2,1,0:T(8,128)(2,1)S(1)}, u32[]{:S(2)}, u32[]{:S(2)}) %collective-permute-start.9) | collective-permute-done | bytes 131104 | tf_op jit(solution)/shard_map/ppermute | solution.py:70
  33.8 1.2 %conv.1 = (bf16[768,512]{1,0:T(8,128)(2,1)S(1)}, bf16[512,256]{1,0:T(8,128)(2,1)S(1)}, bf16[544,256]{1,0:T(8,128)(2,1)S(1)}, f32[544,256]{1,0:T(8,128)S(1)}, f32[544,512]{1,0:T(8,128)S(1)}) custom-call(f32[544,512]{1,0:T(8,128)S(1)} %get-tuple-element.98.start_ref, bf16[544,512]{1,0:T(8,128)(2,1)S(1)} %get-tuple-element.101.act_ref, ...), custom_call_target="tpu_custom_call" | custom-call | tf_op jit(solution)/shard_map/conv/pallas_call | solution.py:726
  35.1 4.0 %quant.1 = (bf16[2,256,512]{2,1,0:T(8,128)(2,1)}, s16[2,1056,256]{2,1,0:T(8,128)(2,1)S(1)}, bf16[544,512]{1,0:T(8,128)(2,1)S(1)}, f32[512,512]{1,0:T(8,128)S(1)}, bf16[4,512,512]{2,1,0:T(8,128)(2,1)S(1)}) custom-call(s32[2]{0:T(128)S(1)} %copy-done.12, f32[544,512]{1,0:T(8,128)S(1)} %get-tuple-element.106.latent_ref, bf16[2,256,512]{2,1,0:T(8,128)(2,1)S(1)} %copy-done, ...), custom_call_target="tpu_custom_call" | custom-call | tf_op jit(solution)/shard_map/quant/pallas_call | solution.py:738
  39.3 1.4 %backward.1 = (bf16[544,256]{1,0:T(8,128)(2,1)S(1)}, f32[2,512,256]{2,1,0:T(8,128)S(1)}, f32[2,512,256]{2,1,0:T(8,128)S(1)}) custom-call(bf16[512,1536]{1,0:T(8,128)(2,1)S(1)} %get-tuple-element.113.window_ref, bf16[544,256]{1,0:T(8,128)(2,1)S(1)} %get-tuple-element.114.gated_ref, bf16[544,512]{1,0:T(8,128)(2,1)S(1)} %get-tuple-element.115.bg_ref, ...), custom_call_target="tpu_custom_call" | custom-call | tf_op jit(solution)/shard_map/backward/pallas_call | solution.py:769
  41.1 1.2 %keep.1.keep_ref = f32[2,1024,256]{2,1,0:T(8,128)S(1)} custom-call(bf16[4,1024,512]{2,1,0:T(8,128)(2,1)S(1)} %get-tuple-element.109.hott_ref, bf16[4,512,512]{2,1,0:T(8,128)(2,1)S(1)} %get-tuple-element.120.cgs_ref), custom_call_target="tpu_custom_call" | custom-call | tf_op jit(solution)/shard_map/keep/pallas_call | solution.py:756
  43.1 1.5 %collective-permute-start.21 = (s16[528,256]{1,0:T(8,128)(2,1)S(1)}, s16[528,256]{1,0:T(8,128)(2,1)S(1)}, u32[]{:S(2)}, u32[]{:S(2)}) collective-permute-start(s16[528,256]{1,0:T(8,128)(2,1)S(1)} %get-tuple-element.127), channel_id=1, source_target_pairs={{0,4},{1,5},{2,6},{3,7},{4,0},{5,1},{6,2},{7,3},{8,12},{9,13},{10,... | collective-permute-start | bytes 811016 | tf_op jit(solution)/shard_map/ppermute | solution.py:70
  44.6 2.0 %collective-permute-start.23 = (s16[528,256]{1,0:T(8,128)(2,1)S(1)}, s16[528,256]{1,0:T(8,128)(2,1)S(1)}, u32[]{:S(2)}, u32[]{:S(2)}) collective-permute-start(s16[528,256]{1,0:T(8,128)(2,1)S(1)} %get-tuple-element.129), channel_id=1, source_target_pairs={{0,6},{1,7},{2,4},{3,5},{4,2},{5,3},{6,0},{7,1},{8,14},{9,15},{10,... | collective-permute-start | bytes 811016 | tf_op jit(solution)/shard_map/ppermute | solution.py:70
  47.8 3.5 %collective-permute-start.27 = (s16[272,256]{1,0:T(8,128)(2,1)S(1)}, s16[272,256]{1,0:T(8,128)(2,1)S(1)}, u32[]{:S(2)}, u32[]{:S(2)}) collective-permute-start(s16[272,256]{1,0:T(8,128)(2,1)S(1)} %get-tuple-element.136), channel_id=1, source_target_pairs={{0,16},{1,17},{2,18},{3,19},{4,20},{5,21},{6,22},{7,23},{8,24},{9,... | collective-permute-start | bytes 417800 | tf_op jit(solution)/shard_map/ppermute | solution.py:70
  51.3 1.2 %collective-permute-done.21.refs_0_ = s16[528,256]{1,0:T(8,128)(2,1)S(1)} collective-permute-done((s16[528,256]{1,0:T(8,128)(2,1)S(1)}, s16[528,256]{1,0:T(8,128)(2,1)S(1)}, u32[]{:S(2)}, u32[]{:S(2)}) %collective-permute-start.21) | collective-permute-done | bytes 270368 | tf_op jit(solution)/shard_map/ppermute | solution.py:70
  52.5 3.5 %collective-permute-start.28 = (s16[272,256]{1,0:T(8,128)(2,1)S(1)}, s16[272,256]{1,0:T(8,128)(2,1)S(1)}, u32[]{:S(2)}, u32[]{:S(2)}) collective-permute-start(s16[272,256]{1,0:T(8,128)(2,1)S(1)} %get-tuple-element.137), channel_id=1, source_target_pairs={{0,24},{1,25},{2,26},{3,27},{4,28},{5,29},{6,30},{7,31},{8,16},{9,... | collective-permute-start | bytes 417800 | tf_op jit(solution)/shard_map/ppermute | solution.py:70
  56.0 2.2 %features.1 = f32[2,256,512]{2,1,0:T(8,128)} custom-call(s32[2]{0:T(128)S(1)} %copy-done.12, f32[544,512]{1,0:T(8,128)S(1)} %get-tuple-element.98.start_ref, f32[512,512]{1,0:T(8,128)S(1)} %get-tuple-element.112.lg_ref, bf16[544,256]{1,0:T(8,128)(2,1)S(1)} %get-tuple-element.118.hg_ref, bf16[768,512]{1,0:T(8,128)(2,1)S(1)} %get-tuple-element.119.d_ref), custom_call_target="tpu_custom_call" | custom-call | tf_op jit(solution)/shard_map/features/pallas_call | solution.py:778
  59.7 3.5 %collective-permute-start.32 = (s16[144,256]{1,0:T(8,128)(2,1)S(1)}, s16[144,256]{1,0:T(8,128)(2,1)S(1)}, u32[]{:S(2)}, u32[]{:S(2)}) collective-permute-start(s16[144,256]{1,0:T(8,128)(2,1)S(1)} %get-tuple-element.144), channel_id=1, source_target_pairs={{0,16},{1,17},{2,18},{3,19},{4,20},{5,21},{6,22},{7,23},{8,24},{9,... | collective-permute-start | bytes 221192 | tf_op jit(solution)/shard_map/ppermute | solution.py:70
  63.7 3.4 %collective-permute-start.33 = (s16[144,256]{1,0:T(8,128)(2,1)S(1)}, s16[144,256]{1,0:T(8,128)(2,1)S(1)}, u32[]{:S(2)}, u32[]{:S(2)}) collective-permute-start(s16[144,256]{1,0:T(8,128)(2,1)S(1)} %get-tuple-element.145), channel_id=1, source_target_pairs={{0,24},{1,25},{2,26},{3,27},{4,28},{5,29},{6,30},{7,31},{8,16},{9,... | collective-permute-start | bytes 221192 | tf_op jit(solution)/shard_map/ppermute | solution.py:70
  67.8 1.4 %collective-permute-start.30 = (s16[80,256]{1,0:T(8,128)(2,1)S(1)}, s16[80,256]{1,0:T(8,128)(2,1)S(1)}, u32[]{:S(2)}, u32[]{:S(2)}) collective-permute-start(s16[80,256]{1,0:T(8,128)(2,1)S(1)} %get-tuple-element.140), channel_id=1, source_target_pairs={{0,2},{1,3},{2,0},{3,1},{4,6},{5,7},{6,4},{7,5},{8,10},{9,11},{10,... | collective-permute-start | bytes 122888 | tf_op jit(solution)/shard_map/ppermute | solution.py:70
  69.3 1.7 %collective-permute-start.31 = (s16[80,256]{1,0:T(8,128)(2,1)S(1)}, s16[80,256]{1,0:T(8,128)(2,1)S(1)}, u32[]{:S(2)}, u32[]{:S(2)}) collective-permute-start(s16[80,256]{1,0:T(8,128)(2,1)S(1)} %get-tuple-element.141), channel_id=1, source_target_pairs={{0,6},{1,7},{2,4},{3,5},{4,2},{5,3},{6,0},{7,1},{8,14},{9,15},{10,... | collective-permute-start | bytes 122888 | tf_op jit(solution)/shard_map/ppermute | solution.py:70
  71.8 2.4 %collective-permute-done.31.refs_3_ = s16[80,256]{1,0:T(8,128)(2,1)S(1)} collective-permute-done((s16[80,256]{1,0:T(8,128)(2,1)S(1)}, s16[80,256]{1,0:T(8,128)(2,1)S(1)}, u32[]{:S(2)}, u32[]{:S(2)}) %collective-permute-start.31) | collective-permute-done | bytes 40992 | tf_op jit(solution)/shard_map/ppermute | solution.py:70
  75.6 2.6 %all-to-all-start = ((f32[32,8,128]{2,1,0:T(8,128)}), f32[32,8,128]{2,1,0:T(8,128)S(1)}, u32[]{:S(2)}, u32[]{:S(2)}) async-start(f32[32,8,128]{2,1,0:T(8,128)} %get-tuple-element.146), calls=%async_computation | async-start | bytes 262144 | tf_op jit(solution)/shard_map/all_to_all | solution.py:856
  78.4 2.4 %collective-permute-done.35.refs_2_ = f32[192,256]{1,0:T(8,128)S(1)} collective-permute-done((f32[192,256]{1,0:T(8,128)S(1)}, f32[192,256]{1,0:T(8,128)S(1)}, u32[]{:S(2)}, u32[]{:S(2)}) %collective-permute-start.35) | collective-permute-done | bytes 196640 | tf_op jit(solution)/shard_map/ppermute | solution.py:70
  81.7 4.8 %all-to-all-done.square_ref = f32[32,8,128]{2,1,0:T(8,128)S(1)} async-done(((f32[32,8,128]{2,1,0:T(8,128)}), f32[32,8,128]{2,1,0:T(8,128)S(1)}, u32[]{:S(2)}, u32[]{:S(2)}) %all-to-all-start) | async-done | bytes 131104 | tf_op jit(solution)/shard_map/all_to_all | solution.py:856
  86.5 3.0 %update.1 = (f32[1,1]{1,0:T(1,128)}, f32[3,32,512]{2,1,0:T(8,128)}, f32[3,32,512]{2,1,0:T(8,128)}, f32[3,32,512]{2,1,0:T(8,128)}, f32[64,256]{1,0:T(8,128)}, /*i...) custom-call(f32[2]{0:T(128)S(1)} %pad_maximum_fusion.2.fix_ref, ...), custom_call_target="tpu_custom_call" | custom-call | tf_op jit(solution)/shard_map/update/pallas_call | solution.py:862
  (88 shorter events, 14.8 us)
Async XLA Ops:
  1.8 8.5 %collective-permute-start.5 = (bf16[2,64,256]{2,1,0:T(8,128)(2,1)S(1)}, bf16[2,64,256]{2,1,0:T(8,128)(2,1)S(1)}, u32[]{:S(2)}, u32[]{:S(2)}) collective-permute-start(bf16[2,64,256]{2,1,0:T(8,128)(2,1)S(1)} %get-tuple-element.100), channel_id=1, source_target_pairs={{0,4},{1,5},{2,6},{3,7},{4,0},{5,1},{6,2},{7,3},{8,12},{9,13},{10,... | collective-permute-start | bytes 196616 | tf_op jit(solution)/shard_map/ppermute | solution.py:70
  4.8 6.2 %collective-permute-start.2 = (bf16[128,256]{1,0:T(8,128)(2,1)S(1)}, bf16[128,256]{1,0:T(8,128)(2,1)S(1)}, u32[]{:S(2)}, u32[]{:S(2)}) collective-permute-start(bf16[128,256]{1,0:T(8,128)(2,1)S(1)} %get-tuple-element.90), channel_id=1, source_target_pairs={{0,8},{1,9},{2,10},{3,11},{4,12},{5,13},{6,14},{7,15},{8,0},{9,1},... | collective-permute-start | bytes 196616 | tf_op jit(solution)/shard_map/ppermute | solution.py:70
  6.3 7.0 %collective-permute-start.3 = (bf16[128,256]{1,0:T(8,128)(2,1)S(1)}, bf16[128,256]{1,0:T(8,128)(2,1)S(1)}, u32[]{:S(2)}, u32[]{:S(2)}) collective-permute-start(bf16[128,256]{1,0:T(8,128)(2,1)S(1)} %get-tuple-element.90), channel_id=1, source_target_pairs={{0,16},{1,17},{2,18},{3,19},{4,20},{5,21},{6,22},{7,23},{8,24},{9,... | collective-permute-start | bytes 196616 | tf_op jit(solution)/shard_map/ppermute | solution.py:70
  8.9 6.2 %collective-permute-start.4 = (bf16[128,256]{1,0:T(8,128)(2,1)S(1)}, bf16[128,256]{1,0:T(8,128)(2,1)S(1)}, u32[]{:S(2)}, u32[]{:S(2)}) collective-permute-start(bf16[128,256]{1,0:T(8,128)(2,1)S(1)} %get-tuple-element.90), channel_id=1, source_target_pairs={{0,24},{1,25},{2,26},{3,27},{4,28},{5,29},{6,30},{7,31},{8,16},{9,... | collective-permute-start | bytes 196616 | tf_op jit(solution)/shard_map/ppermute | solution.py:70
  10.1 6.4 %collective-permute-start = (bf16[2,16,1024]{2,1,0:T(8,128)(2,1)S(1)}, bf16[2,16,1024]{2,1,0:T(8,128)(2,1)S(1)}, u32[]{:S(2)}, u32[]{:S(2)}) collective-permute-start(bf16[2,16,1024]{2,1,0:T(8,128)(2,1)S(1)} %get-tuple-element.88), channel_id=1, source_target_pairs={{0,1},{1,0},{2,3},{3,2},{4,5},{5,4},{6,7},{7,6},{8,9},{9,8},{10,11... | collective-permute-start | bytes 196616 | tf_op jit(solution)/shard_map/ppermute | solution.py:673
  10.2 6.3 %collective-permute-start.1 = (bf16[2,16,1024]{2,1,0:T(8,128)(2,1)S(1)}, bf16[2,16,1024]{2,1,0:T(8,128)(2,1)S(1)}, u32[]{:S(2)}, u32[]{:S(2)}) collective-permute-start(bf16[2,16,1024]{2,1,0:T(8,128)(2,1)S(1)} %get-tuple-element.89), channel_id=1, source_target_pairs={{1,2},{2,1},{5,6},{6,5},{9,10},{10,9},{13,14},{14,13},{17,18},{18,... | collective-permute-start | bytes 196616 | tf_op jit(solution)/shard_map/ppermute | solution.py:675
  10.9 8.3 %collective-permute-start.6 = (bf16[2,2,64,256]{3,2,1,0:T(8,128)(2,1)S(1)}, bf16[2,2,64,256]{3,2,1,0:T(8,128)(2,1)S(1)}, u32[]{:S(2)}, u32[]{:S(2)}) collective-permute-start(bf16[2,2,64,256]{3,2,1,0:T(8,128)(2,1)S(1)} %pad_maximum_fusion.1.refs_0_), channel_id=1, source_target_pairs={{0,8},{1,9},{2,10},{3,11},{4,12},{5,13},{6,14},{7,15},{8,0},{9,1},... | collective-permute-start | bytes 393224 | tf_op jit(solution)/shard_map/ppermute | solution.py:70
  13.3 12.5 %collective-permute-start.7 = (bf16[2,2,64,256]{3,2,1,0:T(8,128)(2,1)S(1)}, bf16[2,2,64,256]{3,2,1,0:T(8,128)(2,1)S(1)}, u32[]{:S(2)}, u32[]{:S(2)}) collective-permute-start(bf16[2,2,64,256]{3,2,1,0:T(8,128)(2,1)S(1)} %pad_maximum_fusion.1.refs_0_), channel_id=1, source_target_pairs={{0,16},{1,17},{2,18},{3,19},{4,20},{5,21},{6,22},{7,23},{8,24},{9,... | collective-permute-start | bytes 393224 | tf_op jit(solution)/shard_map/ppermute | solution.py:70
  15.2 10.7 %collective-permute-start.8 = (bf16[2,2,64,256]{3,2,1,0:T(8,128)(2,1)S(1)}, bf16[2,2,64,256]{3,2,1,0:T(8,128)(2,1)S(1)}, u32[]{:S(2)}, u32[]{:S(2)}) collective-permute-start(bf16[2,2,64,256]{3,2,1,0:T(8,128)(2,1)S(1)} %pad_maximum_fusion.1.refs_0_), channel_id=1, source_target_pairs={{0,24},{1,25},{2,26},{3,27},{4,28},{5,29},{6,30},{7,31},{8,16},{9,... | collective-permute-start | bytes 393224 | tf_op jit(solution)/shard_map/ppermute | solution.py:70
  16.6 11.4 %collective-permute-start.13 = (bf16[4,128,256]{2,1,0:T(8,128)(2,1)S(1)}, bf16[4,128,256]{2,1,0:T(8,128)(2,1)S(1)}, u32[]{:S(2)}, u32[]{:S(2)}) collective-permute-start(bf16[4,128,256]{2,1,0:T(8,128)(2,1)S(1)} %pad_maximum_fusion.refs_0_), channel_id=1, source_target_pairs={{0,4},{1,5},{2,6},{3,7},{4,0},{5,1},{6,2},{7,3},{8,12},{9,13},{10,... | collective-permute-start | bytes 786440 | tf_op jit(solution)/shard_map/ppermute | solution.py:70
  17.2 14.5 %collective-permute-start.16 = (bf16[4,128,256]{2,1,0:T(8,128)(2,1)S(1)}, bf16[4,128,256]{2,1,0:T(8,128)(2,1)S(1)}, u32[]{:S(2)}, u32[]{:S(2)}) collective-permute-start(bf16[4,128,256]{2,1,0:T(8,128)(2,1)S(1)} %pad_maximum_fusion.refs_0_), channel_id=1, source_target_pairs={{0,2},{1,3},{2,0},{3,1},{4,6},{5,7},{6,4},{7,5},{8,10},{9,11},{10,... | collective-permute-start | bytes 786440 | tf_op jit(solution)/shard_map/ppermute | solution.py:70
  19.2 12.5 %collective-permute-start.17 = (bf16[4,128,256]{2,1,0:T(8,128)(2,1)S(1)}, bf16[4,128,256]{2,1,0:T(8,128)(2,1)S(1)}, u32[]{:S(2)}, u32[]{:S(2)}) collective-permute-start(bf16[4,128,256]{2,1,0:T(8,128)(2,1)S(1)} %pad_maximum_fusion.refs_0_), channel_id=1, source_target_pairs={{0,6},{1,7},{2,4},{3,5},{4,2},{5,3},{6,0},{7,1},{8,14},{9,15},{10,... | collective-permute-start | bytes 786440 | tf_op jit(solution)/shard_map/ppermute | solution.py:70
  27.4 4.8 %collective-permute-start.12 = (bf16[2,2,64,256]{3,2,1,0:T(8,128)(2,1)S(1)}, bf16[2,2,64,256]{3,2,1,0:T(8,128)(2,1)S(1)}, u32[]{:S(2)}, u32[]{:S(2)}) collective-permute-start(bf16[2,2,64,256]{3,2,1,0:T(8,128)(2,1)S(1)} %collective-permute-done.8.refs_3_), channel_id=1, source_target_pairs={{0,1},{1,0},{2,3},{3,2},{4,5},{5,4},{6,7},{7,6},{8,9},{9,8},{10,11... | collective-permute-start | bytes 393224 | tf_op jit(solution)/shard_map/ppermute | solution.py:70
  27.8 7.3 %collective-permute-start.14 = (bf16[4,128,256]{2,1,0:T(8,128)(2,1)S(1)}, bf16[4,128,256]{2,1,0:T(8,128)(2,1)S(1)}, u32[]{:S(2)}, u32[]{:S(2)}) collective-permute-start(bf16[4,128,256]{2,1,0:T(8,128)(2,1)S(1)} %pad_maximum_fusion.refs_0_), channel_id=1, source_target_pairs={{0,1},{1,0},{2,3},{3,2},{4,5},{5,4},{6,7},{7,6},{8,9},{9,8},{10,11... | collective-permute-start | bytes 786440 | tf_op jit(solution)/shard_map/ppermute | solution.py:70
  27.9 7.1 %collective-permute-start.15 = (bf16[4,128,256]{2,1,0:T(8,128)(2,1)S(1)}, bf16[4,128,256]{2,1,0:T(8,128)(2,1)S(1)}, u32[]{:S(2)}, u32[]{:S(2)}) collective-permute-start(bf16[4,128,256]{2,1,0:T(8,128)(2,1)S(1)} %collective-permute-done.13.refs_1_), channel_id=1, source_target_pairs={{0,1},{1,0},{2,3},{3,2},{4,5},{5,4},{6,7},{7,6},{8,9},{9,8},{10,11... | collective-permute-start | bytes 786440 | tf_op jit(solution)/shard_map/ppermute | solution.py:70
  40.7 5.9 %collective-permute-start.25 = (f32[2,512,256]{2,1,0:T(8,128)S(1)}, f32[2,512,256]{2,1,0:T(8,128)S(1)}, u32[]{:S(2)}, u32[]{:S(2)}) collective-permute-start(f32[2,512,256]{2,1,0:T(8,128)S(1)} %get-tuple-element.132), channel_id=1, source_target_pairs={{0,1},{1,0},{2,3},{3,2},{4,5},{5,4},{6,7},{7,6},{8,9},{9,8},{10,11... | collective-permute-start | bytes 3145736 | tf_op jit(solution)/shard_map/ppermute | solution.py:70
  43.1 9.4 %collective-permute-start.21 = (s16[528,256]{1,0:T(8,128)(2,1)S(1)}, s16[528,256]{1,0:T(8,128)(2,1)S(1)}, u32[]{:S(2)}, u32[]{:S(2)}) collective-permute-start(s16[528,256]{1,0:T(8,128)(2,1)S(1)} %get-tuple-element.127), channel_id=1, source_target_pairs={{0,4},{1,5},{2,6},{3,7},{4,0},{5,1},{6,2},{7,3},{8,12},{9,13},{10,... | collective-permute-start | bytes 811016 | tf_op jit(solution)/shard_map/ppermute | solution.py:70
  44.6 14.0 %collective-permute-start.22 = (s16[528,256]{1,0:T(8,128)(2,1)S(1)}, s16[528,256]{1,0:T(8,128)(2,1)S(1)}, u32[]{:S(2)}, u32[]{:S(2)}) collective-permute-start(s16[528,256]{1,0:T(8,128)(2,1)S(1)} %get-tuple-element.128), channel_id=1, source_target_pairs={{0,2},{1,3},{2,0},{3,1},{4,6},{5,7},{6,4},{7,5},{8,10},{9,11},{10,... | collective-permute-start | bytes 811016 | tf_op jit(solution)/shard_map/ppermute | solution.py:70
  44.6 14.0 %collective-permute-start.23 = (s16[528,256]{1,0:T(8,128)(2,1)S(1)}, s16[528,256]{1,0:T(8,128)(2,1)S(1)}, u32[]{:S(2)}, u32[]{:S(2)}) collective-permute-start(s16[528,256]{1,0:T(8,128)(2,1)S(1)} %get-tuple-element.129), channel_id=1, source_target_pairs={{0,6},{1,7},{2,4},{3,5},{4,2},{5,3},{6,0},{7,1},{8,14},{9,15},{10,... | collective-permute-start | bytes 811016 | tf_op jit(solution)/shard_map/ppermute | solution.py:70
  47.2 20.0 %collective-permute-start.26 = (s16[272,256]{1,0:T(8,128)(2,1)S(1)}, s16[272,256]{1,0:T(8,128)(2,1)S(1)}, u32[]{:S(2)}, u32[]{:S(2)}) collective-permute-start(s16[272,256]{1,0:T(8,128)(2,1)S(1)} %get-tuple-element.135), channel_id=1, source_target_pairs={{0,8},{1,9},{2,10},{3,11},{4,12},{5,13},{6,14},{7,15},{8,0},{9,1},... | collective-permute-start | bytes 417800 | tf_op jit(solution)/shard_map/ppermute | solution.py:70
  47.8 19.3 %collective-permute-start.27 = (s16[272,256]{1,0:T(8,128)(2,1)S(1)}, s16[272,256]{1,0:T(8,128)(2,1)S(1)}, u32[]{:S(2)}, u32[]{:S(2)}) collective-permute-start(s16[272,256]{1,0:T(8,128)(2,1)S(1)} %get-tuple-element.136), channel_id=1, source_target_pairs={{0,16},{1,17},{2,18},{3,19},{4,20},{5,21},{6,22},{7,23},{8,24},{9,... | collective-permute-start | bytes 417800 | tf_op jit(solution)/shard_map/ppermute | solution.py:70
  52.5 14.7 %collective-permute-start.28 = (s16[272,256]{1,0:T(8,128)(2,1)S(1)}, s16[272,256]{1,0:T(8,128)(2,1)S(1)}, u32[]{:S(2)}, u32[]{:S(2)}) collective-permute-start(s16[272,256]{1,0:T(8,128)(2,1)S(1)} %get-tuple-element.137), channel_id=1, source_target_pairs={{0,24},{1,25},{2,26},{3,27},{4,28},{5,29},{6,30},{7,31},{8,16},{9,... | collective-permute-start | bytes 417800 | tf_op jit(solution)/shard_map/ppermute | solution.py:70
  59.0 4.7 %collective-permute-start.24 = (s16[144,256]{1,0:T(8,128)(2,1)S(1)}, s16[144,256]{1,0:T(8,128)(2,1)S(1)}, u32[]{:S(2)}, u32[]{:S(2)}) collective-permute-start(s16[144,256]{1,0:T(8,128)(2,1)S(1)} %get-tuple-element.130), channel_id=1, source_target_pairs={{0,8},{1,9},{2,10},{3,11},{4,12},{5,13},{6,14},{7,15},{8,0},{9,1},... | collective-permute-start | bytes 221192 | tf_op jit(solution)/shard_map/ppermute | solution.py:70
  59.7 11.2 %collective-permute-start.32 = (s16[144,256]{1,0:T(8,128)(2,1)S(1)}, s16[144,256]{1,0:T(8,128)(2,1)S(1)}, u32[]{:S(2)}, u32[]{:S(2)}) collective-permute-start(s16[144,256]{1,0:T(8,128)(2,1)S(1)} %get-tuple-element.144), channel_id=1, source_target_pairs={{0,16},{1,17},{2,18},{3,19},{4,20},{5,21},{6,22},{7,23},{8,24},{9,... | collective-permute-start | bytes 221192 | tf_op jit(solution)/shard_map/ppermute | solution.py:70
  63.7 7.2 %collective-permute-start.33 = (s16[144,256]{1,0:T(8,128)(2,1)S(1)}, s16[144,256]{1,0:T(8,128)(2,1)S(1)}, u32[]{:S(2)}, u32[]{:S(2)}) collective-permute-start(s16[144,256]{1,0:T(8,128)(2,1)S(1)} %get-tuple-element.145), channel_id=1, source_target_pairs={{0,24},{1,25},{2,26},{3,27},{4,28},{5,29},{6,30},{7,31},{8,16},{9,... | collective-permute-start | bytes 221192 | tf_op jit(solution)/shard_map/ppermute | solution.py:70
  67.4 4.1 %collective-permute-start.29 = (s16[80,256]{1,0:T(8,128)(2,1)S(1)}, s16[80,256]{1,0:T(8,128)(2,1)S(1)}, u32[]{:S(2)}, u32[]{:S(2)}) collective-permute-start(s16[80,256]{1,0:T(8,128)(2,1)S(1)} %get-tuple-element.139), channel_id=1, source_target_pairs={{0,4},{1,5},{2,6},{3,7},{4,0},{5,1},{6,2},{7,3},{8,12},{9,13},{10,... | collective-permute-start | bytes 122888 | tf_op jit(solution)/shard_map/ppermute | solution.py:70
  67.8 4.0 %collective-permute-start.30 = (s16[80,256]{1,0:T(8,128)(2,1)S(1)}, s16[80,256]{1,0:T(8,128)(2,1)S(1)}, u32[]{:S(2)}, u32[]{:S(2)}) collective-permute-start(s16[80,256]{1,0:T(8,128)(2,1)S(1)} %get-tuple-element.140), channel_id=1, source_target_pairs={{0,2},{1,3},{2,0},{3,1},{4,6},{5,7},{6,4},{7,5},{8,10},{9,11},{10,... | collective-permute-start | bytes 122888 | tf_op jit(solution)/shard_map/ppermute | solution.py:70
  69.3 5.0 %collective-permute-start.31 = (s16[80,256]{1,0:T(8,128)(2,1)S(1)}, s16[80,256]{1,0:T(8,128)(2,1)S(1)}, u32[]{:S(2)}, u32[]{:S(2)}) collective-permute-start(s16[80,256]{1,0:T(8,128)(2,1)S(1)} %get-tuple-element.141), channel_id=1, source_target_pairs={{0,6},{1,7},{2,4},{3,5},{4,2},{5,3},{6,0},{7,1},{8,14},{9,15},{10,... | collective-permute-start | bytes 122888 | tf_op jit(solution)/shard_map/ppermute | solution.py:70
  75.1 5.7 %collective-permute-start.35 = (f32[192,256]{1,0:T(8,128)S(1)}, f32[192,256]{1,0:T(8,128)S(1)}, u32[]{:S(2)}, u32[]{:S(2)}) collective-permute-start(f32[192,256]{1,0:T(8,128)S(1)} %get-tuple-element.147.refs_0_), channel_id=1, source_target_pairs={{0,2},{1,3},{2,0},{3,1},{4,6},{5,7},{6,4},{7,5},{8,10},{9,11},{10,... | collective-permute-start | bytes 589832 | tf_op jit(solution)/shard_map/ppermute | solution.py:70
  75.6 10.8 %all-to-all-start = ((f32[32,8,128]{2,1,0:T(8,128)}), f32[32,8,128]{2,1,0:T(8,128)S(1)}, u32[]{:S(2)}, u32[]{:S(2)}) async-start(f32[32,8,128]{2,1,0:T(8,128)} %get-tuple-element.146), calls=%async_computation | async-start | bytes 262144 | tf_op jit(solution)/shard_map/all_to_all | solution.py:856
  78.2 3.5 %collective-permute-start.34 = (f32[192,256]{1,0:T(8,128)S(1)}, f32[192,256]{1,0:T(8,128)S(1)}, u32[]{:S(2)}, u32[]{:S(2)}) collective-permute-start(f32[192,256]{1,0:T(8,128)S(1)} %get-tuple-element.147.refs_0_), channel_id=1, source_target_pairs={{0,1},{1,0},{2,3},{3,2},{4,5},{5,4},{6,7},{7,6},{8,9},{9,8},{10,11... | collective-permute-start | bytes 589832 | tf_op jit(solution)/shard_map/ppermute | solution.py:70
  80.8 5.7 %collective-permute-start.36 = (f32[192,256]{1,0:T(8,128)S(1)}, f32[192,256]{1,0:T(8,128)S(1)}, u32[]{:S(2)}, u32[]{:S(2)}) collective-permute-start(f32[192,256]{1,0:T(8,128)S(1)} %collective-permute-done.35.refs_2_), channel_id=1, source_target_pairs={{0,1},{1,0},{2,3},{3,2},{4,5},{5,4},{6,7},{7,6},{8,9},{9,8},{10,11... | collective-permute-start | bytes 589832 | tf_op jit(solution)/shard_map/ppermute | solution.py:70
  (19 other events, 344.0 us)

commit v6 on v5

--- a/solution.py
+++ b/solution.py
@@ -166,11 +166,13 @@
         far_ref[c] = jnp.where(odd == 1, last, first).astype(BF16)
 
 
-def own_kernel(ranks, ids_ref, hot_ref, hott_ref):
+def own_kernel(ranks, len_ref, ids_ref, hot_ref, hott_ref):
     _, clips, frames = ids_ref.shape
     codes = lax.broadcasted_iota(jnp.int32, (frames, CODES), 1)
     spots = lax.broadcasted_iota(jnp.int32, (CODES, frames), 0)
+    where = lax.broadcasted_iota(jnp.int32, (1, frames), 1) + lax.axis_index("tm") * frames
     for c in range(clips):
+        weight = jnp.where(where < len_ref[c], -2.0, 0.0)
         ids = renamed(ids_ref[:, c, :], ranks)
         turned = jnp.concatenate([ids.astype(F32), jnp.zeros((8 - SLOTS, frames), F32)], axis=0)
         turned = turned.T.astype(jnp.int32)
@@ -179,7 +181,7 @@
             hot_ref[slot, at, :] = jnp.where(codes == turned[:, slot : slot + 1], 1.0, 0.0).astype(
                 BF16
             )
-            hott_ref[slot, :, at] = jnp.where(spots == ids[slot : slot + 1], 1.0, 0.0).astype(BF16)
+            hott_ref[slot, :, at] = jnp.where(spots == ids[slot : slot + 1], weight, 0.0).astype(BF16)
     hot_ref[:, clips * frames :, :] = jnp.zeros((SLOTS, 2 * PAD * clips, CODES), BF16)
 
 
@@ -205,6 +207,7 @@
     act_ref,
     window_ref,
     cot_ref,
+    mask_ref,
     hot_ref,
 ):
     del old_ref
@@ -214,7 +217,9 @@
     for c in range(clips):
         near, far = near_ref[c].astype(F32), far_ref[c].astype(F32)
         both += [jnp.where(odd == 1, near, far), jnp.where(odd == 1, far, near)]
-    start = masks(clips, frames, len_ref, D) * jnp.concatenate(
+    mask = masks(clips, frames, len_ref, D)
+    mask_ref[...] = mask[:, :DG]
+    start = mask * jnp.concatenate(
         [f_ref[c].astype(F32) for c in range(clips)] + [part[:PAD, :D] for part in both], axis=0
     )
     start_ref[...] = start
@@ -290,15 +295,14 @@
     latent_ref[...] = start_ref[...] + mmg(gated, pwt_ref[...], NT)
 
 
-def quant_kernel(ranks, len_ref, latent_ref, c_ref, cot_ref, hot_ref, hott_ref, *refs):
+def quant_kernel(ranks, mask_ref, latent_ref, c_ref, cot_ref, hot_ref, hott_ref, *refs):
     half, block = ranks // 2, CODES // ranks
     pieces, refs = refs[:8], refs[8:]
     quant_ref, send_ref, bg_ref, lg_ref, cgs_ref, tab_ref = refs
     clips, frames, _ = c_ref.shape
     time = lax.axis_index("tm")
-    mask = masks(clips, frames, len_ref, DG)
+    mask = mask_ref[...]
     local = clips * frames
-    twice = -2.0 * mask[:local]
     for other in range(SLOTS):
         slot = time ^ other
         for x in range(2):
@@ -323,10 +327,10 @@
         for clip in range(clips):
             quant_ref[clip, :, at] = quant[clip * frames : (clip + 1) * frames]
         for level, diff in ((0, gap), (1, gap2)):
-            code_grad = twice * diff[:local]
-            high = code_grad.astype(BF16)
+            diff = diff[:local]
+            high = diff.astype(BF16)
             cgs_ref[2 * group + level, :, :DG] = high
-            cgs_ref[2 * group + level, :, DG:] = (code_grad - high.astype(F32)).astype(BF16)
+            cgs_ref[2 * group + level, :, DG:] = (diff - high.astype(F32)).astype(BF16)
     size = block // SCALE_GROUPS
     for far in range(2):
         total = summed(2 * far + 1, hott_ref, cgs_ref)
@@ -683,26 +687,27 @@
             shape((SLOTS, rows, CODES), BF16),
             shape((SLOTS, CODES, clips * frames), BF16),
         ),
-        in_specs=whole(1),
+        in_specs=[smem] + whole(1),
         out_specs=tuple(whole(2)),
         compiler_params=params(8),
         name="own",
-    )(late_ids)
+    )(clip_lengths, late_ids)
     plane_c = [line_c, swap(line_c, 1, 0), swap(line_c, 0, 2), swap(line_c, 1, 2)]
     line_d = [pair_d] + [swap(pair_d, 2 * z, 0) for z in range(1, half)]
 
-    start, act, windows, cot, hot = pl.pallas_call(
+    start, act, windows, cot, mask, hot = pl.pallas_call(
         functools.partial(margin_kernel, ranks),
         out_shape=(
             shape((rows, D), F32),
             shape((rows, D), BF16),
             shape((clips * frames, KERNEL * D), BF16),
             shape((2 * PAD * clips, D), F32),
+            shape((rows, DG), F32),
             shape(hot.shape, BF16),
         ),
         in_specs=[smem] + whole(4),
-        out_specs=tuple(whole(5)),
-        input_output_aliases={4: 4},
+        out_specs=tuple(whole(6)),
+        input_output_aliases={4: 5},
         compiler_params=params(8),
         name="margin",
     )(clip_lengths, features, near, far, hot)
@@ -744,14 +749,14 @@
             shape((clips * frames, D), F32),
             shape((SLOTS, clips * frames, 2 * DG), BF16),
         ),
-        in_specs=[smem] + whole(5 + len(pieces_c)),
+        in_specs=whole(6 + len(pieces_c)),
         out_specs=tuple(whole(5)),
         scratch_shapes=[
             pltpu.VMEM((SLOTS, CODES, DG), BF16),
         ],
         compiler_params=params(16),
         name="quant",
-    )(clip_lengths, latent, cotangent, cot, hot, hott, *pieces_c)
+    )(mask, latent, cotangent, cot, hot, hott, *pieces_c)
 
     keep = pl.pallas_call(
         keep_kernel,
@@ -819,7 +824,7 @@
         return pl.pallas_call(
             functools.partial(pass_kernel, size),
             out_shape=(shape((size, DG), F32),)
-            + (shape((size + 16, DG), jnp.int16),) * (count - 1),
+            + (shape((size + 8, DG), jnp.int16),) * (count - 1),
             in_specs=whole(len(parts)),
             out_specs=tuple(whole(count)),
             compiler_params=params(),
@@ -833,11 +838,13 @@
         return [parts[0]] + [swap(parts[z], 2 * z, 0) for z in range(1, half)]
 
     by_plane = [[(jy, x * half + z) for z in range(half)] for jy in range(2) for x in range(2)]
-    by_line = [[(jy, x * half + z) for jy in range(2) for x in range(2)] for z in range(half)]
+    order = (0, 2, 1, 3) if half == 4 else tuple(range(half))
+    by_line = [[(jy, x * half + z) for jy in range(2) for x in range(2)] for z in order]
     got_c, got_d = swap(send, 0, 1), swap(send_d, 0, 1)
     parts_c = over_plane(sent(keep, got_c, by_plane, block, "codes"))
     parts_c[0], keep_d = lax.optimization_barrier((parts_c[0], keep_d))
-    parts_d = over_line(sent(keep_d, got_d, by_line, small, "conv"))
+    parts_d = sent(keep_d, got_d, by_line, small, "conv")
+    parts_d = [parts_d[0]] + [swap(parts_d[i], 2 * order[i], 0) for i in range(1, half)]
     fg, parts_c[0] = lax.optimization_barrier((fg, parts_c[0]))
     parts_c = over_line(passed(parts_c, block, "codes"))
     parts_c[1], parts_d[0] = lax.optimization_barrier((parts_c[1], parts_d[0]))

time: 90 us -> 89.2 us (level)
  transfers between devices with their start and end apart: 38 -> 38, of which waited for: 13 -> 13; matrix products, arithmetic and copies ran while one was open for 0% -> 0% of each run, Pallas kernels for 15% -> 16%
where the time goes in v6:
time: 89.2 us; the launch traced here: 88.9 us
  starting transfers between devices  44.2 us (50%)
  Pallas kernels  22.1 us (25%)
  waiting for transfers between devices  20.4 us (23%)
  between operations  1.98 us (2%)
    ppermute x35, starting transfers between devices, swap(): return lax.ppermute(value, ('clip', 'tm'), pairs)  40.8 us
    ppermute x35, waiting for transfers between devices, swap(): return lax.ppermute(value, ('clip', 'tm'), pairs)  15.4 us
    all_to_all x1, waiting for transfers between devices, shards(): squares = lax.all_to_all(squares, ('clip', 'tm'), 0, 0, tiled=True)  5 us
    pallas_call x1, Pallas kernels, shards(): pl.pallas_call(functools.partial(own_kernel, ranks), out_shape=(shape((SL...  3.39 us
    pallas_call x1, Pallas kernels, shards(): pl.pallas_call(functools.partial(quant_kernel, ranks), out_shape=(shape((...  3.32 us
    pallas_call x1, Pallas kernels, shards(): pl.pallas_call(update_kernel, out_shape=(shape((1, 1), F32),) + tuple((sh...  2.98 us
    all_to_all x1, starting transfers between devices, shards(): squares = lax.all_to_all(squares, ('clip', 'tm'), 0, 0, tiled=True)  2.58 us
    pallas_call x1, Pallas kernels, shards(): pl.pallas_call(functools.partial(features_kernel, clips), out_shape=shape...  2.21 us
  transfers between devices with their start and end apart: 38, of which 13 were waited for; matrix products, arithmetic and copies ran while one was open for 0% of the time, Pallas kernels for 16%

profile of v6, /device:TPU:0, one launch (start us, length us, event | category | flops | bytes accessed | tf_op | source)
XLA Modules:
  0.0 88.9 jit_solution(257866860355189251)
XLA Ops:
  1.8 3.0 %collective-permute-start.5 = (bf16[2,64,256]{2,1,0:T(8,128)(2,1)S(1)}, bf16[2,64,256]{2,1,0:T(8,128)(2,1)S(1)}, u32[]{:S(2)}, u32[]{:S(2)}) collective-permute-start(bf16[2,64,256]{2,1,0:T(8,128)(2,1)S(1)} %get-tuple-element.102), channel_id=1, source_target_pairs={{0,4},{1,5},{2,6},{3,7},{4,0},{5,1},{6,2},{7,3},{8,12},{9,13},{10,... | collective-permute-start | bytes 196616 | tf_op jit(solution)/shard_map/ppermute | solution.py:70
  4.8 1.6 %collective-permute-start.2 = (bf16[128,256]{1,0:T(8,128)(2,1)S(1)}, bf16[128,256]{1,0:T(8,128)(2,1)S(1)}, u32[]{:S(2)}, u32[]{:S(2)}) collective-permute-start(bf16[128,256]{1,0:T(8,128)(2,1)S(1)} %get-tuple-element.91), channel_id=1, source_target_pairs={{0,8},{1,9},{2,10},{3,11},{4,12},{5,13},{6,14},{7,15},{8,0},{9,1},... | collective-permute-start | bytes 196616 | tf_op jit(solution)/shard_map/ppermute | solution.py:70
  6.3 2.6 %collective-permute-start.3 = (bf16[128,256]{1,0:T(8,128)(2,1)S(1)}, bf16[128,256]{1,0:T(8,128)(2,1)S(1)}, u32[]{:S(2)}, u32[]{:S(2)}) collective-permute-start(bf16[128,256]{1,0:T(8,128)(2,1)S(1)} %get-tuple-element.91), channel_id=1, source_target_pairs={{0,16},{1,17},{2,18},{3,19},{4,20},{5,21},{6,22},{7,23},{8,24},{9,... | collective-permute-start | bytes 196616 | tf_op jit(solution)/shard_map/ppermute | solution.py:70
  11.7 1.6 %collective-permute-done.3 = bf16[128,256]{1,0:T(8,128)(2,1)S(1)} collective-permute-done((bf16[128,256]{1,0:T(8,128)(2,1)S(1)}, bf16[128,256]{1,0:T(8,128)(2,1)S(1)}, u32[]{:S(2)}, u32[]{:S(2)}) %collective-permute-start.3) | collective-permute-done | bytes 65568 | tf_op jit(solution)/shard_map/ppermute | solution.py:70
  13.3 1.8 %collective-permute-start.7 = (bf16[2,2,64,256]{3,2,1,0:T(8,128)(2,1)S(1)}, bf16[2,2,64,256]{3,2,1,0:T(8,128)(2,1)S(1)}, u32[]{:S(2)}, u32[]{:S(2)}) collective-permute-start(bf16[2,2,64,256]{3,2,1,0:T(8,128)(2,1)S(1)} %pad_maximum_fusion.1.refs_0_), channel_id=1, source_target_pairs={{0,16},{1,17},{2,18},{3,19},{4,20},{5,21},{6,22},{7,23},{8,24},{9,... | collective-permute-start | bytes 393224 | tf_op jit(solution)/shard_map/ppermute | solution.py:70
  15.2 1.3 %collective-permute-start.8 = (bf16[2,2,64,256]{3,2,1,0:T(8,128)(2,1)S(1)}, bf16[2,2,64,256]{3,2,1,0:T(8,128)(2,1)S(1)}, u32[]{:S(2)}, u32[]{:S(2)}) collective-permute-start(bf16[2,2,64,256]{3,2,1,0:T(8,128)(2,1)S(1)} %pad_maximum_fusion.1.refs_0_), channel_id=1, source_target_pairs={{0,24},{1,25},{2,26},{3,27},{4,28},{5,29},{6,30},{7,31},{8,16},{9,... | collective-permute-start | bytes 393224 | tf_op jit(solution)/shard_map/ppermute | solution.py:70
  17.2 2.0 %collective-permute-start.16 = (bf16[4,128,256]{2,1,0:T(8,128)(2,1)S(1)}, bf16[4,128,256]{2,1,0:T(8,128)(2,1)S(1)}, u32[]{:S(2)}, u32[]{:S(2)}) collective-permute-start(bf16[4,128,256]{2,1,0:T(8,128)(2,1)S(1)} %pad_maximum_fusion.refs_0_), channel_id=1, source_target_pairs={{0,2},{1,3},{2,0},{3,1},{4,6},{5,7},{6,4},{7,5},{8,10},{9,11},{10,... | collective-permute-start | bytes 786440 | tf_op jit(solution)/shard_map/ppermute | solution.py:70
  19.2 1.4 %collective-permute-start.17 = (bf16[4,128,256]{2,1,0:T(8,128)(2,1)S(1)}, bf16[4,128,256]{2,1,0:T(8,128)(2,1)S(1)}, u32[]{:S(2)}, u32[]{:S(2)}) collective-permute-start(bf16[4,128,256]{2,1,0:T(8,128)(2,1)S(1)} %pad_maximum_fusion.refs_0_), channel_id=1, source_target_pairs={{0,6},{1,7},{2,4},{3,5},{4,2},{5,3},{6,0},{7,1},{8,14},{9,15},{10,... | collective-permute-start | bytes 786440 | tf_op jit(solution)/shard_map/ppermute | solution.py:70
  20.6 3.4 %own.1 = (bf16[4,544,1024]{2,1,0:T(8,128)(2,1)S(1)}, bf16[4,1024,512]{2,1,0:T(8,128)(2,1)S(1)}) custom-call(s32[2]{0:T(128)S(1)} %copy-done.12, s32[4,2,256]{2,1,0:T(2,128)S(1)} %copy-done.11), custom_call_target="tpu_custom_call" | custom-call | tf_op jit(solution)/shard_map/own/pallas_call | solution.py:684
  24.0 1.7 %margin.1 = (f32[544,512]{1,0:T(8,128)S(1)}, bf16[544,512]{1,0:T(8,128)(2,1)S(1)}, bf16[512,1536]{1,0:T(8,128)(2,1)S(1)}, f32[32,512]{1,0:T(8,128)S(1)}, f32[544...) custom-call(s32[2]{0:T(128)S(1)} %copy-done.12, ...), custom_call_target="tpu_custom_call", output_to_operand_aliasing={{5}: (4, {})} | custom-call | tf_op jit(solution)/shard_map/margin/pallas_call | solution.py:698
  28.3 3.4 %collective-permute-done.16.refs_4_ = bf16[4,128,256]{2,1,0:T(8,128)(2,1)S(1)} collective-permute-done((bf16[4,128,256]{2,1,0:T(8,128)(2,1)S(1)}, bf16[4,128,256]{2,1,0:T(8,128)(2,1)S(1)}, u32[]{:S(2)}, u32[]{:S(2)}) %collective-permute-start.16) | collective-permute-done | bytes 262176 | tf_op jit(solution)/shard_map/ppermute | solution.py:70
  32.3 1.5 %collective-permute-done.9.refs_4_ = bf16[2,2,64,256]{3,2,1,0:T(8,128)(2,1)S(1)} collective-permute-done((bf16[2,2,64,256]{3,2,1,0:T(8,128)(2,1)S(1)}, bf16[2,2,64,256]{3,2,1,0:T(8,128)(2,1)S(1)}, u32[]{:S(2)}, u32[]{:S(2)}) %collective-permute-start.9) | collective-permute-done | bytes 131104 | tf_op jit(solution)/shard_map/ppermute | solution.py:70
  33.8 1.2 %conv.1 = (bf16[768,512]{1,0:T(8,128)(2,1)S(1)}, bf16[512,256]{1,0:T(8,128)(2,1)S(1)}, bf16[544,256]{1,0:T(8,128)(2,1)S(1)}, f32[544,256]{1,0:T(8,128)S(1)}, f32[544,512]{1,0:T(8,128)S(1)}) custom-call(f32[544,512]{1,0:T(8,128)S(1)} %get-tuple-element.100.start_ref, bf16[544,512]{1,0:T(8,128)(2,1)S(1)} %get-tuple-element.103.act_ref, ...), custom_call_target="tpu_custom_call" | custom-call | tf_op jit(solution)/shard_map/conv/pallas_call | solution.py:731
  35.1 3.3 %quant.1 = (bf16[2,256,512]{2,1,0:T(8,128)(2,1)}, s16[2,1056,256]{2,1,0:T(8,128)(2,1)S(1)}, bf16[544,512]{1,0:T(8,128)(2,1)S(1)}, f32[512,512]{1,0:T(8,128)S(1)}, bf16[4,512,512]{2,1,0:T(8,128)(2,1)S(1)}) custom-call(f32[544,256]{1,0:T(8,128)S(1)} %get-tuple-element.99.mask_ref, f32[544,512]{1,0:T(8,128)S(1)} %get-tuple-element.108.latent_ref, ...), custom_call_target="tpu_custom_call" | custom-call | tf_op jit(solution)/shard_map/quant/pallas_call | solution.py:743
  38.6 1.4 %backward.1 = (bf16[544,256]{1,0:T(8,128)(2,1)S(1)}, f32[2,512,256]{2,1,0:T(8,128)S(1)}, f32[2,512,256]{2,1,0:T(8,128)S(1)}) custom-call(bf16[512,1536]{1,0:T(8,128)(2,1)S(1)} %get-tuple-element.115.window_ref, bf16[544,256]{1,0:T(8,128)(2,1)S(1)} %get-tuple-element.116.gated_ref, bf16[544,512]{1,0:T(8,128)(2,1)S(1)} %get-tuple-element.117.bg_ref, ...), custom_call_target="tpu_custom_call" | custom-call | tf_op jit(solution)/shard_map/backward/pallas_call | solution.py:774
  40.4 1.2 %keep.1.keep_ref = f32[2,1024,256]{2,1,0:T(8,128)S(1)} custom-call(bf16[4,1024,512]{2,1,0:T(8,128)(2,1)S(1)} %get-tuple-element.111.hott_ref, bf16[4,512,512]{2,1,0:T(8,128)(2,1)S(1)} %get-tuple-element.122.cgs_ref), custom_call_target="tpu_custom_call" | custom-call | tf_op jit(solution)/shard_map/keep/pallas_call | solution.py:761
  42.4 1.6 %collective-permute-start.21 = (s16[528,256]{1,0:T(8,128)(2,1)S(1)}, s16[528,256]{1,0:T(8,128)(2,1)S(1)}, u32[]{:S(2)}, u32[]{:S(2)}) collective-permute-start(s16[528,256]{1,0:T(8,128)(2,1)S(1)} %get-tuple-element.129), channel_id=1, source_target_pairs={{0,4},{1,5},{2,6},{3,7},{4,0},{5,1},{6,2},{7,3},{8,12},{9,13},{10,... | collective-permute-start | bytes 811016 | tf_op jit(solution)/shard_map/ppermute | solution.py:70
  43.9 2.0 %collective-permute-start.23 = (s16[528,256]{1,0:T(8,128)(2,1)S(1)}, s16[528,256]{1,0:T(8,128)(2,1)S(1)}, u32[]{:S(2)}, u32[]{:S(2)}) collective-permute-start(s16[528,256]{1,0:T(8,128)(2,1)S(1)} %get-tuple-element.131), channel_id=1, source_target_pairs={{0,6},{1,7},{2,4},{3,5},{4,2},{5,3},{6,0},{7,1},{8,14},{9,15},{10,... | collective-permute-start | bytes 811016 | tf_op jit(solution)/shard_map/ppermute | solution.py:70
  46.4 1.6 %collective-permute-start.26 = (s16[272,256]{1,0:T(8,128)(2,1)S(1)}, s16[272,256]{1,0:T(8,128)(2,1)S(1)}, u32[]{:S(2)}, u32[]{:S(2)}) collective-permute-start(s16[272,256]{1,0:T(8,128)(2,1)S(1)} %get-tuple-element.137), channel_id=1, source_target_pairs={{0,16},{1,17},{2,18},{3,19},{4,20},{5,21},{6,22},{7,23},{8,24},{9,... | collective-permute-start | bytes 417800 | tf_op jit(solution)/shard_map/ppermute | solution.py:70
  48.0 2.6 %collective-permute-start.27 = (s16[272,256]{1,0:T(8,128)(2,1)S(1)}, s16[272,256]{1,0:T(8,128)(2,1)S(1)}, u32[]{:S(2)}, u32[]{:S(2)}) collective-permute-start(s16[272,256]{1,0:T(8,128)(2,1)S(1)} %get-tuple-element.138), channel_id=1, source_target_pairs={{0,8},{1,9},{2,10},{3,11},{4,12},{5,13},{6,14},{7,15},{8,0},{9,1},... | collective-permute-start | bytes 417800 | tf_op jit(solution)/shard_map/ppermute | solution.py:70
  50.6 1.2 %collective-permute-done.21.refs_0_ = s16[528,256]{1,0:T(8,128)(2,1)S(1)} collective-permute-done((s16[528,256]{1,0:T(8,128)(2,1)S(1)}, s16[528,256]{1,0:T(8,128)(2,1)S(1)}, u32[]{:S(2)}, u32[]{:S(2)}) %collective-permute-start.21) | collective-permute-done | bytes 270368 | tf_op jit(solution)/shard_map/ppermute | solution.py:70
  51.8 3.5 %collective-permute-start.28 = (s16[272,256]{1,0:T(8,128)(2,1)S(1)}, s16[272,256]{1,0:T(8,128)(2,1)S(1)}, u32[]{:S(2)}, u32[]{:S(2)}) collective-permute-start(s16[272,256]{1,0:T(8,128)(2,1)S(1)} %get-tuple-element.139), channel_id=1, source_target_pairs={{0,24},{1,25},{2,26},{3,27},{4,28},{5,29},{6,30},{7,31},{8,16},{9,... | collective-permute-start | bytes 417800 | tf_op jit(solution)/shard_map/ppermute | solution.py:70
  55.3 2.2 %features.1 = f32[2,256,512]{2,1,0:T(8,128)} custom-call(s32[2]{0:T(128)S(1)} %copy-done.12, f32[544,512]{1,0:T(8,128)S(1)} %get-tuple-element.100.start_ref, f32[512,512]{1,0:T(8,128)S(1)} %get-tuple-element.114.lg_ref, bf16[544,256]{1,0:T(8,128)(2,1)S(1)} %get-tuple-element.120.hg_ref, bf16[768,512]{1,0:T(8,128)(2,1)S(1)} %get-tuple-element.121.d_ref), custom_call_target="tpu_custom_call" | custom-call | tf_op jit(solution)/shard_map/features/pallas_call | solution.py:783
  59.0 3.5 %collective-permute-start.32 = (s16[136,256]{1,0:T(8,128)(2,1)S(1)}, s16[136,256]{1,0:T(8,128)(2,1)S(1)}, u32[]{:S(2)}, u32[]{:S(2)}) collective-permute-start(s16[136,256]{1,0:T(8,128)(2,1)S(1)} %get-tuple-element.146), channel_id=1, source_target_pairs={{0,16},{1,17},{2,18},{3,19},{4,20},{5,21},{6,22},{7,23},{8,24},{9,... | collective-permute-start | bytes 208904 | tf_op jit(solution)/shard_map/ppermute | solution.py:70
  63.3 3.0 %collective-permute-start.33 = (s16[136,256]{1,0:T(8,128)(2,1)S(1)}, s16[136,256]{1,0:T(8,128)(2,1)S(1)}, u32[]{:S(2)}, u32[]{:S(2)}) collective-permute-start(s16[136,256]{1,0:T(8,128)(2,1)S(1)} %get-tuple-element.147), channel_id=1, source_target_pairs={{0,24},{1,25},{2,26},{3,27},{4,28},{5,29},{6,30},{7,31},{8,16},{9,... | collective-permute-start | bytes 208904 | tf_op jit(solution)/shard_map/ppermute | solution.py:70
  67.1 1.3 %collective-permute-start.30 = (s16[72,256]{1,0:T(8,128)(2,1)S(1)}, s16[72,256]{1,0:T(8,128)(2,1)S(1)}, u32[]{:S(2)}, u32[]{:S(2)}) collective-permute-start(s16[72,256]{1,0:T(8,128)(2,1)S(1)} %get-tuple-element.142), channel_id=1, source_target_pairs={{0,2},{1,3},{2,0},{3,1},{4,6},{5,7},{6,4},{7,5},{8,10},{9,11},{10,... | collective-permute-start | bytes 110600 | tf_op jit(solution)/shard_map/ppermute | solution.py:70
  68.3 1.7 %collective-permute-start.31 = (s16[72,256]{1,0:T(8,128)(2,1)S(1)}, s16[72,256]{1,0:T(8,128)(2,1)S(1)}, u32[]{:S(2)}, u32[]{:S(2)}) collective-permute-start(s16[72,256]{1,0:T(8,128)(2,1)S(1)} %get-tuple-element.143), channel_id=1, source_target_pairs={{0,6},{1,7},{2,4},{3,5},{4,2},{5,3},{6,0},{7,1},{8,14},{9,15},{10,... | collective-permute-start | bytes 110600 | tf_op jit(solution)/shard_map/ppermute | solution.py:70
  71.0 2.2 %collective-permute-done.31.refs_3_ = s16[72,256]{1,0:T(8,128)(2,1)S(1)} collective-permute-done((s16[72,256]{1,0:T(8,128)(2,1)S(1)}, s16[72,256]{1,0:T(8,128)(2,1)S(1)}, u32[]{:S(2)}, u32[]{:S(2)}) %collective-permute-start.31) | collective-permute-done | bytes 36896 | tf_op jit(solution)/shard_map/ppermute | solution.py:70
  74.8 2.6 %all-to-all-start = ((f32[32,8,128]{2,1,0:T(8,128)}), f32[32,8,128]{2,1,0:T(8,128)S(1)}, u32[]{:S(2)}, u32[]{:S(2)}) async-start(f32[32,8,128]{2,1,0:T(8,128)} %get-tuple-element.148), calls=%async_computation | async-start | bytes 262144 | tf_op jit(solution)/shard_map/all_to_all | solution.py:863
  77.6 2.2 %collective-permute-done.35.refs_2_ = f32[192,256]{1,0:T(8,128)S(1)} collective-permute-done((f32[192,256]{1,0:T(8,128)S(1)}, f32[192,256]{1,0:T(8,128)S(1)}, u32[]{:S(2)}, u32[]{:S(2)}) %collective-permute-start.35) | collective-permute-done | bytes 196640 | tf_op jit(solution)/shard_map/ppermute | solution.py:70
  80.6 5.0 %all-to-all-done.square_ref = f32[32,8,128]{2,1,0:T(8,128)S(1)} async-done(((f32[32,8,128]{2,1,0:T(8,128)}), f32[32,8,128]{2,1,0:T(8,128)S(1)}, u32[]{:S(2)}, u32[]{:S(2)}) %all-to-all-start) | async-done | bytes 131104 | tf_op jit(solution)/shard_map/all_to_all | solution.py:863
  85.7 3.0 %update.1 = (f32[1,1]{1,0:T(1,128)}, f32[3,32,512]{2,1,0:T(8,128)}, f32[3,32,512]{2,1,0:T(8,128)}, f32[3,32,512]{2,1,0:T(8,128)}, f32[64,256]{1,0:T(8,128)}, /*i...) custom-call(f32[2]{0:T(128)S(1)} %pad_maximum_fusion.2.fix_ref, ...), custom_call_target="tpu_custom_call" | custom-call | tf_op jit(solution)/shard_map/update/pallas_call | solution.py:869
  (88 shorter events, 15.4 us)
Async XLA Ops:
  1.8 8.5 %collective-permute-start.5 = (bf16[2,64,256]{2,1,0:T(8,128)(2,1)S(1)}, bf16[2,64,256]{2,1,0:T(8,128)(2,1)S(1)}, u32[]{:S(2)}, u32[]{:S(2)}) collective-permute-start(bf16[2,64,256]{2,1,0:T(8,128)(2,1)S(1)} %get-tuple-element.102), channel_id=1, source_target_pairs={{0,4},{1,5},{2,6},{3,7},{4,0},{5,1},{6,2},{7,3},{8,12},{9,13},{10,... | collective-permute-start | bytes 196616 | tf_op jit(solution)/shard_map/ppermute | solution.py:70
  4.8 6.2 %collective-permute-start.2 = (bf16[128,256]{1,0:T(8,128)(2,1)S(1)}, bf16[128,256]{1,0:T(8,128)(2,1)S(1)}, u32[]{:S(2)}, u32[]{:S(2)}) collective-permute-start(bf16[128,256]{1,0:T(8,128)(2,1)S(1)} %get-tuple-element.91), channel_id=1, source_target_pairs={{0,8},{1,9},{2,10},{3,11},{4,12},{5,13},{6,14},{7,15},{8,0},{9,1},... | collective-permute-start | bytes 196616 | tf_op jit(solution)/shard_map/ppermute | solution.py:70
  6.3 7.0 %collective-permute-start.3 = (bf16[128,256]{1,0:T(8,128)(2,1)S(1)}, bf16[128,256]{1,0:T(8,128)(2,1)S(1)}, u32[]{:S(2)}, u32[]{:S(2)}) collective-permute-start(bf16[128,256]{1,0:T(8,128)(2,1)S(1)} %get-tuple-element.91), channel_id=1, source_target_pairs={{0,16},{1,17},{2,18},{3,19},{4,20},{5,21},{6,22},{7,23},{8,24},{9,... | collective-permute-start | bytes 196616 | tf_op jit(solution)/shard_map/ppermute | solution.py:70
  8.9 6.2 %collective-permute-start.4 = (bf16[128,256]{1,0:T(8,128)(2,1)S(1)}, bf16[128,256]{1,0:T(8,128)(2,1)S(1)}, u32[]{:S(2)}, u32[]{:S(2)}) collective-permute-start(bf16[128,256]{1,0:T(8,128)(2,1)S(1)} %get-tuple-element.91), channel_id=1, source_target_pairs={{0,24},{1,25},{2,26},{3,27},{4,28},{5,29},{6,30},{7,31},{8,16},{9,... | collective-permute-start | bytes 196616 | tf_op jit(solution)/shard_map/ppermute | solution.py:70
  10.1 6.4 %collective-permute-start = (bf16[2,16,1024]{2,1,0:T(8,128)(2,1)S(1)}, bf16[2,16,1024]{2,1,0:T(8,128)(2,1)S(1)}, u32[]{:S(2)}, u32[]{:S(2)}) collective-permute-start(bf16[2,16,1024]{2,1,0:T(8,128)(2,1)S(1)} %get-tuple-element.89), channel_id=1, source_target_pairs={{0,1},{1,0},{2,3},{3,2},{4,5},{5,4},{6,7},{7,6},{8,9},{9,8},{10,11... | collective-permute-start | bytes 196616 | tf_op jit(solution)/shard_map/ppermute | solution.py:677
  10.2 6.3 %collective-permute-start.1 = (bf16[2,16,1024]{2,1,0:T(8,128)(2,1)S(1)}, bf16[2,16,1024]{2,1,0:T(8,128)(2,1)S(1)}, u32[]{:S(2)}, u32[]{:S(2)}) collective-permute-start(bf16[2,16,1024]{2,1,0:T(8,128)(2,1)S(1)} %get-tuple-element.90), channel_id=1, source_target_pairs={{1,2},{2,1},{5,6},{6,5},{9,10},{10,9},{13,14},{14,13},{17,18},{18,... | collective-permute-start | bytes 196616 | tf_op jit(solution)/shard_map/ppermute | solution.py:679
  10.9 8.3 %collective-permute-start.6 = (bf16[2,2,64,256]{3,2,1,0:T(8,128)(2,1)S(1)}, bf16[2,2,64,256]{3,2,1,0:T(8,128)(2,1)S(1)}, u32[]{:S(2)}, u32[]{:S(2)}) collective-permute-start(bf16[2,2,64,256]{3,2,1,0:T(8,128)(2,1)S(1)} %pad_maximum_fusion.1.refs_0_), channel_id=1, source_target_pairs={{0,8},{1,9},{2,10},{3,11},{4,12},{5,13},{6,14},{7,15},{8,0},{9,1},... | collective-permute-start | bytes 393224 | tf_op jit(solution)/shard_map/ppermute | solution.py:70
  13.3 12.5 %collective-permute-start.7 = (bf16[2,2,64,256]{3,2,1,0:T(8,128)(2,1)S(1)}, bf16[2,2,64,256]{3,2,1,0:T(8,128)(2,1)S(1)}, u32[]{:S(2)}, u32[]{:S(2)}) collective-permute-start(bf16[2,2,64,256]{3,2,1,0:T(8,128)(2,1)S(1)} %pad_maximum_fusion.1.refs_0_), channel_id=1, source_target_pairs={{0,16},{1,17},{2,18},{3,19},{4,20},{5,21},{6,22},{7,23},{8,24},{9,... | collective-permute-start | bytes 393224 | tf_op jit(solution)/shard_map/ppermute | solution.py:70
  15.2 10.7 %collective-permute-start.8 = (bf16[2,2,64,256]{3,2,1,0:T(8,128)(2,1)S(1)}, bf16[2,2,64,256]{3,2,1,0:T(8,128)(2,1)S(1)}, u32[]{:S(2)}, u32[]{:S(2)}) collective-permute-start(bf16[2,2,64,256]{3,2,1,0:T(8,128)(2,1)S(1)} %pad_maximum_fusion.1.refs_0_), channel_id=1, source_target_pairs={{0,24},{1,25},{2,26},{3,27},{4,28},{5,29},{6,30},{7,31},{8,16},{9,... | collective-permute-start | bytes 393224 | tf_op jit(solution)/shard_map/ppermute | solution.py:70
  16.6 11.4 %collective-permute-start.13 = (bf16[4,128,256]{2,1,0:T(8,128)(2,1)S(1)}, bf16[4,128,256]{2,1,0:T(8,128)(2,1)S(1)}, u32[]{:S(2)}, u32[]{:S(2)}) collective-permute-start(bf16[4,128,256]{2,1,0:T(8,128)(2,1)S(1)} %pad_maximum_fusion.refs_0_), channel_id=1, source_target_pairs={{0,4},{1,5},{2,6},{3,7},{4,0},{5,1},{6,2},{7,3},{8,12},{9,13},{10,... | collective-permute-start | bytes 786440 | tf_op jit(solution)/shard_map/ppermute | solution.py:70
  17.2 14.5 %collective-permute-start.16 = (bf16[4,128,256]{2,1,0:T(8,128)(2,1)S(1)}, bf16[4,128,256]{2,1,0:T(8,128)(2,1)S(1)}, u32[]{:S(2)}, u32[]{:S(2)}) collective-permute-start(bf16[4,128,256]{2,1,0:T(8,128)(2,1)S(1)} %pad_maximum_fusion.refs_0_), channel_id=1, source_target_pairs={{0,2},{1,3},{2,0},{3,1},{4,6},{5,7},{6,4},{7,5},{8,10},{9,11},{10,... | collective-permute-start | bytes 786440 | tf_op jit(solution)/shard_map/ppermute | solution.py:70
  19.2 12.5 %collective-permute-start.17 = (bf16[4,128,256]{2,1,0:T(8,128)(2,1)S(1)}, bf16[4,128,256]{2,1,0:T(8,128)(2,1)S(1)}, u32[]{:S(2)}, u32[]{:S(2)}) collective-permute-start(bf16[4,128,256]{2,1,0:T(8,128)(2,1)S(1)} %pad_maximum_fusion.refs_0_), channel_id=1, source_target_pairs={{0,6},{1,7},{2,4},{3,5},{4,2},{5,3},{6,0},{7,1},{8,14},{9,15},{10,... | collective-permute-start | bytes 786440 | tf_op jit(solution)/shard_map/ppermute | solution.py:70
  27.4 4.8 %collective-permute-start.12 = (bf16[2,2,64,256]{3,2,1,0:T(8,128)(2,1)S(1)}, bf16[2,2,64,256]{3,2,1,0:T(8,128)(2,1)S(1)}, u32[]{:S(2)}, u32[]{:S(2)}) collective-permute-start(bf16[2,2,64,256]{3,2,1,0:T(8,128)(2,1)S(1)} %collective-permute-done.8.refs_3_), channel_id=1, source_target_pairs={{0,1},{1,0},{2,3},{3,2},{4,5},{5,4},{6,7},{7,6},{8,9},{9,8},{10,11... | collective-permute-start | bytes 393224 | tf_op jit(solution)/shard_map/ppermute | solution.py:70
  27.8 7.3 %collective-permute-start.14 = (bf16[4,128,256]{2,1,0:T(8,128)(2,1)S(1)}, bf16[4,128,256]{2,1,0:T(8,128)(2,1)S(1)}, u32[]{:S(2)}, u32[]{:S(2)}) collective-permute-start(bf16[4,128,256]{2,1,0:T(8,128)(2,1)S(1)} %pad_maximum_fusion.refs_0_), channel_id=1, source_target_pairs={{0,1},{1,0},{2,3},{3,2},{4,5},{5,4},{6,7},{7,6},{8,9},{9,8},{10,11... | collective-permute-start | bytes 786440 | tf_op jit(solution)/shard_map/ppermute | solution.py:70
  27.9 7.1 %collective-permute-start.15 = (bf16[4,128,256]{2,1,0:T(8,128)(2,1)S(1)}, bf16[4,128,256]{2,1,0:T(8,128)(2,1)S(1)}, u32[]{:S(2)}, u32[]{:S(2)}) collective-permute-start(bf16[4,128,256]{2,1,0:T(8,128)(2,1)S(1)} %collective-permute-done.13.refs_1_), channel_id=1, source_target_pairs={{0,1},{1,0},{2,3},{3,2},{4,5},{5,4},{6,7},{7,6},{8,9},{9,8},{10,11... | collective-permute-start | bytes 786440 | tf_op jit(solution)/shard_map/ppermute | solution.py:70
  31.7 3.4 %collective-permute-start.19 = (bf16[4,128,256]{2,1,0:T(8,128)(2,1)S(1)}, bf16[4,128,256]{2,1,0:T(8,128)(2,1)S(1)}, u32[]{:S(2)}, u32[]{:S(2)}) collective-permute-start(bf16[4,128,256]{2,1,0:T(8,128)(2,1)S(1)} %collective-permute-done.17.refs_5_), channel_id=1, source_target_pairs={{0,1},{1,0},{2,3},{3,2},{4,5},{5,4},{6,7},{7,6},{8,9},{9,8},{10,11... | collective-permute-start | bytes 786440 | tf_op jit(solution)/shard_map/ppermute | solution.py:70
  40.0 5.9 %collective-permute-start.25 = (f32[2,512,256]{2,1,0:T(8,128)S(1)}, f32[2,512,256]{2,1,0:T(8,128)S(1)}, u32[]{:S(2)}, u32[]{:S(2)}) collective-permute-start(f32[2,512,256]{2,1,0:T(8,128)S(1)} %get-tuple-element.134), channel_id=1, source_target_pairs={{0,1},{1,0},{2,3},{3,2},{4,5},{5,4},{6,7},{7,6},{8,9},{9,8},{10,11... | collective-permute-start | bytes 3145736 | tf_op jit(solution)/shard_map/ppermute | solution.py:70
  42.4 9.4 %collective-permute-start.21 = (s16[528,256]{1,0:T(8,128)(2,1)S(1)}, s16[528,256]{1,0:T(8,128)(2,1)S(1)}, u32[]{:S(2)}, u32[]{:S(2)}) collective-permute-start(s16[528,256]{1,0:T(8,128)(2,1)S(1)} %get-tuple-element.129), channel_id=1, source_target_pairs={{0,4},{1,5},{2,6},{3,7},{4,0},{5,1},{6,2},{7,3},{8,12},{9,13},{10,... | collective-permute-start | bytes 811016 | tf_op jit(solution)/shard_map/ppermute | solution.py:70
  43.9 14.0 %collective-permute-start.22 = (s16[528,256]{1,0:T(8,128)(2,1)S(1)}, s16[528,256]{1,0:T(8,128)(2,1)S(1)}, u32[]{:S(2)}, u32[]{:S(2)}) collective-permute-start(s16[528,256]{1,0:T(8,128)(2,1)S(1)} %get-tuple-element.130), channel_id=1, source_target_pairs={{0,2},{1,3},{2,0},{3,1},{4,6},{5,7},{6,4},{7,5},{8,10},{9,11},{10,... | collective-permute-start | bytes 811016 | tf_op jit(solution)/shard_map/ppermute | solution.py:70
  43.9 14.0 %collective-permute-start.23 = (s16[528,256]{1,0:T(8,128)(2,1)S(1)}, s16[528,256]{1,0:T(8,128)(2,1)S(1)}, u32[]{:S(2)}, u32[]{:S(2)}) collective-permute-start(s16[528,256]{1,0:T(8,128)(2,1)S(1)} %get-tuple-element.131), channel_id=1, source_target_pairs={{0,6},{1,7},{2,4},{3,5},{4,2},{5,3},{6,0},{7,1},{8,14},{9,15},{10,... | collective-permute-start | bytes 811016 | tf_op jit(solution)/shard_map/ppermute | solution.py:70
  46.4 19.8 %collective-permute-start.26 = (s16[272,256]{1,0:T(8,128)(2,1)S(1)}, s16[272,256]{1,0:T(8,128)(2,1)S(1)}, u32[]{:S(2)}, u32[]{:S(2)}) collective-permute-start(s16[272,256]{1,0:T(8,128)(2,1)S(1)} %get-tuple-element.137), channel_id=1, source_target_pairs={{0,16},{1,17},{2,18},{3,19},{4,20},{5,21},{6,22},{7,23},{8,24},{9,... | collective-permute-start | bytes 417800 | tf_op jit(solution)/shard_map/ppermute | solution.py:70
  48.0 18.2 %collective-permute-start.27 = (s16[272,256]{1,0:T(8,128)(2,1)S(1)}, s16[272,256]{1,0:T(8,128)(2,1)S(1)}, u32[]{:S(2)}, u32[]{:S(2)}) collective-permute-start(s16[272,256]{1,0:T(8,128)(2,1)S(1)} %get-tuple-element.138), channel_id=1, source_target_pairs={{0,8},{1,9},{2,10},{3,11},{4,12},{5,13},{6,14},{7,15},{8,0},{9,1},... | collective-permute-start | bytes 417800 | tf_op jit(solution)/shard_map/ppermute | solution.py:70
  51.8 14.5 %collective-permute-start.28 = (s16[272,256]{1,0:T(8,128)(2,1)S(1)}, s16[272,256]{1,0:T(8,128)(2,1)S(1)}, u32[]{:S(2)}, u32[]{:S(2)}) collective-permute-start(s16[272,256]{1,0:T(8,128)(2,1)S(1)} %get-tuple-element.139), channel_id=1, source_target_pairs={{0,24},{1,25},{2,26},{3,27},{4,28},{5,29},{6,30},{7,31},{8,16},{9,... | collective-permute-start | bytes 417800 | tf_op jit(solution)/shard_map/ppermute | solution.py:70
  58.3 4.9 %collective-permute-start.24 = (s16[136,256]{1,0:T(8,128)(2,1)S(1)}, s16[136,256]{1,0:T(8,128)(2,1)S(1)}, u32[]{:S(2)}, u32[]{:S(2)}) collective-permute-start(s16[136,256]{1,0:T(8,128)(2,1)S(1)} %get-tuple-element.132), channel_id=1, source_target_pairs={{0,8},{1,9},{2,10},{3,11},{4,12},{5,13},{6,14},{7,15},{8,0},{9,1},... | collective-permute-start | bytes 208904 | tf_op jit(solution)/shard_map/ppermute | solution.py:70
  59.0 11.0 %collective-permute-start.32 = (s16[136,256]{1,0:T(8,128)(2,1)S(1)}, s16[136,256]{1,0:T(8,128)(2,1)S(1)}, u32[]{:S(2)}, u32[]{:S(2)}) collective-permute-start(s16[136,256]{1,0:T(8,128)(2,1)S(1)} %get-tuple-element.146), channel_id=1, source_target_pairs={{0,16},{1,17},{2,18},{3,19},{4,20},{5,21},{6,22},{7,23},{8,24},{9,... | collective-permute-start | bytes 208904 | tf_op jit(solution)/shard_map/ppermute | solution.py:70
  63.3 6.8 %collective-permute-start.33 = (s16[136,256]{1,0:T(8,128)(2,1)S(1)}, s16[136,256]{1,0:T(8,128)(2,1)S(1)}, u32[]{:S(2)}, u32[]{:S(2)}) collective-permute-start(s16[136,256]{1,0:T(8,128)(2,1)S(1)} %get-tuple-element.147), channel_id=1, source_target_pairs={{0,24},{1,25},{2,26},{3,27},{4,28},{5,29},{6,30},{7,31},{8,16},{9,... | collective-permute-start | bytes 208904 | tf_op jit(solution)/shard_map/ppermute | solution.py:70
  66.5 4.0 %collective-permute-start.29 = (s16[72,256]{1,0:T(8,128)(2,1)S(1)}, s16[72,256]{1,0:T(8,128)(2,1)S(1)}, u32[]{:S(2)}, u32[]{:S(2)}) collective-permute-start(s16[72,256]{1,0:T(8,128)(2,1)S(1)} %get-tuple-element.141), channel_id=1, source_target_pairs={{0,4},{1,5},{2,6},{3,7},{4,0},{5,1},{6,2},{7,3},{8,12},{9,13},{10,... | collective-permute-start | bytes 110600 | tf_op jit(solution)/shard_map/ppermute | solution.py:70
  67.1 4.0 %collective-permute-start.30 = (s16[72,256]{1,0:T(8,128)(2,1)S(1)}, s16[72,256]{1,0:T(8,128)(2,1)S(1)}, u32[]{:S(2)}, u32[]{:S(2)}) collective-permute-start(s16[72,256]{1,0:T(8,128)(2,1)S(1)} %get-tuple-element.142), channel_id=1, source_target_pairs={{0,2},{1,3},{2,0},{3,1},{4,6},{5,7},{6,4},{7,5},{8,10},{9,11},{10,... | collective-permute-start | bytes 110600 | tf_op jit(solution)/shard_map/ppermute | solution.py:70
  68.3 4.9 %collective-permute-start.31 = (s16[72,256]{1,0:T(8,128)(2,1)S(1)}, s16[72,256]{1,0:T(8,128)(2,1)S(1)}, u32[]{:S(2)}, u32[]{:S(2)}) collective-permute-start(s16[72,256]{1,0:T(8,128)(2,1)S(1)} %get-tuple-element.143), channel_id=1, source_target_pairs={{0,6},{1,7},{2,4},{3,5},{4,2},{5,3},{6,0},{7,1},{8,14},{9,15},{10,... | collective-permute-start | bytes 110600 | tf_op jit(solution)/shard_map/ppermute | solution.py:70
  74.1 5.7 %collective-permute-start.35 = (f32[192,256]{1,0:T(8,128)S(1)}, f32[192,256]{1,0:T(8,128)S(1)}, u32[]{:S(2)}, u32[]{:S(2)}) collective-permute-start(f32[192,256]{1,0:T(8,128)S(1)} %get-tuple-element.149.refs_0_), channel_id=1, source_target_pairs={{0,2},{1,3},{2,0},{3,1},{4,6},{5,7},{6,4},{7,5},{8,10},{9,11},{10,... | collective-permute-start | bytes 589832 | tf_op jit(solution)/shard_map/ppermute | solution.py:70
  74.8 10.8 %all-to-all-start = ((f32[32,8,128]{2,1,0:T(8,128)}), f32[32,8,128]{2,1,0:T(8,128)S(1)}, u32[]{:S(2)}, u32[]{:S(2)}) async-start(f32[32,8,128]{2,1,0:T(8,128)} %get-tuple-element.148), calls=%async_computation | async-start | bytes 262144 | tf_op jit(solution)/shard_map/all_to_all | solution.py:863
  79.7 5.9 %collective-permute-start.36 = (f32[192,256]{1,0:T(8,128)S(1)}, f32[192,256]{1,0:T(8,128)S(1)}, u32[]{:S(2)}, u32[]{:S(2)}) collective-permute-start(f32[192,256]{1,0:T(8,128)S(1)} %collective-permute-done.35.refs_2_), channel_id=1, source_target_pairs={{0,1},{1,0},{2,3},{3,2},{4,5},{5,4},{6,7},{7,6},{8,9},{9,8},{10,11... | collective-permute-start | bytes 589832 | tf_op jit(solution)/shard_map/ppermute | solution.py:70
  (19 other events, 340.3 us)

commit v7 on v6

--- a/solution.py
+++ b/solution.py
@@ -714,7 +714,9 @@
 
     act, *line_d = lax.optimization_barrier((act, *line_d))
     pieces_d = line_d + [swap(v, 0, 1) for v in line_d]
-    turned = [swap(v, 0, 1) for v in plane_c]
+    held = list(plane_c)
+    held[3], pieces_d[4] = lax.optimization_barrier((held[3], pieces_d[4]))
+    turned = [swap(v, 0, 1) for v in held]
     pieces_c = plane_c[:2] + turned[:2] + plane_c[2:] + turned[2:]
 
     weights = (shape((KERNEL * HID, D), BF16), shape((D, HID), BF16))
@@ -848,7 +850,8 @@
     fg, parts_c[0] = lax.optimization_barrier((fg, parts_c[0]))
     parts_c = over_line(passed(parts_c, block, "codes"))
     parts_c[1], parts_d[0] = lax.optimization_barrier((parts_c[1], parts_d[0]))
-    parts_d = over_plane(passed(parts_d, small, "conv"))
+    parts_d = passed(parts_d, small, "conv")
+    parts_d = [parts_d[0], swap(parts_d[3], 1, 2), swap(parts_d[2], 0, 2), swap(parts_d[1], 1, 0)]
     total = small + block
     piece, squares = pl.pallas_call(
         functools.partial(final_kernel, (small, block), (4, half)),

time: 89.2 us -> 88.3 us (0.990)
  no operation moved by 1% of the time
where the time goes in v7:
time: 88.3 us; the launch traced here: 88 us
  starting transfers between devices  43.5 us (49%)
  Pallas kernels  22.1 us (25%)
  waiting for transfers between devices  20.2 us (23%)
  between operations  1.98 us (2%)
    ppermute x35, starting transfers between devices, swap(): return lax.ppermute(value, ('clip', 'tm'), pairs)  40.2 us
    ppermute x35, waiting for transfers between devices, swap(): return lax.ppermute(value, ('clip', 'tm'), pairs)  15 us
    all_to_all x1, waiting for transfers between devices, shards(): squares = lax.all_to_all(squares, ('clip', 'tm'), 0, 0, tiled=True)  5.22 us
    pallas_call x1, Pallas kernels, shards(): pl.pallas_call(functools.partial(own_kernel, ranks), out_shape=(shape((SL...  3.39 us
    pallas_call x1, Pallas kernels, shards(): pl.pallas_call(functools.partial(quant_kernel, ranks), out_shape=(shape((...  3.33 us
    pallas_call x1, Pallas kernels, shards(): pl.pallas_call(update_kernel, out_shape=(shape((1, 1), F32),) + tuple((sh...  2.98 us
    all_to_all x1, starting transfers between devices, shards(): squares = lax.all_to_all(squares, ('clip', 'tm'), 0, 0, tiled=True)  2.58 us
    pallas_call x1, Pallas kernels, shards(): pl.pallas_call(functools.partial(features_kernel, clips), out_shape=shape...  2.22 us
  transfers between devices with their start and end apart: 38, of which 13 were waited for; matrix products, arithmetic and copies ran while one was open for 0% of the time, Pallas kernels for 16%

profile of v7, /device:TPU:0, one launch (start us, length us, event | category | flops | bytes accessed | tf_op | source)
XLA Modules:
  0.0 88.0 jit_solution(9140270715009879083)
XLA Ops:
  1.8 3.0 %collective-permute-start.5 = (bf16[2,64,256]{2,1,0:T(8,128)(2,1)S(1)}, bf16[2,64,256]{2,1,0:T(8,128)(2,1)S(1)}, u32[]{:S(2)}, u32[]{:S(2)}) collective-permute-start(bf16[2,64,256]{2,1,0:T(8,128)(2,1)S(1)} %get-tuple-element.104), channel_id=1, source_target_pairs={{0,4},{1,5},{2,6},{3,7},{4,0},{5,1},{6,2},{7,3},{8,12},{9,13},{10,... | collective-permute-start | bytes 196616 | tf_op jit(solution)/shard_map/ppermute | solution.py:70
  4.8 1.6 %collective-permute-start.2 = (bf16[128,256]{1,0:T(8,128)(2,1)S(1)}, bf16[128,256]{1,0:T(8,128)(2,1)S(1)}, u32[]{:S(2)}, u32[]{:S(2)}) collective-permute-start(bf16[128,256]{1,0:T(8,128)(2,1)S(1)} %get-tuple-element.93), channel_id=1, source_target_pairs={{0,8},{1,9},{2,10},{3,11},{4,12},{5,13},{6,14},{7,15},{8,0},{9,1},... | collective-permute-start | bytes 196616 | tf_op jit(solution)/shard_map/ppermute | solution.py:70
  6.3 2.6 %collective-permute-start.3 = (bf16[128,256]{1,0:T(8,128)(2,1)S(1)}, bf16[128,256]{1,0:T(8,128)(2,1)S(1)}, u32[]{:S(2)}, u32[]{:S(2)}) collective-permute-start(bf16[128,256]{1,0:T(8,128)(2,1)S(1)} %get-tuple-element.93), channel_id=1, source_target_pairs={{0,16},{1,17},{2,18},{3,19},{4,20},{5,21},{6,22},{7,23},{8,24},{9,... | collective-permute-start | bytes 196616 | tf_op jit(solution)/shard_map/ppermute | solution.py:70
  11.7 1.6 %collective-permute-done.3 = bf16[128,256]{1,0:T(8,128)(2,1)S(1)} collective-permute-done((bf16[128,256]{1,0:T(8,128)(2,1)S(1)}, bf16[128,256]{1,0:T(8,128)(2,1)S(1)}, u32[]{:S(2)}, u32[]{:S(2)}) %collective-permute-start.3) | collective-permute-done | bytes 65568 | tf_op jit(solution)/shard_map/ppermute | solution.py:70
  13.3 1.8 %collective-permute-start.7 = (bf16[2,2,64,256]{3,2,1,0:T(8,128)(2,1)S(1)}, bf16[2,2,64,256]{3,2,1,0:T(8,128)(2,1)S(1)}, u32[]{:S(2)}, u32[]{:S(2)}) collective-permute-start(bf16[2,2,64,256]{3,2,1,0:T(8,128)(2,1)S(1)} %pad_maximum_fusion.1.refs_0_), channel_id=1, source_target_pairs={{0,16},{1,17},{2,18},{3,19},{4,20},{5,21},{6,22},{7,23},{8,24},{9,... | collective-permute-start | bytes 393224 | tf_op jit(solution)/shard_map/ppermute | solution.py:70
  15.2 1.3 %collective-permute-start.8 = (bf16[2,2,64,256]{3,2,1,0:T(8,128)(2,1)S(1)}, bf16[2,2,64,256]{3,2,1,0:T(8,128)(2,1)S(1)}, u32[]{:S(2)}, u32[]{:S(2)}) collective-permute-start(bf16[2,2,64,256]{3,2,1,0:T(8,128)(2,1)S(1)} %pad_maximum_fusion.1.refs_0_), channel_id=1, source_target_pairs={{0,24},{1,25},{2,26},{3,27},{4,28},{5,29},{6,30},{7,31},{8,16},{9,... | collective-permute-start | bytes 393224 | tf_op jit(solution)/shard_map/ppermute | solution.py:70
  16.6 2.1 %collective-permute-start.9 = (bf16[4,128,256]{2,1,0:T(8,128)(2,1)S(1)}, bf16[4,128,256]{2,1,0:T(8,128)(2,1)S(1)}, u32[]{:S(2)}, u32[]{:S(2)}) collective-permute-start(bf16[4,128,256]{2,1,0:T(8,128)(2,1)S(1)} %pad_maximum_fusion.refs_0_), channel_id=1, source_target_pairs={{0,6},{1,7},{2,4},{3,5},{4,2},{5,3},{6,0},{7,1},{8,14},{9,15},{10,... | collective-permute-start | bytes 786440 | tf_op jit(solution)/shard_map/ppermute | solution.py:70
  18.6 1.7 %collective-permute-start.14 = (bf16[4,128,256]{2,1,0:T(8,128)(2,1)S(1)}, bf16[4,128,256]{2,1,0:T(8,128)(2,1)S(1)}, u32[]{:S(2)}, u32[]{:S(2)}) collective-permute-start(bf16[4,128,256]{2,1,0:T(8,128)(2,1)S(1)} %pad_maximum_fusion.refs_0_), channel_id=1, source_target_pairs={{0,4},{1,5},{2,6},{3,7},{4,0},{5,1},{6,2},{7,3},{8,12},{9,13},{10,... | collective-permute-start | bytes 786440 | tf_op jit(solution)/shard_map/ppermute | solution.py:70
  20.7 3.4 %own.1 = (bf16[4,544,1024]{2,1,0:T(8,128)(2,1)S(1)}, bf16[4,1024,512]{2,1,0:T(8,128)(2,1)S(1)}) custom-call(s32[2]{0:T(128)S(1)} %copy-done.12, s32[4,2,256]{2,1,0:T(2,128)S(1)} %copy-done.11), custom_call_target="tpu_custom_call" | custom-call | tf_op jit(solution)/shard_map/own/pallas_call | solution.py:684
  24.1 1.7 %margin.1 = (f32[544,512]{1,0:T(8,128)S(1)}, bf16[544,512]{1,0:T(8,128)(2,1)S(1)}, bf16[512,1536]{1,0:T(8,128)(2,1)S(1)}, f32[32,512]{1,0:T(8,128)S(1)}, f32[544...) custom-call(s32[2]{0:T(128)S(1)} %copy-done.12, ...), custom_call_target="tpu_custom_call", output_to_operand_aliasing={{5}: (4, {})} | custom-call | tf_op jit(solution)/shard_map/margin/pallas_call | solution.py:698
  28.6 1.7 %collective-permute-done.14.refs_1_ = bf16[4,128,256]{2,1,0:T(8,128)(2,1)S(1)} collective-permute-done((bf16[4,128,256]{2,1,0:T(8,128)(2,1)S(1)}, bf16[4,128,256]{2,1,0:T(8,128)(2,1)S(1)}, u32[]{:S(2)}, u32[]{:S(2)}) %collective-permute-start.14) | collective-permute-done | bytes 262176 | tf_op jit(solution)/shard_map/ppermute | solution.py:70
  30.2 2.1 %collective-permute-done.17.refs_4_ = bf16[4,128,256]{2,1,0:T(8,128)(2,1)S(1)} collective-permute-done((bf16[4,128,256]{2,1,0:T(8,128)(2,1)S(1)}, bf16[4,128,256]{2,1,0:T(8,128)(2,1)S(1)}, u32[]{:S(2)}, u32[]{:S(2)}) %collective-permute-start.17) | collective-permute-done | bytes 262176 | tf_op jit(solution)/shard_map/ppermute | solution.py:70
  32.8 1.2 %collective-permute-done.13.refs_7_ = bf16[2,2,64,256]{3,2,1,0:T(8,128)(2,1)S(1)} collective-permute-done((bf16[2,2,64,256]{3,2,1,0:T(8,128)(2,1)S(1)}, bf16[2,2,64,256]{3,2,1,0:T(8,128)(2,1)S(1)}, u32[]{:S(2)}, u32[]{:S(2)}) %collective-permute-start.13) | collective-permute-done | bytes 131104 | tf_op jit(solution)/shard_map/ppermute | solution.py:70
  34.0 1.2 %conv.1 = (bf16[768,512]{1,0:T(8,128)(2,1)S(1)}, bf16[512,256]{1,0:T(8,128)(2,1)S(1)}, bf16[544,256]{1,0:T(8,128)(2,1)S(1)}, f32[544,256]{1,0:T(8,128)S(1)}, f32[544,512]{1,0:T(8,128)S(1)}) custom-call(f32[544,512]{1,0:T(8,128)S(1)} %get-tuple-element.102.start_ref, bf16[544,512]{1,0:T(8,128)(2,1)S(1)} %get-tuple-element.105.act_ref, ...), custom_call_target="tpu_custom_call" | custom-call | tf_op jit(solution)/shard_map/conv/pallas_call | solution.py:733
  35.3 3.3 %quant.1 = (bf16[2,256,512]{2,1,0:T(8,128)(2,1)}, s16[2,1056,256]{2,1,0:T(8,128)(2,1)S(1)}, bf16[544,512]{1,0:T(8,128)(2,1)S(1)}, f32[512,512]{1,0:T(8,128)S(1)}, bf16[4,512,512]{2,1,0:T(8,128)(2,1)S(1)}) custom-call(f32[544,256]{1,0:T(8,128)S(1)} %get-tuple-element.101.mask_ref, f32[544,512]{1,0:T(8,128)S(1)} %get-tuple-element.112.latent_ref, ...), custom_call_target="tpu_custom_call" | custom-call | tf_op jit(solution)/shard_map/quant/pallas_call | solution.py:745
  38.9 1.4 %backward.1 = (bf16[544,256]{1,0:T(8,128)(2,1)S(1)}, f32[2,512,256]{2,1,0:T(8,128)S(1)}, f32[2,512,256]{2,1,0:T(8,128)S(1)}) custom-call(bf16[512,1536]{1,0:T(8,128)(2,1)S(1)} %get-tuple-element.119.window_ref, bf16[544,256]{1,0:T(8,128)(2,1)S(1)} %get-tuple-element.120.gated_ref, bf16[544,512]{1,0:T(8,128)(2,1)S(1)} %get-tuple-element.121.bg_ref, ...), custom_call_target="tpu_custom_call" | custom-call | tf_op jit(solution)/shard_map/backward/pallas_call | solution.py:776
  40.7 1.2 %keep.1.keep_ref = f32[2,1024,256]{2,1,0:T(8,128)S(1)} custom-call(bf16[4,1024,512]{2,1,0:T(8,128)(2,1)S(1)} %get-tuple-element.115.hott_ref, bf16[4,512,512]{2,1,0:T(8,128)(2,1)S(1)} %get-tuple-element.126.cgs_ref), custom_call_target="tpu_custom_call" | custom-call | tf_op jit(solution)/shard_map/keep/pallas_call | solution.py:763
  44.2 1.9 %collective-permute-start.23 = (s16[528,256]{1,0:T(8,128)(2,1)S(1)}, s16[528,256]{1,0:T(8,128)(2,1)S(1)}, u32[]{:S(2)}, u32[]{:S(2)}) collective-permute-start(s16[528,256]{1,0:T(8,128)(2,1)S(1)} %get-tuple-element.135), channel_id=1, source_target_pairs={{0,6},{1,7},{2,4},{3,5},{4,2},{5,3},{6,0},{7,1},{8,14},{9,15},{10,... | collective-permute-start | bytes 811016 | tf_op jit(solution)/shard_map/ppermute | solution.py:70
  46.7 1.6 %collective-permute-start.26 = (s16[272,256]{1,0:T(8,128)(2,1)S(1)}, s16[272,256]{1,0:T(8,128)(2,1)S(1)}, u32[]{:S(2)}, u32[]{:S(2)}) collective-permute-start(s16[272,256]{1,0:T(8,128)(2,1)S(1)} %get-tuple-element.141), channel_id=1, source_target_pairs={{0,16},{1,17},{2,18},{3,19},{4,20},{5,21},{6,22},{7,23},{8,24},{9,... | collective-permute-start | bytes 417800 | tf_op jit(solution)/shard_map/ppermute | solution.py:70
  48.3 1.9 %collective-permute-start.27 = (s16[272,256]{1,0:T(8,128)(2,1)S(1)}, s16[272,256]{1,0:T(8,128)(2,1)S(1)}, u32[]{:S(2)}, u32[]{:S(2)}) collective-permute-start(s16[272,256]{1,0:T(8,128)(2,1)S(1)} %get-tuple-element.142), channel_id=1, source_target_pairs={{0,8},{1,9},{2,10},{3,11},{4,12},{5,13},{6,14},{7,15},{8,0},{9,1},... | collective-permute-start | bytes 417800 | tf_op jit(solution)/shard_map/ppermute | solution.py:70
  50.2 1.8 %collective-permute-done.21.refs_0_ = s16[528,256]{1,0:T(8,128)(2,1)S(1)} collective-permute-done((s16[528,256]{1,0:T(8,128)(2,1)S(1)}, s16[528,256]{1,0:T(8,128)(2,1)S(1)}, u32[]{:S(2)}, u32[]{:S(2)}) %collective-permute-start.21) | collective-permute-done | bytes 270368 | tf_op jit(solution)/shard_map/ppermute | solution.py:70
  52.0 2.9 %collective-permute-start.28 = (s16[272,256]{1,0:T(8,128)(2,1)S(1)}, s16[272,256]{1,0:T(8,128)(2,1)S(1)}, u32[]{:S(2)}, u32[]{:S(2)}) collective-permute-start(s16[272,256]{1,0:T(8,128)(2,1)S(1)} %get-tuple-element.143), channel_id=1, source_target_pairs={{0,24},{1,25},{2,26},{3,27},{4,28},{5,29},{6,30},{7,31},{8,16},{9,... | collective-permute-start | bytes 417800 | tf_op jit(solution)/shard_map/ppermute | solution.py:70
  54.9 2.2 %features.1 = f32[2,256,512]{2,1,0:T(8,128)} custom-call(s32[2]{0:T(128)S(1)} %copy-done.12, f32[544,512]{1,0:T(8,128)S(1)} %get-tuple-element.102.start_ref, f32[512,512]{1,0:T(8,128)S(1)} %get-tuple-element.118.lg_ref, bf16[544,256]{1,0:T(8,128)(2,1)S(1)} %get-tuple-element.124.hg_ref, bf16[768,512]{1,0:T(8,128)(2,1)S(1)} %get-tuple-element.125.d_ref), custom_call_target="tpu_custom_call" | custom-call | tf_op jit(solution)/shard_map/features/pallas_call | solution.py:785
  58.3 3.5 %collective-permute-start.32 = (s16[136,256]{1,0:T(8,128)(2,1)S(1)}, s16[136,256]{1,0:T(8,128)(2,1)S(1)}, u32[]{:S(2)}, u32[]{:S(2)}) collective-permute-start(s16[136,256]{1,0:T(8,128)(2,1)S(1)} %get-tuple-element.150), channel_id=1, source_target_pairs={{0,16},{1,17},{2,18},{3,19},{4,20},{5,21},{6,22},{7,23},{8,24},{9,... | collective-permute-start | bytes 208904 | tf_op jit(solution)/shard_map/ppermute | solution.py:70
  62.4 3.1 %collective-permute-start.33 = (s16[136,256]{1,0:T(8,128)(2,1)S(1)}, s16[136,256]{1,0:T(8,128)(2,1)S(1)}, u32[]{:S(2)}, u32[]{:S(2)}) collective-permute-start(s16[136,256]{1,0:T(8,128)(2,1)S(1)} %get-tuple-element.151), channel_id=1, source_target_pairs={{0,24},{1,25},{2,26},{3,27},{4,28},{5,29},{6,30},{7,31},{8,16},{9,... | collective-permute-start | bytes 208904 | tf_op jit(solution)/shard_map/ppermute | solution.py:70
  65.8 1.3 %collective-permute-start.29 = (s16[72,256]{1,0:T(8,128)(2,1)S(1)}, s16[72,256]{1,0:T(8,128)(2,1)S(1)}, u32[]{:S(2)}, u32[]{:S(2)}) collective-permute-start(s16[72,256]{1,0:T(8,128)(2,1)S(1)} %get-tuple-element.145), channel_id=1, source_target_pairs={{0,6},{1,7},{2,4},{3,5},{4,2},{5,3},{6,0},{7,1},{8,14},{9,15},{10,... | collective-permute-start | bytes 110600 | tf_op jit(solution)/shard_map/ppermute | solution.py:70
  68.1 1.2 %collective-permute-start.31 = (s16[72,256]{1,0:T(8,128)(2,1)S(1)}, s16[72,256]{1,0:T(8,128)(2,1)S(1)}, u32[]{:S(2)}, u32[]{:S(2)}) collective-permute-start(s16[72,256]{1,0:T(8,128)(2,1)S(1)} %get-tuple-element.147), channel_id=1, source_target_pairs={{0,4},{1,5},{2,6},{3,7},{4,0},{5,1},{6,2},{7,3},{8,12},{9,13},{10,... | collective-permute-start | bytes 110600 | tf_op jit(solution)/shard_map/ppermute | solution.py:70
  69.3 1.4 %collective-permute-done.29.refs_1_ = s16[72,256]{1,0:T(8,128)(2,1)S(1)} collective-permute-done((s16[72,256]{1,0:T(8,128)(2,1)S(1)}, s16[72,256]{1,0:T(8,128)(2,1)S(1)}, u32[]{:S(2)}, u32[]{:S(2)}) %collective-permute-start.29) | collective-permute-done | bytes 36896 | tf_op jit(solution)/shard_map/ppermute | solution.py:70
  73.9 2.6 %all-to-all-start = ((f32[32,8,128]{2,1,0:T(8,128)}), f32[32,8,128]{2,1,0:T(8,128)S(1)}, u32[]{:S(2)}, u32[]{:S(2)}) async-start(f32[32,8,128]{2,1,0:T(8,128)} %get-tuple-element.152), calls=%async_computation | async-start | bytes 262144 | tf_op jit(solution)/shard_map/all_to_all | solution.py:866
  76.7 1.9 %collective-permute-done.35.refs_2_ = f32[192,256]{1,0:T(8,128)S(1)} collective-permute-done((f32[192,256]{1,0:T(8,128)S(1)}, f32[192,256]{1,0:T(8,128)S(1)}, u32[]{:S(2)}, u32[]{:S(2)}) %collective-permute-start.35) | collective-permute-done | bytes 196640 | tf_op jit(solution)/shard_map/ppermute | solution.py:70
  79.5 5.2 %all-to-all-done.square_ref = f32[32,8,128]{2,1,0:T(8,128)S(1)} async-done(((f32[32,8,128]{2,1,0:T(8,128)}), f32[32,8,128]{2,1,0:T(8,128)S(1)}, u32[]{:S(2)}, u32[]{:S(2)}) %all-to-all-start) | async-done | bytes 131104 | tf_op jit(solution)/shard_map/all_to_all | solution.py:866
  84.8 3.0 %update.1 = (f32[1,1]{1,0:T(1,128)}, f32[3,32,512]{2,1,0:T(8,128)}, f32[3,32,512]{2,1,0:T(8,128)}, f32[3,32,512]{2,1,0:T(8,128)}, f32[64,256]{1,0:T(8,128)}, /*i...) custom-call(f32[2]{0:T(128)S(1)} %pad_maximum_fusion.2.fix_ref, ...), custom_call_target="tpu_custom_call" | custom-call | tf_op jit(solution)/shard_map/update/pallas_call | solution.py:872
  (88 shorter events, 17.5 us)
Async XLA Ops:
  1.8 8.5 %collective-permute-start.5 = (bf16[2,64,256]{2,1,0:T(8,128)(2,1)S(1)}, bf16[2,64,256]{2,1,0:T(8,128)(2,1)S(1)}, u32[]{:S(2)}, u32[]{:S(2)}) collective-permute-start(bf16[2,64,256]{2,1,0:T(8,128)(2,1)S(1)} %get-tuple-element.104), channel_id=1, source_target_pairs={{0,4},{1,5},{2,6},{3,7},{4,0},{5,1},{6,2},{7,3},{8,12},{9,13},{10,... | collective-permute-start | bytes 196616 | tf_op jit(solution)/shard_map/ppermute | solution.py:70
  4.8 6.2 %collective-permute-start.2 = (bf16[128,256]{1,0:T(8,128)(2,1)S(1)}, bf16[128,256]{1,0:T(8,128)(2,1)S(1)}, u32[]{:S(2)}, u32[]{:S(2)}) collective-permute-start(bf16[128,256]{1,0:T(8,128)(2,1)S(1)} %get-tuple-element.93), channel_id=1, source_target_pairs={{0,8},{1,9},{2,10},{3,11},{4,12},{5,13},{6,14},{7,15},{8,0},{9,1},... | collective-permute-start | bytes 196616 | tf_op jit(solution)/shard_map/ppermute | solution.py:70
  6.3 7.0 %collective-permute-start.3 = (bf16[128,256]{1,0:T(8,128)(2,1)S(1)}, bf16[128,256]{1,0:T(8,128)(2,1)S(1)}, u32[]{:S(2)}, u32[]{:S(2)}) collective-permute-start(bf16[128,256]{1,0:T(8,128)(2,1)S(1)} %get-tuple-element.93), channel_id=1, source_target_pairs={{0,16},{1,17},{2,18},{3,19},{4,20},{5,21},{6,22},{7,23},{8,24},{9,... | collective-permute-start | bytes 196616 | tf_op jit(solution)/shard_map/ppermute | solution.py:70
  8.9 6.2 %collective-permute-start.4 = (bf16[128,256]{1,0:T(8,128)(2,1)S(1)}, bf16[128,256]{1,0:T(8,128)(2,1)S(1)}, u32[]{:S(2)}, u32[]{:S(2)}) collective-permute-start(bf16[128,256]{1,0:T(8,128)(2,1)S(1)} %get-tuple-element.93), channel_id=1, source_target_pairs={{0,24},{1,25},{2,26},{3,27},{4,28},{5,29},{6,30},{7,31},{8,16},{9,... | collective-permute-start | bytes 196616 | tf_op jit(solution)/shard_map/ppermute | solution.py:70
  10.1 6.4 %collective-permute-start = (bf16[2,16,1024]{2,1,0:T(8,128)(2,1)S(1)}, bf16[2,16,1024]{2,1,0:T(8,128)(2,1)S(1)}, u32[]{:S(2)}, u32[]{:S(2)}) collective-permute-start(bf16[2,16,1024]{2,1,0:T(8,128)(2,1)S(1)} %get-tuple-element.91), channel_id=1, source_target_pairs={{0,1},{1,0},{2,3},{3,2},{4,5},{5,4},{6,7},{7,6},{8,9},{9,8},{10,11... | collective-permute-start | bytes 196616 | tf_op jit(solution)/shard_map/ppermute | solution.py:677
  10.2 6.3 %collective-permute-start.1 = (bf16[2,16,1024]{2,1,0:T(8,128)(2,1)S(1)}, bf16[2,16,1024]{2,1,0:T(8,128)(2,1)S(1)}, u32[]{:S(2)}, u32[]{:S(2)}) collective-permute-start(bf16[2,16,1024]{2,1,0:T(8,128)(2,1)S(1)} %get-tuple-element.92), channel_id=1, source_target_pairs={{1,2},{2,1},{5,6},{6,5},{9,10},{10,9},{13,14},{14,13},{17,18},{18,... | collective-permute-start | bytes 196616 | tf_op jit(solution)/shard_map/ppermute | solution.py:679
  10.9 9.4 %collective-permute-start.6 = (bf16[2,2,64,256]{3,2,1,0:T(8,128)(2,1)S(1)}, bf16[2,2,64,256]{3,2,1,0:T(8,128)(2,1)S(1)}, u32[]{:S(2)}, u32[]{:S(2)}) collective-permute-start(bf16[2,2,64,256]{3,2,1,0:T(8,128)(2,1)S(1)} %pad_maximum_fusion.1.refs_0_), channel_id=1, source_target_pairs={{0,8},{1,9},{2,10},{3,11},{4,12},{5,13},{6,14},{7,15},{8,0},{9,1},... | collective-permute-start | bytes 393224 | tf_op jit(solution)/shard_map/ppermute | solution.py:70
  13.3 12.5 %collective-permute-start.7 = (bf16[2,2,64,256]{3,2,1,0:T(8,128)(2,1)S(1)}, bf16[2,2,64,256]{3,2,1,0:T(8,128)(2,1)S(1)}, u32[]{:S(2)}, u32[]{:S(2)}) collective-permute-start(bf16[2,2,64,256]{3,2,1,0:T(8,128)(2,1)S(1)} %pad_maximum_fusion.1.refs_0_), channel_id=1, source_target_pairs={{0,16},{1,17},{2,18},{3,19},{4,20},{5,21},{6,22},{7,23},{8,24},{9,... | collective-permute-start | bytes 393224 | tf_op jit(solution)/shard_map/ppermute | solution.py:70
  15.2 10.7 %collective-permute-start.8 = (bf16[2,2,64,256]{3,2,1,0:T(8,128)(2,1)S(1)}, bf16[2,2,64,256]{3,2,1,0:T(8,128)(2,1)S(1)}, u32[]{:S(2)}, u32[]{:S(2)}) collective-permute-start(bf16[2,2,64,256]{3,2,1,0:T(8,128)(2,1)S(1)} %pad_maximum_fusion.1.refs_0_), channel_id=1, source_target_pairs={{0,24},{1,25},{2,26},{3,27},{4,28},{5,29},{6,30},{7,31},{8,16},{9,... | collective-permute-start | bytes 393224 | tf_op jit(solution)/shard_map/ppermute | solution.py:70
  16.6 11.5 %collective-permute-start.9 = (bf16[4,128,256]{2,1,0:T(8,128)(2,1)S(1)}, bf16[4,128,256]{2,1,0:T(8,128)(2,1)S(1)}, u32[]{:S(2)}, u32[]{:S(2)}) collective-permute-start(bf16[4,128,256]{2,1,0:T(8,128)(2,1)S(1)} %pad_maximum_fusion.refs_0_), channel_id=1, source_target_pairs={{0,6},{1,7},{2,4},{3,5},{4,2},{5,3},{6,0},{7,1},{8,14},{9,15},{10,... | collective-permute-start | bytes 786440 | tf_op jit(solution)/shard_map/ppermute | solution.py:70
  18.6 11.6 %collective-permute-start.14 = (bf16[4,128,256]{2,1,0:T(8,128)(2,1)S(1)}, bf16[4,128,256]{2,1,0:T(8,128)(2,1)S(1)}, u32[]{:S(2)}, u32[]{:S(2)}) collective-permute-start(bf16[4,128,256]{2,1,0:T(8,128)(2,1)S(1)} %pad_maximum_fusion.refs_0_), channel_id=1, source_target_pairs={{0,4},{1,5},{2,6},{3,7},{4,0},{5,1},{6,2},{7,3},{8,12},{9,13},{10,... | collective-permute-start | bytes 786440 | tf_op jit(solution)/shard_map/ppermute | solution.py:70
  20.3 12.0 %collective-permute-start.17 = (bf16[4,128,256]{2,1,0:T(8,128)(2,1)S(1)}, bf16[4,128,256]{2,1,0:T(8,128)(2,1)S(1)}, u32[]{:S(2)}, u32[]{:S(2)}) collective-permute-start(bf16[4,128,256]{2,1,0:T(8,128)(2,1)S(1)} %pad_maximum_fusion.refs_0_), channel_id=1, source_target_pairs={{0,2},{1,3},{2,0},{3,1},{4,6},{5,7},{6,4},{7,5},{8,10},{9,11},{10,... | collective-permute-start | bytes 786440 | tf_op jit(solution)/shard_map/ppermute | solution.py:70
  27.7 4.7 %collective-permute-start.12 = (bf16[2,2,64,256]{3,2,1,0:T(8,128)(2,1)S(1)}, bf16[2,2,64,256]{3,2,1,0:T(8,128)(2,1)S(1)}, u32[]{:S(2)}, u32[]{:S(2)}) collective-permute-start(bf16[2,2,64,256]{3,2,1,0:T(8,128)(2,1)S(1)} %collective-permute-done.7.refs_2_), channel_id=1, source_target_pairs={{0,1},{1,0},{2,3},{3,2},{4,5},{5,4},{6,7},{7,6},{8,9},{9,8},{10,11... | collective-permute-start | bytes 393224 | tf_op jit(solution)/shard_map/ppermute | solution.py:70
  28.1 7.2 %collective-permute-start.15 = (bf16[4,128,256]{2,1,0:T(8,128)(2,1)S(1)}, bf16[4,128,256]{2,1,0:T(8,128)(2,1)S(1)}, u32[]{:S(2)}, u32[]{:S(2)}) collective-permute-start(bf16[4,128,256]{2,1,0:T(8,128)(2,1)S(1)} %pad_maximum_fusion.refs_0_), channel_id=1, source_target_pairs={{0,1},{1,0},{2,3},{3,2},{4,5},{5,4},{6,7},{7,6},{8,9},{9,8},{10,11... | collective-permute-start | bytes 786440 | tf_op jit(solution)/shard_map/ppermute | solution.py:70
  28.2 7.1 %collective-permute-start.19 = (bf16[4,128,256]{2,1,0:T(8,128)(2,1)S(1)}, bf16[4,128,256]{2,1,0:T(8,128)(2,1)S(1)}, u32[]{:S(2)}, u32[]{:S(2)}) collective-permute-start(bf16[4,128,256]{2,1,0:T(8,128)(2,1)S(1)} %collective-permute-done.9.refs_5_), channel_id=1, source_target_pairs={{0,1},{1,0},{2,3},{3,2},{4,5},{5,4},{6,7},{7,6},{8,9},{9,8},{10,11... | collective-permute-start | bytes 786440 | tf_op jit(solution)/shard_map/ppermute | solution.py:70
  30.2 5.1 %collective-permute-start.16 = (bf16[4,128,256]{2,1,0:T(8,128)(2,1)S(1)}, bf16[4,128,256]{2,1,0:T(8,128)(2,1)S(1)}, u32[]{:S(2)}, u32[]{:S(2)}) collective-permute-start(bf16[4,128,256]{2,1,0:T(8,128)(2,1)S(1)} %collective-permute-done.14.refs_1_), channel_id=1, source_target_pairs={{0,1},{1,0},{2,3},{3,2},{4,5},{5,4},{6,7},{7,6},{8,9},{9,8},{10,11... | collective-permute-start | bytes 786440 | tf_op jit(solution)/shard_map/ppermute | solution.py:70
  40.2 5.9 %collective-permute-start.25 = (f32[2,512,256]{2,1,0:T(8,128)S(1)}, f32[2,512,256]{2,1,0:T(8,128)S(1)}, u32[]{:S(2)}, u32[]{:S(2)}) collective-permute-start(f32[2,512,256]{2,1,0:T(8,128)S(1)} %get-tuple-element.138), channel_id=1, source_target_pairs={{0,1},{1,0},{2,3},{3,2},{4,5},{5,4},{6,7},{7,6},{8,9},{9,8},{10,11... | collective-permute-start | bytes 3145736 | tf_op jit(solution)/shard_map/ppermute | solution.py:70
  42.6 9.4 %collective-permute-start.21 = (s16[528,256]{1,0:T(8,128)(2,1)S(1)}, s16[528,256]{1,0:T(8,128)(2,1)S(1)}, u32[]{:S(2)}, u32[]{:S(2)}) collective-permute-start(s16[528,256]{1,0:T(8,128)(2,1)S(1)} %get-tuple-element.133), channel_id=1, source_target_pairs={{0,4},{1,5},{2,6},{3,7},{4,0},{5,1},{6,2},{7,3},{8,12},{9,13},{10,... | collective-permute-start | bytes 811016 | tf_op jit(solution)/shard_map/ppermute | solution.py:70
  43.2 13.9 %collective-permute-start.22 = (s16[528,256]{1,0:T(8,128)(2,1)S(1)}, s16[528,256]{1,0:T(8,128)(2,1)S(1)}, u32[]{:S(2)}, u32[]{:S(2)}) collective-permute-start(s16[528,256]{1,0:T(8,128)(2,1)S(1)} %get-tuple-element.134), channel_id=1, source_target_pairs={{0,2},{1,3},{2,0},{3,1},{4,6},{5,7},{6,4},{7,5},{8,10},{9,11},{10,... | collective-permute-start | bytes 811016 | tf_op jit(solution)/shard_map/ppermute | solution.py:70
  44.2 13.2 %collective-permute-start.23 = (s16[528,256]{1,0:T(8,128)(2,1)S(1)}, s16[528,256]{1,0:T(8,128)(2,1)S(1)}, u32[]{:S(2)}, u32[]{:S(2)}) collective-permute-start(s16[528,256]{1,0:T(8,128)(2,1)S(1)} %get-tuple-element.135), channel_id=1, source_target_pairs={{0,6},{1,7},{2,4},{3,5},{4,2},{5,3},{6,0},{7,1},{8,14},{9,15},{10,... | collective-permute-start | bytes 811016 | tf_op jit(solution)/shard_map/ppermute | solution.py:70
  46.7 18.9 %collective-permute-start.26 = (s16[272,256]{1,0:T(8,128)(2,1)S(1)}, s16[272,256]{1,0:T(8,128)(2,1)S(1)}, u32[]{:S(2)}, u32[]{:S(2)}) collective-permute-start(s16[272,256]{1,0:T(8,128)(2,1)S(1)} %get-tuple-element.141), channel_id=1, source_target_pairs={{0,16},{1,17},{2,18},{3,19},{4,20},{5,21},{6,22},{7,23},{8,24},{9,... | collective-permute-start | bytes 417800 | tf_op jit(solution)/shard_map/ppermute | solution.py:70
  48.3 17.2 %collective-permute-start.27 = (s16[272,256]{1,0:T(8,128)(2,1)S(1)}, s16[272,256]{1,0:T(8,128)(2,1)S(1)}, u32[]{:S(2)}, u32[]{:S(2)}) collective-permute-start(s16[272,256]{1,0:T(8,128)(2,1)S(1)} %get-tuple-element.142), channel_id=1, source_target_pairs={{0,8},{1,9},{2,10},{3,11},{4,12},{5,13},{6,14},{7,15},{8,0},{9,1},... | collective-permute-start | bytes 417800 | tf_op jit(solution)/shard_map/ppermute | solution.py:70
  52.0 13.5 %collective-permute-start.28 = (s16[272,256]{1,0:T(8,128)(2,1)S(1)}, s16[272,256]{1,0:T(8,128)(2,1)S(1)}, u32[]{:S(2)}, u32[]{:S(2)}) collective-permute-start(s16[272,256]{1,0:T(8,128)(2,1)S(1)} %get-tuple-element.143), channel_id=1, source_target_pairs={{0,24},{1,25},{2,26},{3,27},{4,28},{5,29},{6,30},{7,31},{8,16},{9,... | collective-permute-start | bytes 417800 | tf_op jit(solution)/shard_map/ppermute | solution.py:70
  57.7 4.7 %collective-permute-start.24 = (s16[136,256]{1,0:T(8,128)(2,1)S(1)}, s16[136,256]{1,0:T(8,128)(2,1)S(1)}, u32[]{:S(2)}, u32[]{:S(2)}) collective-permute-start(s16[136,256]{1,0:T(8,128)(2,1)S(1)} %get-tuple-element.136), channel_id=1, source_target_pairs={{0,8},{1,9},{2,10},{3,11},{4,12},{5,13},{6,14},{7,15},{8,0},{9,1},... | collective-permute-start | bytes 208904 | tf_op jit(solution)/shard_map/ppermute | solution.py:70
  58.3 11.0 %collective-permute-start.32 = (s16[136,256]{1,0:T(8,128)(2,1)S(1)}, s16[136,256]{1,0:T(8,128)(2,1)S(1)}, u32[]{:S(2)}, u32[]{:S(2)}) collective-permute-start(s16[136,256]{1,0:T(8,128)(2,1)S(1)} %get-tuple-element.150), channel_id=1, source_target_pairs={{0,16},{1,17},{2,18},{3,19},{4,20},{5,21},{6,22},{7,23},{8,24},{9,... | collective-permute-start | bytes 208904 | tf_op jit(solution)/shard_map/ppermute | solution.py:70
  62.4 6.9 %collective-permute-start.33 = (s16[136,256]{1,0:T(8,128)(2,1)S(1)}, s16[136,256]{1,0:T(8,128)(2,1)S(1)}, u32[]{:S(2)}, u32[]{:S(2)}) collective-permute-start(s16[136,256]{1,0:T(8,128)(2,1)S(1)} %get-tuple-element.151), channel_id=1, source_target_pairs={{0,24},{1,25},{2,26},{3,27},{4,28},{5,29},{6,30},{7,31},{8,16},{9,... | collective-permute-start | bytes 208904 | tf_op jit(solution)/shard_map/ppermute | solution.py:70
  65.8 4.9 %collective-permute-start.29 = (s16[72,256]{1,0:T(8,128)(2,1)S(1)}, s16[72,256]{1,0:T(8,128)(2,1)S(1)}, u32[]{:S(2)}, u32[]{:S(2)}) collective-permute-start(s16[72,256]{1,0:T(8,128)(2,1)S(1)} %get-tuple-element.145), channel_id=1, source_target_pairs={{0,6},{1,7},{2,4},{3,5},{4,2},{5,3},{6,0},{7,1},{8,14},{9,15},{10,... | collective-permute-start | bytes 110600 | tf_op jit(solution)/shard_map/ppermute | solution.py:70
  67.1 4.0 %collective-permute-start.30 = (s16[72,256]{1,0:T(8,128)(2,1)S(1)}, s16[72,256]{1,0:T(8,128)(2,1)S(1)}, u32[]{:S(2)}, u32[]{:S(2)}) collective-permute-start(s16[72,256]{1,0:T(8,128)(2,1)S(1)} %get-tuple-element.146), channel_id=1, source_target_pairs={{0,2},{1,3},{2,0},{3,1},{4,6},{5,7},{6,4},{7,5},{8,10},{9,11},{10,... | collective-permute-start | bytes 110600 | tf_op jit(solution)/shard_map/ppermute | solution.py:70
  68.1 4.0 %collective-permute-start.31 = (s16[72,256]{1,0:T(8,128)(2,1)S(1)}, s16[72,256]{1,0:T(8,128)(2,1)S(1)}, u32[]{:S(2)}, u32[]{:S(2)}) collective-permute-start(s16[72,256]{1,0:T(8,128)(2,1)S(1)} %get-tuple-element.147), channel_id=1, source_target_pairs={{0,4},{1,5},{2,6},{3,7},{4,0},{5,1},{6,2},{7,3},{8,12},{9,13},{10,... | collective-permute-start | bytes 110600 | tf_op jit(solution)/shard_map/ppermute | solution.py:70
  73.0 5.7 %collective-permute-start.35 = (f32[192,256]{1,0:T(8,128)S(1)}, f32[192,256]{1,0:T(8,128)S(1)}, u32[]{:S(2)}, u32[]{:S(2)}) collective-permute-start(f32[192,256]{1,0:T(8,128)S(1)} %get-tuple-element.153.refs_0_), channel_id=1, source_target_pairs={{0,2},{1,3},{2,0},{3,1},{4,6},{5,7},{6,4},{7,5},{8,10},{9,11},{10,... | collective-permute-start | bytes 589832 | tf_op jit(solution)/shard_map/ppermute | solution.py:70
  73.9 10.8 %all-to-all-start = ((f32[32,8,128]{2,1,0:T(8,128)}), f32[32,8,128]{2,1,0:T(8,128)S(1)}, u32[]{:S(2)}, u32[]{:S(2)}) async-start(f32[32,8,128]{2,1,0:T(8,128)} %get-tuple-element.152), calls=%async_computation | async-start | bytes 262144 | tf_op jit(solution)/shard_map/all_to_all | solution.py:866
  78.6 6.1 %collective-permute-start.36 = (f32[192,256]{1,0:T(8,128)S(1)}, f32[192,256]{1,0:T(8,128)S(1)}, u32[]{:S(2)}, u32[]{:S(2)}) collective-permute-start(f32[192,256]{1,0:T(8,128)S(1)} %collective-permute-done.35.refs_2_), channel_id=1, source_target_pairs={{0,1},{1,0},{2,3},{3,2},{4,5},{5,4},{6,7},{7,6},{8,9},{9,8},{10,11... | collective-permute-start | bytes 589832 | tf_op jit(solution)/shard_map/ppermute | solution.py:70
  (19 other events, 336.1 us)

commit v8 on v7

--- a/solution.py
+++ b/solution.py
@@ -713,7 +713,7 @@
     )(clip_lengths, features, near, far, hot)
 
     act, *line_d = lax.optimization_barrier((act, *line_d))
-    pieces_d = line_d + [swap(v, 0, 1) for v in line_d]
+    pieces_d = line_d + [swap(pair_d, 0, 1)] + [swap(v, 0, 1) for v in line_d[1:]]
     held = list(plane_c)
     held[3], pieces_d[4] = lax.optimization_barrier((held[3], pieces_d[4]))
     turned = [swap(v, 0, 1) for v in held]

time: 88.3 us -> 88.3 us (level)
  transfers between devices with their start and end apart: 38 -> 38, of which waited for: 13 -> 14; matrix products, arithmetic and copies ran while one was open for 0% -> 0% of each run, Pallas kernels for 16% -> 16%
where the time goes in v8:
time: 88.3 us; the launch traced here: 88 us
  starting transfers between devices  43.5 us (49%)
  Pallas kernels  22.1 us (25%)
  waiting for transfers between devices  20.1 us (23%)
  between operations  2 us (2%)
    ppermute x35, starting transfers between devices, swap(): return lax.ppermute(value, ('clip', 'tm'), pairs)  40.2 us
    ppermute x35, waiting for transfers between devices, swap(): return lax.ppermute(value, ('clip', 'tm'), pairs)  14.9 us
    all_to_all x1, waiting for transfers between devices, shards(): squares = lax.all_to_all(squares, ('clip', 'tm'), 0, 0, tiled=True)  5.22 us
    pallas_call x1, Pallas kernels, shards(): pl.pallas_call(functools.partial(own_kernel, ranks), out_shape=(shape((SL...  3.39 us
    pallas_call x1, Pallas kernels, shards(): pl.pallas_call(functools.partial(quant_kernel, ranks), out_shape=(shape((...  3.33 us
    pallas_call x1, Pallas kernels, shards(): pl.pallas_call(update_kernel, out_shape=(shape((1, 1), F32),) + tuple((sh...  2.98 us
    all_to_all x1, starting transfers between devices, shards(): squares = lax.all_to_all(squares, ('clip', 'tm'), 0, 0, tiled=True)  2.58 us
    pallas_call x1, Pallas kernels, shards(): pl.pallas_call(functools.partial(features_kernel, clips), out_shape=shape...  2.22 us
  transfers between devices with their start and end apart: 38, of which 14 were waited for; matrix products, arithmetic and copies ran while one was open for 0% of the time, Pallas kernels for 16%

profile of v8, /device:TPU:0, one launch (start us, length us, event | category | flops | bytes accessed | tf_op | source)
XLA Modules:
  0.0 88.0 jit_solution(6531604673537922994)
XLA Ops:
  1.8 3.0 %collective-permute-start.5 = (bf16[2,64,256]{2,1,0:T(8,128)(2,1)S(1)}, bf16[2,64,256]{2,1,0:T(8,128)(2,1)S(1)}, u32[]{:S(2)}, u32[]{:S(2)}) collective-permute-start(bf16[2,64,256]{2,1,0:T(8,128)(2,1)S(1)} %get-tuple-element.104), channel_id=1, source_target_pairs={{0,4},{1,5},{2,6},{3,7},{4,0},{5,1},{6,2},{7,3},{8,12},{9,13},{10,... | collective-permute-start | bytes 196616 | tf_op jit(solution)/shard_map/ppermute | solution.py:70
  4.8 1.6 %collective-permute-start.2 = (bf16[128,256]{1,0:T(8,128)(2,1)S(1)}, bf16[128,256]{1,0:T(8,128)(2,1)S(1)}, u32[]{:S(2)}, u32[]{:S(2)}) collective-permute-start(bf16[128,256]{1,0:T(8,128)(2,1)S(1)} %get-tuple-element.93), channel_id=1, source_target_pairs={{0,8},{1,9},{2,10},{3,11},{4,12},{5,13},{6,14},{7,15},{8,0},{9,1},... | collective-permute-start | bytes 196616 | tf_op jit(solution)/shard_map/ppermute | solution.py:70
  6.3 2.6 %collective-permute-start.3 = (bf16[128,256]{1,0:T(8,128)(2,1)S(1)}, bf16[128,256]{1,0:T(8,128)(2,1)S(1)}, u32[]{:S(2)}, u32[]{:S(2)}) collective-permute-start(bf16[128,256]{1,0:T(8,128)(2,1)S(1)} %get-tuple-element.93), channel_id=1, source_target_pairs={{0,16},{1,17},{2,18},{3,19},{4,20},{5,21},{6,22},{7,23},{8,24},{9,... | collective-permute-start | bytes 196616 | tf_op jit(solution)/shard_map/ppermute | solution.py:70
  11.7 1.6 %collective-permute-done.3 = bf16[128,256]{1,0:T(8,128)(2,1)S(1)} collective-permute-done((bf16[128,256]{1,0:T(8,128)(2,1)S(1)}, bf16[128,256]{1,0:T(8,128)(2,1)S(1)}, u32[]{:S(2)}, u32[]{:S(2)}) %collective-permute-start.3) | collective-permute-done | bytes 65568 | tf_op jit(solution)/shard_map/ppermute | solution.py:70
  13.3 1.8 %collective-permute-start.7 = (bf16[2,2,64,256]{3,2,1,0:T(8,128)(2,1)S(1)}, bf16[2,2,64,256]{3,2,1,0:T(8,128)(2,1)S(1)}, u32[]{:S(2)}, u32[]{:S(2)}) collective-permute-start(bf16[2,2,64,256]{3,2,1,0:T(8,128)(2,1)S(1)} %pad_maximum_fusion.1.refs_0_), channel_id=1, source_target_pairs={{0,16},{1,17},{2,18},{3,19},{4,20},{5,21},{6,22},{7,23},{8,24},{9,... | collective-permute-start | bytes 393224 | tf_op jit(solution)/shard_map/ppermute | solution.py:70
  15.2 1.3 %collective-permute-start.8 = (bf16[2,2,64,256]{3,2,1,0:T(8,128)(2,1)S(1)}, bf16[2,2,64,256]{3,2,1,0:T(8,128)(2,1)S(1)}, u32[]{:S(2)}, u32[]{:S(2)}) collective-permute-start(bf16[2,2,64,256]{3,2,1,0:T(8,128)(2,1)S(1)} %pad_maximum_fusion.1.refs_0_), channel_id=1, source_target_pairs={{0,24},{1,25},{2,26},{3,27},{4,28},{5,29},{6,30},{7,31},{8,16},{9,... | collective-permute-start | bytes 393224 | tf_op jit(solution)/shard_map/ppermute | solution.py:70
  16.6 2.1 %collective-permute-start.9 = (bf16[4,128,256]{2,1,0:T(8,128)(2,1)S(1)}, bf16[4,128,256]{2,1,0:T(8,128)(2,1)S(1)}, u32[]{:S(2)}, u32[]{:S(2)}) collective-permute-start(bf16[4,128,256]{2,1,0:T(8,128)(2,1)S(1)} %pad_maximum_fusion.refs_0_), channel_id=1, source_target_pairs={{0,6},{1,7},{2,4},{3,5},{4,2},{5,3},{6,0},{7,1},{8,14},{9,15},{10,... | collective-permute-start | bytes 786440 | tf_op jit(solution)/shard_map/ppermute | solution.py:70
  18.6 1.7 %collective-permute-start.14 = (bf16[4,128,256]{2,1,0:T(8,128)(2,1)S(1)}, bf16[4,128,256]{2,1,0:T(8,128)(2,1)S(1)}, u32[]{:S(2)}, u32[]{:S(2)}) collective-permute-start(bf16[4,128,256]{2,1,0:T(8,128)(2,1)S(1)} %pad_maximum_fusion.refs_0_), channel_id=1, source_target_pairs={{0,4},{1,5},{2,6},{3,7},{4,0},{5,1},{6,2},{7,3},{8,12},{9,13},{10,... | collective-permute-start | bytes 786440 | tf_op jit(solution)/shard_map/ppermute | solution.py:70
  20.7 3.4 %own.1 = (bf16[4,544,1024]{2,1,0:T(8,128)(2,1)S(1)}, bf16[4,1024,512]{2,1,0:T(8,128)(2,1)S(1)}) custom-call(s32[2]{0:T(128)S(1)} %copy-done.12, s32[4,2,256]{2,1,0:T(2,128)S(1)} %copy-done.11), custom_call_target="tpu_custom_call" | custom-call | tf_op jit(solution)/shard_map/own/pallas_call | solution.py:684
  24.1 1.8 %collective-permute-done.7.refs_2_ = bf16[2,2,64,256]{3,2,1,0:T(8,128)(2,1)S(1)} collective-permute-done((bf16[2,2,64,256]{3,2,1,0:T(8,128)(2,1)S(1)}, bf16[2,2,64,256]{3,2,1,0:T(8,128)(2,1)S(1)}, u32[]{:S(2)}, u32[]{:S(2)}) %collective-permute-start.7) | collective-permute-done | bytes 131104 | tf_op jit(solution)/shard_map/ppermute | solution.py:70
  26.7 1.7 %margin.1 = (f32[544,512]{1,0:T(8,128)S(1)}, bf16[544,512]{1,0:T(8,128)(2,1)S(1)}, bf16[512,1536]{1,0:T(8,128)(2,1)S(1)}, f32[32,512]{1,0:T(8,128)S(1)}, f32[544...) custom-call(s32[2]{0:T(128)S(1)} %copy-done.12, ...), custom_call_target="tpu_custom_call", output_to_operand_aliasing={{5}: (4, {})} | custom-call | tf_op jit(solution)/shard_map/margin/pallas_call | solution.py:698
  30.4 2.0 %collective-permute-done.17.refs_4_ = bf16[4,128,256]{2,1,0:T(8,128)(2,1)S(1)} collective-permute-done((bf16[4,128,256]{2,1,0:T(8,128)(2,1)S(1)}, bf16[4,128,256]{2,1,0:T(8,128)(2,1)S(1)}, u32[]{:S(2)}, u32[]{:S(2)}) %collective-permute-start.17) | collective-permute-done | bytes 262176 | tf_op jit(solution)/shard_map/ppermute | solution.py:70
  32.8 1.2 %collective-permute-done.13.refs_7_ = bf16[2,2,64,256]{3,2,1,0:T(8,128)(2,1)S(1)} collective-permute-done((bf16[2,2,64,256]{3,2,1,0:T(8,128)(2,1)S(1)}, bf16[2,2,64,256]{3,2,1,0:T(8,128)(2,1)S(1)}, u32[]{:S(2)}, u32[]{:S(2)}) %collective-permute-start.13) | collective-permute-done | bytes 131104 | tf_op jit(solution)/shard_map/ppermute | solution.py:70
  34.0 1.2 %conv.1 = (bf16[768,512]{1,0:T(8,128)(2,1)S(1)}, bf16[512,256]{1,0:T(8,128)(2,1)S(1)}, bf16[544,256]{1,0:T(8,128)(2,1)S(1)}, f32[544,256]{1,0:T(8,128)S(1)}, f32[544,512]{1,0:T(8,128)S(1)}) custom-call(f32[544,512]{1,0:T(8,128)S(1)} %get-tuple-element.102.start_ref, bf16[544,512]{1,0:T(8,128)(2,1)S(1)} %get-tuple-element.105.act_ref, ...), custom_call_target="tpu_custom_call" | custom-call | tf_op jit(solution)/shard_map/conv/pallas_call | solution.py:733
  35.3 3.3 %quant.1 = (bf16[2,256,512]{2,1,0:T(8,128)(2,1)}, s16[2,1056,256]{2,1,0:T(8,128)(2,1)S(1)}, bf16[544,512]{1,0:T(8,128)(2,1)S(1)}, f32[512,512]{1,0:T(8,128)S(1)}, bf16[4,512,512]{2,1,0:T(8,128)(2,1)S(1)}) custom-call(f32[544,256]{1,0:T(8,128)S(1)} %get-tuple-element.101.mask_ref, f32[544,512]{1,0:T(8,128)S(1)} %get-tuple-element.112.latent_ref, ...), custom_call_target="tpu_custom_call" | custom-call | tf_op jit(solution)/shard_map/quant/pallas_call | solution.py:745
  38.9 1.4 %backward.1 = (bf16[544,256]{1,0:T(8,128)(2,1)S(1)}, f32[2,512,256]{2,1,0:T(8,128)S(1)}, f32[2,512,256]{2,1,0:T(8,128)S(1)}) custom-call(bf16[512,1536]{1,0:T(8,128)(2,1)S(1)} %get-tuple-element.119.window_ref, bf16[544,256]{1,0:T(8,128)(2,1)S(1)} %get-tuple-element.120.gated_ref, bf16[544,512]{1,0:T(8,128)(2,1)S(1)} %get-tuple-element.121.bg_ref, ...), custom_call_target="tpu_custom_call" | custom-call | tf_op jit(solution)/shard_map/backward/pallas_call | solution.py:776
  40.7 1.2 %keep.1.keep_ref = f32[2,1024,256]{2,1,0:T(8,128)S(1)} custom-call(bf16[4,1024,512]{2,1,0:T(8,128)(2,1)S(1)} %get-tuple-element.115.hott_ref, bf16[4,512,512]{2,1,0:T(8,128)(2,1)S(1)} %get-tuple-element.126.cgs_ref), custom_call_target="tpu_custom_call" | custom-call | tf_op jit(solution)/shard_map/keep/pallas_call | solution.py:763
  44.2 1.9 %collective-permute-start.23 = (s16[528,256]{1,0:T(8,128)(2,1)S(1)}, s16[528,256]{1,0:T(8,128)(2,1)S(1)}, u32[]{:S(2)}, u32[]{:S(2)}) collective-permute-start(s16[528,256]{1,0:T(8,128)(2,1)S(1)} %get-tuple-element.135), channel_id=1, source_target_pairs={{0,6},{1,7},{2,4},{3,5},{4,2},{5,3},{6,0},{7,1},{8,14},{9,15},{10,... | collective-permute-start | bytes 811016 | tf_op jit(solution)/shard_map/ppermute | solution.py:70
  46.7 1.6 %collective-permute-start.26 = (s16[272,256]{1,0:T(8,128)(2,1)S(1)}, s16[272,256]{1,0:T(8,128)(2,1)S(1)}, u32[]{:S(2)}, u32[]{:S(2)}) collective-permute-start(s16[272,256]{1,0:T(8,128)(2,1)S(1)} %get-tuple-element.141), channel_id=1, source_target_pairs={{0,16},{1,17},{2,18},{3,19},{4,20},{5,21},{6,22},{7,23},{8,24},{9,... | collective-permute-start | bytes 417800 | tf_op jit(solution)/shard_map/ppermute | solution.py:70
  48.3 1.9 %collective-permute-start.27 = (s16[272,256]{1,0:T(8,128)(2,1)S(1)}, s16[272,256]{1,0:T(8,128)(2,1)S(1)}, u32[]{:S(2)}, u32[]{:S(2)}) collective-permute-start(s16[272,256]{1,0:T(8,128)(2,1)S(1)} %get-tuple-element.142), channel_id=1, source_target_pairs={{0,8},{1,9},{2,10},{3,11},{4,12},{5,13},{6,14},{7,15},{8,0},{9,1},... | collective-permute-start | bytes 417800 | tf_op jit(solution)/shard_map/ppermute | solution.py:70
  50.2 1.8 %collective-permute-done.21.refs_0_ = s16[528,256]{1,0:T(8,128)(2,1)S(1)} collective-permute-done((s16[528,256]{1,0:T(8,128)(2,1)S(1)}, s16[528,256]{1,0:T(8,128)(2,1)S(1)}, u32[]{:S(2)}, u32[]{:S(2)}) %collective-permute-start.21) | collective-permute-done | bytes 270368 | tf_op jit(solution)/shard_map/ppermute | solution.py:70
  52.0 2.9 %collective-permute-start.28 = (s16[272,256]{1,0:T(8,128)(2,1)S(1)}, s16[272,256]{1,0:T(8,128)(2,1)S(1)}, u32[]{:S(2)}, u32[]{:S(2)}) collective-permute-start(s16[272,256]{1,0:T(8,128)(2,1)S(1)} %get-tuple-element.143), channel_id=1, source_target_pairs={{0,24},{1,25},{2,26},{3,27},{4,28},{5,29},{6,30},{7,31},{8,16},{9,... | collective-permute-start | bytes 417800 | tf_op jit(solution)/shard_map/ppermute | solution.py:70
  54.9 2.2 %features.1 = f32[2,256,512]{2,1,0:T(8,128)} custom-call(s32[2]{0:T(128)S(1)} %copy-done.12, f32[544,512]{1,0:T(8,128)S(1)} %get-tuple-element.102.start_ref, f32[512,512]{1,0:T(8,128)S(1)} %get-tuple-element.118.lg_ref, bf16[544,256]{1,0:T(8,128)(2,1)S(1)} %get-tuple-element.124.hg_ref, bf16[768,512]{1,0:T(8,128)(2,1)S(1)} %get-tuple-element.125.d_ref), custom_call_target="tpu_custom_call" | custom-call | tf_op jit(solution)/shard_map/features/pallas_call | solution.py:785
  58.3 3.5 %collective-permute-start.32 = (s16[136,256]{1,0:T(8,128)(2,1)S(1)}, s16[136,256]{1,0:T(8,128)(2,1)S(1)}, u32[]{:S(2)}, u32[]{:S(2)}) collective-permute-start(s16[136,256]{1,0:T(8,128)(2,1)S(1)} %get-tuple-element.150), channel_id=1, source_target_pairs={{0,16},{1,17},{2,18},{3,19},{4,20},{5,21},{6,22},{7,23},{8,24},{9,... | collective-permute-start | bytes 208904 | tf_op jit(solution)/shard_map/ppermute | solution.py:70
  62.4 3.1 %collective-permute-start.33 = (s16[136,256]{1,0:T(8,128)(2,1)S(1)}, s16[136,256]{1,0:T(8,128)(2,1)S(1)}, u32[]{:S(2)}, u32[]{:S(2)}) collective-permute-start(s16[136,256]{1,0:T(8,128)(2,1)S(1)} %get-tuple-element.151), channel_id=1, source_target_pairs={{0,24},{1,25},{2,26},{3,27},{4,28},{5,29},{6,30},{7,31},{8,16},{9,... | collective-permute-start | bytes 208904 | tf_op jit(solution)/shard_map/ppermute | solution.py:70
  65.8 1.3 %collective-permute-start.29 = (s16[72,256]{1,0:T(8,128)(2,1)S(1)}, s16[72,256]{1,0:T(8,128)(2,1)S(1)}, u32[]{:S(2)}, u32[]{:S(2)}) collective-permute-start(s16[72,256]{1,0:T(8,128)(2,1)S(1)} %get-tuple-element.145), channel_id=1, source_target_pairs={{0,6},{1,7},{2,4},{3,5},{4,2},{5,3},{6,0},{7,1},{8,14},{9,15},{10,... | collective-permute-start | bytes 110600 | tf_op jit(solution)/shard_map/ppermute | solution.py:70
  68.1 1.2 %collective-permute-start.31 = (s16[72,256]{1,0:T(8,128)(2,1)S(1)}, s16[72,256]{1,0:T(8,128)(2,1)S(1)}, u32[]{:S(2)}, u32[]{:S(2)}) collective-permute-start(s16[72,256]{1,0:T(8,128)(2,1)S(1)} %get-tuple-element.147), channel_id=1, source_target_pairs={{0,4},{1,5},{2,6},{3,7},{4,0},{5,1},{6,2},{7,3},{8,12},{9,13},{10,... | collective-permute-start | bytes 110600 | tf_op jit(solution)/shard_map/ppermute | solution.py:70
  69.3 1.4 %collective-permute-done.29.refs_1_ = s16[72,256]{1,0:T(8,128)(2,1)S(1)} collective-permute-done((s16[72,256]{1,0:T(8,128)(2,1)S(1)}, s16[72,256]{1,0:T(8,128)(2,1)S(1)}, u32[]{:S(2)}, u32[]{:S(2)}) %collective-permute-start.29) | collective-permute-done | bytes 36896 | tf_op jit(solution)/shard_map/ppermute | solution.py:70
  73.9 2.6 %all-to-all-start = ((f32[32,8,128]{2,1,0:T(8,128)}), f32[32,8,128]{2,1,0:T(8,128)S(1)}, u32[]{:S(2)}, u32[]{:S(2)}) async-start(f32[32,8,128]{2,1,0:T(8,128)} %get-tuple-element.152), calls=%async_computation | async-start | bytes 262144 | tf_op jit(solution)/shard_map/all_to_all | solution.py:866
  76.7 1.9 %collective-permute-done.35.refs_2_ = f32[192,256]{1,0:T(8,128)S(1)} collective-permute-done((f32[192,256]{1,0:T(8,128)S(1)}, f32[192,256]{1,0:T(8,128)S(1)}, u32[]{:S(2)}, u32[]{:S(2)}) %collective-permute-start.35) | collective-permute-done | bytes 196640 | tf_op jit(solution)/shard_map/ppermute | solution.py:70
  79.5 5.2 %all-to-all-done.square_ref = f32[32,8,128]{2,1,0:T(8,128)S(1)} async-done(((f32[32,8,128]{2,1,0:T(8,128)}), f32[32,8,128]{2,1,0:T(8,128)S(1)}, u32[]{:S(2)}, u32[]{:S(2)}) %all-to-all-start) | async-done | bytes 131104 | tf_op jit(solution)/shard_map/all_to_all | solution.py:866
  84.8 3.0 %update.1 = (f32[1,1]{1,0:T(1,128)}, f32[3,32,512]{2,1,0:T(8,128)}, f32[3,32,512]{2,1,0:T(8,128)}, f32[3,32,512]{2,1,0:T(8,128)}, f32[64,256]{1,0:T(8,128)}, /*i...) custom-call(f32[2]{0:T(128)S(1)} %pad_maximum_fusion.2.fix_ref, ...), custom_call_target="tpu_custom_call" | custom-call | tf_op jit(solution)/shard_map/update/pallas_call | solution.py:872
  (88 shorter events, 17.5 us)
Async XLA Ops:
  1.8 8.5 %collective-permute-start.5 = (bf16[2,64,256]{2,1,0:T(8,128)(2,1)S(1)}, bf16[2,64,256]{2,1,0:T(8,128)(2,1)S(1)}, u32[]{:S(2)}, u32[]{:S(2)}) collective-permute-start(bf16[2,64,256]{2,1,0:T(8,128)(2,1)S(1)} %get-tuple-element.104), channel_id=1, source_target_pairs={{0,4},{1,5},{2,6},{3,7},{4,0},{5,1},{6,2},{7,3},{8,12},{9,13},{10,... | collective-permute-start | bytes 196616 | tf_op jit(solution)/shard_map/ppermute | solution.py:70
  4.8 6.2 %collective-permute-start.2 = (bf16[128,256]{1,0:T(8,128)(2,1)S(1)}, bf16[128,256]{1,0:T(8,128)(2,1)S(1)}, u32[]{:S(2)}, u32[]{:S(2)}) collective-permute-start(bf16[128,256]{1,0:T(8,128)(2,1)S(1)} %get-tuple-element.93), channel_id=1, source_target_pairs={{0,8},{1,9},{2,10},{3,11},{4,12},{5,13},{6,14},{7,15},{8,0},{9,1},... | collective-permute-start | bytes 196616 | tf_op jit(solution)/shard_map/ppermute | solution.py:70
  6.3 7.0 %collective-permute-start.3 = (bf16[128,256]{1,0:T(8,128)(2,1)S(1)}, bf16[128,256]{1,0:T(8,128)(2,1)S(1)}, u32[]{:S(2)}, u32[]{:S(2)}) collective-permute-start(bf16[128,256]{1,0:T(8,128)(2,1)S(1)} %get-tuple-element.93), channel_id=1, source_target_pairs={{0,16},{1,17},{2,18},{3,19},{4,20},{5,21},{6,22},{7,23},{8,24},{9,... | collective-permute-start | bytes 196616 | tf_op jit(solution)/shard_map/ppermute | solution.py:70
  8.9 6.2 %collective-permute-start.4 = (bf16[128,256]{1,0:T(8,128)(2,1)S(1)}, bf16[128,256]{1,0:T(8,128)(2,1)S(1)}, u32[]{:S(2)}, u32[]{:S(2)}) collective-permute-start(bf16[128,256]{1,0:T(8,128)(2,1)S(1)} %get-tuple-element.93), channel_id=1, source_target_pairs={{0,24},{1,25},{2,26},{3,27},{4,28},{5,29},{6,30},{7,31},{8,16},{9,... | collective-permute-start | bytes 196616 | tf_op jit(solution)/shard_map/ppermute | solution.py:70
  10.1 6.4 %collective-permute-start = (bf16[2,16,1024]{2,1,0:T(8,128)(2,1)S(1)}, bf16[2,16,1024]{2,1,0:T(8,128)(2,1)S(1)}, u32[]{:S(2)}, u32[]{:S(2)}) collective-permute-start(bf16[2,16,1024]{2,1,0:T(8,128)(2,1)S(1)} %get-tuple-element.91), channel_id=1, source_target_pairs={{0,1},{1,0},{2,3},{3,2},{4,5},{5,4},{6,7},{7,6},{8,9},{9,8},{10,11... | collective-permute-start | bytes 196616 | tf_op jit(solution)/shard_map/ppermute | solution.py:677
  10.2 6.3 %collective-permute-start.1 = (bf16[2,16,1024]{2,1,0:T(8,128)(2,1)S(1)}, bf16[2,16,1024]{2,1,0:T(8,128)(2,1)S(1)}, u32[]{:S(2)}, u32[]{:S(2)}) collective-permute-start(bf16[2,16,1024]{2,1,0:T(8,128)(2,1)S(1)} %get-tuple-element.92), channel_id=1, source_target_pairs={{1,2},{2,1},{5,6},{6,5},{9,10},{10,9},{13,14},{14,13},{17,18},{18,... | collective-permute-start | bytes 196616 | tf_op jit(solution)/shard_map/ppermute | solution.py:679
  10.9 9.4 %collective-permute-start.6 = (bf16[2,2,64,256]{3,2,1,0:T(8,128)(2,1)S(1)}, bf16[2,2,64,256]{3,2,1,0:T(8,128)(2,1)S(1)}, u32[]{:S(2)}, u32[]{:S(2)}) collective-permute-start(bf16[2,2,64,256]{3,2,1,0:T(8,128)(2,1)S(1)} %pad_maximum_fusion.1.refs_0_), channel_id=1, source_target_pairs={{0,8},{1,9},{2,10},{3,11},{4,12},{5,13},{6,14},{7,15},{8,0},{9,1},... | collective-permute-start | bytes 393224 | tf_op jit(solution)/shard_map/ppermute | solution.py:70
  13.3 12.5 %collective-permute-start.7 = (bf16[2,2,64,256]{3,2,1,0:T(8,128)(2,1)S(1)}, bf16[2,2,64,256]{3,2,1,0:T(8,128)(2,1)S(1)}, u32[]{:S(2)}, u32[]{:S(2)}) collective-permute-start(bf16[2,2,64,256]{3,2,1,0:T(8,128)(2,1)S(1)} %pad_maximum_fusion.1.refs_0_), channel_id=1, source_target_pairs={{0,16},{1,17},{2,18},{3,19},{4,20},{5,21},{6,22},{7,23},{8,24},{9,... | collective-permute-start | bytes 393224 | tf_op jit(solution)/shard_map/ppermute | solution.py:70
  15.2 13.2 %collective-permute-start.8 = (bf16[2,2,64,256]{3,2,1,0:T(8,128)(2,1)S(1)}, bf16[2,2,64,256]{3,2,1,0:T(8,128)(2,1)S(1)}, u32[]{:S(2)}, u32[]{:S(2)}) collective-permute-start(bf16[2,2,64,256]{3,2,1,0:T(8,128)(2,1)S(1)} %pad_maximum_fusion.1.refs_0_), channel_id=1, source_target_pairs={{0,24},{1,25},{2,26},{3,27},{4,28},{5,29},{6,30},{7,31},{8,16},{9,... | collective-permute-start | bytes 393224 | tf_op jit(solution)/shard_map/ppermute | solution.py:70
  16.6 12.5 %collective-permute-start.9 = (bf16[4,128,256]{2,1,0:T(8,128)(2,1)S(1)}, bf16[4,128,256]{2,1,0:T(8,128)(2,1)S(1)}, u32[]{:S(2)}, u32[]{:S(2)}) collective-permute-start(bf16[4,128,256]{2,1,0:T(8,128)(2,1)S(1)} %pad_maximum_fusion.refs_0_), channel_id=1, source_target_pairs={{0,6},{1,7},{2,4},{3,5},{4,2},{5,3},{6,0},{7,1},{8,14},{9,15},{10,... | collective-permute-start | bytes 786440 | tf_op jit(solution)/shard_map/ppermute | solution.py:70
  18.6 11.6 %collective-permute-start.14 = (bf16[4,128,256]{2,1,0:T(8,128)(2,1)S(1)}, bf16[4,128,256]{2,1,0:T(8,128)(2,1)S(1)}, u32[]{:S(2)}, u32[]{:S(2)}) collective-permute-start(bf16[4,128,256]{2,1,0:T(8,128)(2,1)S(1)} %pad_maximum_fusion.refs_0_), channel_id=1, source_target_pairs={{0,4},{1,5},{2,6},{3,7},{4,0},{5,1},{6,2},{7,3},{8,12},{9,13},{10,... | collective-permute-start | bytes 786440 | tf_op jit(solution)/shard_map/ppermute | solution.py:70
  20.3 12.0 %collective-permute-start.17 = (bf16[4,128,256]{2,1,0:T(8,128)(2,1)S(1)}, bf16[4,128,256]{2,1,0:T(8,128)(2,1)S(1)}, u32[]{:S(2)}, u32[]{:S(2)}) collective-permute-start(bf16[4,128,256]{2,1,0:T(8,128)(2,1)S(1)} %pad_maximum_fusion.refs_0_), channel_id=1, source_target_pairs={{0,2},{1,3},{2,0},{3,1},{4,6},{5,7},{6,4},{7,5},{8,10},{9,11},{10,... | collective-permute-start | bytes 786440 | tf_op jit(solution)/shard_map/ppermute | solution.py:70
  28.5 3.8 %collective-permute-start.12 = (bf16[2,2,64,256]{3,2,1,0:T(8,128)(2,1)S(1)}, bf16[2,2,64,256]{3,2,1,0:T(8,128)(2,1)S(1)}, u32[]{:S(2)}, u32[]{:S(2)}) collective-permute-start(bf16[2,2,64,256]{3,2,1,0:T(8,128)(2,1)S(1)} %collective-permute-done.7.refs_2_), channel_id=1, source_target_pairs={{0,1},{1,0},{2,3},{3,2},{4,5},{5,4},{6,7},{7,6},{8,9},{9,8},{10,11... | collective-permute-start | bytes 393224 | tf_op jit(solution)/shard_map/ppermute | solution.py:70
  29.0 6.3 %collective-permute-start.15 = (bf16[4,128,256]{2,1,0:T(8,128)(2,1)S(1)}, bf16[4,128,256]{2,1,0:T(8,128)(2,1)S(1)}, u32[]{:S(2)}, u32[]{:S(2)}) collective-permute-start(bf16[4,128,256]{2,1,0:T(8,128)(2,1)S(1)} %pad_maximum_fusion.refs_0_), channel_id=1, source_target_pairs={{0,1},{1,0},{2,3},{3,2},{4,5},{5,4},{6,7},{7,6},{8,9},{9,8},{10,11... | collective-permute-start | bytes 786440 | tf_op jit(solution)/shard_map/ppermute | solution.py:70
  29.8 5.4 %collective-permute-start.19 = (bf16[4,128,256]{2,1,0:T(8,128)(2,1)S(1)}, bf16[4,128,256]{2,1,0:T(8,128)(2,1)S(1)}, u32[]{:S(2)}, u32[]{:S(2)}) collective-permute-start(bf16[4,128,256]{2,1,0:T(8,128)(2,1)S(1)} %collective-permute-done.9.refs_5_), channel_id=1, source_target_pairs={{0,1},{1,0},{2,3},{3,2},{4,5},{5,4},{6,7},{7,6},{8,9},{9,8},{10,11... | collective-permute-start | bytes 786440 | tf_op jit(solution)/shard_map/ppermute | solution.py:70
  30.2 5.1 %collective-permute-start.16 = (bf16[4,128,256]{2,1,0:T(8,128)(2,1)S(1)}, bf16[4,128,256]{2,1,0:T(8,128)(2,1)S(1)}, u32[]{:S(2)}, u32[]{:S(2)}) collective-permute-start(bf16[4,128,256]{2,1,0:T(8,128)(2,1)S(1)} %collective-permute-done.14.refs_1_), channel_id=1, source_target_pairs={{0,1},{1,0},{2,3},{3,2},{4,5},{5,4},{6,7},{7,6},{8,9},{9,8},{10,11... | collective-permute-start | bytes 786440 | tf_op jit(solution)/shard_map/ppermute | solution.py:70
  40.2 5.9 %collective-permute-start.25 = (f32[2,512,256]{2,1,0:T(8,128)S(1)}, f32[2,512,256]{2,1,0:T(8,128)S(1)}, u32[]{:S(2)}, u32[]{:S(2)}) collective-permute-start(f32[2,512,256]{2,1,0:T(8,128)S(1)} %get-tuple-element.138), channel_id=1, source_target_pairs={{0,1},{1,0},{2,3},{3,2},{4,5},{5,4},{6,7},{7,6},{8,9},{9,8},{10,11... | collective-permute-start | bytes 3145736 | tf_op jit(solution)/shard_map/ppermute | solution.py:70
  42.6 9.4 %collective-permute-start.21 = (s16[528,256]{1,0:T(8,128)(2,1)S(1)}, s16[528,256]{1,0:T(8,128)(2,1)S(1)}, u32[]{:S(2)}, u32[]{:S(2)}) collective-permute-start(s16[528,256]{1,0:T(8,128)(2,1)S(1)} %get-tuple-element.133), channel_id=1, source_target_pairs={{0,4},{1,5},{2,6},{3,7},{4,0},{5,1},{6,2},{7,3},{8,12},{9,13},{10,... | collective-permute-start | bytes 811016 | tf_op jit(solution)/shard_map/ppermute | solution.py:70
  43.2 13.9 %collective-permute-start.22 = (s16[528,256]{1,0:T(8,128)(2,1)S(1)}, s16[528,256]{1,0:T(8,128)(2,1)S(1)}, u32[]{:S(2)}, u32[]{:S(2)}) collective-permute-start(s16[528,256]{1,0:T(8,128)(2,1)S(1)} %get-tuple-element.134), channel_id=1, source_target_pairs={{0,2},{1,3},{2,0},{3,1},{4,6},{5,7},{6,4},{7,5},{8,10},{9,11},{10,... | collective-permute-start | bytes 811016 | tf_op jit(solution)/shard_map/ppermute | solution.py:70
  44.2 13.2 %collective-permute-start.23 = (s16[528,256]{1,0:T(8,128)(2,1)S(1)}, s16[528,256]{1,0:T(8,128)(2,1)S(1)}, u32[]{:S(2)}, u32[]{:S(2)}) collective-permute-start(s16[528,256]{1,0:T(8,128)(2,1)S(1)} %get-tuple-element.135), channel_id=1, source_target_pairs={{0,6},{1,7},{2,4},{3,5},{4,2},{5,3},{6,0},{7,1},{8,14},{9,15},{10,... | collective-permute-start | bytes 811016 | tf_op jit(solution)/shard_map/ppermute | solution.py:70
  46.7 18.9 %collective-permute-start.26 = (s16[272,256]{1,0:T(8,128)(2,1)S(1)}, s16[272,256]{1,0:T(8,128)(2,1)S(1)}, u32[]{:S(2)}, u32[]{:S(2)}) collective-permute-start(s16[272,256]{1,0:T(8,128)(2,1)S(1)} %get-tuple-element.141), channel_id=1, source_target_pairs={{0,16},{1,17},{2,18},{3,19},{4,20},{5,21},{6,22},{7,23},{8,24},{9,... | collective-permute-start | bytes 417800 | tf_op jit(solution)/shard_map/ppermute | solution.py:70
  48.3 17.2 %collective-permute-start.27 = (s16[272,256]{1,0:T(8,128)(2,1)S(1)}, s16[272,256]{1,0:T(8,128)(2,1)S(1)}, u32[]{:S(2)}, u32[]{:S(2)}) collective-permute-start(s16[272,256]{1,0:T(8,128)(2,1)S(1)} %get-tuple-element.142), channel_id=1, source_target_pairs={{0,8},{1,9},{2,10},{3,11},{4,12},{5,13},{6,14},{7,15},{8,0},{9,1},... | collective-permute-start | bytes 417800 | tf_op jit(solution)/shard_map/ppermute | solution.py:70
  52.0 13.5 %collective-permute-start.28 = (s16[272,256]{1,0:T(8,128)(2,1)S(1)}, s16[272,256]{1,0:T(8,128)(2,1)S(1)}, u32[]{:S(2)}, u32[]{:S(2)}) collective-permute-start(s16[272,256]{1,0:T(8,128)(2,1)S(1)} %get-tuple-element.143), channel_id=1, source_target_pairs={{0,24},{1,25},{2,26},{3,27},{4,28},{5,29},{6,30},{7,31},{8,16},{9,... | collective-permute-start | bytes 417800 | tf_op jit(solution)/shard_map/ppermute | solution.py:70
  57.7 4.7 %collective-permute-start.24 = (s16[136,256]{1,0:T(8,128)(2,1)S(1)}, s16[136,256]{1,0:T(8,128)(2,1)S(1)}, u32[]{:S(2)}, u32[]{:S(2)}) collective-permute-start(s16[136,256]{1,0:T(8,128)(2,1)S(1)} %get-tuple-element.136), channel_id=1, source_target_pairs={{0,8},{1,9},{2,10},{3,11},{4,12},{5,13},{6,14},{7,15},{8,0},{9,1},... | collective-permute-start | bytes 208904 | tf_op jit(solution)/shard_map/ppermute | solution.py:70
  58.3 11.0 %collective-permute-start.32 = (s16[136,256]{1,0:T(8,128)(2,1)S(1)}, s16[136,256]{1,0:T(8,128)(2,1)S(1)}, u32[]{:S(2)}, u32[]{:S(2)}) collective-permute-start(s16[136,256]{1,0:T(8,128)(2,1)S(1)} %get-tuple-element.150), channel_id=1, source_target_pairs={{0,16},{1,17},{2,18},{3,19},{4,20},{5,21},{6,22},{7,23},{8,24},{9,... | collective-permute-start | bytes 208904 | tf_op jit(solution)/shard_map/ppermute | solution.py:70
  62.4 6.9 %collective-permute-start.33 = (s16[136,256]{1,0:T(8,128)(2,1)S(1)}, s16[136,256]{1,0:T(8,128)(2,1)S(1)}, u32[]{:S(2)}, u32[]{:S(2)}) collective-permute-start(s16[136,256]{1,0:T(8,128)(2,1)S(1)} %get-tuple-element.151), channel_id=1, source_target_pairs={{0,24},{1,25},{2,26},{3,27},{4,28},{5,29},{6,30},{7,31},{8,16},{9,... | collective-permute-start | bytes 208904 | tf_op jit(solution)/shard_map/ppermute | solution.py:70
  65.8 4.9 %collective-permute-start.29 = (s16[72,256]{1,0:T(8,128)(2,1)S(1)}, s16[72,256]{1,0:T(8,128)(2,1)S(1)}, u32[]{:S(2)}, u32[]{:S(2)}) collective-permute-start(s16[72,256]{1,0:T(8,128)(2,1)S(1)} %get-tuple-element.145), channel_id=1, source_target_pairs={{0,6},{1,7},{2,4},{3,5},{4,2},{5,3},{6,0},{7,1},{8,14},{9,15},{10,... | collective-permute-start | bytes 110600 | tf_op jit(solution)/shard_map/ppermute | solution.py:70
  67.1 4.0 %collective-permute-start.30 = (s16[72,256]{1,0:T(8,128)(2,1)S(1)}, s16[72,256]{1,0:T(8,128)(2,1)S(1)}, u32[]{:S(2)}, u32[]{:S(2)}) collective-permute-start(s16[72,256]{1,0:T(8,128)(2,1)S(1)} %get-tuple-element.146), channel_id=1, source_target_pairs={{0,2},{1,3},{2,0},{3,1},{4,6},{5,7},{6,4},{7,5},{8,10},{9,11},{10,... | collective-permute-start | bytes 110600 | tf_op jit(solution)/shard_map/ppermute | solution.py:70
  68.1 4.0 %collective-permute-start.31 = (s16[72,256]{1,0:T(8,128)(2,1)S(1)}, s16[72,256]{1,0:T(8,128)(2,1)S(1)}, u32[]{:S(2)}, u32[]{:S(2)}) collective-permute-start(s16[72,256]{1,0:T(8,128)(2,1)S(1)} %get-tuple-element.147), channel_id=1, source_target_pairs={{0,4},{1,5},{2,6},{3,7},{4,0},{5,1},{6,2},{7,3},{8,12},{9,13},{10,... | collective-permute-start | bytes 110600 | tf_op jit(solution)/shard_map/ppermute | solution.py:70
  73.0 5.7 %collective-permute-start.35 = (f32[192,256]{1,0:T(8,128)S(1)}, f32[192,256]{1,0:T(8,128)S(1)}, u32[]{:S(2)}, u32[]{:S(2)}) collective-permute-start(f32[192,256]{1,0:T(8,128)S(1)} %get-tuple-element.153.refs_0_), channel_id=1, source_target_pairs={{0,2},{1,3},{2,0},{3,1},{4,6},{5,7},{6,4},{7,5},{8,10},{9,11},{10,... | collective-permute-start | bytes 589832 | tf_op jit(solution)/shard_map/ppermute | solution.py:70
  73.9 10.8 %all-to-all-start = ((f32[32,8,128]{2,1,0:T(8,128)}), f32[32,8,128]{2,1,0:T(8,128)S(1)}, u32[]{:S(2)}, u32[]{:S(2)}) async-start(f32[32,8,128]{2,1,0:T(8,128)} %get-tuple-element.152), calls=%async_computation | async-start | bytes 262144 | tf_op jit(solution)/shard_map/all_to_all | solution.py:866
  78.6 6.1 %collective-permute-start.36 = (f32[192,256]{1,0:T(8,128)S(1)}, f32[192,256]{1,0:T(8,128)S(1)}, u32[]{:S(2)}, u32[]{:S(2)}) collective-permute-start(f32[192,256]{1,0:T(8,128)S(1)} %collective-permute-done.35.refs_2_), channel_id=1, source_target_pairs={{0,1},{1,0},{2,3},{3,2},{4,5},{5,4},{6,7},{7,6},{8,9},{9,8},{10,11... | collective-permute-start | bytes 589832 | tf_op jit(solution)/shard_map/ppermute | solution.py:70
  (19 other events, 336.8 us)
